TPU v7x, 32 devices: a whole 2x2x4 slice. The times are simulated.
32 devices in a mesh: shard: 4 (over z), ctx: 4 (over y, x), tp: 2 (over core).
Axes of the slice: x: 2, y: 2, z: 4, core: 2. Of those that a mesh axis runs over, the one named last changes fastest.
Arguments:
- seq_in: bfloat16 [4, 4096, 1024], P('shard', 'ctx'), may hold values from -6 to 6
- w_zx: bfloat16 [2, 1024, 2, 2048], P(None, 'shard', None, 'tp'), may hold values from -0.1875 to 0.1875
- w_bc: bfloat16 [2, 1024, 256], P(None, 'shard'), may hold values from -0.1875 to 0.1875
- w_dt: bfloat16 [2, 1024, 32], P(None, 'shard', 'tp'), may hold values from -0.1875 to 0.1875
- w_out: bfloat16 [2, 2048, 1024], P(None, 'tp', 'shard'), may hold values from -0.125 to 0.125
- norm_gain: float32 [2, 1024], replicated, may hold values from 0.5 to 1.5
- conv_x: float32 [2, 5, 2048], P(None, None, 'tp'), may hold values from -3 to 3
- conv_bc: float32 [2, 5, 256], replicated, may hold values from -3 to 3
- head_params: float32 [2, 3, 32], P(None, None, 'tp'), may hold values from -7 to 3
- gate_gain: float32 [2, 2048], P(None, 'tp'), may hold values from 0.5 to 1.5
- segments: int32 [4, 4096], P('shard'), may hold values from 0 to 8, as said below
- pad_mask: int32 [4, 4096], P('shard'), may hold values from 0 to 1, as said below
- cotangent: bfloat16 [4, 4096, 1024], P('shard', 'ctx'), may hold values from -6 to 6
Outputs:
- output: float32 [4, 4096, 1024], P('shard', 'ctx')
- input_grad: float32 [4, 4096, 1024], P('shard', 'ctx')
- grad_zx: float32 [2, 1024, 2, 2048], P(None, ('shard', 'ctx'), None, 'tp')
- grad_bc: float32 [2, 1024, 256], P(None, ('shard', 'ctx'))
- grad_dt: float32 [2, 1024, 32], P(None, ('shard', 'ctx'), 'tp')
- grad_out: float32 [2, 2048, 1024], P(None, 'tp', ('shard', 'ctx'))
- grad_norm_gain: float32 [2, 1024], replicated
- grad_conv_x: float32 [2, 5, 2048], P(None, None, 'tp')
- grad_conv_bc: float32 [2, 5, 256], replicated
- grad_head_params: float32 [2, 3, 32], P(None, None, 'tp')
- grad_gate_gain: float32 [2, 2048], P(None, 'tp')
Inputs may be any that keep to these rules, and one draw needn't show every extreme that they name: `segments`: within a sequence the numbers never fall; a sequence holds at most 8 documents, numbered below 8, and ends with one or more padding positions numbered 8. `pad_mask`: 0 exactly on the padding positions that end every sequence.
All inputs are finite; a program needn't handle non-finite values.
Results may differ from a plain program's by a relative error of at most 0.015.
Values may be sent and summed in bfloat16 or wider, within the bound.
No kernel may reach another device: no remote copies, remote signals or barrier semaphores. Data moves between devices by JAX's collectives and lax.ppermute only.
A program may use at most 768 MiB of HBM per device.

v0:
```python
import jax
import jax.numpy as jnp
from jax import lax
from jax.sharding import PartitionSpec as P

BLOCK = 256


EPSILON = 1e-05
PRECISE = lax.Precision.HIGHEST


def shifted(shard, axis, by):
    peers = lax.axis_size(axis)
    pairs = [(i, i + by) for i in range(peers) if 0 <= i + by < peers]
    return lax.ppermute(shard, axis, pairs)


def entering(shard, axis, join, neutral):
    place = lax.axis_index(axis)
    gathered = jax.tree.map(
        lambda a, kind: lax.all_gather(a.astype(kind), axis), shard, (jnp.bfloat16, jnp.bfloat16)
    )
    state = jax.tree.map(lambda a, e: jnp.zeros_like(a) + jnp.asarray(e, a.dtype), shard, neutral)

    def one(lap, state):
        return join(
            state,
            jax.tree.map(
                lambda a, own: lax.dynamic_index_in_dim(a, lap, 0, False).astype(own.dtype),
                gathered,
                shard,
            ),
        )

    return lax.fori_loop(0, place, one, state)


def carried_in(shard, axis, combine, identity):
    peers, place = (lax.axis_size(axis), lax.axis_index(axis))
    everything = jax.tree.map(
        lambda part, kind: lax.all_gather(part.astype(kind), axis),
        shard,
        jax.tree.map(lambda a: jnp.bfloat16 if a.dtype == jnp.float32 else a.dtype, shard),
    )
    start = jax.tree.map(
        lambda part, zero: jnp.broadcast_to(jnp.asarray(zero, part.dtype), part.shape),
        shard,
        identity,
    )

    def lap(k, before):
        at = peers - 1 - k
        reached = at > place
        new = combine(
            before, jax.tree.map(lambda part, own: part[at].astype(own.dtype), everything, shard)
        )
        return jax.tree.map(lambda a, b: jnp.where(reached, a, b), new, before)

    return lax.fori_loop(0, peers, lap, start)


def rounded(values):
    return lax.optimization_barrier(values.astype(jnp.bfloat16)).astype(jnp.float32)


def silu_slope(values):
    sigmoid_of = jax.nn.sigmoid(values)
    return sigmoid_of * (1.0 + values * (1.0 - sigmoid_of))


def conv_block(values, params, same_doc):
    length = same_doc.shape[2]
    summed = params[4]
    for shift_lag in range(4):
        summed = (
            summed
            + params[shift_lag]
            * values[:, 3 - shift_lag : 3 - shift_lag + length]
            * same_doc[shift_lag][:, :, None]
        )
    return jax.nn.silu(summed)


def block_step(running, pieces):
    state_now, factor, seg_last = running
    x_part, b_part, c_part, dt_part, rate_part, seg_part = pieces
    length = seg_part.shape[1]
    cumulative = jnp.cumsum(rate_part, axis=1)
    gaps = cumulative[:, :, None, :] - cumulative[:, None, :, :]
    causal = jnp.arange(length)[:, None] >= jnp.arange(length)[None, :]
    kept_pairs = (causal[None] & (seg_part[:, :, None] == seg_part[:, None, :]))[..., None]
    decays = jnp.where(kept_pairs, jnp.exp(jnp.where(kept_pairs, gaps, 0.0)), 0.0)
    intersection = jnp.einsum("btn,bsn->bts", c_part, b_part, precision=PRECISE)
    weighted = x_part * dt_part[..., None]
    result = jnp.einsum(
        "btsh,bshp->bthp", decays * intersection[..., None], weighted, precision=PRECISE
    )
    carried = (seg_part == seg_last[:, None]).astype(jnp.float32)[..., None] * jnp.exp(cumulative)
    result = result + carried[..., None] * jnp.einsum(
        "btn,bhpn->bthp", c_part, state_now, precision=PRECISE
    )
    tail_decay = (seg_part == seg_part[:, length - 1 :]).astype(jnp.float32)[..., None] * jnp.exp(
        cumulative[:, length - 1 :] - cumulative
    )
    state_next = carried[:, length - 1, :, None, None] * state_now + jnp.einsum(
        "bsh,bshp,bsn->bhpn", tail_decay, weighted, b_part, precision=PRECISE
    )
    return (
        (state_next, carried[:, length - 1] * factor, seg_part[:, length - 1]),
        (result, carried * factor[:, None, :]),
    )


def ssd_local(x_heads, b_in, c_in, dt_raw, head_rows, mask_rows, seg_rows, seg_prev):
    seq_count, row_count, head_count, head_width = x_heads.shape
    block_count = row_count // BLOCK
    step_size = jax.nn.softplus(dt_raw + head_rows[0]) * mask_rows[:, :, None]
    rates = -jnp.exp(head_rows[1]) * step_size

    def blocks(values):
        return jnp.moveaxis(
            values.reshape((seq_count, block_count, BLOCK) + values.shape[2:]), 1, 0
        )

    def rows_back(values):
        return jnp.moveaxis(values, 0, 1).reshape((seq_count, row_count) + values.shape[3:])

    start_state = (
        jnp.zeros((seq_count, head_count, head_width, b_in.shape[2]), jnp.float32),
        jnp.ones((seq_count, head_count), jnp.float32),
        seg_prev,
    )
    final_state, outputs = lax.scan(
        block_step,
        start_state,
        (
            blocks(x_heads),
            blocks(b_in),
            blocks(c_in),
            blocks(step_size),
            blocks(rates),
            blocks(seg_rows),
        ),
    )
    mixed_heads = rows_back(outputs[0]) + head_rows[2][:, None] * x_heads
    return (mixed_heads, final_state[0], final_state[1], rows_back(outputs[1]))


def inter_term(c_in, weight, state_in):
    return weight[..., None] * jnp.einsum("btn,bhpn->bthp", c_in, state_in, precision=PRECISE)


def carry_forward(earlier, later):
    return (earlier[0] * later[0], later[0][..., None, None] * earlier[1] + later[1])


def carry_backward(earlier, later):
    return (earlier[0] * later[0], later[1] + later[0][..., None, None] * earlier[1])


def per_device(
    seq_in,
    w_zx,
    w_bc,
    w_dt,
    w_out,
    norm_gain,
    conv_x,
    conv_bc,
    head_params,
    gate_gain,
    segments,
    pad_mask,
    cotangent,
):
    seq_count, row_count, model_width = seq_in.shape
    tp_size = lax.axis_size("tp")
    row_start = lax.axis_index("ctx") * row_count
    padded_ids = jnp.concatenate([jnp.full((seq_count, 3), -1, jnp.int32), segments], axis=1)
    seg_ext = lax.dynamic_slice_in_dim(padded_ids, row_start, row_count + 3, 1)
    seg_rows = seg_ext[:, 3:]
    seg_prev = seg_ext[:, 2]
    mask_rows = lax.dynamic_slice_in_dim(pad_mask, row_start, row_count, 1).astype(jnp.float32)
    same_doc = jnp.stack(
        [
            (seg_ext[:, 3 - shift_lag : 3 - shift_lag + row_count] == seg_rows).astype(jnp.float32)
            for shift_lag in range(4)
        ]
    )
    layer_count = w_zx.shape[0]
    hidden = seq_in.astype(jnp.float32)
    kept_list = []
    for layer_idx in range(layer_count):
        w_in, w_bcl, w_dtl, w_outl = (
            lax.all_gather(w_zx[layer_idx], "shard", axis=0, tiled=True),
            lax.all_gather(w_bc[layer_idx], "shard", axis=0, tiled=True),
            lax.all_gather(w_dt[layer_idx], "shard", axis=0, tiled=True),
            lax.all_gather(w_out[layer_idx], "shard", axis=1, tiled=True),
        )
        inner_width = w_in.shape[2]
        head_count = head_params.shape[2]
        head_width = inner_width // head_count
        state_width = w_bcl.shape[1] // 2
        norm_scale = lax.rsqrt(jnp.mean(hidden * hidden, axis=-1, keepdims=True) + EPSILON)
        lowered = (hidden * norm_scale * norm_gain[layer_idx]).astype(jnp.bfloat16)
        flat_rows = lowered.reshape(seq_count * row_count, model_width)
        projected = jnp.dot(
            flat_rows,
            w_in.reshape(model_width, 2 * inner_width),
            preferred_element_type=jnp.float32,
        ).reshape(seq_count, row_count, 2, inner_width)
        gate_raw = projected[:, :, 0]
        x_low = projected[:, :, 1].astype(jnp.bfloat16)
        bc_low = (
            jnp.dot(flat_rows, w_bcl, preferred_element_type=jnp.float32)
            .reshape(seq_count, row_count, 2 * state_width)
            .astype(jnp.bfloat16)
        )
        dt_raw = jnp.dot(flat_rows, w_dtl, preferred_element_type=jnp.float32).reshape(
            seq_count, row_count, head_count
        )
        x_edge, bc_edge = shifted((x_low[:, row_count - 3 :], bc_low[:, row_count - 3 :]), "ctx", 1)
        x_ext = jnp.concatenate([x_edge, x_low], axis=1).astype(jnp.float32)
        bc_ext = jnp.concatenate([bc_edge, bc_low], axis=1).astype(jnp.float32)

        def conv_local(values, params):
            return conv_block(values, params, same_doc)

        x_conv, x_pull = jax.vjp(conv_local, x_ext, conv_x[layer_idx])
        bc_conv, bc_pull = jax.vjp(conv_local, bc_ext, conv_bc[layer_idx])
        x_heads = rounded(x_conv).reshape(seq_count, row_count, head_count, head_width)
        bc_round = rounded(bc_conv)

        def scan_local(x_part, b_part, c_part, dt_part, head_rows):
            return ssd_local(
                x_part, b_part, c_part, dt_part, head_rows, mask_rows, seg_rows, seg_prev
            )

        c_in = bc_round[..., state_width:]
        local_out, ssd_pull = jax.vjp(
            scan_local, x_heads, bc_round[..., :state_width], c_in, dt_raw, head_params[layer_idx]
        )
        mixed_local, state_local, factor, weight = local_out
        prefix, state_in = entering(
            (factor, state_local),
            "ctx",
            carry_forward,
            (jnp.ones_like(factor), jnp.zeros_like(state_local)),
        )
        mixed_inter, inter_pull = jax.vjp(inter_term, c_in, weight, state_in)
        mixed_all = (mixed_local + mixed_inter).reshape(seq_count, row_count, inner_width)
        gated_out = mixed_all * jax.nn.silu(gate_raw)
        square_sum = lax.psum(jnp.sum(gated_out * gated_out, axis=-1), "tp")
        gate_scale = lax.rsqrt(square_sum / (inner_width * tp_size) + EPSILON)[..., None]
        normed = (gated_out * gate_scale * gate_gain[layer_idx]).astype(jnp.bfloat16)
        partial_out = jnp.dot(
            normed.reshape(seq_count * row_count, inner_width),
            w_outl,
            preferred_element_type=jnp.float32,
        )
        mixed_sum = lax.psum(partial_out.reshape(seq_count, row_count, model_width), "tp")
        kept_list.append(
            (
                hidden,
                norm_scale,
                flat_rows,
                gate_raw,
                mixed_all,
                gated_out,
                gate_scale,
                normed,
                w_in,
                w_bcl,
                w_dtl,
                w_outl,
                x_pull,
                bc_pull,
                ssd_pull,
                inter_pull,
                factor,
                state_in,
            )
        )
        hidden = hidden + mixed_sum
    upstream = cotangent.astype(jnp.float32)
    grads_big = []
    grads_small = []
    for layer_idx in reversed(range(layer_count)):
        (
            hidden_in,
            norm_scale,
            flat_rows,
            gate_raw,
            mixed_all,
            gated_out,
            gate_scale,
            normed,
            w_in,
            w_bcl,
            w_dtl,
            w_outl,
            x_pull,
            bc_pull,
            ssd_pull,
            inter_pull,
            factor,
            state_in,
        ) = kept_list[layer_idx]
        inner_width = w_in.shape[2]
        head_count = head_params.shape[2]
        head_width = inner_width // head_count
        up_low = upstream.astype(jnp.bfloat16).reshape(seq_count * row_count, model_width)
        grad_outl = jnp.einsum(
            "ti,td->id",
            normed.reshape(seq_count * row_count, inner_width),
            up_low,
            preferred_element_type=jnp.float32,
        )
        d_normed = jnp.einsum(
            "td,id->ti", up_low, w_outl, preferred_element_type=jnp.float32
        ).reshape(seq_count, row_count, inner_width)
        gain_row = gate_gain[layer_idx]
        grad_gain_gate = jnp.sum(d_normed * gated_out * gate_scale, axis=(0, 1))
        spread = lax.psum(jnp.sum(d_normed * gain_row * gated_out, axis=-1), "tp")
        d_gated = d_normed * gain_row * gate_scale - gated_out * (
            spread[..., None] * gate_scale**3 / (inner_width * tp_size)
        )
        d_mixed = (d_gated * jax.nn.silu(gate_raw)).reshape(
            seq_count, row_count, head_count, head_width
        )
        d_gate = (d_gated * mixed_all * silu_slope(gate_raw)).astype(jnp.bfloat16)
        dc_inter, d_weight, state_grad = inter_pull(d_mixed)
        prefix_back, later_grad = carried_in(
            (factor, state_grad),
            "ctx",
            carry_backward,
            (jnp.ones_like(factor), jnp.zeros_like(state_grad)),
        )
        d_factor = jnp.sum(later_grad * state_in, axis=(2, 3))
        d_xheads, d_bpart, d_cpart, d_dtraw, d_heads = ssd_pull(
            (d_mixed, later_grad, d_factor, d_weight)
        )
        d_bc = lax.psum(
            jnp.concatenate([d_bpart, d_cpart + dc_inter], axis=-1).astype(jnp.bfloat16), "tp"
        ).astype(jnp.float32)
        d_xext, d_convx = x_pull(d_xheads.reshape(seq_count, row_count, inner_width))
        d_bcext, d_convbc = bc_pull(d_bc)
        x_back, bc_back = shifted((d_xext[:, :3], d_bcext[:, :3]), "ctx", -1)
        d_xraw = d_xext[:, 3:].at[:, row_count - 3 :].add(x_back).astype(jnp.bfloat16)
        d_bcraw = d_bcext[:, 3:].at[:, row_count - 3 :].add(bc_back).astype(jnp.bfloat16)
        d_dtlow = d_dtraw.astype(jnp.bfloat16).reshape(seq_count * row_count, head_count)
        d_proj = jnp.stack([d_gate, d_xraw], axis=2).reshape(seq_count * row_count, 2 * inner_width)
        d_bcflat = d_bcraw.reshape(seq_count * row_count, d_bcraw.shape[2])
        grad_in = jnp.einsum(
            "td,tc->dc", flat_rows, d_proj, preferred_element_type=jnp.float32
        ).reshape(model_width, 2, inner_width)
        grad_bcl = jnp.einsum("td,tc->dc", flat_rows, d_bcflat, preferred_element_type=jnp.float32)
        grad_dtl = jnp.einsum("td,th->dh", flat_rows, d_dtlow, preferred_element_type=jnp.float32)
        d_part = jnp.einsum(
            "tc,dc->td",
            d_proj,
            w_in.reshape(model_width, 2 * inner_width),
            preferred_element_type=jnp.float32,
        )
        d_part = d_part + jnp.einsum(
            "th,dh->td", d_dtlow, w_dtl, preferred_element_type=jnp.float32
        )
        d_lowered = lax.psum(d_part.astype(jnp.bfloat16), "tp").astype(jnp.float32) + jnp.einsum(
            "tc,dc->td", d_bcflat, w_bcl, preferred_element_type=jnp.float32
        )
        d_lowered = d_lowered.reshape(seq_count, row_count, model_width)
        gain_in = norm_gain[layer_idx]
        grad_gain_in = jnp.sum(d_lowered * hidden_in * norm_scale, axis=(0, 1))
        inner_sum = jnp.sum(d_lowered * gain_in * hidden_in, axis=-1, keepdims=True)
        upstream = (
            upstream
            + d_lowered * gain_in * norm_scale
            - hidden_in * inner_sum * norm_scale**3 / model_width
        )
        small_sums = lax.psum(
            (grad_gain_in, d_convx, d_convbc, d_heads, grad_gain_gate), ("shard", "ctx")
        )
        owned = (
            lax.psum_scatter(grad_in, ("shard", "ctx"), scatter_dimension=0, tiled=True),
            lax.psum_scatter(grad_bcl, ("shard", "ctx"), scatter_dimension=0, tiled=True),
            lax.psum_scatter(grad_dtl, ("shard", "ctx"), scatter_dimension=0, tiled=True),
            lax.psum_scatter(grad_outl, ("shard", "ctx"), scatter_dimension=1, tiled=True),
        )
        grads_big.insert(0, owned)
        grads_small.insert(0, small_sums)
    grad_zx = jnp.stack([item[0] for item in grads_big])
    grad_bc = jnp.stack([item[1] for item in grads_big])
    grad_dt = jnp.stack([item[2] for item in grads_big])
    grad_out = jnp.stack([item[3] for item in grads_big])
    grad_norm_gain = jnp.stack([item[0] for item in grads_small])
    grad_conv_x = jnp.stack([item[1] for item in grads_small])
    grad_conv_bc = jnp.stack([item[2] for item in grads_small])
    grad_head_params = jnp.stack([item[3] for item in grads_small])
    grad_gate_gain = jnp.stack([item[4] for item in grads_small])
    return (
        hidden,
        upstream,
        grad_zx,
        grad_bc,
        grad_dt,
        grad_out,
        grad_norm_gain,
        grad_conv_x,
        grad_conv_bc,
        grad_head_params,
        grad_gate_gain,
    )


def solution(mesh):
    in_specs = (
        P("shard", "ctx", None),
        P(None, "shard", None, "tp"),
        P(None, "shard", None),
        P(None, "shard", "tp"),
        P(None, "tp", "shard"),
        P(),
        P(None, None, "tp"),
        P(),
        P(None, None, "tp"),
        P(None, "tp"),
        P("shard", None),
        P("shard", None),
        P("shard", "ctx", None),
    )
    out_specs = (
        P("shard", "ctx", None),
        P("shard", "ctx", None),
        P(None, ("shard", "ctx"), None, "tp"),
        P(None, ("shard", "ctx"), None),
        P(None, ("shard", "ctx"), "tp"),
        P(None, "tp", ("shard", "ctx")),
        P(),
        P(None, None, "tp"),
        P(),
        P(None, None, "tp"),
        P(None, "tp"),
    )
    return jax.shard_map(
        per_device, mesh=mesh, in_specs=in_specs, out_specs=out_specs, check_vma=False
    )
```

profile of v0, /device:TPU:1, one launch (start us, length us, event | category | flops | bytes accessed | tf_op | source)
XLA Modules:
  0.0 2904.5 jit_solution(8446126332712509849)
XLA Ops:
  11.2 15.7 all-gather.2
  34.3 12.4 all-gather
  58.4 37.8 %all-gather.25.cloned.1.call-done = bf16[1,1024,2,1024]{3,2,0,1:T(2,128)(2,1)} async-done(((bf16[1,256,2,1024]{3,2,0,1:T(2,128)(2,1)}), bf16[1,1024,2,1024]{3,2,0,1:T(2,128)(2,1)}) %all-gather.25.cloned.1.call-update) | async-done | bytes 4194320 | tf_op jit(solution)/shard_map/all_gather | solution.py:196
  187.7 259.6 %while.248 = (s32[]{:T(128)}, f32[1,16,64,128]{3,2,1,0:T(8,128)S(1)}, f32[1,16]{1,0:T(1,128)S(1)}, s32[1]{0:T(128)}, f32[4,1,256,16,64]{2,0,4,3,1:T(4,128)}, /*i...) while((s32[]{:T(128)}, ...), condition=%wide.region_4.6_spmd.clone, body=%wide.region_1.5_spmd.clone.sunk | while | flops 1723156480 | bytes 32647868 | solution.py:134
  209.0 23.4 dynamic_update_slice.596
  273.7 23.4 dynamic_update_slice.596
  338.7 23.4 dynamic_update_slice.596
  403.5 23.4 dynamic_update_slice.596
  504.4 18.3 all-gather.29.cloned.1.call-done
  530.7 12.1 all-gather.6
  542.8 20.2 all-gather.8
  563.0 50.1 %all-gather.31.cloned.1.call-done = bf16[1,1024,2,1024]{3,2,0,1:T(2,128)(2,1)} async-done(((bf16[1,256,2,1024]{3,2,0,1:T(2,128)(2,1)}), bf16[1,1024,2,1024]{3,2,0,1:T(2,128)(2,1)}) %all-gather.31.cloned.1.call-update) | async-done | bytes 4194320 | tf_op jit(solution)/shard_map/all_gather | solution.py:196
  625.6 17.8 all-reduce.58.cloned.1.call-done
  734.5 251.8 %while.249 = (s32[]{:T(128)}, f32[1,16,64,128]{3,2,1,0:T(8,128)S(1)}, f32[1,16]{1,0:T(1,128)S(1)}, s32[1]{0:T(128)}, f32[4,1,256,16,64]{2,0,4,3,1:T(4,128)}, /*i...) while((s32[]{:T(128)}, ...), condition=%wide.region_14.16_spmd.clone, body=%wide.region_11.15_spmd.clone.sunk | while | flops 1723156480 | bytes 32647300 | solution.py:134
  756.1 23.4 dynamic_update_slice.615
  818.9 23.4 dynamic_update_slice.615
  881.8 23.4 dynamic_update_slice.615
  944.4 23.4 dynamic_update_slice.615
  1040.2 23.2 all-gather.35.cloned.1.call-done
  1149.8 221.6 %while.246 = (s32[]{:T(128)}, f32[1,16,64,128]{3,2,1,0:T(8,128)S(1)}, f32[1,16]{1,0:T(1,128)S(1)}, f32[4,1,256,16,64]{2,4,3,1,0:T(8,128)}, bf16[4,1,256,128]{3,2...) while((s32[]{:T(128)}, ...), condition=%wide.region_37.39_spmd, body=%wide.region_26.38_spmd.sunk | while | flops 3434930176 | bytes 80856664 | solution.py:134
  1486.2 15.4 all-reduce.60.cloned.1.call-done
  1592.1 213.4 %while.247 = (s32[]{:T(128)}, f32[1,16,64,128]{3,2,1,0:T(8,128)S(1)}, f32[1,16]{1,0:T(1,128)S(1)}, f32[4,1,256,16,64]{2,4,3,1,0:T(8,128)}, bf16[4,1,256,128]{3,2...) while((s32[]{:T(128)}, ...), condition=%wide.region_58.60_spmd, body=%wide.region_47.59_spmd.sunk | while | flops 3434930176 | bytes 80856664 | solution.py:134
  1821.3 22.0 multiply_reduce_fusion.5
  1902.3 15.0 all-reduce.64.cloned.1.call-done
  1986.4 74.3 %reduce-scatter.25.cloned.1.call-done = f32[64,16]{1,0:T(8,128)} async-done(((f32[1024,16]{1,0:T(8,128)}), f32[64,16]{1,0:T(8,128)}) %reduce-scatter.25.cloned.1.call-update) | async-done | bytes 4112
  2067.6 114.7 %all-reduce.62.cloned.1.call-done = (f32[1,1024]{1,0:T(1,128)}, f32[1,1024]{1,0:T(1,128)}, f32[1,5,1024]{2,1,0:T(8,128)}, f32[1,5,1024]{2,1,0:T(8,128)}, f32[1,5...) async-done(((f32[1,1024]{1,0:T(1,128)}, f32[1,1024]{1,0:T(1,128)}, ...) | async-done | bytes 67984 | tf_op jit(solution)/shard_map/psum | solution.py:381
  2188.9 64.5 %reduce-scatter.19.cloned.1.call-done = f32[64,256]{1,0:T(8,128)} async-done(((f32[1024,256]{1,0:T(8,128)}), f32[64,256]{1,0:T(8,128)}) %reduce-scatter.19.cloned.1.call-update) | async-done | bytes 65552 | tf_op jit(solution)/shard_map/reduce_scatter | solution.py:386
  2253.5 76.3 %reduce-scatter.17.cloned.1.call-done = f32[64,256]{1,0:T(8,128)} async-done(((f32[1024,256]{1,0:T(8,128)}), f32[64,256]{1,0:T(8,128)}) %reduce-scatter.17.cloned.1.call-update) | async-done | bytes 65552 | tf_op jit(solution)/shard_map/reduce_scatter | solution.py:386
  2331.3 102.8 %reduce-scatter.23.cloned.1.call-done = f32[1024,64]{0,1:T(8,128)} async-done(((f32[1024,1024]{0,1:T(8,128)}), f32[1024,64]{0,1:T(8,128)}) %reduce-scatter.23.cloned.1.call-update) | async-done | bytes 262160 | tf_op jit(solution)/shard_map/reduce_scatter | solution.py:388
  2434.1 97.2 %reduce-scatter.21.cloned.1.call-done = f32[1024,64]{0,1:T(8,128)} async-done(((f32[1024,1024]{0,1:T(8,128)}), f32[1024,64]{0,1:T(8,128)}) %reduce-scatter.21.cloned.1.call-update) | async-done | bytes 262160 | tf_op jit(solution)/shard_map/reduce_scatter | solution.py:388
  2533.2 178.5 %reduce-scatter.15.cloned.1.call-done = f32[64,2,1024]{2,0,1:T(8,128)} async-done(((f32[1024,2,1024]{2,0,1:T(8,128)}), f32[64,2,1024]{2,0,1:T(8,128)}) %reduce-scatter.15.cloned.1.call-update) | async-done | bytes 524304 | tf_op jit(solution)/shard_map/reduce_scatter | solution.py:385
  2711.6 182.7 %reduce-scatter.13.cloned.1.call-done = f32[64,2,1024]{2,0,1:T(8,128)} async-done(((f32[1024,2,1024]{2,0,1:T(8,128)}), f32[64,2,1024]{2,0,1:T(8,128)}) %reduce-scatter.13.cloned.1.call-update) | async-done | bytes 524304 | tf_op jit(solution)/shard_map/reduce_scatter | solution.py:385
  (1428 shorter events, 1551.1 us)
Async XLA Ops:
  7.2 89.0 %all-gather.25.cloned.1.call-start = ((), (), s32[]{:S(2)}) async-start(), calls=%async_computation.16 | async-start | bytes 5242880 | tf_op jit(solution)/shard_map/all_gather | solution.py:196
  11.1 464.6 %all-gather.27.cloned.1.call-start = ((), (), s32[]{:S(2)}) async-start(), calls=%async_computation.17 | async-start | bytes 1310720 | tf_op jit(solution)/shard_map/all_gather | solution.py:22
  29.9 24.2 collective-permute-start.1
  48.1 619.2 %copy-start.70 = (f32[1,1024]{1,0:T(1,128)}, f32[1,1024]{1,0:T(1,128)S(1)}, u32[]{:S(2)}) copy-start(f32[1,1024]{1,0:T(1,128)S(1)} %get-tuple-element.4367) | copy-start | bytes 12292
  52.1 615.2 %copy-start.67 = (f32[1,1024]{1,0:T(1,128)}, f32[1,1024]{1,0:T(1,128)S(1)}, u32[]{:S(2)}) copy-start(f32[1,1024]{1,0:T(1,128)S(1)} %get-tuple-element.4482) | copy-start | bytes 12292
  52.2 615.2 %copy-start.73 = (f32[1,1024]{1,0:T(1,128)}, f32[1,1024]{1,0:T(1,128)S(1)}, u32[]{:S(2)}) copy-start(f32[1,1024]{1,0:T(1,128)S(1)} %get-tuple-element.4481) | copy-start | bytes 12292
  115.1 4.0 collective-permute-start
  448.2 74.5 %all-gather.29.cloned.1.call-start = ((), (), s32[]{:S(2)}) async-start(), calls=%async_computation.18 | async-start | bytes 2621440 | tf_op jit(solution)/shard_map/all_gather | solution.py:199
  450.5 162.6 %all-gather.31.cloned.1.call-start = ((), (), s32[]{:S(2)}) async-start(), calls=%async_computation.19 | async-start | bytes 5242880 | tf_op jit(solution)/shard_map/all_gather | solution.py:196
  451.1 192.4 %all-reduce.58.cloned.1.call-start = ((), (), s32[]{:S(2)}) async-start(), calls=%async_computation.8 | async-start | bytes 8388608 | tf_op jit(solution)/shard_map/psum | solution.py:262
  530.0 489.4 %all-gather.33.cloned.1.call-start = ((), (), s32[]{:S(2)}) async-start(), calls=%async_computation.20 | async-start | bytes 1310720 | tf_op jit(solution)/shard_map/all_gather | solution.py:22
  655.5 11.2 collective-permute-start.2
  659.8 4.5 collective-permute-start.3
  987.2 76.2 %all-gather.35.cloned.1.call-start = ((), (), s32[]{:S(2)}) async-start(), calls=%async_computation.21 | async-start | bytes 2621440 | tf_op jit(solution)/shard_map/all_gather | solution.py:199
  987.9 153.3 %all-gather.37.cloned.1.call-start = ((), (), s32[]{:S(2)}) async-start(), calls=%async_computation.22 | async-start | bytes 1310720 | tf_op jit(solution)/shard_map/all_gather | solution.py:42
  1116.5 353.2 %all-reduce.66.cloned.1.call-start = ((), (), s32[]{:S(2)}) async-start(), calls=%async_computation.28 | async-start | bytes 5242880 | tf_op jit(solution)/shard_map/psum | solution.py:369
  1415.7 6.7 collective-permute-start.4
  1444.8 56.8 %all-reduce.60.cloned.1.call-start = ((), (), s32[]{:S(2)}) async-start(), calls=%async_computation.9 | async-start | bytes 8388608 | tf_op jit(solution)/shard_map/psum | solution.py:262
  1451.6 130.8 %all-gather.39.cloned.1.call-start = ((), (), s32[]{:S(2)}) async-start(), calls=%async_computation.23 | async-start | bytes 1310720 | tf_op jit(solution)/shard_map/all_gather | solution.py:42
  1472.2 4.6 collective-permute-start.5
  1554.8 362.4 %all-reduce.64.cloned.1.call-start = ((), (), s32[]{:S(2)}) async-start(), calls=%async_computation.27 | async-start | bytes 5242880 | tf_op jit(solution)/shard_map/psum | solution.py:369
  1865.5 4.5 collective-permute-start.6
  1892.5 93.1 %reduce-scatter.27.cloned.1.call-start = ((), (), s32[]{:S(2)}) async-start(), calls=%async_computation.25 | async-start | bytes 557056
  1896.3 164.4 %reduce-scatter.25.cloned.1.call-start = ((), (), s32[]{:S(2)}) async-start(), calls=%async_computation.24 | async-start | bytes 557056
  1900.9 281.4 %all-reduce.62.cloned.1.call-start = ((), (), s32[]{:S(2)}) async-start(), calls=%async_computation.26 | async-start | bytes 204800 | tf_op jit(solution)/shard_map/psum | solution.py:381
  1921.2 4.6 collective-permute-start.7
  1932.6 320.8 %reduce-scatter.19.cloned.1.call-start = ((), (), s32[]{:S(2)}) async-start(), calls=%async_computation.13 | async-start | bytes 1114112 | tf_op jit(solution)/shard_map/reduce_scatter | solution.py:386
  1936.1 393.7 %reduce-scatter.17.cloned.1.call-start = ((), (), s32[]{:S(2)}) async-start(), calls=%async_computation.12 | async-start | bytes 1114112 | tf_op jit(solution)/shard_map/reduce_scatter | solution.py:386
  1938.1 496.0 %reduce-scatter.23.cloned.1.call-start = ((), (), s32[]{:S(2)}) async-start(), calls=%async_computation.15 | async-start | bytes 4456448 | tf_op jit(solution)/shard_map/reduce_scatter | solution.py:388
  1945.7 585.6 %reduce-scatter.21.cloned.1.call-start = ((), (), s32[]{:S(2)}) async-start(), calls=%async_computation.14 | async-start | bytes 4456448 | tf_op jit(solution)/shard_map/reduce_scatter | solution.py:388
  1954.4 757.3 %reduce-scatter.15.cloned.1.call-start = ((), (), s32[]{:S(2)}) async-start(), calls=%async_computation.11 | async-start | bytes 8912896 | tf_op jit(solution)/shard_map/reduce_scatter | solution.py:385
  1965.1 929.2 %reduce-scatter.13.cloned.1.call-start = ((), (), s32[]{:S(2)}) async-start(), calls=%async_computation.10 | async-start | bytes 8912896 | tf_op jit(solution)/shard_map/reduce_scatter | solution.py:385
  (188 other events, 3329.4 us)
Sparse Core Ops, SparseCore 0:
  11.2 85.0 all-gather.24
  448.3 27.2 all-gather.26
  477.1 45.5 all-gather.28
  524.7 88.3 all-gather.30
  616.0 27.3 all-reduce.57
  987.3 28.2 all-gather.32
  1017.8 45.5 all-gather.34
  1116.6 24.5 all-gather.36
  1444.9 24.6 all-reduce.65
  1472.0 29.6 all-reduce.59
  1554.9 27.3 all-gather.38
  1892.5 24.6 all-reduce.63
  1919.5 66.0 reduce-scatter.26
  1987.8 72.8 reduce-scatter.24
  2068.1 114.1 all-reduce.61
  2185.1 68.3 reduce-scatter.18
  2255.6 74.1 reduce-scatter.16
  2332.0 102.0 reduce-scatter.22
  2436.5 94.7 reduce-scatter.20
  2533.5 178.0 reduce-scatter.14
  2714.0 180.2 reduce-scatter.12
where the time goes:
time: 2930 us; the launch traced here: 2900 us
  waiting for transfers between devices  1110 us (38%)
  local copies, waits for them, and re-layouts  810 us (28%)
  matrix products  491 us (17%)
  other arithmetic  358 us (12%)
  blocking collectives  92.2 us (3%)
    reduce_scatter x2, waiting for transfers between devices, per_device(): lax.psum_scatter(grad_in, ('shard', 'ctx'), scatter_dimension=0, tiled=True)  361 us
    dynamic_update_slice x128, local copies, waits for them, and re-layouts, ssd_local(): lax.scan(block_step, start_state, (blocks(x_heads), blocks(b_in), blocks(...  302 us
    reduce_scatter x2, waiting for transfers between devices, per_device(): lax.psum_scatter(grad_outl, ('shard', 'ctx'), scatter_dimension=1, tiled=...  200 us
    dot_general x24, matrix products, block_step(): jnp.einsum('btsh,bshp->bthp', decays * intersection[..., None], weighted,...  185 us
    reduce_scatter x2, waiting for transfers between devices, per_device(): lax.psum_scatter(grad_bcl, ('shard', 'ctx'), scatter_dimension=0, tiled=T...  141 us
    psum x1, waiting for transfers between devices, per_device(): lax.psum((grad_gain_in, d_convx, d_convbc, d_heads, grad_gain_gate), ('sh...  115 us
    another operation x152, local copies, waits for them, and re-layouts  107 us
    dynamic_slice x104, local copies, waits for them, and re-layouts, ssd_local(): lax.scan(block_step, start_state, (blocks(x_heads), blocks(b_in), blocks(...  105 us
  transfers between devices with their start and end apart: 29, of which 22 were waited for; matrix products, arithmetic and copies ran while one was open for 9% of the time, Pallas kernels for 0%

commit v1 on v0

v1 whole, which is shorter than its diff:
```python
import functools

import jax
import jax.numpy as jnp
from jax import lax
from jax.experimental import pallas as pl
from jax.experimental.pallas import tpu as pltpu
from jax.sharding import PartitionSpec as P

EPSILON = 1e-05
EXACT = lax.Precision.HIGHEST
F32 = jnp.float32
BF16 = jnp.bfloat16
CHUNK = 128
LANES = 128
EDGE = 8
CLOSED = -1e30
VMEM = 48 << 20


def dot(a, b, dims=((1,), (0,)), precision=None):
    return lax.dot_general(a, b, (dims, ((), ())), precision=precision, preferred_element_type=F32)


def split(values):
    high = values.astype(BF16)
    return high, (values - high.astype(F32)).astype(BF16)


def expand(values, spread):
    high, rest = split(values)
    return dot(high, spread) + dot(rest, spread)


def head_sum(values, spread):
    high, rest = split(values)
    return dot(high, spread, ((1,), (1,))) + dot(rest, spread, ((1,), (1,)))


def conv_shifts(ext, same):
    return [ext[EDGE:]] + [pltpu.roll(ext, lag, 0)[EDGE:] * same[lag] for lag in (1, 2, 3)]


def conv_sum(shifts, taps):
    total = taps[4:5] + taps[0:1] * shifts[0]
    for lag in (1, 2, 3):
        total = total + taps[lag : lag + 1] * shifts[lag]
    return total


def same_columns(cols, width):
    return [None] + [jnp.broadcast_to(cols[:, lag - 1 : lag], (cols.shape[0], width)) for lag in (1, 2, 3)]


def pair_masked(values):
    lane = lax.broadcasted_iota(jnp.int32, values.shape, 1)
    zero = jnp.zeros_like(values)
    first = lane < LANES // 2
    return jnp.concatenate([jnp.where(first, values, zero), jnp.where(first, zero, values)], axis=0)


def pairs_bias(seg_col, seg_row, later_rows):
    size = seg_col.shape[0]
    row = lax.broadcasted_iota(jnp.int32, (size, size), 0)
    col = lax.broadcasted_iota(jnp.int32, (size, size), 1)
    ordered = (row >= col) if later_rows else (row <= col)
    return jnp.where(ordered & (seg_col == seg_row), 0.0, CLOSED)


def silu_parts(values):
    sig = jax.nn.sigmoid(values)
    return sig, values * sig


def call(body, grid, ins, outs, scratch=(), scalars=None, flops=0, name=None):
    count = 0 if scalars is None else 1

    def adapt(block, fn):
        if block is None:
            return pl.BlockSpec(memory_space=pl.ANY)
        return pl.BlockSpec(block, fn)

    in_specs = [adapt(block, fn) for _, block, fn in ins]
    out_specs = [adapt(block, fn) for _, _, block, fn in outs]
    shapes = [jax.ShapeDtypeStruct(shape, dtype) for shape, dtype, _, _ in outs]
    moved = sum(a.size * a.dtype.itemsize for a, _, _ in ins) + sum(
        s.size * s.dtype.itemsize for s in shapes
    )
    made = pl.pallas_call(
        body,
        out_shape=shapes,
        grid_spec=pltpu.PrefetchScalarGridSpec(
            num_scalar_prefetch=count,
            grid=grid,
            in_specs=in_specs,
            out_specs=out_specs,
            scratch_shapes=list(scratch),
        ),
        compiler_params=pltpu.CompilerParams(
            vmem_limit_bytes=VMEM, dimension_semantics=("arbitrary",) * len(grid)
        ),
        cost_estimate=pl.CostEstimate(flops=int(flops), bytes_accessed=int(moved), transcendentals=0),
        name=name,
    )
    arrays = [a for a, _, _ in ins]
    return made(*(([scalars] if count else []) + arrays))


def rows_at(i, *_):
    return (i, 0)


def fixed(*_):
    return (0, 0)


def enter_body(first, inner_total, *refs):
    if first:
        h_ref, gain, w_main, w_other, u_ref, x_ref, mine_ref, other_ref, dt_ref = refs
        hidden = h_ref[...].astype(F32)
    else:
        (h_ref, p_ref, q_ref, s_ref, t_ref, gain, w_main, w_other) = refs[:8]
        (h_out, u_ref, x_ref, mine_ref, other_ref, dt_ref) = refs[8:]
        scale = lax.rsqrt((s_ref[...] + t_ref[...])[:, :1] / inner_total + EPSILON)
        hidden = h_ref[...].astype(F32) + scale * (p_ref[...].astype(F32) + q_ref[...].astype(F32))
        h_out[...] = hidden
    norm = lax.rsqrt(jnp.mean(hidden * hidden, axis=1, keepdims=True) + EPSILON)
    lowered = (hidden * norm * gain[0:1]).astype(BF16)
    u_ref[...] = lowered
    width = x_ref.shape[1]
    state = mine_ref.shape[1]
    made = dot(lowered, w_main[...])
    x_ref[...] = made[:, :width].astype(BF16)
    mine_ref[...] = made[:, width : width + state].astype(BF16)
    dt_ref[...] = made[:, width + state :]
    other_ref[...] = dot(lowered, w_other[...]).astype(BF16)


def enter(hidden, parts, gain, w_main, w_other, width, inner_total):
    rows, model = hidden.shape
    state = w_other.shape[1]
    block = min(256, rows)
    wide = (block, model)
    ins = [(hidden, wide, rows_at)]
    outs = []
    if parts is not None:
        ins += [(parts[0], wide, rows_at), (parts[1], wide, rows_at)]
        ins += [(parts[2], (block, LANES), rows_at), (parts[3], (block, LANES), rows_at)]
        outs.append(((rows, model), F32, wide, rows_at))
    ins += [
        (gain, gain.shape, fixed),
        (w_main, w_main.shape, fixed),
        (w_other, w_other.shape, fixed),
    ]
    outs += [
        ((rows, model), BF16, wide, rows_at),
        ((rows, width), BF16, (block, width), rows_at),
        ((rows, state), BF16, (block, state), rows_at),
        ((rows, state), BF16, (block, state), rows_at),
        ((rows, LANES), F32, (block, LANES), rows_at),
    ]
    flops = 2 * rows * model * (w_main.shape[1] + state)
    made = call(
        functools.partial(enter_body, parts is None, inner_total), (rows // block,), ins, outs, flops=flops, name="enter"
    )
    return made if parts is not None else [hidden] + list(made)


def states_body(
    flag, x_ref, mine_ref, other_ref, dt_ref, edge_ref, cols_ref, taps_ref, taps_bc_ref, head_ref,
    spread_ref, lower_ref, xc_ref, bc_ref, step_ref, cum_ref, enter_ref, phi_ref, last_ref,
    tail_x, tail_bc, state, phi,
):
    chunk = pl.program_id(0)
    width = x_ref.shape[1]
    ns = mine_ref.shape[1]

    @pl.when(chunk == 0)
    def _():
        tail_x[...] = edge_ref[:, :width].astype(F32)
        tail_bc[...] = edge_ref[:, width:].astype(F32)
        state[...] = jnp.zeros_like(state)
        phi[...] = jnp.ones_like(phi)

    cols = cols_ref[...]
    same = same_columns(cols, LANES)
    dt = jax.nn.softplus(dt_ref[...] + head_ref[0:1]) * cols[:, 3:4]
    rates = head_ref[1:2] * dt
    cum = dot(lower_ref[...], rates, precision=EXACT)
    step_ref[...] = dt
    cum_ref[...] = cum
    size = cum.shape[0]
    tail_dt = cols[:, 5:6] * jnp.exp(cum[size - 1 : size] - cum) * dt
    tail_wide = expand(tail_dt, spread_ref[...])
    fold = cols[size - 1 : size, 4:5] * jnp.exp(cum[size - EDGE : size])[EDGE - 1 : EDGE]
    fold_rows = jnp.broadcast_to(fold, phi.shape)
    fold_wide = expand(fold_rows, spread_ref[...])[0:1]

    halves = []
    for i, source in enumerate((mine_ref, other_ref)):
        part = slice(i * ns, (i + 1) * ns)
        now = source[...].astype(F32)
        shifts = conv_shifts(jnp.concatenate([tail_bc[:, part], now], axis=0), same)
        tail_bc[:, part] = now[size - EDGE :]
        halves.append(silu_parts(conv_sum(shifts, taps_bc_ref[:, part]))[1].astype(BF16))
    swap = flag[0] != 0
    b_part = jnp.where(swap, halves[1].astype(F32), halves[0].astype(F32)).astype(BF16)
    c_part = jnp.where(swap, halves[0].astype(F32), halves[1].astype(F32)).astype(BF16)
    bc_ref[:, :ns] = b_part
    bc_ref[:, ns:] = c_part
    b_turned = b_part.astype(F32).T.astype(BF16)

    enter_ref[0] = state[...].astype(BF16)
    phi_ref[0] = phi[...]
    for i in range(width // LANES):
        part = slice(i * LANES, (i + 1) * LANES)
        now = x_ref[:, part].astype(F32)
        shifts = conv_shifts(jnp.concatenate([tail_x[:, part], now], axis=0), same)
        tail_x[:, part] = now[size - EDGE :]
        x_conv = silu_parts(conv_sum(shifts, taps_ref[:, part]))[1].astype(BF16)
        xc_ref[:, part] = x_conv
        held = (x_conv.astype(F32) * tail_wide[:, part]).astype(BF16)
        state[:, part] = fold_wide[:, part] * state[:, part] + dot(b_turned, held)
    phi[...] = phi[...] * fold_rows

    @pl.when(chunk == pl.num_programs(0) - 1)
    def _():
        last_ref[:ns] = state[...].astype(BF16)
        last_ref[ns:] = expand(phi[...], spread_ref[...]).astype(BF16)


def states(flag, x_raw, mine, other, dt_raw, edge, cols, taps, taps_bc, head, spread, lower):
    rows, width = x_raw.shape
    ns = mine.shape[1]
    count = rows // CHUNK
    ins = [
        (x_raw, (CHUNK, width), rows_at),
        (mine, (CHUNK, ns), rows_at),
        (other, (CHUNK, ns), rows_at),
        (dt_raw, (CHUNK, LANES), rows_at),
        (edge, edge.shape, fixed),
        (cols, (CHUNK, cols.shape[1]), rows_at),
        (taps, taps.shape, fixed),
        (taps_bc, taps_bc.shape, fixed),
        (head, head.shape, fixed),
        (spread, spread.shape, fixed),
        (lower, lower.shape, fixed),
    ]
    outs = [
        ((rows, width), BF16, (CHUNK, width), rows_at),
        ((rows, 2 * ns), BF16, (CHUNK, 2 * ns), rows_at),
        ((rows, LANES), F32, (CHUNK, LANES), rows_at),
        ((rows, LANES), F32, (CHUNK, LANES), rows_at),
        ((count, ns, width), BF16, (1, ns, width), lambda i, *_: (i, 0, 0)),
        ((count, EDGE, LANES), F32, (1, EDGE, LANES), lambda i, *_: (i, 0, 0)),
        ((ns + EDGE, width), BF16, (ns + EDGE, width), fixed),
    ]
    scratch = [
        pltpu.VMEM((EDGE, width), F32),
        pltpu.VMEM((EDGE, 2 * ns), F32),
        pltpu.VMEM((ns, width), F32),
        pltpu.VMEM((EDGE, LANES), F32),
    ]
    return call(states_body, (count,), ins, outs, scratch, flag, flops=2 * rows * width * ns * 4, name="states")


def within_body(xc_ref, bc_ref, step_ref, cum_ref, cols_ref, segs_ref, spread_ref, y_ref):
    ns = bc_ref.shape[1] // 2
    width = xc_ref.shape[1]
    cum = cum_ref[...]
    cum_rows = cum.T
    bias = pairs_bias(cols_ref[:, 7:8], segs_ref[0:1], True)
    both = dot(bc_ref[:, ns:], bc_ref[:, :ns], ((1,), (1,)))
    step_wide = expand(step_ref[...], spread_ref[...])
    for pair in range(width // LANES):
        part = slice(pair * LANES, (pair + 1) * LANES)
        weighted = (xc_ref[:, part].astype(F32) * step_wide[:, part]).astype(BF16)
        maps = []
        for head in (2 * pair, 2 * pair + 1):
            gap = (cum[:, head : head + 1] - cum_rows[head : head + 1]) + bias
            maps.append((jnp.exp(gap) * both).astype(BF16))
        y_ref[:, part] = dot(jnp.concatenate(maps, axis=1), pair_masked(weighted))


def within(xc, bc, step, cum, cols, segs, spread):
    rows, width = xc.shape
    ins = [
        (xc, (CHUNK, width), rows_at),
        (bc, (CHUNK, bc.shape[1]), rows_at),
        (step, (CHUNK, LANES), rows_at),
        (cum, (CHUNK, LANES), rows_at),
        (cols, (CHUNK, cols.shape[1]), rows_at),
        (segs, (EDGE, CHUNK), lambda i, *_: (0, i)),
        (spread, spread.shape, fixed),
    ]
    outs = [((rows, width), F32, (CHUNK, width), rows_at)]
    return call(within_body, (rows // CHUNK,), ins, outs, flops=2 * rows * CHUNK * width * 4, name="within")[0]


def leave_body(
    y_ref, xc_ref, bc_ref, cum_ref, cols_ref, enter_ref, phi_ref, in_ref, gate_ref, rows_ref, spread_ref, w_ref,
    ssm_ref, p_ref, sq_ref, normed,
):
    ns = in_ref.shape[0]
    width = xc_ref.shape[1]
    spread = spread_ref[...]
    for sub in range(y_ref.shape[0] // CHUNK):
        here = slice(sub * CHUNK, (sub + 1) * CHUNK)
        phi_wide = expand(phi_ref[sub], spread)[0:1]
        begun = (enter_ref[sub].astype(F32) + phi_wide * in_ref[...]).astype(BF16)
        carried = cols_ref[here, 4:5] * jnp.exp(cum_ref[here])
        carried_wide = expand(carried, spread)
        far = dot(bc_ref[here, ns:], begun)
        ssm_ref[here] = y_ref[here] + carried_wide * far
    total = jnp.zeros((y_ref.shape[0], LANES), F32)
    for i in range(width // LANES):
        part = slice(i * LANES, (i + 1) * LANES)
        mixed = ssm_ref[:, part] + rows_ref[1:2, part] * xc_ref[:, part].astype(F32)
        gated = mixed * silu_parts(gate_ref[:, part])[1]
        total = total + gated * gated
        normed[:, part] = (gated * rows_ref[0:1, part]).astype(BF16)
    sq_ref[...] = jnp.broadcast_to(jnp.sum(total, axis=1, keepdims=True), total.shape)
    p_ref[...] = dot(normed[...], w_ref[...]).astype(BF16)


def leave(y_in, xc, bc, cum, cols, entered, phi, state_in, gate, rowpack, spread, w_out):
    rows, width = xc.shape
    model = w_out.shape[1]
    ns = state_in.shape[0]
    block = min(256, rows)
    subs = block // CHUNK
    ins = [
        (y_in, (block, width), rows_at),
        (xc, (block, width), rows_at),
        (bc, (block, bc.shape[1]), rows_at),
        (cum, (block, LANES), rows_at),
        (cols, (block, cols.shape[1]), rows_at),
        (entered, (subs, ns, width), lambda i, *_: (i, 0, 0)),
        (phi, (subs, EDGE, LANES), lambda i, *_: (i, 0, 0)),
        (state_in, state_in.shape, fixed),
        (gate, (block, width), rows_at),
        (rowpack, rowpack.shape, fixed),
        (spread, spread.shape, fixed),
        (w_out, w_out.shape, fixed),
    ]
    outs = [
        ((rows, width), F32, (block, width), rows_at),
        ((rows, model), BF16, (block, model), rows_at),
        ((rows, LANES), F32, (block, LANES), rows_at),
    ]
    scratch = [pltpu.VMEM((block, width), BF16)]
    return call(leave_body, (rows // block,), ins, outs, scratch, flops=2 * rows * width * model * 1.3, name="leave")


def back_gate_body(
    inner_total, up_ref, p_ref, q_ref, s_ref, t_ref, ssm_ref, xc_ref, gate_ref, bc_ref, cum_ref, cols_ref, phi_ref,
    factor_ref, rows_ref, spread_ref, w_ref,
    do_ref, dy_ref, dgate_ref, n_ref, gain_ref, out_ref, state,
):
    step = pl.program_id(0)
    ns = state.shape[0]
    width = xc_ref.shape[1]
    spread = spread_ref[...]

    @pl.when(step == 0)
    def _():
        gain_ref[...] = jnp.zeros_like(gain_ref)
        state[...] = jnp.zeros_like(state)

    scale = lax.rsqrt((s_ref[...] + t_ref[...])[:, :1] / inner_total + EPSILON)
    up = up_ref[...].astype(BF16)
    do_ref[...] = up
    summed = p_ref[...].astype(F32) + q_ref[...].astype(F32)
    spread_sum = jnp.sum(up.astype(F32) * summed, axis=1, keepdims=True)
    pull = scale * scale * scale * spread_sum / inner_total
    scale_wide = jnp.broadcast_to(scale, (scale.shape[0], LANES))
    pull_wide = jnp.broadcast_to(pull, scale_wide.shape)
    back = dot(up, w_ref[...], ((1,), (1,)))
    for i in range(width // LANES):
        part = slice(i * LANES, (i + 1) * LANES)
        gain = rows_ref[0:1, part]
        gate = gate_ref[:, part]
        sig, soft = silu_parts(gate)
        mixed = ssm_ref[:, part] + rows_ref[1:2, part] * xc_ref[:, part].astype(F32)
        gated = mixed * soft
        scaled = gated * scale_wide
        grad = back[:, part]
        gain_ref[0:1, part] += jnp.sum(grad * scaled, axis=0, keepdims=True)
        grad_gated = grad * gain * scale_wide - gated * pull_wide
        dy_ref[:, part] = (grad_gated * soft).astype(BF16)
        dgate_ref[:, part] = (grad_gated * mixed * (sig * (1.0 + gate * (1.0 - sig)))).astype(BF16)
        n_ref[:, part] = (scaled * gain).astype(BF16)
    for sub in range(up_ref.shape[0] // CHUNK):
        here = slice(sub * CHUNK, (sub + 1) * CHUNK)
        phi_wide = expand(phi_ref[sub], spread)[0:1]
        carried_wide = expand(cols_ref[here, 4:5] * jnp.exp(cum_ref[here]), spread)
        c_turned = bc_ref[here, ns:].astype(F32).T.astype(BF16)
        carried_dy = (dy_ref[here].astype(F32) * carried_wide).astype(BF16)
        state[...] += phi_wide * dot(c_turned, carried_dy)

    @pl.when(step == pl.num_programs(0) - 1)
    def _():
        out_ref[:ns] = state[...].astype(BF16)
        out_ref[ns:] = factor_ref[...]


def back_gate(up, parts, ssm, xc, gate, bc, cum, cols, phi, ended, rowpack, spread, w_out, inner_total):
    rows, width = xc.shape
    model = w_out.shape[1]
    ns = bc.shape[1] // 2
    block = min(256, rows)
    subs = block // CHUNK
    wide = (block, model)
    ins = [
        (up, wide, rows_at),
        (parts[0], wide, rows_at),
        (parts[1], wide, rows_at),
        (parts[2], (block, LANES), rows_at),
        (parts[3], (block, LANES), rows_at),
        (ssm, (block, width), rows_at),
        (xc, (block, width), rows_at),
        (gate, (block, width), rows_at),
        (bc, (block, 2 * ns), rows_at),
        (cum, (block, LANES), rows_at),
        (cols, (block, cols.shape[1]), rows_at),
        (phi, (subs, EDGE, LANES), lambda i, *_: (i, 0, 0)),
        (ended, (EDGE, width), lambda i, *_: (ns // EDGE, 0)),
        (rowpack, rowpack.shape, fixed),
        (spread, spread.shape, fixed),
        (w_out, w_out.shape, fixed),
    ]
    outs = [
        ((rows, model), BF16, wide, rows_at),
        ((rows, width), BF16, (block, width), rows_at),
        ((rows, width), BF16, (block, width), rows_at),
        ((rows, width), BF16, (block, width), rows_at),
        ((EDGE, width), F32, (EDGE, width), fixed),
        ((ns + EDGE, width), BF16, (ns + EDGE, width), fixed),
    ]
    scratch = [pltpu.VMEM((ns, width), F32)]
    return call(
        functools.partial(back_gate_body, inner_total), (rows // block,), ins, outs, scratch,
        flops=2 * rows * width * model * 1.3, name="back_gate",
    )


def back_within_body(
    xc_ref, bc_ref, step_ref, cum_ref, cols_ref, segs_ref, spread_ref, dy_ref, dx_ref, left_ref, dbc_ref
):
    ns = bc_ref.shape[1] // 2
    width = xc_ref.shape[1]
    size = xc_ref.shape[0]
    spread = spread_ref[...]
    cum = cum_ref[...]
    cum_rows = cum.T
    bias = pairs_bias(cols_ref[:, 7:8], segs_ref[0:1], False)
    b_part = bc_ref[:, :ns]
    c_part = bc_ref[:, ns:]
    both = dot(b_part, c_part, ((1,), (1,)))
    step_wide = expand(step_ref[...], spread)
    grad_both = jnp.zeros((size, size), F32)
    left = jnp.zeros((size, LANES), F32)
    for pair in range(width // LANES):
        part = slice(pair * LANES, (pair + 1) * LANES)
        weighted = (xc_ref[:, part].astype(F32) * step_wide[:, part]).astype(BF16)
        dy_pair = pair_masked(dy_ref[:, part])
        grad_maps = dot(weighted, dy_pair, ((1,), (1,)))
        maps = []
        for k in (0, 1):
            head = 2 * pair + k
            decay = jnp.exp((cum_rows[head : head + 1] - cum[:, head : head + 1]) + bias)
            maps.append((decay * both).astype(BF16))
            grad_both = grad_both + decay * grad_maps[:, k * size : (k + 1) * size]
        grad_x = dot(jnp.concatenate(maps, axis=1), dy_pair)
        dx_ref[:, part] = grad_x.astype(BF16)
        left = left + head_sum(weighted.astype(F32) * grad_x, spread[:, part])
    left_ref[...] = left
    grad_low = grad_both.astype(BF16)
    dbc_ref[:, :ns] = dot(grad_low, c_part)
    dbc_ref[:, ns:] = dot(grad_both.T.astype(BF16), b_part)


def back_within(xc, bc, step, cum, cols, segs, spread, dy):
    rows, width = xc.shape
    ins = [
        (xc, (CHUNK, width), rows_at),
        (bc, (CHUNK, bc.shape[1]), rows_at),
        (step, (CHUNK, LANES), rows_at),
        (cum, (CHUNK, LANES), rows_at),
        (cols, (CHUNK, cols.shape[1]), rows_at),
        (segs, (EDGE, CHUNK), lambda i, *_: (0, i)),
        (spread, spread.shape, fixed),
        (dy, (CHUNK, width), rows_at),
    ]
    outs = [
        ((rows, width), BF16, (CHUNK, width), rows_at),
        ((rows, LANES), F32, (CHUNK, LANES), rows_at),
        ((rows, bc.shape[1]), F32, (CHUNK, bc.shape[1]), rows_at),
    ]
    return call(back_within_body, (rows // CHUNK,), ins, outs, flops=2 * rows * CHUNK * width * 8, name="back_within")


def conv_back(ext, same, taps, grad_conv, next_rows):
    size = ext.shape[0] - EDGE
    shifts = conv_shifts(ext, same)
    pre = conv_sum(shifts, taps)
    sig = jax.nn.sigmoid(pre)
    grad_pre = grad_conv * (sig * (1.0 + pre * (1.0 - sig)))
    sums = [jnp.sum(grad_pre * shifts[lag], axis=0, keepdims=True) for lag in range(4)]
    sums.append(jnp.sum(grad_pre, axis=0, keepdims=True))
    zero = jnp.zeros((EDGE, ext.shape[1]), F32)
    length = size + 2 * EDGE
    raw = taps[0:1] * jnp.concatenate([zero, grad_pre], axis=0)
    firsts = []
    for lag in (1, 2, 3):
        term = grad_pre * same[lag] * taps[lag : lag + 1]
        firsts.append(term[:EDGE])
        padded = jnp.concatenate([zero, term, next_rows[lag - 1]], axis=0)
        raw = raw + pltpu.roll(padded, length - lag, 0)[: size + EDGE]
    return raw, firsts, sums


def back_inter_body(
    x_ref, before_ref, edge_ref, xc_ref, bc_ref, step_ref, cum_ref, cols_ref, dt_ref, dy_ref, ssm_ref, dxi_ref,
    left_ref, dbci_ref, enter_ref, phi_ref, in_ref, later_ref, taps_ref, head_ref, rows_ref, spread_ref, sums_ref,
    dx_ref, last_ref, prior_ref, dbc_ref, ddt_ref, conv_ref, heads_ref, skip_ref,
    grad_state, next_rows,
):
    step = pl.program_id(0)
    count = pl.num_programs(0)
    chunk = count - 1 - step
    ns = in_ref.shape[0]
    size, width = xc_ref.shape
    spread = spread_ref[...]

    @pl.when(step == 0)
    def _():
        grad_state[...] = later_ref[...]
        next_rows[...] = jnp.zeros_like(next_rows)
        conv_ref[...] = jnp.zeros_like(conv_ref)
        heads_ref[...] = jnp.zeros_like(heads_ref)
        skip_ref[...] = jnp.zeros_like(skip_ref)

    cols = cols_ref[...]
    same = same_columns(cols, LANES)
    cum = cum_ref[...]
    dt = step_ref[...]
    decay_in = cols[:, 4:5] * jnp.exp(cum)
    decay_out = cols[:, 5:6] * jnp.exp(cum[size - 1 : size] - cum)
    fold_rows = jnp.broadcast_to(decay_in[size - EDGE : size][EDGE - 1 : EDGE], (EDGE, LANES))
    b_part = bc_ref[:, :ns]
    c_part = bc_ref[:, ns:]
    c_turned = c_part.astype(F32).T.astype(BF16)
    dbc_b = dbci_ref[:, :ns]
    dbc_c = dbci_ref[:, ns:]
    right = jnp.zeros((size, LANES), F32)
    outward = jnp.zeros((size, LANES), F32)
    direct = jnp.zeros((size, LANES), F32)
    through = jnp.zeros((EDGE, LANES), F32)
    in_split = split(decay_in)
    out_split = split(decay_out)
    dt_split = split(dt)
    fold_split = split(fold_rows)
    phi_split = split(phi_ref[0])
    first_chunk = chunk == 0
    for i in range(width // LANES):
        part = slice(i * LANES, (i + 1) * LANES)
        across = spread[:, part]

        def over(pieces, across=across):
            return dot(pieces[0], across) + dot(pieces[1], across)

        in_wide, out_wide, dt_wide = over(in_split), over(out_split), over(dt_split)
        fold_wide, phi_wide = over(fold_split)[0:1], over(phi_split)[0:1]
        begun = enter_ref[0, :, part].astype(F32) + phi_wide * in_ref[:, part]
        grad_end = grad_state[:, part]
        x_conv = xc_ref[:, part].astype(F32)
        dy = dy_ref[:, part].astype(F32)
        weighted = x_conv * dt_wide
        carried_dy = (dy * in_wide).astype(BF16)
        held = (weighted * out_wide).astype(BF16)
        end_low = grad_end.astype(BF16)
        dbc_c = dbc_c + dot(carried_dy, begun.astype(BF16), ((1,), (1,)))
        dbc_b = dbc_b + dot(held, end_low, ((1,), (1,)))
        grad_far = out_wide * dot(b_part, end_low)
        grad_weighted = dxi_ref[:, part].astype(F32) + grad_far
        right = right + head_sum(dy * ssm_ref[:, part], across)
        outward = outward + head_sum(weighted * grad_far, across)
        direct = direct + head_sum(x_conv * grad_weighted, across)
        pass_sum = jnp.sum(begun * grad_end, axis=0, keepdims=True) * fold_wide
        through = through + head_sum(jnp.broadcast_to(pass_sum, (EDGE, LANES)), across)
        skip_ref[0:1, part] += jnp.sum(dy * x_conv, axis=0, keepdims=True)
        grad_state[:, part] = fold_wide * grad_end + dot(c_turned, carried_dy)
        grad_conv = dt_wide * grad_weighted + rows_ref[1:2, part] * dy

        ahead = jnp.where(first_chunk, edge_ref[:, part].astype(F32), before_ref[:, part].astype(F32))
        ext = jnp.concatenate([ahead, x_ref[:, part].astype(F32)], axis=0)
        raw, firsts, sums = conv_back(
            ext, same, taps_ref[:, part], grad_conv, [next_rows[k, :, part] for k in range(3)]
        )
        for k in range(3):
            next_rows[k, :, part] = firsts[k]
        for k in range(5):
            conv_ref[k : k + 1, part] += sums[k]
        dx_ref[:, part] = raw[EDGE:].astype(BF16)
        prior_ref[:, part] = raw[:EDGE]

        @pl.when(step == 0)
        def _(raw=raw, part=part):
            last_ref[:, part] = raw[size:]

    dbc_ref[:, :ns] = dbc_b.astype(BF16)
    dbc_ref[:, ns:] = dbc_c.astype(BF16)
    stacked = jnp.concatenate([right - left_ref[...], outward], axis=0)
    grad_rate = dot(sums_ref[...], stacked, precision=EXACT) + through[0:1]
    grad_dt = direct + head_ref[1:2] * grad_rate
    grad_raw = grad_dt * cols[:, 3:4] * jax.nn.sigmoid(dt_ref[...] + head_ref[0:1])
    ddt_ref[...] = grad_raw.astype(BF16)
    heads_ref[0:1] += jnp.sum(grad_raw, axis=0, keepdims=True)
    heads_ref[1:2] += jnp.sum(grad_rate * head_ref[1:2] * dt, axis=0, keepdims=True)


def back_inter(
    x_raw, edge_x, xc, bc, step, cum, cols, dt_raw, dy, ssm, dx_in, left, dbc_in, entered, phi, state_in, later,
    taps, head, rowpack, spread, sums,
):
    rows, width = xc.shape
    ns = bc.shape[1] // 2
    count = rows // CHUNK

    def back(i, *_):
        return (count - 1 - i, 0)

    def back3(i, *_):
        return (count - 1 - i, 0, 0)

    def before(i, *_):
        return (jnp.maximum((count - 1 - i) * (CHUNK // EDGE) - 1, 0), 0)

    def at(width_now):
        return (CHUNK, width_now)

    ins = [
        (x_raw, at(width), back),
        (x_raw, (EDGE, width), before),
        (edge_x, edge_x.shape, fixed),
        (xc, at(width), back),
        (bc, at(2 * ns), back),
        (step, at(LANES), back),
        (cum, at(LANES), back),
        (cols, at(cols.shape[1]), back),
        (dt_raw, at(LANES), back),
        (dy, at(width), back),
        (ssm, at(width), back),
        (dx_in, at(width), back),
        (left, at(LANES), back),
        (dbc_in, at(2 * ns), back),
        (entered, (1, ns, width), back3),
        (phi, (1, EDGE, LANES), back3),
        (state_in, state_in.shape, fixed),
        (later, later.shape, fixed),
        (taps, taps.shape, fixed),
        (head, head.shape, fixed),
        (rowpack, rowpack.shape, fixed),
        (spread, spread.shape, fixed),
        (sums, sums.shape, fixed),
    ]
    outs = [
        ((rows, width), BF16, at(width), back),
        ((EDGE, width), F32, (EDGE, width), fixed),
        ((EDGE, width), F32, (EDGE, width), fixed),
        ((rows, 2 * ns), BF16, at(2 * ns), back),
        ((rows, LANES), BF16, at(LANES), back),
        ((EDGE, width), F32, (EDGE, width), fixed),
        ((EDGE, LANES), F32, (EDGE, LANES), fixed),
        ((EDGE, width), F32, (EDGE, width), fixed),
    ]
    scratch = [pltpu.VMEM((ns, width), F32), pltpu.VMEM((3, EDGE, width), F32)]
    return call(back_inter_body, (count,), ins, outs, scratch, flops=2 * rows * width * ns * 16, name="back_inter")


def back_bc_body(raw_ref, edge_ref, cols_ref, taps_ref, mine_ref, theirs_ref, out_ref, last_ref, prior_ref, sums_ref):
    size, width = raw_ref.shape
    same = same_columns(cols_ref[...], width)
    ext = jnp.concatenate([edge_ref[...].astype(F32), raw_ref[...].astype(F32)], axis=0)
    grad = mine_ref[...].astype(F32) + theirs_ref[...].astype(F32)
    zero = jnp.zeros((EDGE, width), F32)
    raw, _, sums = conv_back(ext, same, taps_ref[...], grad, [zero] * 3)
    out_ref[...] = raw[EDGE:].astype(BF16)
    last_ref[...] = raw[size:]
    prior_ref[...] = raw[:EDGE]
    sums_ref[...] = jnp.concatenate(sums + [zero[:3]], axis=0)


def back_bc(raw, edge, cols, taps, mine, theirs):
    rows, width = raw.shape
    ins = [(a, a.shape, fixed) for a in (raw, edge, cols, taps, mine, theirs)]
    outs = [((rows, width), BF16, (rows, width), fixed)]
    outs += [((EDGE, width), F32, (EDGE, width), fixed)] * 3
    return call(back_bc_body, (1,), ins, outs, name="back_bc")


def back_norm_body(up_ref, a_ref, b_ref, h_ref, gain_ref, out_ref, sum_ref):
    @pl.when(pl.program_id(0) == 0)
    def _():
        sum_ref[...] = jnp.zeros_like(sum_ref)

    hidden = h_ref[...].astype(F32)
    grad = a_ref[...].astype(F32) + b_ref[...].astype(F32)
    model = hidden.shape[1]
    norm = lax.rsqrt(jnp.mean(hidden * hidden, axis=1, keepdims=True) + EPSILON)
    normed = hidden * norm
    sum_ref[0:1] += jnp.sum(grad * normed, axis=0, keepdims=True)
    gained = grad * gain_ref[0:1]
    inner = jnp.sum(gained * normed, axis=1, keepdims=True) / model
    out_ref[...] = up_ref[...].astype(F32) + norm * (gained - normed * inner)


def back_norm(up, a, b, hidden, gain):
    rows, model = hidden.shape
    block = min(256, rows)
    wide = (block, model)
    ins = [(v, wide, rows_at) for v in (up, a, b, hidden)] + [(gain, gain.shape, fixed)]
    outs = [((rows, model), F32, wide, rows_at), ((EDGE, model), F32, (EDGE, model), fixed)]
    return call(back_norm_body, (rows // block,), ins, outs, name="back_norm")


def weight_grad_body(places, count, shards, where, a_ref, b_ref, *refs):
    outs, (turned, result) = refs[:places], refs[places:]
    model = a_ref.shape[1]
    rows = model // (places * shards)

    @pl.when(pl.program_id(0) == 0)
    def _():
        for i in range(0, model, 256):
            turned[i : i + 256] = a_ref[:, i : i + 256].T

    result[...] = dot(turned[...], b_ref[...])
    for k in range(places):
        for z in range(shards):
            start = pl.multiple_of((z * places + where[k]) * rows, rows)
            outs[k][z * rows : (z + 1) * rows] = result[pl.ds(start, rows)].astype(BF16)


def weight_grad(where, places, shards, a, b):
    rows, model = a.shape
    width = b.shape[1]
    tile = min(256, width)
    ins = [(a, a.shape, fixed), (b, (rows, tile), lambda i, *_: (0, i))]
    part = model // places
    outs = [((part, width), BF16, (part, tile), lambda i, *_: (0, i))] * places
    scratch = [pltpu.VMEM((model, rows), BF16), pltpu.VMEM((model, tile), F32)]
    return call(
        functools.partial(weight_grad_body, places, None, shards), (width // tile,), ins, outs, scratch, where,
        flops=2 * rows * model * width, name="weight_grad",
    )


def relative(value, axis, by):
    size = lax.axis_size(axis)
    return lax.ppermute(value, axis, [(i, i ^ by) for i in range(size)])


def shifted(value, axis, by):
    size = lax.axis_size(axis)
    return lax.ppermute(value, axis, [(i, i + by) for i in range(size) if 0 <= i + by < size])


def tree_sum(values):
    while len(values) > 1:
        values = [a + b for a, b in zip(values[0::2], values[1::2])]
    return values[0]


def place_body(shards, places, rows, by_rows, where, *refs):
    sources, out, sems = refs[:places], refs[places], refs[places + 1]
    width = sources[0].shape[1]
    copies = []
    for k in range(places):
        for z in range(shards):
            if by_rows:
                start = (where[z] * places + where[shards + k]) * rows
                target = out.at[pl.ds(pl.multiple_of(start, rows), rows)]
            else:
                target = out.at[
                    pl.ds(pl.multiple_of(where[shards + k] * rows, rows), rows),
                    pl.ds(pl.multiple_of(where[z] * width, width), width),
                ]
            copies.append(
                pltpu.make_async_copy(sources[k].at[pl.ds(z * rows, rows)], target, sems.at[k * shards + z])
            )
    for one in copies:
        one.start()
    for one in copies:
        one.wait()


def gather_pieces(piece):
    shards, places = lax.axis_size("shard"), lax.axis_size("ctx")
    along = jnp.concatenate([piece] + [relative(piece, "shard", k) for k in range(1, shards)], axis=0)
    return [along] + [relative(along, "ctx", k) for k in range(1, places)]


def gather_weight(value, by_rows):
    shards, places = lax.axis_size("shard"), lax.axis_size("ctx")
    rows = value.shape[0] // places
    if rows % 16:
        return lax.all_gather(value, "shard", axis=0 if by_rows else 1, tiled=True)
    z, c = lax.axis_index("shard"), lax.axis_index("ctx")
    piece = lax.dynamic_slice_in_dim(value, c * rows, rows, 0)
    pieces = gather_pieces(piece)
    where = jnp.concatenate([z ^ jnp.arange(shards), c ^ jnp.arange(places)]).astype(jnp.int32)
    if by_rows:
        shape = (value.shape[0] * shards, value.shape[1])
    else:
        shape = (value.shape[0], value.shape[1] * shards)
    ins = [(p, None, None) for p in pieces]
    outs = [(shape, value.dtype, None, None)]
    scratch = [pltpu.SemaphoreType.DMA((shards * places,))]
    return call(
        functools.partial(place_body, shards, places, rows, by_rows), (1,), ins, outs, scratch, where, name="place"
    )[0]


def own_rows(pieces):
    shards, places = lax.axis_size("shard"), lax.axis_size("ctx")
    z = lax.axis_index("shard")
    rows = pieces[0].shape[0] // shards
    near = [pieces[0]] + [relative(p, "ctx", k) for k, p in enumerate(pieces) if k]
    sums = []
    for k in range(shards):
        start = (z ^ k) * rows
        sums.append(tree_sum([lax.dynamic_slice_in_dim(p, start, rows, 0).astype(F32) for p in near]))
    far = [sums[0]] + [relative(sums[k].astype(BF16), "shard", k).astype(F32) for k in range(1, shards)]
    return tree_sum(far)


def all_sum(value):
    for axis in ("ctx", "shard"):
        value = tree_sum([value] + [relative(value, axis, k) for k in range(1, lax.axis_size(axis))])
    return value


def state_before(ended, sign):
    ns = ended.shape[0] - EDGE
    got = [shifted(ended, "ctx", sign * d).astype(F32) for d in range(1, lax.axis_size("ctx"))]
    total = got[-1][:ns]
    for one in reversed(got[:-1]):
        total = one[:ns] + one[ns : ns + 1] * total
    return total


def swap(value):
    return lax.ppermute(value, "tp", [(0, 1), (1, 0)])


def pad_rows(value):
    return jnp.pad(value, ((0, EDGE - value.shape[0]), (0, 0)))


def per_device(
    seq_in, w_zx, w_bc, w_dt, w_out, norm_gain, conv_x, conv_bc, head_params, gate_gain, segments, pad_mask, cotangent
):
    rows, model = seq_in.shape[1:]
    layers = w_zx.shape[0]
    width = w_zx.shape[3]
    heads = head_params.shape[2]
    ns = w_bc.shape[2] // 2
    shards, places = lax.axis_size("shard"), lax.axis_size("ctx")
    inner_total = width * lax.axis_size("tp")
    z, c, t = lax.axis_index("shard"), lax.axis_index("ctx"), lax.axis_index("tp")
    flag = t.astype(jnp.int32).reshape(1)
    chunks = rows // CHUNK

    ids = jnp.concatenate([jnp.full((3,), -1, jnp.int32), segments[0]])
    ext = lax.dynamic_slice_in_dim(ids, c * rows, rows + 3, 0)
    seg = ext[3:]
    mask = lax.dynamic_slice_in_dim(pad_mask[0], c * rows, rows, 0)
    firsts = ext[2 : 2 + rows].reshape(chunks, CHUNK)[:, :1]
    lasts = seg.reshape(chunks, CHUNK)[:, CHUNK - 1 :]
    by_chunk = seg.reshape(chunks, CHUNK)
    columns = [(ext[3 - lag : 3 - lag + rows] == seg) for lag in (1, 2, 3)]
    columns += [mask, (by_chunk == firsts).reshape(rows), (by_chunk == lasts).reshape(rows), mask, seg]
    cols = jnp.stack([v.astype(F32) for v in columns], axis=1)
    segs = jnp.broadcast_to(seg.astype(F32)[None], (EDGE, rows))

    head_of = jnp.arange(width)[None] // (width // heads)
    spread = (jnp.arange(LANES)[:, None] == head_of).astype(BF16)
    at = jnp.arange(CHUNK)
    lower = (at[:, None] >= at[None]).astype(F32)
    sums = jnp.concatenate([(at[:, None] <= at[None]).astype(F32), (at[:, None] > at[None]).astype(F32)], axis=1)

    def half(value, which):
        return lax.dynamic_slice_in_dim(value, which * ns, ns, value.ndim - 1)

    weights = []
    for layer in range(layers):
        lanes_dt = jnp.pad(w_dt[layer], ((0, 0), (0, LANES - heads)))
        main = jnp.concatenate([w_zx[layer, :, 1], half(w_bc[layer], t), lanes_dt], axis=1)
        w_main = gather_weight(main, True)
        w_other = swap(w_main[:, width : width + ns])
        w_gate = gather_weight(w_zx[layer, :, 0], True)
        w_down = gather_weight(w_out[layer], False)
        weights.append((w_main, w_other, w_gate, w_down))

    hidden = seq_in[0]
    parts = None
    kept = []
    for layer in range(layers):
        w_main, w_other, w_gate, w_down = weights[layer]
        gain_in = pad_rows(norm_gain[layer][None])
        taps = pad_rows(conv_x[layer])
        taps_mine = pad_rows(half(conv_bc[layer], t))
        taps_bc = jnp.concatenate([taps_mine, pad_rows(half(conv_bc[layer], 1 - t))], axis=1)
        decay = -jnp.exp(head_params[layer, 1])
        head = jnp.pad(
            jnp.stack([head_params[layer, 0], decay]), ((0, EDGE - 2), (0, LANES - heads))
        )
        skip = jnp.repeat(head_params[layer, 2], width // heads)
        rowpack = pad_rows(jnp.stack([gate_gain[layer], skip]))

        hidden, low, x_raw, mine, other, dt_raw = enter(hidden, parts, gain_in, w_main, w_other, width, inner_total)
        tails = jnp.concatenate([v[rows - EDGE :] for v in (x_raw, mine, other)], axis=1)
        edge = shifted(tails, "ctx", 1)
        gate = jnp.dot(low, w_gate, preferred_element_type=F32)
        xc, bc, step, cum, entered, phi, ended = states(
            flag, x_raw, mine, other, dt_raw, edge, cols, taps, taps_bc, head, spread, lower
        )
        y_in = within(xc, bc, step, cum, cols, segs, spread)
        state_in = state_before(ended, 1)
        ssm, p_own, sq_own = leave(y_in, xc, bc, cum, cols, entered, phi, state_in, gate, rowpack, spread, w_down)
        parts = (p_own, swap(p_own), sq_own, swap(sq_own))
        kept.append(
            dict(
                hidden=hidden, low=low, x_raw=x_raw, mine=mine, dt_raw=dt_raw, edge=edge, gate=gate, xc=xc, bc=bc,
                step=step, cum=cum, entered=entered, phi=phi, ended=ended, state_in=state_in, ssm=ssm, parts=parts,
                gain_in=gain_in, taps=taps, taps_mine=taps_mine, head=head, rowpack=rowpack,
            )
        )
    scale = lax.rsqrt((parts[2] + parts[3])[:, :1] / inner_total + EPSILON)
    output = hidden + scale * (parts[0].astype(F32) + parts[1].astype(F32))

    direct = (model // (shards * places)) % 16 == 0
    where = (c ^ jnp.arange(places)).astype(jnp.int32)

    def weight_sum(a, b):
        if direct:
            return own_rows(weight_grad(where, places, shards, a, b))
        full = lax.dot_general(a, b, (((0,), (0,)), ((), ())), preferred_element_type=F32)
        return lax.psum_scatter(full, ("shard", "ctx"), scatter_dimension=0, tiled=True)

    up = cotangent[0]
    grads = []
    for layer in reversed(range(layers)):
        w_main, w_other, w_gate, w_down = weights[layer]
        k = kept[layer]
        do, dy, dgate, normed, gain_rows, begun = back_gate(
            up, k["parts"], k["ssm"], k["xc"], k["gate"], k["bc"], k["cum"], cols, k["phi"], k["ended"],
            k["rowpack"], spread, w_down, inner_total,
        )
        later = state_before(begun, -1)
        dx_in, left, dbc_in = back_within(k["xc"], k["bc"], k["step"], k["cum"], cols, segs, spread, dy)
        g_out = weight_sum(do, normed)
        g_gate = weight_sum(k["low"], dgate)
        edge = k["edge"]
        dx, last, prior, dbc, ddt, conv_rows, head_rows, skip_rows = back_inter(
            k["x_raw"], edge[:, :width], k["xc"], k["bc"], k["step"], k["cum"], cols, k["dt_raw"], dy, k["ssm"],
            dx_in, left, dbc_in, k["entered"], k["phi"], k["state_in"], later, k["taps"], k["head"], k["rowpack"],
            spread, sums,
        )
        dbc_theirs = swap(half(dbc, 1 - t))
        db, last_bc, prior_bc, conv_bc_rows = back_bc(
            k["mine"], edge[:, width : width + ns], cols, k["taps_mine"], half(dbc, t), dbc_theirs
        )
        back_rows = shifted(jnp.concatenate([prior, prior_bc], axis=1), "ctx", -1)
        dx = lax.dynamic_update_slice_in_dim(dx, (last + back_rows[:, :width]).astype(BF16), rows - EDGE, 0)
        db = lax.dynamic_update_slice_in_dim(db, (last_bc + back_rows[:, width:]).astype(BF16), rows - EDGE, 0)
        small = jnp.concatenate([db, ddt], axis=1)
        dlow = (
            lax.dot_general(dgate, w_gate, (((1,), (1,)), ((), ())), preferred_element_type=F32)
            + lax.dot_general(dx, w_main[:, :width], (((1,), (1,)), ((), ())), preferred_element_type=F32)
            + lax.dot_general(small, w_main[:, width:], (((1,), (1,)), ((), ())), preferred_element_type=F32)
        ).astype(BF16)
        up, norm_rows = back_norm(up, dlow, swap(dlow), k["hidden"], k["gain_in"])
        g_x = weight_sum(k["low"], dx)
        g_small = weight_sum(k["low"], small)
        packed = jnp.concatenate(
            [norm_rows[0], conv_rows[:5].reshape(-1), gain_rows[0], skip_rows[0], conv_bc_rows[:5].reshape(-1),
             head_rows[:2].reshape(-1)]
        )
        grads.insert(0, (g_gate, g_x, g_small, g_out, packed))

    packed = all_sum(jnp.concatenate([g[4] for g in grads])).reshape(layers, -1)
    cuts = [model, 5 * width, width, width, 5 * ns, 2 * LANES]
    ends = [sum(cuts[: i + 1]) for i in range(len(cuts))]
    n_sum, cx_sum, gg_sum, sk_sum, cb_sum, hd_sum = jnp.split(packed, ends[:-1], axis=1)
    cb_mine = cb_sum.reshape(layers, 5, ns)
    small_mine = jnp.stack([g[2][:, :ns] for g in grads])
    cb_other, small_other = swap(cb_mine), swap(small_mine)

    def ordered(own, other):
        first = jnp.where(t == 0, own, other)
        return jnp.concatenate([first, jnp.where(t == 0, other, own)], axis=-1)

    hd = hd_sum.reshape(layers, 2, LANES)[:, :, :heads]
    skip_sum = jnp.sum(sk_sum.reshape(layers, heads, width // heads), axis=-1)
    return (
        output[None],
        up[None],
        jnp.stack([jnp.stack([g[0], g[1]], axis=1) for g in grads]),
        ordered(small_mine, small_other),
        jnp.stack([g[2][:, ns : ns + heads] for g in grads]),
        jnp.stack([g[3].T for g in grads]),
        n_sum,
        cx_sum.reshape(layers, 5, width),
        ordered(cb_mine, cb_other),
        jnp.concatenate([hd, skip_sum[:, None]], axis=1),
        gg_sum,
    )


def solution(mesh):
    in_specs = (
        P("shard", "ctx", None),
        P(None, "shard", None, "tp"),
        P(None, "shard", None),
        P(None, "shard", "tp"),
        P(None, "tp", "shard"),
        P(),
        P(None, None, "tp"),
        P(),
        P(None, None, "tp"),
        P(None, "tp"),
        P("shard", None),
        P("shard", None),
        P("shard", "ctx", None),
    )
    out_specs = (
        P("shard", "ctx", None),
        P("shard", "ctx", None),
        P(None, ("shard", "ctx"), None, "tp"),
        P(None, ("shard", "ctx"), None),
        P(None, ("shard", "ctx"), "tp"),
        P(None, "tp", ("shard", "ctx")),
        P(),
        P(None, None, "tp"),
        P(),
        P(None, None, "tp"),
        P(None, "tp"),
    )
    return jax.shard_map(per_device, mesh=mesh, in_specs=in_specs, out_specs=out_specs, check_vma=False)
```

time: 2930 us -> 789 us (0.27)
  waiting for transfers between devices: 1110 us -> 185 us
  local copies, waits for them, and re-layouts: 810 us -> 59.5 us
  matrix products: 491 us -> 30.4 us
  other arithmetic: 358 us -> 42.2 us
  Pallas kernels: 0 us -> 298 us
  starting transfers between devices: 20.8 us -> 161 us
  blocking collectives: 92.2 us -> 0 us
    reduce_scatter x6 -> x0, waiting for transfers between devices: 702 us -> none  [the longest x2 361 us: per_device(): lax.psum_scatter(grad_in, ('shard', 'ctx'), scatter_dimension=0, tiled=True)]
    dot_general x124 -> x8, matrix products: 484 us -> 30.4 us  [the longest x2 8.84 us: per_device(): lax.dot_general(dx, w_main[:, :width], (((1,), (1,)), ((), ())), preferre...]
    dynamic_update_slice x128 -> x0, local copies, waits for them, and re-layouts: 302 us -> none  [ssd_local(): lax.scan(block_step, start_state, (blocks(x_heads), blocks(b_in), blocks(...]
    pallas_call x0 -> x32, Pallas kernels: none -> 298 us  [call(): return made(*([scalars] if count else []) + arrays)]
    ppermute x8 -> x118, waiting for transfers between devices: 5.57 us -> 185 us  [the longest x90 183 us: relative(): return lax.ppermute(value, axis, [(i, i ^ by) for i in range(size)])]
    psum x5 -> x0, waiting for transfers between devices: 172 us -> none  [the longest x1 115 us: per_device(): lax.psum((grad_gain_in, d_convx, d_convbc, d_heads, grad_gain_gate), ('sh...]
    another operation x158 -> x10, local copies, waits for them, and re-layouts: 145 us -> 3.12 us  [the longest x2 1.62 us: per_device(): cols = jnp.stack([v.astype(F32) for v in columns], axis=1)]
    ppermute x8 -> x118, starting transfers between devices: 19.5 us -> 161 us  [the longest x90 92.4 us: relative(): return lax.ppermute(value, axis, [(i, i ^ by) for i in range(size)])]
  transfers between devices with their start and end apart: 29 -> 118, of which waited for: 22 -> 39; matrix products, arithmetic and copies ran while one was open for 9% -> 13% of each run, Pallas kernels for 0% -> 27%
where the time goes in v1:
time: 789 us; the launch traced here: 780 us
  Pallas kernels  298 us (38%)
  waiting for transfers between devices  185 us (23%)
  starting transfers between devices  161 us (20%)
  local copies, waits for them, and re-layouts  59.5 us (8%)
  other arithmetic  42.2 us (5%)
  matrix products  30.4 us (4%)
    pallas_call x32, Pallas kernels, call(): return made(*([scalars] if count else []) + arrays)  298 us
    ppermute x90, waiting for transfers between devices, relative(): return lax.ppermute(value, axis, [(i, i ^ by) for i in range(size)])  183 us
    ppermute x90, starting transfers between devices, relative(): return lax.ppermute(value, axis, [(i, i ^ by) for i in range(size)])  92.4 us
    ppermute x12, starting transfers between devices, swap(): return lax.ppermute(value, 'tp', [(0, 1), (1, 0)])  35.7 us
    ppermute x16, starting transfers between devices, shifted(): lax.ppermute(value, axis, [(i, i + by) for i in range(size) if 0 <= i + b...  32.4 us
    unnamed x369, local copies, waits for them, and re-layouts  28.1 us
  transfers between devices with their start and end apart: 118, of which 39 were waited for; matrix products, arithmetic and copies ran while one was open for 13% of the time, Pallas kernels for 27%

profile of v1, /device:TPU:1, one launch (start us, length us, event | category | flops | bytes accessed | tf_op | source)
XLA Modules:
  0.0 779.6 jit_solution(9904674028568488810)
XLA Ops:
  22.6 10.0 %collective-permute-done.1 = bf16[64,1280]{1,0:T(8,128)(2,1)S(1)} collective-permute-done((bf16[64,1280]{1,0:T(8,128)(2,1)S(1)}, bf16[64,1280]{1,0:T(8,128)(2,1)S(1)}, u32[]{:S(2)}, u32[]{:S(2)}) %collective-permute-start.1) | collective-permute-done | bytes 163872 | tf_op jit(solution)/shard_map/ppermute | solution.py:761
  48.6 17.6 %collective-permute-done.4.refs_2_ = bf16[256,1280]{1,0:T(8,128)(2,1)S(1)} collective-permute-done((bf16[256,1280]{1,0:T(8,128)(2,1)S(1)}, bf16[256,1280]{1,0:T(8,128)(2,1)S(1)}, u32[]{:S(2)}, u32[]{:S(2)}) %collective-permute-start.4) | collective-permute-done | bytes 655392 | tf_op jit(solution)/shard_map/ppermute | solution.py:761
  97.7 11.8 %collective-permute-done.15.refs_2_ = bf16[256,1024]{1,0:T(8,128)(2,1)} collective-permute-done((bf16[256,1024]{1,0:T(8,128)(2,1)S(1)}, bf16[256,1024]{1,0:T(8,128)(2,1)}, u32[]{:S(2)}, u32[]{:S(2)}) %collective-permute-start.15) | collective-permute-done | bytes 524320 | tf_op jit(solution)/shard_map/ppermute | solution.py:761
  112.4 12.0 %states.2 = (bf16[1024,1024]{1,0:T(8,128)(2,1)S(1)}, bf16[1024,256]{1,0:T(8,128)(2,1)S(1)}, f32[1024,128]{1,0:T(8,128)S(1)}, f32[1024,128]{1,0:T(8,128)S(1)}, bf...) custom-call(s32[1]{0:T(128)} %bitcast.1.flag, bf16[1024,1024]{1,0:T(8,128)(2,1)} %copy-done.2, ...), custom_call_target="tpu_custom_call" | custom-call | flops 1073741824 | bytes 9650176 | tf_op jit(solution)/shard_map/states/pallas_call | solution.py:106
  136.8 6.5 within.2.y_ref
  143.6 10.1 %leave.2 = (f32[1024,1024]{1,0:T(8,128)}, bf16[1024,1024]{1,0:T(8,128)(2,1)S(1)}, f32[1024,128]{1,0:T(8,128)}) custom-call(f32[1024,1024]{1,0:T(8,128)} %within.2.y_ref, bf16[1024,1024]{1,0:T(8,128)(2,1)} %copy-done, bf16[1024,256]{1,0:T(8,128)(2,1)S(1)} %get-tuple-element.125.bc_ref, f32[1024,128]{1,0:T(8,128)S(1)} %get-tuple-element.127.cum_ref, ...), custom_call_target="tpu_custom_call" | custom-call | flops 2791728640 | bytes 23429120 | tf_op jit(solution)/shard_map/leave/pallas_call | solution.py:106
  166.0 9.3 %collective-permute-done.26 = bf16[64,1280]{1,0:T(8,128)(2,1)S(1)} collective-permute-done((bf16[64,1280]{1,0:T(8,128)(2,1)S(1)}, bf16[64,1280]{1,0:T(8,128)(2,1)S(1)}, u32[]{:S(2)}, u32[]{:S(2)}) %collective-permute-start.26) | collective-permute-done | bytes 163872 | tf_op jit(solution)/shard_map/ppermute | solution.py:761
  228.3 8.6 %enter.3 = (f32[1024,1024]{1,0:T(8,128)}, bf16[1024,1024]{1,0:T(8,128)(2,1)S(1)}, bf16[1024,1024]{1,0:T(8,128)(2,1)}, bf16[1024,128]{1,0:T(8,128)(2,1)S(1)}, bf1...) custom-call(bf16[1024,1024]{1,0:T(8,128)(2,1)} %bitcast.151, bf16[1024,1024]{1,0:T(8,128)(2,1)} %copy-done.23, ...), custom_call_target="tpu_custom_call" | custom-call | flops 2952790016 | bytes 19693568 | tf_op jit(solution)/shard_map/enter/pallas_call | solution.py:106
  242.9 6.7 collective-permute-done.41.refs_3_
  249.6 9.0 %collective-permute-done.40.refs_2_ = bf16[256,1024]{1,0:T(8,128)(2,1)S(1)} collective-permute-done((bf16[256,1024]{1,0:T(8,128)(2,1)S(1)}, bf16[256,1024]{1,0:T(8,128)(2,1)S(1)}, u32[]{:S(2)}, u32[]{:S(2)}) %collective-permute-start.40) | collective-permute-done | bytes 524320 | tf_op jit(solution)/shard_map/ppermute | solution.py:761
  264.4 11.7 %states.3 = (bf16[1024,1024]{1,0:T(8,128)(2,1)S(1)}, bf16[1024,256]{1,0:T(8,128)(2,1)S(1)}, f32[1024,128]{1,0:T(8,128)S(1)}, f32[1024,128]{1,0:T(8,128)S(1)}, bf...) custom-call(s32[1]{0:T(128)} %bitcast.1.flag, ...), custom_call_target="tpu_custom_call" | custom-call | flops 1073741824 | bytes 9650176 | tf_op jit(solution)/shard_map/states/pallas_call | solution.py:106
  287.3 6.5 within.3.y_ref
  294.1 9.9 %leave.3 = (f32[1024,1024]{1,0:T(8,128)}, bf16[1024,1024]{1,0:T(8,128)(2,1)S(1)}, f32[1024,128]{1,0:T(8,128)}) custom-call(f32[1024,1024]{1,0:T(8,128)} %within.3.y_ref, bf16[1024,1024]{1,0:T(8,128)(2,1)} %copy-done.1, bf16[1024,256]{1,0:T(8,128)(2,1)S(1)} %get-tuple-element.140.bc_ref, f32[1024,128]{1,0:T(8,128)S(1)} %get-tuple-element.142.cum_ref, ...), custom_call_target="tpu_custom_call" | custom-call | flops 2791728640 | bytes 23429120 | tf_op jit(solution)/shard_map/leave/pallas_call | solution.py:106
  317.4 14.4 %back_gate.2 = (bf16[1024,1024]{1,0:T(8,128)(2,1)S(1)}, bf16[1024,1024]{1,0:T(8,128)(2,1)}, bf16[1024,1024]{1,0:T(8,128)(2,1)}, bf16[1024,1024]{1,0:T(8,128)(2,1...) custom-call(bf16[1024,1024]{1,0:T(8,128)(2,1)} %bitcast.146, bf16[1024,1024]{1,0:T(8,128)(2,1)} %copy-done.14, ...), custom_call_target="tpu_custom_call" | custom-call | flops 2791728640 | bytes 30310400 | tf_op jit(solution)/shard_map/back_gate/pallas_call | solution.py:106
  336.2 6.9 weight_grad.15
  352.1 10.3 %back_within.2 = (bf16[1024,1024]{1,0:T(8,128)(2,1)S(1)}, f32[1024,128]{1,0:T(8,128)S(1)}, f32[1024,256]{1,0:T(8,128)S(1)}) custom-call(bf16[1024,1024]{1,0:T(8,128)(2,1)} %copy-done.1, bf16[1024,256]{1,0:T(8,128)(2,1)S(1)} %copy-done.10, f32[1024,128]{1,0:T(8,128)S(1)} %copy-done.31, f32[1024,128]{1,0:T(8,128)S(1)} %copy-done.13, ...), custom_call_target="tpu_custom_call" | custom-call | flops 2147483648 | bytes 9764864 | tf_op jit(solution)/shard_map/back_within/pallas_call | solution.py:106
  365.4 49.2 %back_inter.2 = (bf16[1024,1024]{1,0:T(8,128)(2,1)}, f32[8,1024]{1,0:T(8,128)S(1)}, f32[8,1024]{1,0:T(8,128)S(1)}, bf16[1024,256]{1,0:T(8,128)(2,1)S(1)}, bf16[1...) custom-call(bf16[1024,1024]{1,0:T(8,128)(2,1)} %get-tuple-element.135.x_ref.befor, ...), custom_call_target="tpu_custom_call" | custom-call | flops 4294967296 | bytes 25059328 | tf_op jit(solution)/shard_map/back_inter/pallas_call | solution.py:106
  460.8 13.2 %collective-permute-start.55 = (bf16[1024,1024]{1,0:T(8,128)(2,1)}, bf16[1024,1024]{1,0:T(8,128)(2,1)}, u32[]{:S(2)}, u32[]{:S(2)}) collective-permute-start(bf16[1024,1024]{1,0:T(8,128)(2,1)} %add_convert_fusion.1.a_ref), channel_id=1, source_target_pairs={{0,1},{1,0},{2,3},{3,2},{4,5},{5,4},{6,7},{7,6},{8,9},{9,8},{10,11... | collective-permute-start | bytes 6291464 | tf_op jit(solution)/shard_map/ppermute | solution.py:854
  480.6 6.6 weight_grad.11
  495.4 7.6 collective-permute-done.78
  508.4 18.6 %collective-permute-done.81 = bf16[256,1024]{1,0:T(8,128)(2,1)S(1)} collective-permute-done((bf16[256,1024]{1,0:T(8,128)(2,1)}, bf16[256,1024]{1,0:T(8,128)(2,1)S(1)}, u32[]{:S(2)}, u32[]{:S(2)}) %collective-permute-start.81) | collective-permute-done | bytes 524320 | tf_op jit(solution)/shard_map/ppermute | solution.py:761
  535.0 7.3 collective-permute-done.84
  544.2 6.8 back_norm.2
  551.0 15.3 %back_gate.3 = (bf16[1024,1024]{1,0:T(8,128)(2,1)S(1)}, bf16[1024,1024]{1,0:T(8,128)(2,1)}, bf16[1024,1024]{1,0:T(8,128)(2,1)}, bf16[1024,1024]{1,0:T(8,128)(2,1...) custom-call(f32[1024,1024]{1,0:T(8,128)} %get-tuple-element.164.up_ref, bf16[1024,1024]{1,0:T(8,128)(2,1)} %copy-done.23, ...), custom_call_target="tpu_custom_call" | custom-call | flops 2791728640 | bytes 32407552 | tf_op jit(solution)/shard_map/back_gate/pallas_call | solution.py:106
  570.3 6.5 weight_grad.14
  581.0 6.6 weight_grad.8
  588.4 10.3 %back_within.3 = (bf16[1024,1024]{1,0:T(8,128)(2,1)S(1)}, f32[1024,128]{1,0:T(8,128)S(1)}, f32[1024,256]{1,0:T(8,128)S(1)}) custom-call(bf16[1024,1024]{1,0:T(8,128)(2,1)} %copy-done, bf16[1024,256]{1,0:T(8,128)(2,1)S(1)} %get-tuple-element.125.bc_ref, f32[1024,128]{1,0:T(8,128)S(1)} %copy-done.27, f32[1024,128]{1,0:T(8,128)S(1)} %copy-done.7, ...), custom_call_target="tpu_custom_call" | custom-call | flops 2147483648 | bytes 9764864 | tf_op jit(solution)/shard_map/back_within/pallas_call | solution.py:106
  603.4 49.5 %back_inter.3 = (bf16[1024,1024]{1,0:T(8,128)(2,1)}, f32[8,1024]{1,0:T(8,128)S(1)}, f32[8,1024]{1,0:T(8,128)S(1)}, bf16[1024,256]{1,0:T(8,128)(2,1)S(1)}, bf16[1...) custom-call(bf16[1024,1024]{1,0:T(8,128)(2,1)} %copy-done.2, ...), custom_call_target="tpu_custom_call" | custom-call | flops 4294967296 | bytes 25059328 | tf_op jit(solution)/shard_map/back_inter/pallas_call | solution.py:106
  685.8 6.8 weight_grad.9
  717.5 17.7 %collective-permute-done.69 = bf16[256,1024]{1,0:T(8,128)(2,1)} collective-permute-done((bf16[256,1024]{1,0:T(8,128)(2,1)}, bf16[256,1024]{1,0:T(8,128)(2,1)}, u32[]{:S(2)}, u32[]{:S(2)}) %collective-permute-start.69) | collective-permute-done | bytes 524320 | tf_op jit(solution)/shard_map/ppermute | solution.py:761
  744.1 7.2 collective-permute-done.72
  752.6 6.8 back_norm.3
  (765 shorter events, 378.3 us)
Async XLA Ops:
  3.6 31.9 %collective-permute-start.19 = (bf16[256,256]{1,0:T(8,128)(2,1)}, bf16[256,256]{1,0:T(8,128)(2,1)S(1)}, u32[]{:S(2)}, u32[]{:S(2)}) collective-permute-start(bf16[256,256]{1,0:T(8,128)(2,1)} %dynamic-slice_bitcast_fusion.1), channel_id=1, source_target_pairs={{0,24},{8,16},{16,8},{24,0},{1,25},{9,17},{17,9},{25,1},{2,26},{10... | collective-permute-start | bytes 393224 | tf_op jit(solution)/shard_map/ppermute | solution.py:761
  7.7 28.5 %collective-permute-start.18 = (bf16[256,256]{1,0:T(8,128)(2,1)}, bf16[256,256]{1,0:T(8,128)(2,1)}, u32[]{:S(2)}, u32[]{:S(2)}) collective-permute-start(bf16[256,256]{1,0:T(8,128)(2,1)} %dynamic-slice_bitcast_fusion.1), channel_id=1, source_target_pairs={{0,16},{8,24},{16,0},{24,8},{1,17},{9,25},{17,1},{25,9},{2,18},{10... | collective-permute-start | bytes 393224 | tf_op jit(solution)/shard_map/ppermute | solution.py:761
  34.9 31.3 %collective-permute-start.4 = (bf16[256,1280]{1,0:T(8,128)(2,1)S(1)}, bf16[256,1280]{1,0:T(8,128)(2,1)S(1)}, u32[]{:S(2)}, u32[]{:S(2)}) collective-permute-start(bf16[256,1280]{1,0:T(8,128)(2,1)S(1)} %pad_maximum_fusion.1.refs_0_), channel_id=1, source_target_pairs={{0,4},{2,6},{4,0},{6,2},{1,5},{3,7},{5,1},{7,3},{8,12},{10,14},{12... | collective-permute-start | bytes 1966088 | tf_op jit(solution)/shard_map/ppermute | solution.py:761
  35.2 31.1 %collective-permute-start.3 = (bf16[256,1280]{1,0:T(8,128)(2,1)S(1)}, bf16[256,1280]{1,0:T(8,128)(2,1)}, u32[]{:S(2)}, u32[]{:S(2)}) collective-permute-start(bf16[256,1280]{1,0:T(8,128)(2,1)S(1)} %pad_maximum_fusion.1.refs_0_), channel_id=1, source_target_pairs={{0,2},{2,0},{4,6},{6,4},{1,3},{3,1},{5,7},{7,5},{8,10},{10,8},{12,... | collective-permute-start | bytes 1966088 | tf_op jit(solution)/shard_map/ppermute | solution.py:761
  36.3 35.6 %collective-permute-start.13 = (bf16[64,1024]{1,0:T(8,128)(2,1)S(1)}, bf16[64,1024]{1,0:T(8,128)(2,1)S(1)}, u32[]{:S(2)}, u32[]{:S(2)}) collective-permute-start(bf16[64,1024]{1,0:T(8,128)(2,1)S(1)} %bitcast.155), channel_id=1, source_target_pairs={{0,24},{8,16},{16,8},{24,0},{1,25},{9,17},{17,9},{25,1},{2,26},{10... | collective-permute-start | bytes 393224 | tf_op jit(solution)/shard_map/ppermute | solution.py:761
  40.9 33.8 %collective-permute-start.22 = (bf16[1024,256]{1,0:T(8,128)(2,1)S(1)}, bf16[1024,256]{1,0:T(8,128)(2,1)S(1)}, u32[]{:S(2)}, u32[]{:S(2)}) collective-permute-start(bf16[1024,256]{1,0:T(8,128)(2,1)S(1)} %pad_maximum_fusion.4.refs_0_), channel_id=1, source_target_pairs={{0,6},{2,4},{4,2},{6,0},{1,7},{3,5},{5,3},{7,1},{8,14},{10,12},{12... | collective-permute-start | bytes 1572872 | tf_op jit(solution)/shard_map/ppermute | solution.py:761
  75.5 34.0 %collective-permute-start.15 = (bf16[256,1024]{1,0:T(8,128)(2,1)S(1)}, bf16[256,1024]{1,0:T(8,128)(2,1)}, u32[]{:S(2)}, u32[]{:S(2)}) collective-permute-start(bf16[256,1024]{1,0:T(8,128)(2,1)S(1)} %pad_maximum_fusion.3.refs_0_), channel_id=1, source_target_pairs={{0,4},{2,6},{4,0},{6,2},{1,5},{3,7},{5,1},{7,3},{8,12},{10,14},{12... | collective-permute-start | bytes 1572872 | tf_op jit(solution)/shard_map/ppermute | solution.py:761
  76.5 33.0 %collective-permute-start.14 = (bf16[256,1024]{1,0:T(8,128)(2,1)S(1)}, bf16[256,1024]{1,0:T(8,128)(2,1)}, u32[]{:S(2)}, u32[]{:S(2)}) collective-permute-start(bf16[256,1024]{1,0:T(8,128)(2,1)S(1)} %pad_maximum_fusion.3.refs_0_), channel_id=1, source_target_pairs={{0,2},{2,0},{4,6},{6,4},{1,3},{3,1},{5,7},{7,5},{8,10},{10,8},{12,... | collective-permute-start | bytes 1572872 | tf_op jit(solution)/shard_map/ppermute | solution.py:761
  153.7 74.3 %collective-permute-start.23 = (bf16[1024,1024]{1,0:T(8,128)(2,1)S(1)}, bf16[1024,1024]{1,0:T(8,128)(2,1)}, u32[]{:S(2)}, u32[]{:S(2)}) collective-permute-start(bf16[1024,1024]{1,0:T(8,128)(2,1)S(1)} %get-tuple-element.132.refs_1_.p_ref), channel_id=1, source_target_pairs={{0,1},{1,0},{2,3},{3,2},{4,5},{5,4},{6,7},{7,6},{8,9},{9,8},{10,11... | collective-permute-start | bytes 6291464 | tf_op jit(solution)/shard_map/ppermute | solution.py:854
  175.4 30.0 %collective-permute-start.29 = (bf16[256,1280]{1,0:T(8,128)(2,1)S(1)}, bf16[256,1280]{1,0:T(8,128)(2,1)S(1)}, u32[]{:S(2)}, u32[]{:S(2)}) collective-permute-start(bf16[256,1280]{1,0:T(8,128)(2,1)S(1)} %pad_maximum_fusion.2.refs_0_), channel_id=1, source_target_pairs={{0,4},{2,6},{4,0},{6,2},{1,5},{3,7},{5,1},{7,3},{8,12},{10,14},{12... | collective-permute-start | bytes 1966088 | tf_op jit(solution)/shard_map/ppermute | solution.py:761
  176.3 31.3 %collective-permute-start.28 = (bf16[256,1280]{1,0:T(8,128)(2,1)S(1)}, bf16[256,1280]{1,0:T(8,128)(2,1)S(1)}, u32[]{:S(2)}, u32[]{:S(2)}) collective-permute-start(bf16[256,1280]{1,0:T(8,128)(2,1)S(1)} %pad_maximum_fusion.2.refs_0_), channel_id=1, source_target_pairs={{0,2},{2,0},{4,6},{6,4},{1,3},{3,1},{5,7},{7,5},{8,10},{10,8},{12,... | collective-permute-start | bytes 1966088 | tf_op jit(solution)/shard_map/ppermute | solution.py:761
  196.5 28.8 %collective-permute-start.47 = (bf16[1024,256]{1,0:T(8,128)(2,1)}, bf16[1024,256]{1,0:T(8,128)(2,1)}, u32[]{:S(2)}, u32[]{:S(2)}) collective-permute-start(bf16[1024,256]{1,0:T(8,128)(2,1)} %pad_maximum_fusion.6.refs_0_), channel_id=1, source_target_pairs={{0,6},{2,4},{4,2},{6,0},{1,7},{3,5},{5,3},{7,1},{8,14},{10,12},{12... | collective-permute-start | bytes 1572872 | tf_op jit(solution)/shard_map/ppermute | solution.py:761
  196.5 30.2 %collective-permute-start.24 = (f32[1024,128]{1,0:T(8,128)}, f32[1024,128]{1,0:T(8,128)}, u32[]{:S(2)}, u32[]{:S(2)}) collective-permute-start(f32[1024,128]{1,0:T(8,128)} %get-tuple-element.133.refs_3_.s_ref), channel_id=1, source_target_pairs={{0,1},{1,0},{2,3},{3,2},{4,5},{5,4},{6,7},{7,6},{8,9},{9,8},{10,11... | collective-permute-start | bytes 1572872 | tf_op jit(solution)/shard_map/ppermute | solution.py:854
  226.7 32.0 %collective-permute-start.40 = (bf16[256,1024]{1,0:T(8,128)(2,1)S(1)}, bf16[256,1024]{1,0:T(8,128)(2,1)S(1)}, u32[]{:S(2)}, u32[]{:S(2)}) collective-permute-start(bf16[256,1024]{1,0:T(8,128)(2,1)S(1)} %pad_maximum_fusion.5.refs_0_), channel_id=1, source_target_pairs={{0,4},{2,6},{4,0},{6,2},{1,5},{3,7},{5,1},{7,3},{8,12},{10,14},{12... | collective-permute-start | bytes 1572872 | tf_op jit(solution)/shard_map/ppermute | solution.py:761
  228.0 32.7 %collective-permute-start.39 = (bf16[256,1024]{1,0:T(8,128)(2,1)S(1)}, bf16[256,1024]{1,0:T(8,128)(2,1)S(1)}, u32[]{:S(2)}, u32[]{:S(2)}) collective-permute-start(bf16[256,1024]{1,0:T(8,128)(2,1)S(1)} %pad_maximum_fusion.5.refs_0_), channel_id=1, source_target_pairs={{0,2},{2,0},{4,6},{6,4},{1,3},{3,1},{5,7},{7,5},{8,10},{10,8},{12,... | collective-permute-start | bytes 1572872 | tf_op jit(solution)/shard_map/ppermute | solution.py:761
  237.7 26.6 %collective-permute-start.32 = (bf16[8,1280]{1,0:T(8,128)(2,1)S(1)}, bf16[8,1280]{1,0:T(8,128)(2,1)S(1)}, u32[]{:S(2)}, u32[]{:S(2)}) collective-permute-start(bf16[8,1280]{1,0:T(8,128)(2,1)S(1)} %pad_maximum_fusion.15), channel_id=1, source_target_pairs={{0,2},{2,4},{4,6},{1,3},{3,5},{5,7},{8,10},{10,12},{12,14},{9,11},... | collective-permute-start | bytes 61448 | tf_op jit(solution)/shard_map/ppermute | solution.py:766
  331.8 32.2 %collective-permute-start.52 = (bf16[136,1024]{1,0:T(8,128)(2,1)S(1)}, bf16[136,1024]{1,0:T(8,128)(2,1)S(1)}, u32[]{:S(2)}, u32[]{:S(2)}) collective-permute-start(bf16[136,1024]{1,0:T(8,128)(2,1)S(1)} %get-tuple-element.155), channel_id=1, source_target_pairs={{6,0},{7,1},{14,8},{15,9},{22,16},{23,17},{30,24},{31,25}} | collective-permute-start | bytes 835592 | tf_op jit(solution)/shard_map/ppermute | solution.py:766
  333.1 30.7 %collective-permute-start.51 = (bf16[136,1024]{1,0:T(8,128)(2,1)S(1)}, bf16[136,1024]{1,0:T(8,128)(2,1)S(1)}, u32[]{:S(2)}, u32[]{:S(2)}) collective-permute-start(bf16[136,1024]{1,0:T(8,128)(2,1)S(1)} %get-tuple-element.155), channel_id=1, source_target_pairs={{4,0},{6,2},{5,1},{7,3},{12,8},{14,10},{13,9},{15,11},{20,16},{22,... | collective-permute-start | bytes 835592 | tf_op jit(solution)/shard_map/ppermute | solution.py:766
  334.4 29.5 %collective-permute-start.50 = (bf16[136,1024]{1,0:T(8,128)(2,1)S(1)}, bf16[136,1024]{1,0:T(8,128)(2,1)S(1)}, u32[]{:S(2)}, u32[]{:S(2)}) collective-permute-start(bf16[136,1024]{1,0:T(8,128)(2,1)S(1)} %get-tuple-element.155), channel_id=1, source_target_pairs={{2,0},{4,2},{6,4},{3,1},{5,3},{7,5},{10,8},{12,10},{14,12},{11,9},... | collective-permute-start | bytes 835592 | tf_op jit(solution)/shard_map/ppermute | solution.py:766
  343.9 110.8 %collective-permute-start.107 = (bf16[256,1024]{1,0:T(8,128)(2,1)}, bf16[256,1024]{1,0:T(8,128)(2,1)}, u32[]{:S(2)}, u32[]{:S(2)}) collective-permute-start(bf16[256,1024]{1,0:T(8,128)(2,1)} %get-tuple-element.216), channel_id=1, source_target_pairs={{0,6},{2,4},{4,2},{6,0},{1,7},{3,5},{5,3},{7,1},{8,14},{10,12},{12... | collective-permute-start | bytes 1572872 | tf_op jit(solution)/shard_map/ppermute | solution.py:761
  449.3 26.3 %collective-permute-start.76 = (bf16[256,1024]{1,0:T(8,128)(2,1)S(1)}, bf16[256,1024]{1,0:T(8,128)(2,1)S(1)}, u32[]{:S(2)}, u32[]{:S(2)}) collective-permute-start(bf16[256,1024]{1,0:T(8,128)(2,1)S(1)} %copy-done.121), channel_id=1, source_target_pairs={{0,6},{2,4},{4,2},{6,0},{1,7},{3,5},{5,3},{7,1},{8,14},{10,12},{12... | collective-permute-start | bytes 1572872 | tf_op jit(solution)/shard_map/ppermute | solution.py:761
  460.8 83.4 %collective-permute-start.55 = (bf16[1024,1024]{1,0:T(8,128)(2,1)}, bf16[1024,1024]{1,0:T(8,128)(2,1)}, u32[]{:S(2)}, u32[]{:S(2)}) collective-permute-start(bf16[1024,1024]{1,0:T(8,128)(2,1)} %add_convert_fusion.1.a_ref), channel_id=1, source_target_pairs={{0,1},{1,0},{2,3},{3,2},{4,5},{5,4},{6,7},{7,6},{8,9},{9,8},{10,11... | collective-permute-start | bytes 6291464 | tf_op jit(solution)/shard_map/ppermute | solution.py:854
  566.4 35.3 %collective-permute-start.58 = (bf16[136,1024]{1,0:T(8,128)(2,1)S(1)}, bf16[136,1024]{1,0:T(8,128)(2,1)S(1)}, u32[]{:S(2)}, u32[]{:S(2)}) collective-permute-start(bf16[136,1024]{1,0:T(8,128)(2,1)S(1)} %get-tuple-element.171), channel_id=1, source_target_pairs={{6,0},{7,1},{14,8},{15,9},{22,16},{23,17},{30,24},{31,25}} | collective-permute-start | bytes 835592 | tf_op jit(solution)/shard_map/ppermute | solution.py:766
  567.7 32.5 %collective-permute-start.57 = (bf16[136,1024]{1,0:T(8,128)(2,1)S(1)}, bf16[136,1024]{1,0:T(8,128)(2,1)S(1)}, u32[]{:S(2)}, u32[]{:S(2)}) collective-permute-start(bf16[136,1024]{1,0:T(8,128)(2,1)S(1)} %get-tuple-element.171), channel_id=1, source_target_pairs={{4,0},{6,2},{5,1},{7,3},{12,8},{14,10},{13,9},{15,11},{20,16},{22,... | collective-permute-start | bytes 835592 | tf_op jit(solution)/shard_map/ppermute | solution.py:766
  569.0 31.4 %collective-permute-start.56 = (bf16[136,1024]{1,0:T(8,128)(2,1)S(1)}, bf16[136,1024]{1,0:T(8,128)(2,1)S(1)}, u32[]{:S(2)}, u32[]{:S(2)}) collective-permute-start(bf16[136,1024]{1,0:T(8,128)(2,1)S(1)} %get-tuple-element.171), channel_id=1, source_target_pairs={{2,0},{4,2},{6,4},{3,1},{5,3},{7,5},{10,8},{12,10},{14,12},{11,9},... | collective-permute-start | bytes 835592 | tf_op jit(solution)/shard_map/ppermute | solution.py:766
  576.8 76.8 %collective-permute-start.99 = (bf16[256,1024]{1,0:T(8,128)(2,1)S(1)}, bf16[256,1024]{1,0:T(8,128)(2,1)S(1)}, u32[]{:S(2)}, u32[]{:S(2)}) collective-permute-start(bf16[256,1024]{1,0:T(8,128)(2,1)S(1)} %get-tuple-element.208), channel_id=1, source_target_pairs={{0,2},{2,0},{4,6},{6,4},{1,3},{3,1},{5,7},{7,5},{8,10},{10,8},{12,... | collective-permute-start | bytes 1572872 | tf_op jit(solution)/shard_map/ppermute | solution.py:761
  578.9 74.8 %collective-permute-start.100 = (bf16[256,1024]{1,0:T(8,128)(2,1)S(1)}, bf16[256,1024]{1,0:T(8,128)(2,1)S(1)}, u32[]{:S(2)}, u32[]{:S(2)}) collective-permute-start(bf16[256,1024]{1,0:T(8,128)(2,1)S(1)} %get-tuple-element.209), channel_id=1, source_target_pairs={{0,4},{2,6},{4,0},{6,2},{1,5},{3,7},{5,1},{7,3},{8,12},{10,14},{12... | collective-permute-start | bytes 1572872 | tf_op jit(solution)/shard_map/ppermute | solution.py:761
  600.2 64.4 %collective-permute-start.101 = (bf16[256,1024]{1,0:T(8,128)(2,1)}, bf16[256,1024]{1,0:T(8,128)(2,1)}, u32[]{:S(2)}, u32[]{:S(2)}) collective-permute-start(bf16[256,1024]{1,0:T(8,128)(2,1)} %get-tuple-element.210), channel_id=1, source_target_pairs={{0,6},{2,4},{4,2},{6,0},{1,7},{3,5},{5,3},{7,1},{8,14},{10,12},{12... | collective-permute-start | bytes 1572872 | tf_op jit(solution)/shard_map/ppermute | solution.py:761
  600.4 70.3 %collective-permute-start.62 = (bf16[256,1024]{1,0:T(8,128)(2,1)}, bf16[256,1024]{1,0:T(8,128)(2,1)}, u32[]{:S(2)}, u32[]{:S(2)}) collective-permute-start(bf16[256,1024]{1,0:T(8,128)(2,1)} %get-tuple-element.182), channel_id=1, source_target_pairs={{0,2},{2,0},{4,6},{6,4},{1,3},{3,1},{5,7},{7,5},{8,10},{10,8},{12,... | collective-permute-start | bytes 1572872 | tf_op jit(solution)/shard_map/ppermute | solution.py:761
  601.7 69.6 %collective-permute-start.63 = (bf16[256,1024]{1,0:T(8,128)(2,1)}, bf16[256,1024]{1,0:T(8,128)(2,1)}, u32[]{:S(2)}, u32[]{:S(2)}) collective-permute-start(bf16[256,1024]{1,0:T(8,128)(2,1)} %get-tuple-element.183), channel_id=1, source_target_pairs={{0,4},{2,6},{4,0},{6,2},{1,5},{3,7},{5,1},{7,3},{8,12},{10,14},{12... | collective-permute-start | bytes 1572872 | tf_op jit(solution)/shard_map/ppermute | solution.py:761
  666.5 26.7 %collective-permute-start.104 = (bf16[64,1024]{1,0:T(8,128)(2,1)S(1)}, bf16[64,1024]{1,0:T(8,128)(2,1)S(1)}, u32[]{:S(2)}, u32[]{:S(2)}) collective-permute-start(bf16[64,1024]{1,0:T(8,128)(2,1)S(1)} %get-tuple-element.274), channel_id=1, source_target_pairs={{0,24},{8,16},{16,8},{24,0},{1,25},{9,17},{17,9},{25,1},{2,26},{10... | collective-permute-start | bytes 393224 | tf_op jit(solution)/shard_map/ppermute | solution.py:761
  695.2 57.3 %collective-permute-start.61 = (bf16[1024,1024]{1,0:T(8,128)(2,1)S(1)}, bf16[1024,1024]{1,0:T(8,128)(2,1)}, u32[]{:S(2)}, u32[]{:S(2)}) collective-permute-start(bf16[1024,1024]{1,0:T(8,128)(2,1)S(1)} %add_convert_fusion.a_ref), channel_id=1, source_target_pairs={{0,1},{1,0},{2,3},{3,2},{4,5},{5,4},{6,7},{7,6},{8,9},{9,8},{10,11... | collective-permute-start | bytes 6291464 | tf_op jit(solution)/shard_map/ppermute | solution.py:854
  (258 other events, 3505.3 us)

commit v2 on v1

v2 whole, which is shorter than its diff:
```python
import functools

import jax
import jax.numpy as jnp
from jax import lax
from jax.experimental import pallas as pl
from jax.experimental.pallas import tpu as pltpu
from jax.sharding import PartitionSpec as P

EPSILON = 1e-05
EXACT = lax.Precision.HIGHEST
F32 = jnp.float32
BF16 = jnp.bfloat16
CHUNK = 128
LANES = 128
EDGE = 8
CLOSED = -1e30
VMEM = 54 << 20


def dot(a, b, dims=((1,), (0,)), precision=None):
    return lax.dot_general(a, b, (dims, ((), ())), precision=precision, preferred_element_type=F32)


def split(values):
    high = values.astype(BF16)
    return high, (values - high.astype(F32)).astype(BF16)


def expand(values, spread):
    return dot(jnp.concatenate(split(values), axis=1), spread)


def folded(payloads):
    ns = payloads[0].shape[0] - EDGE
    total = payloads[-1][:ns].astype(F32)
    for one in reversed(payloads[:-1]):
        total = one[:ns].astype(F32) + one[ns : ns + 1].astype(F32) * total
    return total


def conv_shifts(ext, same):
    return [ext[EDGE:]] + [pltpu.roll(ext, lag, 0)[EDGE:] * same[lag] for lag in (1, 2, 3)]


def conv_sum(shifts, taps):
    total = taps[4:5] + taps[0:1] * shifts[0]
    for lag in (1, 2, 3):
        total = total + taps[lag : lag + 1] * shifts[lag]
    return total


def same_columns(cols, width):
    return [None] + [jnp.broadcast_to(cols[:, lag - 1 : lag], (cols.shape[0], width)) for lag in (1, 2, 3)]


def pair_masked(values):
    lane = lax.broadcasted_iota(jnp.int32, values.shape, 1)
    zero = jnp.zeros_like(values)
    first = lane < LANES // 2
    return jnp.concatenate([jnp.where(first, values, zero), jnp.where(first, zero, values)], axis=0)


def pairs_bias(seg_col, seg_row, later_rows):
    size = seg_col.shape[0]
    row = lax.broadcasted_iota(jnp.int32, (size, size), 0)
    col = lax.broadcasted_iota(jnp.int32, (size, size), 1)
    ordered = (row >= col) if later_rows else (row <= col)
    return jnp.where(ordered & (seg_col == seg_row), 0.0, CLOSED)


def silu_parts(values):
    sig = jax.nn.sigmoid(values)
    return sig, values * sig


def call(body, grid, ins, outs, scratch=(), scalars=None, flops=0, name=None):
    count = 0 if scalars is None else 1

    def adapt(block, fn):
        if block is None:
            return pl.BlockSpec(memory_space=pl.ANY)
        return pl.BlockSpec(block, fn)

    in_specs = [adapt(block, fn) for _, block, fn in ins]
    out_specs = [adapt(block, fn) for _, _, block, fn in outs]
    shapes = [jax.ShapeDtypeStruct(shape, dtype) for shape, dtype, _, _ in outs]
    moved = sum(a.size * a.dtype.itemsize for a, _, _ in ins) + sum(
        s.size * s.dtype.itemsize for s in shapes
    )
    made = pl.pallas_call(
        body,
        out_shape=shapes,
        grid_spec=pltpu.PrefetchScalarGridSpec(
            num_scalar_prefetch=count,
            grid=grid,
            in_specs=in_specs,
            out_specs=out_specs,
            scratch_shapes=list(scratch),
        ),
        compiler_params=pltpu.CompilerParams(
            vmem_limit_bytes=VMEM, dimension_semantics=("arbitrary",) * len(grid)
        ),
        cost_estimate=pl.CostEstimate(flops=1, bytes_accessed=1, transcendentals=0),
        name=name,
    )
    arrays = [a for a, _, _ in ins]
    return made(*(([scalars] if count else []) + arrays))


def rows_at(i, *_):
    return (i, 0)


def columns_at(i, *_):
    return (0, i)


def fixed(*_):
    return (0, 0)


def piece_copies(pieces, sems):
    copies = []
    for source, target, start in pieces:
        rows = source.shape[0]
        at = target.at[pl.ds(pl.multiple_of(start, rows), rows)]
        copies.append(pltpu.make_async_copy(source, at, sems.at[len(copies)]))
    for one in copies:
        one.start()
    for one in copies:
        one.wait()


def enter_body(first, inner_total, cuts, where, *refs):
    shards, places, rows = cuts
    near, refs = refs[:places], refs[places:]
    far, refs = (refs[:shards], refs[shards:]) if first else ((), refs)
    if first:
        h_ref, gain, u_ref, turned_ref, x_ref, bc_ref, dt_ref, w_x, w_other, sems = refs
        hidden = h_ref[...].astype(F32)
    else:
        h_ref, p_ref, q_ref, gain, h_out, u_ref, turned_ref, x_ref, bc_ref, dt_ref, w_x, w_other, sems = refs
        model = h_ref.shape[1]
        summed = p_ref[:, :model].astype(F32) + q_ref[:, :model].astype(F32)
        hidden = h_ref[...].astype(F32) + gated_scale(p_ref, q_ref, model, inner_total) * summed
        h_out[...] = hidden
    both = bc_ref.shape[1]
    width = x_ref.shape[1]

    @pl.when(pl.program_id(0) == 0)
    def _():
        pieces = [(v, w_other, where[z] * v.shape[0]) for z, v in enumerate(far)]
        for z in range(shards):
            for k in range(places):
                start = (where[z] * places + where[shards + k]) * rows
                source = near[k].at[pl.ds(z * rows, rows)]
                pieces.append((source.at[:, :width], w_x, start))
                if not far:
                    pieces.append((source.at[:, width:], w_other, start))
        piece_copies(pieces, sems)

    norm = lax.rsqrt(jnp.mean(hidden * hidden, axis=1, keepdims=True) + EPSILON)
    lowered = (hidden * norm * gain[0:1]).astype(BF16)
    u_ref[...] = lowered
    turned_ref[...] = lowered.T
    x_ref[...] = dot(lowered, w_x[...]).astype(BF16)
    made = dot(lowered, w_other[...])
    bc_ref[...] = made[:, :both].astype(BF16)
    dt_ref[...] = made[:, both:]


def gated_scale(p_ref, q_ref, model, inner_total):
    squares = p_ref[:, model:].astype(F32) + q_ref[:, model:].astype(F32)
    return lax.rsqrt((squares[:, 0:1] + squares[:, 1:2]) / inner_total + EPSILON)


def block_of(part):
    array, width, index = part
    return (array, (array.shape[0], width), lambda *_: (0, index))


def enter(where, shards, near, far, hidden, parts, gain, width, both, inner_total):
    rows, model = hidden.shape
    first = parts is None
    block = min(256, rows)
    wide = (block, model)
    ins = [(v, None, None) for v in near + far] + [(hidden, wide, rows_at)]
    outs = []
    if not first:
        ins += [(part, (block, model + LANES), rows_at) for part in parts]
        outs.append(((rows, model), F32, wide, rows_at))
    ins += [(gain, gain.shape, fixed)]
    outs += [
        ((rows, model), BF16, wide, rows_at),
        ((model, rows), BF16, (model, block), columns_at),
        ((rows, width), BF16, (block, width), rows_at),
        ((rows, both), BF16, (block, both), rows_at),
        ((rows, LANES), F32, (block, LANES), rows_at),
    ]
    outs += [((model, v), BF16, (model, v), fixed) for v in (width, both + LANES)]
    scratch = [pltpu.SemaphoreType.DMA((shards * (2 * len(near)),))]
    cuts = (shards, len(near), near[0].shape[0] // shards)
    made = call(
        functools.partial(enter_body, first, inner_total, cuts), (rows // block,), ins, outs, scratch, where, name="enter"
    )
    return [hidden] + list(made) if first else list(made)


def states_body(
    x_ref, raw_bc_ref, dt_ref, before_ref, gain_ref, w_x, w_other, cols_ref, taps_ref, taps_bc_ref, head_ref,
    spread_ref, lower_ref, edge_ref, xc_ref, bc_ref, step_ref, cum_ref, enter_ref, phi_ref, last_ref,
    tail_x, tail_bc, state, phi,
):
    chunk = pl.program_id(0)
    width = x_ref.shape[1]
    ns = raw_bc_ref.shape[1] // 2

    @pl.when(chunk == 0)
    def _():
        before = before_ref[...].astype(F32)
        norm = lax.rsqrt(jnp.mean(before * before, axis=1, keepdims=True) + EPSILON)
        lowered = (before * norm * gain_ref[0:1]).astype(BF16)
        edge = dot(lowered, w_x[...]).astype(BF16)
        edge_bc = dot(lowered, w_other[:, : 2 * ns]).astype(BF16)
        edge_ref[:, :width] = edge
        edge_ref[:, width:] = edge_bc
        tail_x[...] = edge.astype(F32)
        tail_bc[...] = edge_bc.astype(F32)
        state[...] = jnp.zeros_like(state)
        phi[...] = jnp.ones_like(phi)

    cols = cols_ref[...]
    same = same_columns(cols, LANES)
    dt = jax.nn.softplus(dt_ref[...] + head_ref[0:1]) * cols[:, 3:4]
    rates = head_ref[1:2] * dt
    cum = dot(lower_ref[...], rates, precision=EXACT)
    step_ref[...] = dt
    cum_ref[...] = cum
    size = cum.shape[0]
    tail_dt = cols[:, 5:6] * jnp.exp(cum[size - 1 : size] - cum) * dt
    tail_wide = expand(tail_dt, spread_ref[...])
    fold = cols[size - 1 : size, 4:5] * jnp.exp(cum[size - EDGE : size])[EDGE - 1 : EDGE]
    fold_rows = jnp.broadcast_to(fold, phi.shape)
    fold_wide = expand(fold_rows, spread_ref[...])[0:1]

    halves = []
    for i in range(2):
        part = slice(i * ns, (i + 1) * ns)
        now = raw_bc_ref[:, part].astype(F32)
        shifts = conv_shifts(jnp.concatenate([tail_bc[:, part], now], axis=0), same)
        tail_bc[:, part] = now[size - EDGE :]
        halves.append(silu_parts(conv_sum(shifts, taps_bc_ref[:, part]))[1].astype(BF16))
        bc_ref[:, part] = halves[i]
    b_part = halves[0]
    b_turned = b_part.astype(F32).T.astype(BF16)

    enter_ref[0] = state[...].astype(BF16)
    phi_ref[0] = phi[...]
    for i in range(width // LANES):
        part = slice(i * LANES, (i + 1) * LANES)
        now = x_ref[:, part].astype(F32)
        shifts = conv_shifts(jnp.concatenate([tail_x[:, part], now], axis=0), same)
        tail_x[:, part] = now[size - EDGE :]
        x_conv = silu_parts(conv_sum(shifts, taps_ref[:, part]))[1].astype(BF16)
        xc_ref[:, part] = x_conv
        held = (x_conv.astype(F32) * tail_wide[:, part]).astype(BF16)
        state[:, part] = fold_wide[:, part] * state[:, part] + dot(b_turned, held)
    phi[...] = phi[...] * fold_rows

    @pl.when(chunk == pl.num_programs(0) - 1)
    def _():
        last_ref[:ns] = state[...].astype(BF16)
        last_ref[ns:] = expand(phi[...], spread_ref[...]).astype(BF16)


def states(x_raw, raw_bc, dt_raw, before, gain, weights, cols, taps, taps_bc, head, spread, lower):
    rows, width = x_raw.shape
    ns = raw_bc.shape[1] // 2
    count = rows // CHUNK
    ins = [
        (x_raw, (CHUNK, width), rows_at),
        (raw_bc, (CHUNK, 2 * ns), rows_at),
        (dt_raw, (CHUNK, LANES), rows_at),
        (before, before.shape, fixed),
        (gain, gain.shape, fixed),
        block_of(weights["x"]),
        block_of(weights["other"]),
        (cols, (CHUNK, cols.shape[1]), rows_at),
        (taps, taps.shape, fixed),
        (taps_bc, taps_bc.shape, fixed),
        (head, head.shape, fixed),
        (spread, spread.shape, fixed),
        (lower, lower.shape, fixed),
    ]
    outs = [
        ((EDGE, width + 2 * ns), BF16, (EDGE, width + 2 * ns), fixed),
        ((rows, width), BF16, (CHUNK, width), rows_at),
        ((rows, 2 * ns), BF16, (CHUNK, 2 * ns), rows_at),
        ((rows, LANES), F32, (CHUNK, LANES), rows_at),
        ((rows, LANES), F32, (CHUNK, LANES), rows_at),
        ((count, ns, width), BF16, (1, ns, width), lambda i, *_: (i, 0, 0)),
        ((count, EDGE, LANES), F32, (1, EDGE, LANES), lambda i, *_: (i, 0, 0)),
        ((ns + EDGE, width), BF16, (ns + EDGE, width), fixed),
    ]
    scratch = [
        pltpu.VMEM((EDGE, width), F32),
        pltpu.VMEM((EDGE, 2 * ns), F32),
        pltpu.VMEM((ns, width), F32),
        pltpu.VMEM((EDGE, LANES), F32),
    ]
    return call(states_body, (count,), ins, outs, scratch, flops=2 * rows * width * ns * 4, name="states")


def within_body(xc_ref, bc_ref, step_ref, cum_ref, cols_ref, segs_ref, spread_ref, y_ref):
    ns = bc_ref.shape[1] // 2
    width = xc_ref.shape[1]
    cum = cum_ref[...]
    cum_rows = cum.T
    bias = pairs_bias(cols_ref[:, 7:8], segs_ref[0:1], True)
    both = dot(bc_ref[:, ns:], bc_ref[:, :ns], ((1,), (1,)))
    step_wide = expand(step_ref[...], spread_ref[...])
    for pair in range(width // LANES):
        part = slice(pair * LANES, (pair + 1) * LANES)
        weighted = (xc_ref[:, part].astype(F32) * step_wide[:, part]).astype(BF16)
        maps = []
        for head in (2 * pair, 2 * pair + 1):
            gap = (cum[:, head : head + 1] - cum_rows[head : head + 1]) + bias
            maps.append((jnp.exp(gap) * both).astype(BF16))
        y_ref[:, part] = dot(jnp.concatenate(maps, axis=1), pair_masked(weighted))


def within(xc, bc, step, cum, cols, segs, spread):
    rows, width = xc.shape
    ins = [
        (xc, (CHUNK, width), rows_at),
        (bc, (CHUNK, bc.shape[1]), rows_at),
        (step, (CHUNK, LANES), rows_at),
        (cum, (CHUNK, LANES), rows_at),
        (cols, (CHUNK, cols.shape[1]), rows_at),
        (segs, (EDGE, CHUNK), lambda i, *_: (0, i)),
        (spread, spread.shape, fixed),
    ]
    outs = [((rows, width), F32, (CHUNK, width), rows_at)]
    return call(within_body, (rows // CHUNK,), ins, outs, flops=2 * rows * CHUNK * width * 4, name="within")[0]


def leave_body(count, *refs):
    payloads, refs = refs[:count], refs[count:]
    (w_gate, w_out, y_ref, low_ref, xc_ref, bc_ref, cum_ref, cols_ref, enter_ref, phi_ref, rows_ref, spread_ref) = refs[:12]
    ssm_ref, gate_ref, p_ref, in_ref, normed = refs[12:]
    ns = in_ref.shape[0]
    width = xc_ref.shape[1]
    spread = spread_ref[...]

    @pl.when(pl.program_id(0) == 0)
    def _():
        in_ref[...] = folded([p[...] for p in payloads])

    gate_ref[...] = dot(low_ref[...], w_gate[...])
    for sub in range(y_ref.shape[0] // CHUNK):
        here = slice(sub * CHUNK, (sub + 1) * CHUNK)
        phi_wide = expand(phi_ref[sub], spread)[0:1]
        begun = (enter_ref[sub].astype(F32) + phi_wide * in_ref[...]).astype(BF16)
        carried = cols_ref[here, 4:5] * jnp.exp(cum_ref[here])
        carried_wide = expand(carried, spread)
        far = dot(bc_ref[here, ns:], begun)
        ssm_ref[here] = y_ref[here] + carried_wide * far
    total = jnp.zeros((y_ref.shape[0], LANES), F32)
    for i in range(width // LANES):
        part = slice(i * LANES, (i + 1) * LANES)
        mixed = ssm_ref[:, part] + rows_ref[1:2, part] * xc_ref[:, part].astype(F32)
        gated = mixed * silu_parts(gate_ref[:, part])[1]
        total = total + gated * gated
        normed[:, part] = (gated * rows_ref[0:1, part]).astype(BF16)
    high, rest = split(jnp.broadcast_to(jnp.sum(total, axis=1, keepdims=True), total.shape))
    lane = lax.broadcasted_iota(jnp.int32, total.shape, 1)
    model = w_out.shape[0]
    p_ref[:, :model] = dot(normed[...], w_out[...], ((1,), (1,))).astype(BF16)
    p_ref[:, model:] = jnp.where(lane == 0, high.astype(F32), rest.astype(F32)).astype(BF16)


def leave(payloads, y_in, low, xc, bc, cum, cols, entered, phi, rowpack, spread, weights):
    rows, width = xc.shape
    model = low.shape[1]
    ns = bc.shape[1] // 2
    block = min(256, rows)
    subs = block // CHUNK
    ins = [(p, p.shape, fixed) for p in payloads]
    ins += [
        block_of(weights["gate"]),
        block_of(weights["out"]),
        (y_in, (block, width), rows_at),
        (low, (block, model), rows_at),
        (xc, (block, width), rows_at),
        (bc, (block, bc.shape[1]), rows_at),
        (cum, (block, LANES), rows_at),
        (cols, (block, cols.shape[1]), rows_at),
        (entered, (subs, ns, width), lambda i, *_: (i, 0, 0)),
        (phi, (subs, EDGE, LANES), lambda i, *_: (i, 0, 0)),
        (rowpack, rowpack.shape, fixed),
        (spread, spread.shape, fixed),
    ]
    outs = [
        ((rows, width), F32, (block, width), rows_at),
        ((rows, width), F32, (block, width), rows_at),
        ((rows, model + LANES), BF16, (block, model + LANES), rows_at),
        ((ns, width), F32, (ns, width), fixed),
    ]
    scratch = [pltpu.VMEM((block, width), BF16)]
    return call(functools.partial(leave_body, len(payloads)), (rows // block,), ins, outs, scratch, name="leave")


def back_gate_body(
    inner_total, ends, *refs
):
    if ends:
        hidden_ref, refs = refs[0], refs[1:]
        output_ref, refs = refs[14], refs[:14] + refs[15:]
    (
        up_ref, p_ref, q_ref, ssm_ref, xc_ref, gate_ref, bc_ref, cum_ref, cols_ref, phi_ref,
        factor_ref, rows_ref, spread_ref, w_ref,
        do_ref, dy_ref, dgate_ref, n_ref, gain_ref, out_ref, state,
    ) = refs
    step = pl.program_id(0)
    ns = state.shape[0]
    width = xc_ref.shape[1]
    spread = spread_ref[...]

    @pl.when(step == 0)
    def _():
        gain_ref[...] = jnp.zeros_like(gain_ref)
        state[...] = jnp.zeros_like(state)

    model = up_ref.shape[1]
    scale = gated_scale(p_ref, q_ref, model, inner_total)
    up = up_ref[...].astype(BF16)
    do_ref[...] = up.T
    summed = p_ref[:, :model].astype(F32) + q_ref[:, :model].astype(F32)
    if ends:
        output_ref[...] = hidden_ref[...].astype(F32) + scale * summed
    spread_sum = jnp.sum(up.astype(F32) * summed, axis=1, keepdims=True)
    pull = scale * scale * scale * spread_sum / inner_total
    scale_wide = jnp.broadcast_to(scale, (scale.shape[0], LANES))
    pull_wide = jnp.broadcast_to(pull, scale_wide.shape)
    back = dot(up, w_ref[...])
    for i in range(width // LANES):
        part = slice(i * LANES, (i + 1) * LANES)
        gain = rows_ref[0:1, part]
        gate = gate_ref[:, part]
        sig, soft = silu_parts(gate)
        mixed = ssm_ref[:, part] + rows_ref[1:2, part] * xc_ref[:, part].astype(F32)
        gated = mixed * soft
        scaled = gated * scale_wide
        grad = back[:, part]
        gain_ref[0:1, part] += jnp.sum(grad * scaled, axis=0, keepdims=True)
        grad_gated = grad * gain * scale_wide - gated * pull_wide
        dy_ref[:, part] = (grad_gated * soft).astype(BF16)
        dgate_ref[:, part] = (grad_gated * mixed * (sig * (1.0 + gate * (1.0 - sig)))).astype(BF16)
        n_ref[:, part] = (scaled * gain).astype(BF16)
    for sub in range(up_ref.shape[0] // CHUNK):
        here = slice(sub * CHUNK, (sub + 1) * CHUNK)
        phi_wide = expand(phi_ref[sub], spread)[0:1]
        carried_wide = expand(cols_ref[here, 4:5] * jnp.exp(cum_ref[here]), spread)
        c_turned = bc_ref[here, ns:].astype(F32).T.astype(BF16)
        carried_dy = (dy_ref[here].astype(F32) * carried_wide).astype(BF16)
        state[...] += phi_wide * dot(c_turned, carried_dy)

    @pl.when(step == pl.num_programs(0) - 1)
    def _():
        out_ref[:ns] = state[...].astype(BF16)
        out_ref[ns:] = factor_ref[...]


def back_gate(up, parts, ssm, xc, gate, bc, cum, cols, phi, ended, rowpack, spread, weights, inner_total, hidden=None):
    rows, width = xc.shape
    model = up.shape[1]
    ns = bc.shape[1] // 2
    block = min(256, rows)
    subs = block // CHUNK
    wide = (block, model)
    ins = [
        (up, wide, rows_at),
        (parts[0], (block, model + LANES), rows_at),
        (parts[1], (block, model + LANES), rows_at),
        (ssm, (block, width), rows_at),
        (xc, (block, width), rows_at),
        (gate, (block, width), rows_at),
        (bc, (block, 2 * ns), rows_at),
        (cum, (block, LANES), rows_at),
        (cols, (block, cols.shape[1]), rows_at),
        (phi, (subs, EDGE, LANES), lambda i, *_: (i, 0, 0)),
        (ended, (EDGE, width), lambda i, *_: (ns // EDGE, 0)),
        (rowpack, rowpack.shape, fixed),
        (spread, spread.shape, fixed),
        block_of(weights["out"]),
    ]
    outs = [
        ((model, rows), BF16, (model, block), columns_at),
        ((rows, width), BF16, (block, width), rows_at),
        ((rows, width), BF16, (block, width), rows_at),
        ((rows, width), BF16, (block, width), rows_at),
        ((EDGE, width), F32, (EDGE, width), fixed),
        ((ns + EDGE, width), BF16, (ns + EDGE, width), fixed),
    ]
    if hidden is not None:
        ins = [(hidden, wide, rows_at)] + ins
        outs = [((rows, model), F32, wide, rows_at)] + outs
    scratch = [pltpu.VMEM((ns, width), F32)]
    return call(
        functools.partial(back_gate_body, inner_total, hidden is not None), (rows // block,), ins, outs, scratch,
        flops=2 * rows * width * model * 1.3, name="back_gate",
    )


def back_within_body(
    xc_ref, bc_ref, step_ref, cum_ref, cols_ref, segs_ref, spread_ref, gather_ref, dy_ref, ssm_ref,
    dx_ref, left_ref, dbc_ref, products,
):
    ns = bc_ref.shape[1] // 2
    size, width = xc_ref.shape
    cum = cum_ref[...]
    cum_rows = cum.T
    bias = pairs_bias(cols_ref[:, 7:8], segs_ref[0:1], False)
    b_part = bc_ref[:, :ns]
    c_part = bc_ref[:, ns:]
    both = dot(b_part, c_part, ((1,), (1,)))
    step_wide = expand(step_ref[...], spread_ref[...])
    grad_both = jnp.zeros((size, size), F32)
    for pair in range(width // LANES):
        part = slice(pair * LANES, (pair + 1) * LANES)
        weighted = (xc_ref[:, part].astype(F32) * step_wide[:, part]).astype(BF16)
        dy = dy_ref[:, part]
        dy_pair = pair_masked(dy)
        grad_maps = dot(weighted, dy_pair, ((1,), (1,)))
        maps = []
        for k in (0, 1):
            head = 2 * pair + k
            decay = jnp.exp((cum_rows[head : head + 1] - cum[:, head : head + 1]) + bias)
            maps.append((decay * both).astype(BF16))
            grad_both = grad_both + decay * grad_maps[:, k * size : (k + 1) * size]
        grad_x = dot(jnp.concatenate(maps, axis=1), dy_pair)
        dx_ref[:, part] = grad_x.astype(BF16)
        high, rest = split(dy.astype(F32) * ssm_ref[:, part] - weighted.astype(F32) * grad_x)
        products[:size, part] = high
        products[size:, part] = rest
    left = dot(products[...], gather_ref[...])
    left_ref[...] = left[:size] + left[size:]
    dbc_ref[:, :ns] = dot(grad_both.astype(BF16), c_part)
    dbc_ref[:, ns:] = dot(grad_both.T.astype(BF16), b_part)


def back_within(xc, bc, step, cum, cols, segs, spread, gather, dy, ssm):
    rows, width = xc.shape
    ins = [
        (xc, (CHUNK, width), rows_at),
        (bc, (CHUNK, bc.shape[1]), rows_at),
        (step, (CHUNK, LANES), rows_at),
        (cum, (CHUNK, LANES), rows_at),
        (cols, (CHUNK, cols.shape[1]), rows_at),
        (segs, (EDGE, CHUNK), lambda i, *_: (0, i)),
        (spread, spread.shape, fixed),
        (gather, gather.shape, fixed),
        (dy, (CHUNK, width), rows_at),
        (ssm, (CHUNK, width), rows_at),
    ]
    outs = [
        ((rows, width), BF16, (CHUNK, width), rows_at),
        ((rows, LANES), F32, (CHUNK, LANES), rows_at),
        ((rows, bc.shape[1]), F32, (CHUNK, bc.shape[1]), rows_at),
    ]
    scratch = [pltpu.VMEM((2 * CHUNK, width), BF16)]
    return call(back_within_body, (rows // CHUNK,), ins, outs, scratch, name="back_within")


def conv_back(ext, same, taps, grad_conv, next_rows):
    size = ext.shape[0] - EDGE
    shifts = conv_shifts(ext, same)
    pre = conv_sum(shifts, taps)
    sig = jax.nn.sigmoid(pre)
    grad_pre = grad_conv * (sig * (1.0 + pre * (1.0 - sig)))
    sums = [jnp.sum(grad_pre * shifts[lag], axis=0, keepdims=True) for lag in range(4)]
    sums.append(jnp.sum(grad_pre, axis=0, keepdims=True))
    zero = jnp.zeros((EDGE, ext.shape[1]), F32)
    length = size + 2 * EDGE
    raw = taps[0:1] * jnp.concatenate([zero, grad_pre], axis=0)
    firsts = []
    for lag in (1, 2, 3):
        term = grad_pre * same[lag] * taps[lag : lag + 1]
        firsts.append(term[:EDGE])
        padded = jnp.concatenate([zero, term, next_rows[lag - 1]], axis=0)
        raw = raw + pltpu.roll(padded, length - lag, 0)[: size + EDGE]
    return raw, firsts, sums


def back_inter_body(count_in, flag, *refs):
    payloads, refs = refs[:count_in], refs[count_in:]
    (
        x_ref, before_ref, edge_ref, xc_ref, bc_ref, step_ref, cum_ref, cols_ref, dt_ref, dy_ref, dxi_ref,
        left_ref, dbci_ref, enter_ref, phi_ref, in_ref, taps_ref, head_ref, rows_ref, spread_ref, gather_ref, sums_ref,
        dx_ref, last_ref, prior_ref, mine_ref, theirs_ref, ddt_ref, conv_ref, heads_ref, skip_ref,
        grad_state, next_rows, wide, far, carried, held, begun, ending, products,
    ) = refs
    step = pl.program_id(0)
    chunk = pl.num_programs(0) - 1 - step
    ns = in_ref.shape[0]
    size, width = xc_ref.shape

    @pl.when(step == 0)
    def _():
        grad_state[...] = folded([p[...] for p in payloads])
        next_rows[...] = jnp.zeros_like(next_rows)
        conv_ref[...] = jnp.zeros_like(conv_ref)
        heads_ref[...] = jnp.zeros_like(heads_ref)
        skip_ref[...] = jnp.zeros_like(skip_ref)

    cols = cols_ref[...]
    same = same_columns(cols, LANES)
    cum = cum_ref[...]
    dt = step_ref[...]
    decay_in = cols[:, 4:5] * jnp.exp(cum)
    decay_out = cols[:, 5:6] * jnp.exp(cum[size - 1 : size] - cum)
    fold_rows = jnp.broadcast_to(decay_in[size - EDGE : size][EDGE - 1 : EDGE], (EDGE, LANES))
    b_part = bc_ref[:, :ns]
    c_part = bc_ref[:, ns:]
    c_turned = c_part.astype(F32).T.astype(BF16)
    stacked = jnp.concatenate([decay_in, decay_out, dt, fold_rows, phi_ref[0]], axis=0)
    wide[...] = expand(stacked, spread_ref[...])
    fold_at = 3 * size
    for i in range(width // LANES):
        part = slice(i * LANES, (i + 1) * LANES)
        dy = dy_ref[:, part].astype(F32)
        weighted = xc_ref[:, part].astype(F32) * wide[2 * size : 3 * size, part]
        fold_wide = wide[fold_at : fold_at + 1, part]
        grad_end = grad_state[:, part]
        start = enter_ref[0, :, part].astype(F32) + wide[fold_at + EDGE : fold_at + EDGE + 1, part] * in_ref[:, part]
        carried[:, part] = (dy * wide[:size, part]).astype(BF16)
        held[:, part] = (weighted * wide[size : 2 * size, part]).astype(BF16)
        begun[:, part] = start.astype(BF16)
        ending[:, part] = grad_end.astype(BF16)
        pass_sum = jnp.sum(start * grad_end, axis=0, keepdims=True) * fold_wide
        products[2 * size :, part] = jnp.broadcast_to(pass_sum, (2 * EDGE, LANES)).astype(BF16)
        grad_state[:, part] = fold_wide * grad_end
    far[...] = dot(b_part, ending[...])
    dbc_c = dbci_ref[:, ns:] + dot(carried[...], begun[...], ((1,), (1,)))
    dbc_b = dbci_ref[:, :ns] + dot(held[...], ending[...], ((1,), (1,)))
    grad_state[...] += dot(c_turned, carried[...])
    own_b = flag[0] == 0
    mine_ref[...] = jnp.where(own_b, dbc_b, dbc_c).astype(BF16)
    theirs_ref[...] = jnp.where(own_b, dbc_c, dbc_b).astype(BF16)

    first_chunk = chunk == 0
    for i in range(width // LANES):
        part = slice(i * LANES, (i + 1) * LANES)
        dy = dy_ref[:, part].astype(F32)
        x_conv = xc_ref[:, part].astype(F32)
        dt_wide = wide[2 * size : 3 * size, part]
        grad_far = wide[size : 2 * size, part] * far[:, part]
        grad_weighted = dxi_ref[:, part].astype(F32) + grad_far
        products[:size, part] = (x_conv * dt_wide * grad_far).astype(BF16)
        products[size : 2 * size, part] = (x_conv * grad_weighted).astype(BF16)
        skip_ref[0:1, part] += jnp.sum(dy * x_conv, axis=0, keepdims=True)
        grad_conv = dt_wide * grad_weighted + rows_ref[1:2, part] * dy
        ahead = jnp.where(first_chunk, edge_ref[:, part].astype(F32), before_ref[:, part].astype(F32))
        ext = jnp.concatenate([ahead, x_ref[:, part].astype(F32)], axis=0)
        raw, firsts, tap_sums = conv_back(
            ext, same, taps_ref[:, part], grad_conv, [next_rows[k, :, part] for k in range(3)]
        )
        for k in range(3):
            next_rows[k, :, part] = firsts[k]
        for k in range(5):
            conv_ref[k : k + 1, part] += tap_sums[k]
        dx_ref[:, part] = raw[EDGE:].astype(BF16)
        prior_ref[:, part] = raw[:EDGE]

        @pl.when(step == 0)
        def _(raw=raw, part=part):
            last_ref[:, part] = raw[size:]

    per_head = dot(products[...], gather_ref[...])
    outward, direct, through = per_head[:size], per_head[size : 2 * size], per_head[2 * size : 2 * size + 1]
    grad_rate = dot(sums_ref[...], jnp.concatenate([left_ref[...], outward], axis=0), precision=EXACT) + through
    grad_dt = direct + head_ref[1:2] * grad_rate
    grad_raw = grad_dt * cols[:, 3:4] * jax.nn.sigmoid(dt_ref[...] + head_ref[0:1])
    ddt_ref[...] = grad_raw.astype(BF16)
    heads_ref[0:1] += jnp.sum(grad_raw, axis=0, keepdims=True)
    heads_ref[1:2] += jnp.sum(grad_rate * head_ref[1:2] * dt, axis=0, keepdims=True)


def back_inter(
    flag, payloads, x_raw, edge, xc, bc, step, cum, cols, dt_raw, dy, dx_in, left, dbc_in, entered, phi, state_in,
    taps, head, rowpack, spread, gather, sums,
):
    rows, width = xc.shape
    ns = bc.shape[1] // 2
    count = rows // CHUNK

    def back(i, *_):
        return (count - 1 - i, 0)

    def back3(i, *_):
        return (count - 1 - i, 0, 0)

    def before(i, *_):
        return (jnp.maximum((count - 1 - i) * (CHUNK // EDGE) - 1, 0), 0)

    def at(width_now):
        return (CHUNK, width_now)

    ins = [(p, p.shape, fixed) for p in payloads] + [
        (x_raw, at(width), back),
        (x_raw, (EDGE, width), before),
        (edge, (EDGE, width), fixed),
        (xc, at(width), back),
        (bc, at(2 * ns), back),
        (step, at(LANES), back),
        (cum, at(LANES), back),
        (cols, at(cols.shape[1]), back),
        (dt_raw, at(LANES), back),
        (dy, at(width), back),
        (dx_in, at(width), back),
        (left, at(LANES), back),
        (dbc_in, at(2 * ns), back),
        (entered, (1, ns, width), back3),
        (phi, (1, EDGE, LANES), back3),
        (state_in, state_in.shape, fixed),
        (taps, taps.shape, fixed),
        (head, head.shape, fixed),
        (rowpack, rowpack.shape, fixed),
        (spread, spread.shape, fixed),
        (gather, gather.shape, fixed),
        (sums, sums.shape, fixed),
    ]
    outs = [
        ((rows, width), BF16, at(width), back),
        ((EDGE, width), F32, (EDGE, width), fixed),
        ((EDGE, width), F32, (EDGE, width), fixed),
        ((rows, ns), BF16, at(ns), back),
        ((rows, ns), BF16, at(ns), back),
        ((rows, LANES), BF16, at(LANES), back),
        ((EDGE, width), F32, (EDGE, width), fixed),
        ((EDGE, LANES), F32, (EDGE, LANES), fixed),
        ((EDGE, width), F32, (EDGE, width), fixed),
    ]
    scratch = [
        pltpu.VMEM((ns, width), F32),
        pltpu.VMEM((3, EDGE, width), F32),
        pltpu.VMEM((3 * CHUNK + 2 * EDGE, width), F32),
        pltpu.VMEM((CHUNK, width), F32),
        pltpu.VMEM((CHUNK, width), BF16),
        pltpu.VMEM((CHUNK, width), BF16),
        pltpu.VMEM((ns, width), BF16),
        pltpu.VMEM((ns, width), BF16),
        pltpu.VMEM((2 * CHUNK + 2 * EDGE, width), BF16),
    ]
    return call(
        functools.partial(back_inter_body, len(payloads)), (count,), ins, outs, scratch, flag, name="back_inter"
    )


def back_bc_body(
    flag, raw_ref, edge_ref, cols_ref, taps_ref, mine_ref, theirs_ref, out_ref, last_ref, prior_ref, sums_ref
):
    size, width = raw_ref.shape
    same = same_columns(cols_ref[...], width)
    ext = jnp.concatenate([edge_ref[...].astype(F32), raw_ref[...].astype(F32)], axis=0)
    grad = mine_ref[...].astype(F32) + theirs_ref[...].astype(F32)
    zero = jnp.zeros((EDGE, width), F32)
    raw, _, sums = conv_back(ext, same, taps_ref[...], grad, [zero] * 3)
    out_ref[...] = raw[EDGE:].astype(BF16)
    last_ref[...] = raw[size:]
    prior_ref[...] = raw[:EDGE]
    sums_ref[...] = jnp.concatenate(sums + [zero[:3]], axis=0)


def back_bc(flag, raw, edge, cols, taps, mine, theirs):
    rows, ns = mine.shape
    before = edge.shape[1] // ns - 2
    ins = [
        (raw, (rows, ns), lambda i, t: (0, t[0])),
        (edge, (EDGE, ns), lambda i, t: (0, before + t[0])),
        (cols, cols.shape, fixed),
        (taps, (EDGE, ns), lambda i, t: (0, t[0])),
        (mine, mine.shape, fixed),
        (theirs, theirs.shape, fixed),
    ]
    outs = [((rows, ns), BF16, (rows, ns), fixed)]
    outs += [((EDGE, ns), F32, (EDGE, ns), fixed)] * 3
    return call(back_bc_body, (1,), ins, outs, (), flag, name="back_bc")


def back_low_body(flag, gate_ref, x_ref, bc_ref, dt_ref, wg_ref, wx_ref, wb_ref, wt_ref, out_ref):
    over = ((1,), (1,))
    total = dot(gate_ref[...], wg_ref[...], over) + dot(x_ref[...], wx_ref[...], over)
    total = total + dot(bc_ref[...], wb_ref[...], over) + dot(dt_ref[...], wt_ref[...], over)
    out_ref[...] = total.astype(BF16)


def back_low(flag, dgate, dx, dbc, ddt, weights):
    rows, width = dx.shape
    ns = dbc.shape[1]
    array, first = weights["lanes"]
    model = array.shape[0]
    block = min(256, rows)
    ins = [(v, (block, v.shape[1]), rows_at) for v in (dgate, dx, dbc, ddt)]
    ins += [
        block_of(weights["gate"]),
        block_of(weights["x"]),
        (array, (model, ns), lambda i, t: (0, first + t[0])),
        block_of((array, LANES, first + 2)),
    ]
    outs = [((rows, model), BF16, (block, model), rows_at)]
    return call(
        back_low_body, (rows // block,), ins, outs, (), flag, flops=2 * rows * model * (2 * width + 256), name="back_low"
    )[0]


def back_norm_body(up_ref, a_ref, b_ref, h_ref, gain_ref, out_ref, sum_ref):
    @pl.when(pl.program_id(0) == 0)
    def _():
        sum_ref[...] = jnp.zeros_like(sum_ref)

    hidden = h_ref[...].astype(F32)
    grad = a_ref[...].astype(F32) + b_ref[...].astype(F32)
    model = hidden.shape[1]
    norm = lax.rsqrt(jnp.mean(hidden * hidden, axis=1, keepdims=True) + EPSILON)
    normed = hidden * norm
    sum_ref[0:1] += jnp.sum(grad * normed, axis=0, keepdims=True)
    gained = grad * gain_ref[0:1]
    inner = jnp.sum(gained * normed, axis=1, keepdims=True) / model
    out_ref[...] = up_ref[...].astype(F32) + norm * (gained - normed * inner)


def back_norm(up, a, b, hidden, gain):
    rows, model = hidden.shape
    block = min(256, rows)
    wide = (block, model)
    ins = [(v, wide, rows_at) for v in (up, a, b, hidden)] + [(gain, gain.shape, fixed)]
    outs = [((rows, model), F32, wide, rows_at), ((EDGE, model), F32, (EDGE, model), fixed)]
    return call(back_norm_body, (rows // block,), ins, outs, name="back_norm")


def weight_grad_body(places, shards, cuts, owners, where, *refs):
    lefts, refs = refs[: max(owners) + 1], refs[max(owners) + 1 :]
    factors, outs, result = refs[: len(cuts)], refs[len(cuts) : len(cuts) + places], refs[len(cuts) + places]
    model = lefts[0].shape[0]
    rows = model // (places * shards)
    step = pl.program_id(0)
    for factor, owner, (start, end) in zip(factors, owners, cuts):

        @pl.when((step >= start) & (step < end))
        def _(factor=factor, owner=owner):
            made = dot(lefts[owner][...], factor[...])
            if places == 1:
                outs[0][...] = made.astype(BF16)
            else:
                result[...] = made

    if places == 1:
        return
    for k in range(places):
        for z in range(shards):
            start = pl.multiple_of((z * places + where[k]) * rows, rows)
            outs[k][z * rows : (z + 1) * rows] = result[pl.ds(start, rows)].astype(BF16)


def weight_grad(where, places, shards, products):
    model, rows = products[0][0].shape
    tile = 512 if places == 1 and all(b.shape[1] % 512 == 0 for _, factors in products for b in factors) else 256
    cuts, owners, ins, at = [], [], [], 0
    for i, (a, factors) in enumerate(products):
        ins.append((a, a.shape, fixed))
        for b in factors:
            cuts.append((at, at + b.shape[1] // tile))
            owners.append(i)
            at = cuts[-1][1]
    for b, (start, end) in zip([b for _, factors in products for b in factors], cuts):
        ins.append((b, (rows, tile), lambda i, *_, s=start, e=end: (0, jnp.clip(i - s, 0, e - s - 1))))
    width = at * tile
    part = model // places
    outs = [((part, width), BF16, (part, tile), columns_at)] * places
    scratch = [pltpu.VMEM((model, tile), F32)]
    return call(
        functools.partial(weight_grad_body, places, shards, cuts, owners), (at,), ins, outs, scratch, where,
        name="weight_grad",
    )


def relative(value, axis, by):
    size = lax.axis_size(axis)
    return lax.ppermute(value, axis, [(i, i ^ by) for i in range(size)])


def shifted(value, axis, by):
    size = lax.axis_size(axis)
    return lax.ppermute(value, axis, [(i, i + by) for i in range(size) if 0 <= i + by < size])


def tree_sum(values):
    while len(values) > 1:
        values = [a + b for a, b in zip(values[0::2], values[1::2])]
    return values[0]


def cut_body(joined, where, zx_ref, wbc_ref, wdt_ref, down_ref, *refs):
    width = zx_ref.shape[3]
    both, heads = wbc_ref.shape[2], wdt_ref.shape[2]
    rest, main, turned = refs[0], refs[1], refs[-1]
    other, at = (main, width) if joined else (refs[2], 0)
    rows = main.shape[0]
    main[:, :width] = zx_ref[0, :, 1]
    other[:, at : at + both] = wbc_ref[0]
    other[:, at + both :] = jnp.zeros((other.shape[0], LANES), BF16)
    other[:, at + both : at + both + heads] = wdt_ref[0]
    turned[...] = down_ref[0].astype(F32).T
    rest[:, :width] = zx_ref[0, :, 0]
    rest[:, width:] = turned[pl.ds(pl.multiple_of(where[0] * rows, rows), rows)].astype(BF16)


def cut_rows(layer, joined, place, rows, w_zx, w_bc, w_dt, w_out):
    local, _, width = w_zx.shape[1:]
    extra = w_bc.shape[2] + LANES
    taken = rows if joined else local
    ins = [(w_zx, (1, rows, 2, width), lambda i, c: (layer, c[0], 0, 0))]
    ins += [(v, (1, taken, v.shape[2]), lambda i, c: (layer, c[0] if joined else 0, 0)) for v in (w_bc, w_dt)]
    ins += [(w_out, (1,) + w_out.shape[1:], lambda i, c: (layer, 0, 0))]
    shapes = [(rows, 2 * width)] + ([(rows, width + extra)] if joined else [(rows, width), (local, extra)])
    outs = [(shape, BF16, shape, fixed) for shape in shapes]
    scratch = [pltpu.VMEM((local, width), F32)]
    return call(functools.partial(cut_body, joined), (1,), ins, outs, scratch, place, name="cut")


def gather_rows(piece):
    return lax.all_gather(piece, ("shard", "ctx"), axis=0, tiled=True)


def gather_shard(piece):
    return jnp.concatenate([piece] + [relative(piece, "shard", k) for k in range(1, lax.axis_size("shard"))], axis=0)


def gather_ctx(along):
    return [along] + [relative(along, "ctx", k) for k in range(1, lax.axis_size("ctx"))]


def gather_far(piece):
    return [piece] + [relative(piece, "shard", k) for k in range(1, lax.axis_size("shard"))]


def near_rows(pieces):
    return [pieces[0]] + [relative(p, "ctx", k) for k, p in enumerate(pieces) if k]


def split_sum_body(counts, where, *refs):
    arrays, outs = refs[: sum(counts)], refs[sum(counts) :]
    rows = outs[0].shape[0]
    for k, out in enumerate(outs):
        at = pl.ds(pl.multiple_of(where[k] * rows, rows), rows)
        done, column = 0, 0
        for count in counts:
            total = tree_sum([v[at].astype(F32) for v in arrays[done : done + count]])
            out[:, column : column + total.shape[1]] = total.astype(out.dtype)
            done, column = done + count, column + total.shape[1]


def split_sum(order, parts, groups):
    ins = [(v, v.shape, fixed) for group in groups for v in group]
    shape = (groups[0][0].shape[0] // parts, sum(group[0].shape[1] for group in groups))
    outs = [(shape, BF16 if k else F32, shape, fixed) for k in range(parts)]
    counts = [len(group) for group in groups]
    return call(functools.partial(split_sum_body, counts), (1,), ins, outs, (), order, name="split_sum")


def scattered(pieces, axis):
    return [pieces[0]] + [relative(pieces[k], axis, k) for k in range(1, len(pieces))]


def finish_body(counts, *refs):
    zx_ref, out_ref, small_ref = refs[-3:]
    layers, width = zx_ref.shape[0], zx_ref.shape[3]
    late = tree_sum([v[...].astype(F32) for v in refs[sum(counts) : -3]])
    span = late.shape[1] // layers
    for layer, count in enumerate(counts):
        early = tree_sum([v[...].astype(F32) for v in refs[:count]])
        refs = refs[count:]
        zx_ref[layer, :, 0] = early[:, :width]
        zx_ref[layer, :, 1] = late[:, layer * span : layer * span + width]
        out_ref[layer] = early[:, width:].T
        small_ref[layer] = late[:, layer * span + width : (layer + 1) * span]


def finish(early, late, width):
    layers = len(early)
    rows, span = late[0].shape
    ins = [(v, v.shape, fixed) for parts in list(early) + [late] for v in parts]
    shapes = [(layers, rows, 2, width), (layers, width, rows), (layers, rows, span // layers - width)]
    outs = [(v, F32, v, lambda *_, n=len(v): (0,) * n) for v in shapes]
    return call(functools.partial(finish_body, [len(parts) for parts in early]), (1,), ins, outs, name="finish")


def axis_sum(value, axis):
    return tree_sum([value] + [relative(value, axis, k) for k in range(1, lax.axis_size(axis))])


def around(value, by=1):
    size = lax.axis_size("shard")
    return lax.ppermute(value, "shard", [(i, (i + by) % size) for i in range(size)])


def neighbours(ended, sign):
    return [shifted(ended, "ctx", sign * d) for d in range(1, lax.axis_size("ctx"))]


def swap(value):
    return lax.ppermute(value, "tp", [(0, 1), (1, 0)])


def pad_rows(value):
    return jnp.pad(value, ((0, EDGE - value.shape[0]), (0, 0)))


def per_device(
    seq_in, w_zx, w_bc, w_dt, w_out, norm_gain, conv_x, conv_bc, head_params, gate_gain, segments, pad_mask, cotangent
):
    rows, model = seq_in.shape[1:]
    layers = w_zx.shape[0]
    width = w_zx.shape[3]
    heads = head_params.shape[2]
    ns = w_bc.shape[2] // 2
    shards, places = lax.axis_size("shard"), lax.axis_size("ctx")
    inner_total = width * lax.axis_size("tp")
    z, c, t = lax.axis_index("shard"), lax.axis_index("ctx"), lax.axis_index("tp")
    flag = t.astype(jnp.int32).reshape(1)
    chunks = rows // CHUNK

    ids = jnp.concatenate([jnp.full((3,), -1, jnp.int32), segments[0]])
    ext = lax.dynamic_slice_in_dim(ids, c * rows, rows + 3, 0)
    seg = ext[3:]
    mask = lax.dynamic_slice_in_dim(pad_mask[0], c * rows, rows, 0)
    firsts = ext[2 : 2 + rows].reshape(chunks, CHUNK)[:, :1]
    lasts = seg.reshape(chunks, CHUNK)[:, CHUNK - 1 :]
    by_chunk = seg.reshape(chunks, CHUNK)
    columns = [(ext[3 - lag : 3 - lag + rows] == seg) for lag in (1, 2, 3)]
    columns += [mask, (by_chunk == firsts).reshape(rows), (by_chunk == lasts).reshape(rows), mask, seg]
    cols = jnp.stack([v.astype(F32) for v in columns], axis=1)
    segs = jnp.broadcast_to(seg.astype(F32)[None], (EDGE, rows))

    head_of = jnp.arange(width)[None] // (width // heads)
    spread = (jnp.arange(2 * LANES)[:, None] % LANES == head_of).astype(BF16)
    gather = (head_of.T == jnp.arange(LANES)[None]).astype(BF16)
    at = jnp.arange(CHUNK)
    lower = (at[:, None] >= at[None]).astype(F32)
    sums = jnp.concatenate([(at[:, None] <= at[None]).astype(F32), (at[:, None] > at[None]).astype(F32)], axis=1)

    own_count = model // (shards * places)
    tie = lax.optimization_barrier
    place = c.astype(jnp.int32).reshape(1)
    crossed = jnp.concatenate([z ^ jnp.arange(shards), c ^ jnp.arange(places)]).astype(jnp.int32)

    rest_piece, x_piece, other_piece = cut_rows(0, False, place, own_count, w_zx, w_bc, w_dt, w_out)
    before = shifted(seq_in[0, rows - EDGE :], "ctx", 1)
    near, far = gather_ctx(gather_shard(x_piece)), gather_far(other_piece)
    extra = 2 * ns + LANES
    rest = gather_rows(rest_piece)
    weights = [dict(gate=(rest, width, 0), out=(rest, width, 1))]
    mains = [None]
    for layer in range(1, layers):
        rest_piece, main_piece = cut_rows(layer, True, place, own_count, w_zx, w_bc, w_dt, w_out)
        rest = gather_rows(rest_piece)
        weights.append(dict(gate=(rest, width, 0), out=(rest, width, 1)))
        mains.append(main_piece)

    hidden = seq_in[0]
    parts = None
    kept = []
    for layer in range(layers):
        gain_in = pad_rows(norm_gain[layer][None])
        taps = pad_rows(conv_x[layer])
        taps_bc = pad_rows(conv_bc[layer])
        decay = -jnp.exp(head_params[layer, 1])
        head = jnp.pad(
            jnp.stack([head_params[layer, 0], decay]), ((0, EDGE - 2), (0, LANES - heads))
        )
        skip = jnp.repeat(head_params[layer, 2], width // heads)
        rowpack = pad_rows(jnp.stack([gate_gain[layer], skip]))

        if layer > 0:
            p_tail, q_tail = parts[0][rows - EDGE :].astype(F32), parts[1][rows - EDGE :].astype(F32)
            squares = p_tail[:, model : model + 2] + q_tail[:, model : model + 2]
            scale = lax.rsqrt(jnp.sum(squares, axis=1, keepdims=True) / inner_total + EPSILON)
            tail = hidden[rows - EDGE :].astype(F32) + scale * (p_tail[:, :model] + q_tail[:, :model])
            before = shifted(tail, "ctx", 1)
        hidden, low, turned, x_raw, raw_bc, dt_raw, w_x, w_other = enter(
            crossed, shards, near, far, hidden, parts, gain_in, width, 2 * ns, inner_total
        )
        weights[layer].update(x=(w_x, width, 0), other=(w_other, extra, 0), lanes=(w_other, 0))
        more = layer + 1 < layers
        if more:
            main, dt_raw = tie((mains[layer + 1], dt_raw))
            coming = gather_shard(main)
        edge, xc, bc, step, cum, entered, phi, ended = states(
            x_raw, raw_bc, dt_raw, before, gain_in, weights[layer], cols, taps, taps_bc, head, spread, lower
        )
        y_in = within(xc, bc, step, cum, cols, segs, spread)
        given = neighbours(ended, 1)
        if more:
            given, coming, y_in = tie((given, coming, y_in))
            near, far = gather_ctx(coming), []
        ssm, gate, p_own, state_in = leave(
            given, y_in, low, xc, bc, cum, cols, entered, phi, rowpack, spread, weights[layer]
        )
        if more:
            p_own, near = tie((p_own, near))
        parts = (p_own, swap(p_own))
        kept.append(
            dict(
                hidden=hidden, turned=turned, x_raw=x_raw, raw_bc=raw_bc, dt_raw=dt_raw, edge=edge, gate=gate, xc=xc, bc=bc,
                step=step, cum=cum, entered=entered, phi=phi, ended=ended, state_in=state_in, ssm=ssm, parts=parts,
                gain_in=gain_in, taps=taps, taps_bc=taps_bc, head=head, rowpack=rowpack,
            )
        )
    direct = own_count % 16 == 0
    ctx_order = (c ^ jnp.arange(places)).astype(jnp.int32)
    ring_order = ((z - 1 - jnp.arange(shards)) % shards).astype(jnp.int32)
    shard_order = (z ^ jnp.arange(shards)).astype(jnp.int32)

    def owned(full):
        return lax.psum_scatter(full, ("shard", "ctx"), scatter_dimension=0, tiled=True)

    def add(a, b):
        return (a.astype(F32) + b.astype(F32)).astype(BF16)

    up = cotangent[0]
    smalls, early_sums, late_above = [], [], []
    for layer in reversed(range(layers)):
        k = kept[layer]
        last_layer = layer == layers - 1
        made = back_gate(
            up, k["parts"], k["ssm"], k["xc"], k["gate"], k["bc"], k["cum"], cols, k["phi"], k["ended"],
            k["rowpack"], spread, weights[layer], inner_total, k["hidden"] if last_layer else None,
        )
        if last_layer:
            output, made = made[0], made[1:]
        do, dy, dgate, normed, gain_rows, begun = made
        early_pair = [(k["turned"], [dgate]), (do, [normed])]
        later = neighbours(begun, -1)
        quick = direct and layer == 0
        if quick:
            early = weight_grad(ring_order, shards, 1, early_pair)
            dy, early = tie((dy, early))
            moving = around(early[0])
        else:
            early = weight_grad(ctx_order, 1, 1, early_pair)[0]
            dy, early = tie((dy, early))
        dx_in, left, dbc_in = back_within(
            k["xc"], k["bc"], k["step"], k["cum"], cols, segs, spread, gather, dy, k["ssm"]
        )
        if not quick:
            dx_in, later, early = tie((dx_in, later, early))
            g_early = owned(early)
        if quick and not last_layer:
            dx_in, early_sums[0] = tie((dx_in, early_sums[0]))
            later, rest_above = tie((later, rest_above))
            rest_above = near_rows(rest_above)
        edge = k["edge"]
        dx, last, prior, dbc_mine, dbc_theirs, ddt, conv_rows, head_rows, skip_rows = back_inter(
            flag, later, k["x_raw"], edge, k["xc"], k["bc"], k["step"], k["cum"], cols, k["dt_raw"], dy,
            dx_in, left, dbc_in, k["entered"], k["phi"], k["state_in"], k["taps"], k["head"], k["rowpack"],
            spread, gather, sums,
        )
        if quick:
            dx, moving = tie((dx, moving))
            moving = around(add(moving, early[1]))
            if not last_layer:
                dbc_theirs, late_above[0] = tie((dbc_theirs, rest_above))
        db, last_bc, prior_bc, conv_bc_rows = back_bc(
            flag, k["raw_bc"], edge, cols, k["taps_bc"], dbc_mine, swap(dbc_theirs)
        )
        back_rows = shifted(jnp.concatenate([prior, prior_bc], axis=1), "ctx", -1)
        dx = lax.dynamic_update_slice_in_dim(dx, (last + back_rows[:, :width]).astype(BF16), rows - EDGE, 0)
        db = lax.dynamic_update_slice_in_dim(db, (last_bc + back_rows[:, width:]).astype(BF16), rows - EDGE, 0)
        late_pair = [(k["turned"], [dx, jnp.concatenate([db, ddt], axis=1)])]
        if direct:
            rest = weight_grad(ctx_order, places, shards, late_pair)
            dgate, rest = tie((dgate, rest))
            if quick:
                rest = near_rows(rest)
        else:
            g_rest = owned(weight_grad(ctx_order, 1, 1, late_pair)[0])
        dlow = back_low(flag, dgate, dx, db, ddt, weights[layer])
        if quick:
            dlow, moving = tie((dlow, moving))
            for one in early[2:-1]:
                moving = around(add(moving, one))
            dlow, rest = tie((dlow, rest))
        up, norm_rows = back_norm(up, dlow, swap(dlow), k["hidden"], k["gain_in"])
        packed = jnp.concatenate(
            [norm_rows[0], conv_rows[:5].reshape(-1), gain_rows[0], skip_rows[0], conv_bc_rows[:5].reshape(-1),
             head_rows[:2].reshape(-1)]
        )
        smalls.insert(0, packed)
        if not direct:
            early_sums.insert(0, [g_early])
            late_above.insert(0, g_rest)
        elif not quick:
            rest_above = rest
            early_sums.insert(0, [g_early])
            late_above.insert(0, None)
        else:
            late_sum = scattered(split_sum(shard_order, shards, [rest] + late_above), "shard")
            partial = axis_sum(jnp.concatenate(smalls), "ctx")
            partial, moving, late_sum = tie((partial, moving, late_sum))
            early_sums.insert(0, scattered(split_sum(ctx_order, places, [[moving, early[-1]]]), "ctx"))
    if not direct:
        late_sum = [jnp.concatenate(late_above, axis=1)]
        partial = axis_sum(jnp.concatenate(smalls), "ctx")
    packed = axis_sum(partial, "shard").reshape(layers, -1)
    cuts = [model, 5 * width, width, width, 5 * ns, 2 * LANES]
    ends = [sum(cuts[: i + 1]) for i in range(len(cuts))]
    n_sum, cx_sum, gg_sum, sk_sum, cb_sum, hd_sum = jnp.split(packed, ends[:-1], axis=1)
    cb_mine = cb_sum.reshape(layers, 5, ns)
    grad_zx, grad_out, grad_small = finish(early_sums, late_sum, width)
    small_mine = grad_small[:, :, :ns]
    cb_other, small_other = swap(cb_mine), swap(small_mine)

    def ordered(own, other):
        first = jnp.where(t == 0, own, other)
        return jnp.concatenate([first, jnp.where(t == 0, other, own)], axis=-1)

    hd = hd_sum.reshape(layers, 2, LANES)[:, :, :heads]
    skip_sum = jnp.sum(sk_sum.reshape(layers, heads, width // heads), axis=-1)
    return (
        output[None],
        up[None],
        grad_zx,
        ordered(small_mine, small_other),
        grad_small[:, :, ns : ns + heads],
        grad_out,
        n_sum,
        cx_sum.reshape(layers, 5, width),
        ordered(cb_mine, cb_other),
        jnp.concatenate([hd, skip_sum[:, None]], axis=1),
        gg_sum,
    )


def solution(mesh):
    in_specs = (
        P("shard", "ctx", None),
        P(None, "shard", None, "tp"),
        P(None, "shard", None),
        P(None, "shard", "tp"),
        P(None, "tp", "shard"),
        P(),
        P(None, None, "tp"),
        P(),
        P(None, None, "tp"),
        P(None, "tp"),
        P("shard", None),
        P("shard", None),
        P("shard", "ctx", None),
    )
    out_specs = (
        P("shard", "ctx", None),
        P("shard", "ctx", None),
        P(None, ("shard", "ctx"), None, "tp"),
        P(None, ("shard", "ctx"), None),
        P(None, ("shard", "ctx"), "tp"),
        P(None, "tp", ("shard", "ctx")),
        P(),
        P(None, None, "tp"),
        P(),
        P(None, None, "tp"),
        P(None, "tp"),
    )
    return jax.shard_map(per_device, mesh=mesh, in_specs=in_specs, out_specs=out_specs, check_vma=False)
```

time: 789 us -> 586 us (0.74)
  waiting for transfers between devices: 185 us -> 88.2 us
  starting transfers between devices: 161 us -> 117 us
  matrix products: 30.4 us -> 0 us
  local copies, waits for them, and re-layouts: 59.5 us -> 32 us
  other arithmetic: 42.2 us -> 21.3 us
  between operations: 3.94 us -> 15.1 us
    ppermute x90 -> x33, waiting for transfers between devices: 183 us -> 56.3 us  [relative(): return lax.ppermute(value, axis, [(i, i ^ by) for i in range(size)])]
    ppermute x90 -> x33, starting transfers between devices: 92.4 us -> 50.5 us  [relative(): return lax.ppermute(value, axis, [(i, i ^ by) for i in range(size)])]
    dot_general x8 -> x0, matrix products: 30.4 us -> none  [the longest x2 8.84 us: per_device(): lax.dot_general(dx, w_main[:, :width], (((1,), (1,)), ((), ())), preferre...]
    ppermute x12 -> x8, waiting for transfers between devices: 1.27 us -> 14.8 us  [swap(): return lax.ppermute(value, 'tp', [(0, 1), (1, 0)])]
    slice x25 -> x3, local copies, waits for them, and re-layouts: 12.7 us -> 1.7 us  [the longest x1 0.84 us: per_device(): small_mine = grad_small[:, :, :ns]]
    unnamed x369 -> x152, local copies, waits for them, and re-layouts: 28.1 us -> 17.1 us
    another operation x12 -> x0, other arithmetic: 10.7 us -> none  [the longest x4 5.16 us: per_device(): jnp.stack([g[0], g[1]], axis=1)]
    all_gather x0 -> x2, waiting for transfers between devices: none -> 8.64 us  [gather_rows(): return lax.all_gather(piece, ('shard', 'ctx'), axis=0, tiled=True)]
  transfers between devices with their start and end apart: 118 -> 63, of which waited for: 39 -> 20; matrix products, arithmetic and copies ran while one was open for 13% -> 7% of each run, Pallas kernels for 27% -> 45%
where the time goes in v2:
time: 586 us; the launch traced here: 574 us
  Pallas kernels  301 us (51%)
  starting transfers between devices  117 us (20%)
  waiting for transfers between devices  88.2 us (15%)
  local copies, waits for them, and re-layouts  32 us (5%)
  other arithmetic  21.3 us (4%)
  between operations  15.1 us (3%)
    pallas_call x29, Pallas kernels, call(): return made(*([scalars] if count else []) + arrays)  301 us
    ppermute x33, waiting for transfers between devices, relative(): return lax.ppermute(value, axis, [(i, i ^ by) for i in range(size)])  56.3 us
    ppermute x33, starting transfers between devices, relative(): return lax.ppermute(value, axis, [(i, i ^ by) for i in range(size)])  50.5 us
    ppermute x8, starting transfers between devices, swap(): return lax.ppermute(value, 'tp', [(0, 1), (1, 0)])  31 us
    ppermute x16, starting transfers between devices, shifted(): lax.ppermute(value, axis, [(i, i + by) for i in range(size) if 0 <= i + b...  30.4 us
    unnamed x152, local copies, waits for them, and re-layouts  17.1 us
    ppermute x8, waiting for transfers between devices, swap(): return lax.ppermute(value, 'tp', [(0, 1), (1, 0)])  14.8 us
  transfers between devices with their start and end apart: 63, of which 20 were waited for; matrix products, arithmetic and copies ran while one was open for 7% of the time, Pallas kernels for 45%

profile of v2, /device:TPU:1, one launch (start us, length us, event | category | flops | bytes accessed | tf_op | source)
XLA Modules:
  0.0 574.3 jit_solution(10794764770054953964)
XLA Ops:
  29.3 5.1 collective-permute-start.8
  34.4 11.3 %collective-permute-done.7.refs_6_ = bf16[256,384]{1,0:T(8,128)(2,1)S(1)} collective-permute-done((bf16[256,384]{1,0:T(8,128)(2,1)}, bf16[256,384]{1,0:T(8,128)(2,1)S(1)}, u32[]{:S(2)}, u32[]{:S(2)}) %collective-permute-start.7) | collective-permute-done | bytes 196640 | tf_op jit(solution)/shard_map/ppermute | solution.py:891
  50.1 10.4 %enter.2 = (bf16[1024,1024]{1,0:T(8,128)(2,1)}, bf16[1024,1024]{1,0:T(8,128)(2,1)}, bf16[1024,1024]{1,0:T(8,128)(2,1)}, bf16[1024,256]{1,0:T(8,128)(2,1)}, f32[1...) custom-call(s32[8]{0:T(128)} %pad_add_fusion.where, bf16[256,1024]{1,0:T(8,128)(2,1)} %copy-done.12, ...), custom_call_target="tpu_custom_call" | custom-call | flops 1 | bytes 1 | tf_op jit(solution)/shard_map/enter/pallas_call | solution.py:108
  68.3 13.3 %states.2 = (bf16[8,1280]{1,0:T(8,128)(2,1)}, bf16[1024,1024]{1,0:T(8,128)(2,1)}, bf16[1024,256]{1,0:T(8,128)(2,1)}, f32[1024,128]{1,0:T(8,128)}, f32[1024,128]{...) custom-call(bf16[1024,1024]{1,0:T(8,128)(2,1)} %get-tuple-element.192.x_ref.refs_3_.ref, ...), custom_call_target="tpu_custom_call" | custom-call | flops 1 | bytes 1 | tf_op jit(solution)/shard_map/states/pallas_call | solution.py:108
  89.9 9.2 %within.2.refs_5_ = f32[1024,1024]{1,0:T(8,128)} custom-call(bf16[1024,1024]{1,0:T(8,128)(2,1)} %get-tuple-element.201.xc_ref.refs_7_.refs_4_.refs_6_, bf16[1024,256]{1,0:T(8,128)(2,1)} %get-tuple-element.202.bc_ref.refs_8_.refs_6_.refs_7_, f32[1024,128]{1,0:T(8,128)} %get-tuple-element.203.step_ref.refs_8_, ...), custom_call_target="tpu_custom_call" | custom-call | flops 1 | bytes 1 | tf_op jit(solution)/shard_map/within/pallas_call | solution.py:108
  103.9 8.6 %all-gather.3.cloned.1.call-done.refs_3_.refs_4_.refs_13_.wg_ref = bf16[1024,2048]{1,0:T(8,128)(2,1)} async-done(((bf16[64,2048]{1,0:T(8,128)(2,1)}), bf16[1024,2048]{1,0:T(8,128)(2,1)}) %all-gather.3.cloned.1.call-update) | async-done | bytes 4194320 | tf_op jit(solution)/shard_map/all_gather | solution.py:934
  112.6 13.5 %leave.2 = (f32[1024,1024]{1,0:T(8,128)}, f32[1024,1024]{1,0:T(8,128)}, bf16[1024,1152]{1,0:T(8,128)(2,1)}, f32[128,1024]{1,0:T(8,128)}) custom-call(bf16[136,1024]{1,0:T(8,128)(2,1)} %copy-done.33, bf16[136,1024]{1,0:T(8,128)(2,1)} %copy-done.34, bf16[136,1024]{1,0:T(8,128)(2,1)} %collective-permute-done.12.refs_2_, ...), custom_call_target="tpu_custom_call" | custom-call | flops 1 | bytes 1 | tf_op jit(solution)/shard_map/leave/pallas_call | solution.py:108
  127.5 17.1 %collective-permute-start.19 = (bf16[1024,1152]{1,0:T(8,128)(2,1)}, bf16[1024,1152]{1,0:T(8,128)(2,1)S(1)}, u32[]{:S(2)}, u32[]{:S(2)}) collective-permute-start(bf16[1024,1152]{1,0:T(8,128)(2,1)} %get-tuple-element.219.refs_5_.refs_1_), channel_id=1, source_target_pairs={{0,1},{1,0},{2,3},{3,2},{4,5},{5,4},{6,7},{7,6},{8,9},{9,8},{10,11... | collective-permute-start | bytes 7077896 | tf_op jit(solution)/shard_map/ppermute | solution.py:1014
  154.9 11.8 %enter.3 = (f32[1024,1024]{1,0:T(8,128)}, bf16[1024,1024]{1,0:T(8,128)(2,1)}, bf16[1024,1024]{1,0:T(8,128)(2,1)}, bf16[1024,1024]{1,0:T(8,128)(2,1)}, bf16[1024,...) custom-call(s32[8]{0:T(128)} %pad_add_fusion.where, ...), custom_call_target="tpu_custom_call" | custom-call | flops 1 | bytes 1 | tf_op jit(solution)/shard_map/enter/pallas_call | solution.py:108
  167.3 13.2 %states.3 = (bf16[8,1280]{1,0:T(8,128)(2,1)}, bf16[1024,1024]{1,0:T(8,128)(2,1)}, bf16[1024,256]{1,0:T(8,128)(2,1)}, f32[1024,128]{1,0:T(8,128)}, f32[1024,128]{...) custom-call(bf16[1024,1024]{1,0:T(8,128)(2,1)} %get-tuple-element.221.x_ref.refs_3_.ref, ...), custom_call_target="tpu_custom_call" | custom-call | flops 1 | bytes 1 | tf_op jit(solution)/shard_map/states/pallas_call | solution.py:108
  187.6 9.1 %within.3.refs_5_ = f32[1024,1024]{1,0:T(8,128)} custom-call(bf16[1024,1024]{1,0:T(8,128)(2,1)} %get-tuple-element.228.xc_ref.refs_7_.refs_5_.refs_6_, bf16[1024,256]{1,0:T(8,128)(2,1)} %get-tuple-element.229.bc_ref.refs_8_.refs_7_, f32[1024,128]{1,0:T(8,128)} %get-tuple-element.230.step_ref.refs_8_, f32[1024,128]{1,0:T(8,128)} %get-tuple-element.231.cum_ref.refs_9_.refs_8_, ...), custom_call_target="tpu_custom_call" | custom-call | flops 1 | bytes 1 | tf_op jit(solution)/shard_map/within/pallas_call | solution.py:108
  197.7 13.6 %leave.3 = (f32[1024,1024]{1,0:T(8,128)}, f32[1024,1024]{1,0:T(8,128)}, bf16[1024,1152]{1,0:T(8,128)(2,1)}, f32[128,1024]{1,0:T(8,128)}) custom-call(bf16[136,1024]{1,0:T(8,128)(2,1)} %copy-done.35, bf16[136,1024]{1,0:T(8,128)(2,1)} %copy-done.36, bf16[136,1024]{1,0:T(8,128)(2,1)} %copy-done.37, ...), custom_call_target="tpu_custom_call" | custom-call | flops 1 | bytes 1 | tf_op jit(solution)/shard_map/leave/pallas_call | solution.py:108
  218.5 17.6 %back_gate.2 = (f32[1024,1024]{1,0:T(8,128)}, bf16[1024,1024]{1,0:T(8,128)(2,1)}, bf16[1024,1024]{1,0:T(8,128)(2,1)}, bf16[1024,1024]{1,0:T(8,128)(2,1)}, bf16[1...) custom-call(f32[1024,1024]{1,0:T(8,128)} %get-tuple-element.220.refs_0_.h_ref, ...), custom_call_target="tpu_custom_call" | custom-call | flops 1 | bytes 1 | tf_op jit(solution)/shard_map/back_gate/pallas_call | solution.py:108
  241.2 10.1 %weight_grad.4 = bf16[1024,2048]{1,0:T(8,128)(2,1)} custom-call(s32[4]{0:T(128)} %copy-done.57, bf16[1024,1024]{1,0:T(8,128)(2,1)} %get-tuple-element.240.refs_0_, bf16[1024,1024]{1,0:T(8,128)(2,1)} %get-tuple-element.242.refs_1_, bf16[1024,1024]{1,0:T(8,128)(2,1)} %get-tuple-element.269.refs_2_.gate_ref, bf16[1024,1024]{1,0:T(8,128)(2,1)} %get-tuple-element.243.refs_3_), custom_call_target="tpu_custom_call" | custom-call | flops 1 | bytes 1 | tf_op jit(solution)/shard_map/weight_grad/pallas_call | solution.py:108
  251.3 11.5 %back_within.2 = (bf16[1024,1024]{1,0:T(8,128)(2,1)}, f32[1024,128]{1,0:T(8,128)}, f32[1024,256]{1,0:T(8,128)}) custom-call(bf16[1024,1024]{1,0:T(8,128)(2,1)} %get-tuple-element.228.xc_ref.refs_7_.refs_5_.refs_6_, bf16[1024,256]{1,0:T(8,128)(2,1)} %get-tuple-element.229.bc_ref.refs_8_.refs_7_, f32[1024,128]{1,0:T(8,128)} %get-tuple-element.230.step_ref.refs_8_, ...), custom_call_target="tpu_custom_call" | custom-call | flops 1 | bytes 1 | tf_op jit(solution)/shard_map/back_within/pallas_call | solution.py:108
  264.5 27.3 %back_inter.2 = (bf16[1024,1024]{1,0:T(8,128)(2,1)}, f32[8,1024]{1,0:T(8,128)}, f32[8,1024]{1,0:T(8,128)}, bf16[1024,128]{1,0:T(8,128)(2,1)}, bf16[1024,128]{1,0...) custom-call(s32[1]{0:T(128)} %bitcast.27.flag, ...), custom_call_target="tpu_custom_call" | custom-call | flops 1 | bytes 1 | tf_op jit(solution)/shard_map/back_inter/pallas_call | solution.py:108
  299.9 4.8 collective-permute-done.29
  309.3 7.9 %weight_grad.5 = (bf16[256,1280]{1,0:T(8,128)(2,1)}, bf16[256,1280]{1,0:T(8,128)(2,1)}, bf16[256,1280]{1,0:T(8,128)(2,1)}, bf16[256,1280]{1,0:T(8,128)(2,1)}) custom-call(s32[4]{0:T(128)} %copy-done.57, bf16[1024,1024]{1,0:T(8,128)(2,1)} %get-tuple-element.240.refs_0_, bf16[1024,1024]{1,0:T(8,128)(2,1)} %fusion.6.refs_1_.x_ref, ...), custom_call_target="tpu_custom_call" | custom-call | flops 1 | bytes 1 | tf_op jit(solution)/shard_map/weight_grad/pallas_call | solution.py:108
  317.3 10.0 %back_low.2.a_ref = bf16[1024,1024]{1,0:T(8,128)(2,1)} custom-call(s32[1]{0:T(128)} %bitcast.27.flag, bf16[1024,1024]{1,0:T(8,128)(2,1)} %get-tuple-element.269.refs_2_.gate_ref, bf16[1024,1024]{1,0:T(8,128)(2,1)} %fusion.6.refs_1_.x_ref, bf16[1024,128]{1,0:T(8,128)(2,1)} %fusion.21.bc_ref, bf16[1024,128]{1,0:T(8,128)(2,1)} %get-tuple-element.264.dt_ref, ...), custom_call_target="tpu_custom_call" | custom-call | flops 1 | bytes 1 | tf_op jit(solution)/shard_map/back_low/pallas_call | solution.py:108
  333.3 7.4 %back_norm.2 = (f32[1024,1024]{1,0:T(8,128)}, f32[8,1024]{1,0:T(8,128)}) custom-call(bf16[1024,1024]{1,0:T(8,128)(2,1)} %bitcast.80, bf16[1024,1024]{1,0:T(8,128)(2,1)} %back_low.2.a_ref, bf16[1024,1024]{1,0:T(8,128)(2,1)} %copy-done.4, f32[1024,1024]{1,0:T(8,128)} %get-tuple-element.220.refs_0_.h_ref, f32[8,1024]{1,0:T(8,128)} %pad.41.refs_7_.gain_ref), custom_call_target="tpu_custom_call" | custom-call | flops 1 | bytes 1 | tf_op jit(solution)/shard_map/back_norm/pallas_call | solution.py:108
  340.8 15.8 %back_gate.3 = (bf16[1024,1024]{1,0:T(8,128)(2,1)}, bf16[1024,1024]{1,0:T(8,128)(2,1)}, bf16[1024,1024]{1,0:T(8,128)(2,1)}, bf16[1024,1024]{1,0:T(8,128)(2,1)}, ...) custom-call(f32[1024,1024]{1,0:T(8,128)} %get-tuple-element.270.refs_0_.up_ref, ...), custom_call_target="tpu_custom_call" | custom-call | flops 1 | bytes 1 | tf_op jit(solution)/shard_map/back_gate/pallas_call | solution.py:108
  361.0 11.8 %weight_grad.6 = (bf16[256,2048]{1,0:T(8,128)(2,1)}, bf16[256,2048]{1,0:T(8,128)(2,1)}, bf16[256,2048]{1,0:T(8,128)(2,1)}, bf16[256,2048]{1,0:T(8,128)(2,1)}) custom-call(s32[4]{0:T(128)} %and_select_fusion.where, bf16[1024,1024]{1,0:T(8,128)(2,1)} %get-tuple-element.274.refs_0_, bf16[1024,1024]{1,0:T(8,128)(2,1)} %get-tuple-element.285.refs_1_, ...), custom_call_target="tpu_custom_call" | custom-call | flops 1 | bytes 1 | tf_op jit(solution)/shard_map/weight_grad/pallas_call | solution.py:108
  381.6 11.5 %back_within.3 = (bf16[1024,1024]{1,0:T(8,128)(2,1)}, f32[1024,128]{1,0:T(8,128)}, f32[1024,256]{1,0:T(8,128)}) custom-call(bf16[1024,1024]{1,0:T(8,128)(2,1)} %get-tuple-element.201.xc_ref.refs_7_.refs_4_.refs_6_, bf16[1024,256]{1,0:T(8,128)(2,1)} %get-tuple-element.202.bc_ref.refs_8_.refs_6_.refs_7_, f32[1024,128]{1,0:T(8,128)} %get-tuple-element.203.step_ref.refs_8_, ...), custom_call_target="tpu_custom_call" | custom-call | flops 1 | bytes 1 | tf_op jit(solution)/shard_map/back_within/pallas_call | solution.py:108
  393.1 27.3 %back_inter.3 = (bf16[1024,1024]{1,0:T(8,128)(2,1)}, f32[8,1024]{1,0:T(8,128)}, f32[8,1024]{1,0:T(8,128)}, bf16[1024,128]{1,0:T(8,128)(2,1)}, bf16[1024,128]{1,0...) custom-call(s32[1]{0:T(128)} %bitcast.27.flag, ...), custom_call_target="tpu_custom_call" | custom-call | flops 1 | bytes 1 | tf_op jit(solution)/shard_map/back_inter/pallas_call | solution.py:108
  434.5 7.9 %weight_grad.7 = (bf16[256,1280]{1,0:T(8,128)(2,1)}, bf16[256,1280]{1,0:T(8,128)(2,1)}, bf16[256,1280]{1,0:T(8,128)(2,1)}, bf16[256,1280]{1,0:T(8,128)(2,1)}) custom-call(s32[4]{0:T(128)} %copy-done.57, bf16[1024,1024]{1,0:T(8,128)(2,1)} %get-tuple-element.274.refs_0_, bf16[1024,1024]{1,0:T(8,128)(2,1)} %fusion.7.refs_1_.x_ref, ...), custom_call_target="tpu_custom_call" | custom-call | flops 1 | bytes 1 | tf_op jit(solution)/shard_map/weight_grad/pallas_call | solution.py:108
  445.8 10.0 %back_low.3.a_ref = bf16[1024,1024]{1,0:T(8,128)(2,1)} custom-call(s32[1]{0:T(128)} %bitcast.27.flag, bf16[1024,1024]{1,0:T(8,128)(2,1)} %get-tuple-element.318.refs_2_.gate_ref, bf16[1024,1024]{1,0:T(8,128)(2,1)} %fusion.7.refs_1_.x_ref, bf16[1024,128]{1,0:T(8,128)(2,1)} %copy-done.7, bf16[1024,128]{1,0:T(8,128)(2,1)} %get-tuple-element.313.dt_ref, ...), custom_call_target="tpu_custom_call" | custom-call | flops 1 | bytes 1 | tf_op jit(solution)/shard_map/back_low/pallas_call | solution.py:108
  459.6 13.2 %collective-permute-done.43.refs_3_ = bf16[256,1280]{1,0:T(8,128)(2,1)S(1)} collective-permute-done((bf16[256,1280]{1,0:T(8,128)(2,1)}, bf16[256,1280]{1,0:T(8,128)(2,1)S(1)}, u32[]{:S(2)}, u32[]{:S(2)}) %collective-permute-start.43) | collective-permute-done | bytes 655392 | tf_op jit(solution)/shard_map/ppermute | solution.py:891
  484.4 7.3 %back_norm.3 = (f32[1024,1024]{1,0:T(8,128)}, f32[8,1024]{1,0:T(8,128)}) custom-call(f32[1024,1024]{1,0:T(8,128)} %get-tuple-element.270.refs_0_.up_ref, bf16[1024,1024]{1,0:T(8,128)(2,1)} %back_low.3.a_ref, bf16[1024,1024]{1,0:T(8,128)(2,1)} %copy-done.3, bf16[1024,1024]{1,0:T(8,128)(2,1)} %bitcast.78, f32[8,1024]{1,0:T(8,128)} %pad.36.refs_9_.gain_ref), custom_call_target="tpu_custom_call" | custom-call | flops 1 | bytes 1 | tf_op jit(solution)/shard_map/back_norm/pallas_call | solution.py:108
  496.6 4.7 split_sum.2
  504.9 18.1 %collective-permute-done.49.refs_6_ = bf16[64,2560]{1,0:T(8,128)(2,1)S(1)} collective-permute-done((bf16[64,2560]{1,0:T(8,128)(2,1)}, bf16[64,2560]{1,0:T(8,128)(2,1)S(1)}, u32[]{:S(2)}, u32[]{:S(2)}) %collective-permute-start.49) | collective-permute-done | bytes 327712 | tf_op jit(solution)/shard_map/ppermute | solution.py:891
  523.0 5.4 collective-permute-done.51.refs_8_
  528.3 7.8 %collective-permute-start.56 = (f32[18176]{0:T(1024)S(1)}, f32[18176]{0:T(1024)S(1)}, u32[]{:S(2)}, u32[]{:S(2)}) collective-permute-start(f32[18176]{0:T(1024)S(1)} %add_add_fusion.1), channel_id=1, source_target_pairs={{0,8},{8,0},{16,24},{24,16},{1,9},{9,1},{17,25},{25,17},{2,10},{10... | collective-permute-start | bytes 218120 | tf_op jit(solution)/shard_map/ppermute | solution.py:891
  (359 shorter events, 185.4 us)
Async XLA Ops:
  7.2 105.4 %all-gather.3.cloned.1.call-start = ((), (), s32[]{:S(2)}) async-start(), calls=%async_computation.1 | async-start | bytes 4456448 | tf_op jit(solution)/shard_map/all_gather | solution.py:934
  11.5 185.2 %all-gather.5.cloned.1.call-start = ((), (), s32[]{:S(2)}) async-start(), calls=%async_computation.2 | async-start | bytes 4456448 | tf_op jit(solution)/shard_map/all_gather | solution.py:934
  16.5 29.2 %collective-permute-start.7 = (bf16[256,384]{1,0:T(8,128)(2,1)}, bf16[256,384]{1,0:T(8,128)(2,1)S(1)}, u32[]{:S(2)}, u32[]{:S(2)}) collective-permute-start(bf16[256,384]{1,0:T(8,128)(2,1)} %get-tuple-element.191.refs_4_), channel_id=1, source_target_pairs={{0,16},{8,24},{16,0},{24,8},{1,17},{9,25},{17,1},{25,9},{2,18},{10... | collective-permute-start | bytes 589832 | tf_op jit(solution)/shard_map/ppermute | solution.py:891
  22.4 370.7 %reduce-scatter.2.cloned.1.call-start = ((), (), s32[]{:S(2)}) async-start(), calls=%async_computation.3 | async-start | bytes 4456448 | tf_op jit(solution)/shard_map/reduce_scatter | solution.py:1127
  26.0 22.9 %collective-permute-start.3 = (bf16[256,1024]{1,0:T(8,128)(2,1)S(1)}, bf16[256,1024]{1,0:T(8,128)(2,1)S(1)}, u32[]{:S(2)}, u32[]{:S(2)}) collective-permute-start(bf16[256,1024]{1,0:T(8,128)(2,1)S(1)} %constant_dynamic-update-slice_fusion.refs_0_), channel_id=1, source_target_pairs={{0,2},{2,0},{4,6},{6,4},{1,3},{3,1},{5,7},{7,5},{8,10},{10,8},{12,... | collective-permute-start | bytes 1572872 | tf_op jit(solution)/shard_map/ppermute | solution.py:891
  27.2 21.6 %collective-permute-start.4 = (bf16[256,1024]{1,0:T(8,128)(2,1)S(1)}, bf16[256,1024]{1,0:T(8,128)(2,1)S(1)}, u32[]{:S(2)}, u32[]{:S(2)}) collective-permute-start(bf16[256,1024]{1,0:T(8,128)(2,1)S(1)} %constant_dynamic-update-slice_fusion.refs_0_), channel_id=1, source_target_pairs={{0,4},{2,6},{4,0},{6,2},{1,5},{3,7},{5,1},{7,3},{8,12},{10,14},{12... | collective-permute-start | bytes 1572872 | tf_op jit(solution)/shard_map/ppermute | solution.py:891
  28.5 20.4 %collective-permute-start.5 = (bf16[256,1024]{1,0:T(8,128)(2,1)S(1)}, bf16[256,1024]{1,0:T(8,128)(2,1)S(1)}, u32[]{:S(2)}, u32[]{:S(2)}) collective-permute-start(bf16[256,1024]{1,0:T(8,128)(2,1)S(1)} %constant_dynamic-update-slice_fusion.refs_0_), channel_id=1, source_target_pairs={{0,6},{2,4},{4,2},{6,0},{1,7},{3,5},{5,3},{7,1},{8,14},{10,12},{12... | collective-permute-start | bytes 1572872 | tf_op jit(solution)/shard_map/ppermute | solution.py:891
  29.3 19.5 %collective-permute-start.8 = (bf16[256,384]{1,0:T(8,128)(2,1)S(1)}, bf16[256,384]{1,0:T(8,128)(2,1)S(1)}, u32[]{:S(2)}, u32[]{:S(2)}) collective-permute-start(bf16[256,384]{1,0:T(8,128)(2,1)S(1)} %copy-done.43), channel_id=1, source_target_pairs={{0,24},{8,16},{16,8},{24,0},{1,25},{9,17},{17,9},{25,1},{2,26},{10... | collective-permute-start | bytes 589832 | tf_op jit(solution)/shard_map/ppermute | solution.py:891
  45.7 22.0 %collective-permute-start.9 = (bf16[8,1024]{1,0:T(8,128)(2,1)S(1)}, bf16[8,1024]{1,0:T(8,128)(2,1)S(1)}, u32[]{:S(2)}, u32[]{:S(2)}) collective-permute-start(bf16[8,1024]{1,0:T(8,128)(2,1)S(1)} %slice_bitcast_fusion), channel_id=1, source_target_pairs={{0,2},{2,4},{4,6},{1,3},{3,5},{5,7},{8,10},{10,12},{12,14},{9,11},... | collective-permute-start | bytes 49160 | tf_op jit(solution)/shard_map/ppermute | solution.py:896
  60.5 26.7 %collective-permute-start.13 = (bf16[64,1408]{1,0:T(8,128)(2,1)S(1)}, bf16[64,1408]{1,0:T(8,128)(2,1)S(1)}, u32[]{:S(2)}, u32[]{:S(2)}) collective-permute-start(bf16[64,1408]{1,0:T(8,128)(2,1)S(1)} %copy-done.47), channel_id=1, source_target_pairs={{0,8},{8,0},{16,24},{24,16},{1,9},{9,1},{17,25},{25,17},{2,10},{10... | collective-permute-start | bytes 540680 | tf_op jit(solution)/shard_map/ppermute | solution.py:891
  61.3 37.8 %collective-permute-start.14 = (bf16[64,1408]{1,0:T(8,128)(2,1)S(1)}, bf16[64,1408]{1,0:T(8,128)(2,1)S(1)}, u32[]{:S(2)}, u32[]{:S(2)}) collective-permute-start(bf16[64,1408]{1,0:T(8,128)(2,1)S(1)} %copy-done.47), channel_id=1, source_target_pairs={{0,16},{8,24},{16,0},{24,8},{1,17},{9,25},{17,1},{25,9},{2,18},{10... | collective-permute-start | bytes 540680 | tf_op jit(solution)/shard_map/ppermute | solution.py:891
  63.3 35.8 %collective-permute-start.15 = (bf16[64,1408]{1,0:T(8,128)(2,1)S(1)}, bf16[64,1408]{1,0:T(8,128)(2,1)S(1)}, u32[]{:S(2)}, u32[]{:S(2)}) collective-permute-start(bf16[64,1408]{1,0:T(8,128)(2,1)S(1)} %copy-done.47), channel_id=1, source_target_pairs={{0,24},{8,16},{16,8},{24,0},{1,25},{9,17},{17,9},{25,1},{2,26},{10... | collective-permute-start | bytes 540680 | tf_op jit(solution)/shard_map/ppermute | solution.py:891
  81.6 17.5 %collective-permute-start.10 = (bf16[136,1024]{1,0:T(8,128)(2,1)}, bf16[136,1024]{1,0:T(8,128)(2,1)S(1)}, u32[]{:S(2)}, u32[]{:S(2)}) collective-permute-start(bf16[136,1024]{1,0:T(8,128)(2,1)} %get-tuple-element.199.refs_10_), channel_id=1, source_target_pairs={{0,2},{2,4},{4,6},{1,3},{3,5},{5,7},{8,10},{10,12},{12,14},{9,11},... | collective-permute-start | bytes 835592 | tf_op jit(solution)/shard_map/ppermute | solution.py:896
  99.7 26.4 %collective-permute-start.16 = (bf16[256,1408]{1,0:T(8,128)(2,1)S(1)}, bf16[256,1408]{1,0:T(8,128)(2,1)S(1)}, u32[]{:S(2)}, u32[]{:S(2)}) collective-permute-start(bf16[256,1408]{1,0:T(8,128)(2,1)S(1)} %pad_maximum_fusion.refs_0_), channel_id=1, source_target_pairs={{0,2},{2,0},{4,6},{6,4},{1,3},{3,1},{5,7},{7,5},{8,10},{10,8},{12,... | collective-permute-start | bytes 2162696 | tf_op jit(solution)/shard_map/ppermute | solution.py:891
  99.8 27.8 %collective-permute-start.17 = (bf16[256,1408]{1,0:T(8,128)(2,1)S(1)}, bf16[256,1408]{1,0:T(8,128)(2,1)S(1)}, u32[]{:S(2)}, u32[]{:S(2)}) collective-permute-start(bf16[256,1408]{1,0:T(8,128)(2,1)S(1)} %pad_maximum_fusion.refs_0_), channel_id=1, source_target_pairs={{0,4},{2,6},{4,0},{6,2},{1,5},{3,7},{5,1},{7,3},{8,12},{10,14},{12... | collective-permute-start | bytes 2162696 | tf_op jit(solution)/shard_map/ppermute | solution.py:891
  103.1 24.4 %collective-permute-start.18 = (bf16[256,1408]{1,0:T(8,128)(2,1)S(1)}, bf16[256,1408]{1,0:T(8,128)(2,1)S(1)}, u32[]{:S(2)}, u32[]{:S(2)}) collective-permute-start(bf16[256,1408]{1,0:T(8,128)(2,1)S(1)} %pad_maximum_fusion.refs_0_), channel_id=1, source_target_pairs={{0,6},{2,4},{4,2},{6,0},{1,7},{3,5},{5,3},{7,1},{8,14},{10,12},{12... | collective-permute-start | bytes 2162696 | tf_op jit(solution)/shard_map/ppermute | solution.py:891
  127.5 21.5 %collective-permute-start.19 = (bf16[1024,1152]{1,0:T(8,128)(2,1)}, bf16[1024,1152]{1,0:T(8,128)(2,1)S(1)}, u32[]{:S(2)}, u32[]{:S(2)}) collective-permute-start(bf16[1024,1152]{1,0:T(8,128)(2,1)} %get-tuple-element.219.refs_5_.refs_1_), channel_id=1, source_target_pairs={{0,1},{1,0},{2,3},{3,2},{4,5},{5,4},{6,7},{7,6},{8,9},{9,8},{10,11... | collective-permute-start | bytes 7077896 | tf_op jit(solution)/shard_map/ppermute | solution.py:1014
  236.1 26.6 %collective-permute-start.25 = (bf16[136,1024]{1,0:T(8,128)(2,1)}, bf16[136,1024]{1,0:T(8,128)(2,1)S(1)}, u32[]{:S(2)}, u32[]{:S(2)}) collective-permute-start(bf16[136,1024]{1,0:T(8,128)(2,1)} %get-tuple-element.246), channel_id=1, source_target_pairs={{2,0},{4,2},{6,4},{3,1},{5,3},{7,5},{10,8},{12,10},{14,12},{11,9},... | collective-permute-start | bytes 835592 | tf_op jit(solution)/shard_map/ppermute | solution.py:896
  237.4 25.3 %collective-permute-start.26 = (bf16[136,1024]{1,0:T(8,128)(2,1)}, bf16[136,1024]{1,0:T(8,128)(2,1)S(1)}, u32[]{:S(2)}, u32[]{:S(2)}) collective-permute-start(bf16[136,1024]{1,0:T(8,128)(2,1)} %get-tuple-element.246), channel_id=1, source_target_pairs={{4,0},{6,2},{5,1},{7,3},{12,8},{14,10},{13,9},{15,11},{20,16},{22,... | collective-permute-start | bytes 835592 | tf_op jit(solution)/shard_map/ppermute | solution.py:896
  238.7 24.1 %collective-permute-start.27 = (bf16[136,1024]{1,0:T(8,128)(2,1)}, bf16[136,1024]{1,0:T(8,128)(2,1)S(1)}, u32[]{:S(2)}, u32[]{:S(2)}) collective-permute-start(bf16[136,1024]{1,0:T(8,128)(2,1)} %get-tuple-element.246), channel_id=1, source_target_pairs={{6,0},{7,1},{14,8},{15,9},{22,16},{23,17},{30,24},{31,25}} | collective-permute-start | bytes 835592 | tf_op jit(solution)/shard_map/ppermute | solution.py:896
  356.6 17.8 %collective-permute-start.31 = (bf16[136,1024]{1,0:T(8,128)(2,1)}, bf16[136,1024]{1,0:T(8,128)(2,1)S(1)}, u32[]{:S(2)}, u32[]{:S(2)}) collective-permute-start(bf16[136,1024]{1,0:T(8,128)(2,1)} %get-tuple-element.275), channel_id=1, source_target_pairs={{2,0},{4,2},{6,4},{3,1},{5,3},{7,5},{10,8},{12,10},{14,12},{11,9},... | collective-permute-start | bytes 835592 | tf_op jit(solution)/shard_map/ppermute | solution.py:896
  359.2 16.9 %collective-permute-start.33 = (bf16[136,1024]{1,0:T(8,128)(2,1)}, bf16[136,1024]{1,0:T(8,128)(2,1)}, u32[]{:S(2)}, u32[]{:S(2)}) collective-permute-start(bf16[136,1024]{1,0:T(8,128)(2,1)} %get-tuple-element.275), channel_id=1, source_target_pairs={{6,0},{7,1},{14,8},{15,9},{22,16},{23,17},{30,24},{31,25}} | collective-permute-start | bytes 835592 | tf_op jit(solution)/shard_map/ppermute | solution.py:896
  372.9 49.2 %collective-permute-start.34 = (bf16[256,2048]{1,0:T(8,128)(2,1)}, bf16[256,2048]{1,0:T(8,128)(2,1)S(1)}, u32[]{:S(2)}, u32[]{:S(2)}) collective-permute-start(bf16[256,2048]{1,0:T(8,128)(2,1)} %get-tuple-element.299), channel_id=1, source_target_pairs={{0,8},{8,16},{16,24},{24,0},{1,9},{9,17},{17,25},{25,1},{2,10},{10... | collective-permute-start | bytes 3145736 | tf_op jit(solution)/shard_map/ppermute | solution.py:1006
  376.1 44.3 %collective-permute-start.35 = (bf16[256,1280]{1,0:T(8,128)(2,1)}, bf16[256,1280]{1,0:T(8,128)(2,1)S(1)}, u32[]{:S(2)}, u32[]{:S(2)}) collective-permute-start(bf16[256,1280]{1,0:T(8,128)(2,1)} %get-tuple-element.306), channel_id=1, source_target_pairs={{0,2},{2,0},{4,6},{6,4},{1,3},{3,1},{5,7},{7,5},{8,10},{10,8},{12,... | collective-permute-start | bytes 1966088 | tf_op jit(solution)/shard_map/ppermute | solution.py:891
  378.1 42.4 %collective-permute-start.36 = (bf16[256,1280]{1,0:T(8,128)(2,1)}, bf16[256,1280]{1,0:T(8,128)(2,1)S(1)}, u32[]{:S(2)}, u32[]{:S(2)}) collective-permute-start(bf16[256,1280]{1,0:T(8,128)(2,1)} %get-tuple-element.307), channel_id=1, source_target_pairs={{0,4},{2,6},{4,0},{6,2},{1,5},{3,7},{5,1},{7,3},{8,12},{10,14},{12... | collective-permute-start | bytes 1966088 | tf_op jit(solution)/shard_map/ppermute | solution.py:891
  381.6 38.9 %collective-permute-start.37 = (bf16[256,1280]{1,0:T(8,128)(2,1)}, bf16[256,1280]{1,0:T(8,128)(2,1)S(1)}, u32[]{:S(2)}, u32[]{:S(2)}) collective-permute-start(bf16[256,1280]{1,0:T(8,128)(2,1)} %get-tuple-element.308), channel_id=1, source_target_pairs={{0,6},{2,4},{4,2},{6,0},{1,7},{3,5},{5,3},{7,1},{8,14},{10,12},{12... | collective-permute-start | bytes 1966088 | tf_op jit(solution)/shard_map/ppermute | solution.py:891
  429.9 26.2 %collective-permute-start.40 = (bf16[256,2048]{1,0:T(8,128)(2,1)S(1)}, bf16[256,2048]{1,0:T(8,128)(2,1)S(1)}, u32[]{:S(2)}, u32[]{:S(2)}) collective-permute-start(bf16[256,2048]{1,0:T(8,128)(2,1)S(1)} %add_convert_fusion.1), channel_id=1, source_target_pairs={{0,8},{8,16},{16,24},{24,0},{1,9},{9,17},{17,25},{25,1},{2,10},{10... | collective-permute-start | bytes 3145736 | tf_op jit(solution)/shard_map/ppermute | solution.py:1006
  444.5 28.2 %collective-permute-start.43 = (bf16[256,1280]{1,0:T(8,128)(2,1)}, bf16[256,1280]{1,0:T(8,128)(2,1)S(1)}, u32[]{:S(2)}, u32[]{:S(2)}) collective-permute-start(bf16[256,1280]{1,0:T(8,128)(2,1)} %get-tuple-element.325), channel_id=1, source_target_pairs={{0,6},{2,4},{4,2},{6,0},{1,7},{3,5},{5,3},{7,1},{8,14},{10,12},{12... | collective-permute-start | bytes 1966088 | tf_op jit(solution)/shard_map/ppermute | solution.py:891
  481.5 46.8 %collective-permute-start.48 = (bf16[256,2048]{1,0:T(8,128)(2,1)S(1)}, bf16[256,2048]{1,0:T(8,128)(2,1)S(1)}, u32[]{:S(2)}, u32[]{:S(2)}) collective-permute-start(bf16[256,2048]{1,0:T(8,128)(2,1)S(1)} %add_convert_fusion), channel_id=1, source_target_pairs={{0,8},{8,16},{16,24},{24,0},{1,9},{9,17},{17,25},{25,1},{2,10},{10... | collective-permute-start | bytes 3145736 | tf_op jit(solution)/shard_map/ppermute | solution.py:1006
  501.3 21.6 %collective-permute-start.49 = (bf16[64,2560]{1,0:T(8,128)(2,1)}, bf16[64,2560]{1,0:T(8,128)(2,1)S(1)}, u32[]{:S(2)}, u32[]{:S(2)}) collective-permute-start(bf16[64,2560]{1,0:T(8,128)(2,1)} %get-tuple-element.351), channel_id=1, source_target_pairs={{0,8},{8,0},{16,24},{24,16},{1,9},{9,1},{17,25},{25,17},{2,10},{10... | collective-permute-start | bytes 983048 | tf_op jit(solution)/shard_map/ppermute | solution.py:891
  502.7 20.3 %collective-permute-start.50 = (bf16[64,2560]{1,0:T(8,128)(2,1)}, bf16[64,2560]{1,0:T(8,128)(2,1)S(1)}, u32[]{:S(2)}, u32[]{:S(2)}) collective-permute-start(bf16[64,2560]{1,0:T(8,128)(2,1)} %get-tuple-element.352), channel_id=1, source_target_pairs={{0,16},{8,24},{16,0},{24,8},{1,17},{9,25},{17,1},{25,9},{2,18},{10... | collective-permute-start | bytes 983048 | tf_op jit(solution)/shard_map/ppermute | solution.py:891
  503.5 24.8 %collective-permute-start.51 = (bf16[64,2560]{1,0:T(8,128)(2,1)}, bf16[64,2560]{1,0:T(8,128)(2,1)S(1)}, u32[]{:S(2)}, u32[]{:S(2)}) collective-permute-start(bf16[64,2560]{1,0:T(8,128)(2,1)} %get-tuple-element.353), channel_id=1, source_target_pairs={{0,24},{8,16},{16,8},{24,0},{1,25},{9,17},{17,9},{25,1},{2,26},{10... | collective-permute-start | bytes 983048 | tf_op jit(solution)/shard_map/ppermute | solution.py:891
  (96 other events, 1062.5 us)
Sparse Core Ops, SparseCore 0:
  11.7 100.8 all-gather.2
  115.3 74.1 all-gather.4
  263.0 98.6 reduce-scatter.1

commit v3 on v2

--- a/solution.py
+++ b/solution.py
@@ -67,6 +67,10 @@
     col = lax.broadcasted_iota(jnp.int32, (size, size), 1)
     ordered = (row >= col) if later_rows else (row <= col)
     return jnp.where(ordered & (seg_col == seg_row), 0.0, CLOSED)
+
+
+def chunks_of(ref):
+    return [slice(at, at + CHUNK) for at in range(0, ref.shape[0], CHUNK)]
 
 
 def silu_parts(values):
@@ -209,7 +213,7 @@
 
 def states_body(
     x_ref, raw_bc_ref, dt_ref, before_ref, gain_ref, w_x, w_other, cols_ref, taps_ref, taps_bc_ref, head_ref,
-    spread_ref, lower_ref, edge_ref, xc_ref, bc_ref, step_ref, cum_ref, enter_ref, phi_ref, last_ref,
+    spread_ref, lower_ref, edge_ref, before_turned, xc_ref, bc_ref, step_ref, cum_ref, enter_ref, phi_ref, last_ref,
     tail_x, tail_bc, state, phi,
 ):
     chunk = pl.program_id(0)
@@ -221,6 +225,8 @@
         before = before_ref[...].astype(F32)
         norm = lax.rsqrt(jnp.mean(before * before, axis=1, keepdims=True) + EPSILON)
         lowered = (before * norm * gain_ref[0:1]).astype(BF16)
+        padding = jnp.zeros((LANES - EDGE, lowered.shape[1]), F32)
+        before_turned[...] = jnp.concatenate([lowered.astype(F32), padding], axis=0).T.astype(BF16)
         edge = dot(lowered, w_x[...]).astype(BF16)
         edge_bc = dot(lowered, w_other[:, : 2 * ns]).astype(BF16)
         edge_ref[:, :width] = edge
@@ -230,43 +236,42 @@
         state[...] = jnp.zeros_like(state)
         phi[...] = jnp.ones_like(phi)
 
-    cols = cols_ref[...]
-    same = same_columns(cols, LANES)
-    dt = jax.nn.softplus(dt_ref[...] + head_ref[0:1]) * cols[:, 3:4]
-    rates = head_ref[1:2] * dt
-    cum = dot(lower_ref[...], rates, precision=EXACT)
-    step_ref[...] = dt
-    cum_ref[...] = cum
-    size = cum.shape[0]
-    tail_dt = cols[:, 5:6] * jnp.exp(cum[size - 1 : size] - cum) * dt
-    tail_wide = expand(tail_dt, spread_ref[...])
-    fold = cols[size - 1 : size, 4:5] * jnp.exp(cum[size - EDGE : size])[EDGE - 1 : EDGE]
-    fold_rows = jnp.broadcast_to(fold, phi.shape)
-    fold_wide = expand(fold_rows, spread_ref[...])[0:1]
-
-    halves = []
-    for i in range(2):
-        part = slice(i * ns, (i + 1) * ns)
-        now = raw_bc_ref[:, part].astype(F32)
-        shifts = conv_shifts(jnp.concatenate([tail_bc[:, part], now], axis=0), same)
-        tail_bc[:, part] = now[size - EDGE :]
-        halves.append(silu_parts(conv_sum(shifts, taps_bc_ref[:, part]))[1].astype(BF16))
-        bc_ref[:, part] = halves[i]
-    b_part = halves[0]
-    b_turned = b_part.astype(F32).T.astype(BF16)
-
-    enter_ref[0] = state[...].astype(BF16)
-    phi_ref[0] = phi[...]
-    for i in range(width // LANES):
-        part = slice(i * LANES, (i + 1) * LANES)
-        now = x_ref[:, part].astype(F32)
-        shifts = conv_shifts(jnp.concatenate([tail_x[:, part], now], axis=0), same)
-        tail_x[:, part] = now[size - EDGE :]
-        x_conv = silu_parts(conv_sum(shifts, taps_ref[:, part]))[1].astype(BF16)
-        xc_ref[:, part] = x_conv
-        held = (x_conv.astype(F32) * tail_wide[:, part]).astype(BF16)
-        state[:, part] = fold_wide[:, part] * state[:, part] + dot(b_turned, held)
-    phi[...] = phi[...] * fold_rows
+    for sub, here in enumerate(chunks_of(x_ref)):
+        cols = cols_ref[here]
+        same = same_columns(cols, LANES)
+        dt = jax.nn.softplus(dt_ref[here] + head_ref[0:1]) * cols[:, 3:4]
+        rates = head_ref[1:2] * dt
+        cum = dot(lower_ref[...], rates, precision=EXACT)
+        step_ref[here] = dt
+        cum_ref[here] = cum
+        size = cum.shape[0]
+        tail_dt = cols[:, 5:6] * jnp.exp(cum[size - 1 : size] - cum) * dt
+        fold = cols[size - 1 : size, 4:5] * jnp.exp(cum[size - EDGE : size])[EDGE - 1 : EDGE]
+        fold_rows = jnp.broadcast_to(fold, phi.shape)
+        wide = expand(jnp.concatenate([tail_dt, fold_rows], axis=0), spread_ref[...])
+
+        halves = []
+        for i in range(2):
+            part = slice(i * ns, (i + 1) * ns)
+            now = raw_bc_ref[here, part].astype(F32)
+            shifts = conv_shifts(jnp.concatenate([tail_bc[:, part], now], axis=0), same)
+            tail_bc[:, part] = now[size - EDGE :]
+            halves.append(silu_parts(conv_sum(shifts, taps_bc_ref[:, part]))[1].astype(BF16))
+            bc_ref[here, part] = halves[i]
+        b_turned = halves[0].astype(F32).T.astype(BF16)
+
+        enter_ref[sub] = state[...].astype(BF16)
+        phi_ref[sub] = phi[...]
+        for i in range(width // LANES):
+            part = slice(i * LANES, (i + 1) * LANES)
+            now = x_ref[here, part].astype(F32)
+            shifts = conv_shifts(jnp.concatenate([tail_x[:, part], now], axis=0), same)
+            tail_x[:, part] = now[size - EDGE :]
+            x_conv = silu_parts(conv_sum(shifts, taps_ref[:, part]))[1].astype(BF16)
+            xc_ref[here, part] = x_conv
+            held = (x_conv.astype(F32) * wide[:size, part]).astype(BF16)
+            state[:, part] = wide[size : size + 1, part] * state[:, part] + dot(b_turned, held)
+        phi[...] = phi[...] * fold_rows
 
     @pl.when(chunk == pl.num_programs(0) - 1)
     def _():
@@ -278,15 +283,17 @@
     rows, width = x_raw.shape
     ns = raw_bc.shape[1] // 2
     count = rows // CHUNK
+    block = min(256, rows)
+    subs = block // CHUNK
     ins = [
-        (x_raw, (CHUNK, width), rows_at),
-        (raw_bc, (CHUNK, 2 * ns), rows_at),
-        (dt_raw, (CHUNK, LANES), rows_at),
+        (x_raw, (block, width), rows_at),
+        (raw_bc, (block, 2 * ns), rows_at),
+        (dt_raw, (block, LANES), rows_at),
         (before, before.shape, fixed),
         (gain, gain.shape, fixed),
         block_of(weights["x"]),
         block_of(weights["other"]),
-        (cols, (CHUNK, cols.shape[1]), rows_at),
+        (cols, (block, cols.shape[1]), rows_at),
         (taps, taps.shape, fixed),
         (taps_bc, taps_bc.shape, fixed),
         (head, head.shape, fixed),
@@ -295,12 +302,13 @@
     ]
     outs = [
         ((EDGE, width + 2 * ns), BF16, (EDGE, width + 2 * ns), fixed),
-        ((rows, width), BF16, (CHUNK, width), rows_at),
-        ((rows, 2 * ns), BF16, (CHUNK, 2 * ns), rows_at),
-        ((rows, LANES), F32, (CHUNK, LANES), rows_at),
-        ((rows, LANES), F32, (CHUNK, LANES), rows_at),
-        ((count, ns, width), BF16, (1, ns, width), lambda i, *_: (i, 0, 0)),
-        ((count, EDGE, LANES), F32, (1, EDGE, LANES), lambda i, *_: (i, 0, 0)),
+        ((before.shape[1], LANES), BF16, (before.shape[1], LANES), fixed),
+        ((rows, width), BF16, (block, width), rows_at),
+        ((rows, 2 * ns), BF16, (block, 2 * ns), rows_at),
+        ((rows, LANES), F32, (block, LANES), rows_at),
+        ((rows, LANES), F32, (block, LANES), rows_at),
+        ((count, ns, width), BF16, (subs, ns, width), lambda i, *_: (i, 0, 0)),
+        ((count, EDGE, LANES), F32, (subs, EDGE, LANES), lambda i, *_: (i, 0, 0)),
         ((ns + EDGE, width), BF16, (ns + EDGE, width), fixed),
     ]
     scratch = [
@@ -309,40 +317,42 @@
         pltpu.VMEM((ns, width), F32),
         pltpu.VMEM((EDGE, LANES), F32),
     ]
-    return call(states_body, (count,), ins, outs, scratch, flops=2 * rows * width * ns * 4, name="states")
+    return call(states_body, (rows // block,), ins, outs, scratch, flops=2 * rows * width * ns * 4, name="states")
 
 
 def within_body(xc_ref, bc_ref, step_ref, cum_ref, cols_ref, segs_ref, spread_ref, y_ref):
     ns = bc_ref.shape[1] // 2
     width = xc_ref.shape[1]
-    cum = cum_ref[...]
-    cum_rows = cum.T
-    bias = pairs_bias(cols_ref[:, 7:8], segs_ref[0:1], True)
-    both = dot(bc_ref[:, ns:], bc_ref[:, :ns], ((1,), (1,)))
-    step_wide = expand(step_ref[...], spread_ref[...])
-    for pair in range(width // LANES):
-        part = slice(pair * LANES, (pair + 1) * LANES)
-        weighted = (xc_ref[:, part].astype(F32) * step_wide[:, part]).astype(BF16)
-        maps = []
-        for head in (2 * pair, 2 * pair + 1):
-            gap = (cum[:, head : head + 1] - cum_rows[head : head + 1]) + bias
-            maps.append((jnp.exp(gap) * both).astype(BF16))
-        y_ref[:, part] = dot(jnp.concatenate(maps, axis=1), pair_masked(weighted))
+    for here in chunks_of(y_ref):
+        cum = cum_ref[here]
+        cum_rows = cum.T
+        bias = pairs_bias(cols_ref[here, 7:8], segs_ref[0:1, here], True)
+        both = dot(bc_ref[here, ns:], bc_ref[here, :ns], ((1,), (1,)))
+        step_wide = expand(step_ref[here], spread_ref[...])
+        for pair in range(width // LANES):
+            part = slice(pair * LANES, (pair + 1) * LANES)
+            weighted = (xc_ref[here, part].astype(F32) * step_wide[:, part]).astype(BF16)
+            maps = []
+            for head in (2 * pair, 2 * pair + 1):
+                gap = (cum[:, head : head + 1] - cum_rows[head : head + 1]) + bias
+                maps.append((jnp.exp(gap) * both).astype(BF16))
+            y_ref[here, part] = dot(jnp.concatenate(maps, axis=1), pair_masked(weighted))
 
 
 def within(xc, bc, step, cum, cols, segs, spread):
     rows, width = xc.shape
+    block = min(512, rows)
     ins = [
-        (xc, (CHUNK, width), rows_at),
-        (bc, (CHUNK, bc.shape[1]), rows_at),
-        (step, (CHUNK, LANES), rows_at),
-        (cum, (CHUNK, LANES), rows_at),
-        (cols, (CHUNK, cols.shape[1]), rows_at),
-        (segs, (EDGE, CHUNK), lambda i, *_: (0, i)),
+        (xc, (block, width), rows_at),
+        (bc, (block, bc.shape[1]), rows_at),
+        (step, (block, LANES), rows_at),
+        (cum, (block, LANES), rows_at),
+        (cols, (block, cols.shape[1]), rows_at),
+        (segs, (EDGE, block), columns_at),
         (spread, spread.shape, fixed),
     ]
-    outs = [((rows, width), F32, (CHUNK, width), rows_at)]
-    return call(within_body, (rows // CHUNK,), ins, outs, flops=2 * rows * CHUNK * width * 4, name="within")[0]
+    outs = [((rows, width), F32, (block, width), rows_at)]
+    return call(within_body, (rows // block,), ins, outs, name="within")[0]
 
 
 def leave_body(count, *refs):
@@ -453,7 +463,7 @@
         gated = mixed * soft
         scaled = gated * scale_wide
         grad = back[:, part]
-        gain_ref[0:1, part] += jnp.sum(grad * scaled, axis=0, keepdims=True)
+        gain_ref[6:7, part] += jnp.sum(grad * scaled, axis=0, keepdims=True)
         grad_gated = grad * gain * scale_wide - gated * pull_wide
         dy_ref[:, part] = (grad_gated * soft).astype(BF16)
         dgate_ref[:, part] = (grad_gated * mixed * (sig * (1.0 + gate * (1.0 - sig)))).astype(BF16)
@@ -518,59 +528,61 @@
     dx_ref, left_ref, dbc_ref, products,
 ):
     ns = bc_ref.shape[1] // 2
-    size, width = xc_ref.shape
-    cum = cum_ref[...]
-    cum_rows = cum.T
-    bias = pairs_bias(cols_ref[:, 7:8], segs_ref[0:1], False)
-    b_part = bc_ref[:, :ns]
-    c_part = bc_ref[:, ns:]
-    both = dot(b_part, c_part, ((1,), (1,)))
-    step_wide = expand(step_ref[...], spread_ref[...])
-    grad_both = jnp.zeros((size, size), F32)
-    for pair in range(width // LANES):
-        part = slice(pair * LANES, (pair + 1) * LANES)
-        weighted = (xc_ref[:, part].astype(F32) * step_wide[:, part]).astype(BF16)
-        dy = dy_ref[:, part]
-        dy_pair = pair_masked(dy)
-        grad_maps = dot(weighted, dy_pair, ((1,), (1,)))
-        maps = []
-        for k in (0, 1):
-            head = 2 * pair + k
-            decay = jnp.exp((cum_rows[head : head + 1] - cum[:, head : head + 1]) + bias)
-            maps.append((decay * both).astype(BF16))
-            grad_both = grad_both + decay * grad_maps[:, k * size : (k + 1) * size]
-        grad_x = dot(jnp.concatenate(maps, axis=1), dy_pair)
-        dx_ref[:, part] = grad_x.astype(BF16)
-        high, rest = split(dy.astype(F32) * ssm_ref[:, part] - weighted.astype(F32) * grad_x)
-        products[:size, part] = high
-        products[size:, part] = rest
-    left = dot(products[...], gather_ref[...])
-    left_ref[...] = left[:size] + left[size:]
-    dbc_ref[:, :ns] = dot(grad_both.astype(BF16), c_part)
-    dbc_ref[:, ns:] = dot(grad_both.T.astype(BF16), b_part)
+    size, width = CHUNK, xc_ref.shape[1]
+    for here in chunks_of(xc_ref):
+        cum = cum_ref[here]
+        cum_rows = cum.T
+        bias = pairs_bias(cols_ref[here, 7:8], segs_ref[0:1, here], False)
+        b_part = bc_ref[here, :ns]
+        c_part = bc_ref[here, ns:]
+        both = dot(b_part, c_part, ((1,), (1,)))
+        step_wide = expand(step_ref[here], spread_ref[...])
+        grad_both = jnp.zeros((size, size), F32)
+        for pair in range(width // LANES):
+            part = slice(pair * LANES, (pair + 1) * LANES)
+            weighted = (xc_ref[here, part].astype(F32) * step_wide[:, part]).astype(BF16)
+            dy = dy_ref[here, part]
+            dy_pair = pair_masked(dy)
+            grad_maps = dot(weighted, dy_pair, ((1,), (1,)))
+            maps = []
+            for k in (0, 1):
+                head = 2 * pair + k
+                decay = jnp.exp((cum_rows[head : head + 1] - cum[:, head : head + 1]) + bias)
+                maps.append((decay * both).astype(BF16))
+                grad_both = grad_both + decay * grad_maps[:, k * size : (k + 1) * size]
+            grad_x = dot(jnp.concatenate(maps, axis=1), dy_pair)
+            dx_ref[here, part] = grad_x.astype(BF16)
+            high, rest = split(dy.astype(F32) * ssm_ref[here, part] - weighted.astype(F32) * grad_x)
+            products[:size, part] = high
+            products[size:, part] = rest
+        left = dot(products[...], gather_ref[...])
+        left_ref[here] = left[:size] + left[size:]
+        dbc_ref[here, :ns] = dot(grad_both.astype(BF16), c_part)
+        dbc_ref[here, ns:] = dot(grad_both.T.astype(BF16), b_part)
 
 
 def back_within(xc, bc, step, cum, cols, segs, spread, gather, dy, ssm):
     rows, width = xc.shape
+    block = min(256, rows)
     ins = [
-        (xc, (CHUNK, width), rows_at),
-        (bc, (CHUNK, bc.shape[1]), rows_at),
-        (step, (CHUNK, LANES), rows_at),
-        (cum, (CHUNK, LANES), rows_at),
-        (cols, (CHUNK, cols.shape[1]), rows_at),
-        (segs, (EDGE, CHUNK), lambda i, *_: (0, i)),
+        (xc, (block, width), rows_at),
+        (bc, (block, bc.shape[1]), rows_at),
+        (step, (block, LANES), rows_at),
+        (cum, (block, LANES), rows_at),
+        (cols, (block, cols.shape[1]), rows_at),
+        (segs, (EDGE, block), columns_at),
         (spread, spread.shape, fixed),
         (gather, gather.shape, fixed),
-        (dy, (CHUNK, width), rows_at),
-        (ssm, (CHUNK, width), rows_at),
+        (dy, (block, width), rows_at),
+        (ssm, (block, width), rows_at),
     ]
     outs = [
-        ((rows, width), BF16, (CHUNK, width), rows_at),
-        ((rows, LANES), F32, (CHUNK, LANES), rows_at),
-        ((rows, bc.shape[1]), F32, (CHUNK, bc.shape[1]), rows_at),
+        ((rows, width), BF16, (block, width), rows_at),
+        ((rows, LANES), F32, (block, LANES), rows_at),
+        ((rows, bc.shape[1]), F32, (block, bc.shape[1]), rows_at),
     ]
     scratch = [pltpu.VMEM((2 * CHUNK, width), BF16)]
-    return call(back_within_body, (rows // CHUNK,), ins, outs, scratch, name="back_within")
+    return call(back_within_body, (rows // block,), ins, outs, scratch, name="back_within")
 
 
 def conv_back(ext, same, taps, grad_conv, next_rows):
@@ -598,13 +610,13 @@
     (
         x_ref, before_ref, edge_ref, xc_ref, bc_ref, step_ref, cum_ref, cols_ref, dt_ref, dy_ref, dxi_ref,
         left_ref, dbci_ref, enter_ref, phi_ref, in_ref, taps_ref, head_ref, rows_ref, spread_ref, gather_ref, sums_ref,
-        dx_ref, last_ref, prior_ref, mine_ref, theirs_ref, ddt_ref, conv_ref, heads_ref, skip_ref,
+        dx_ref, last_ref, prior_ref, mine_ref, theirs_ref, ddt_ref, conv_ref, heads_ref,
         grad_state, next_rows, wide, far, carried, held, begun, ending, products,
     ) = refs
     step = pl.program_id(0)
-    chunk = pl.num_programs(0) - 1 - step
+    first_block = step == pl.num_programs(0) - 1
     ns = in_ref.shape[0]
-    size, width = xc_ref.shape
+    size, width = CHUNK, xc_ref.shape[1]
 
     @pl.when(step == 0)
     def _():
@@ -612,79 +624,84 @@
         next_rows[...] = jnp.zeros_like(next_rows)
         conv_ref[...] = jnp.zeros_like(conv_ref)
         heads_ref[...] = jnp.zeros_like(heads_ref)
-        skip_ref[...] = jnp.zeros_like(skip_ref)
-
-    cols = cols_ref[...]
-    same = same_columns(cols, LANES)
-    cum = cum_ref[...]
-    dt = step_ref[...]
-    decay_in = cols[:, 4:5] * jnp.exp(cum)
-    decay_out = cols[:, 5:6] * jnp.exp(cum[size - 1 : size] - cum)
-    fold_rows = jnp.broadcast_to(decay_in[size - EDGE : size][EDGE - 1 : EDGE], (EDGE, LANES))
-    b_part = bc_ref[:, :ns]
-    c_part = bc_ref[:, ns:]
-    c_turned = c_part.astype(F32).T.astype(BF16)
-    stacked = jnp.concatenate([decay_in, decay_out, dt, fold_rows, phi_ref[0]], axis=0)
-    wide[...] = expand(stacked, spread_ref[...])
-    fold_at = 3 * size
-    for i in range(width // LANES):
-        part = slice(i * LANES, (i + 1) * LANES)
-        dy = dy_ref[:, part].astype(F32)
-        weighted = xc_ref[:, part].astype(F32) * wide[2 * size : 3 * size, part]
-        fold_wide = wide[fold_at : fold_at + 1, part]
-        grad_end = grad_state[:, part]
-        start = enter_ref[0, :, part].astype(F32) + wide[fold_at + EDGE : fold_at + EDGE + 1, part] * in_ref[:, part]
-        carried[:, part] = (dy * wide[:size, part]).astype(BF16)
-        held[:, part] = (weighted * wide[size : 2 * size, part]).astype(BF16)
-        begun[:, part] = start.astype(BF16)
-        ending[:, part] = grad_end.astype(BF16)
-        pass_sum = jnp.sum(start * grad_end, axis=0, keepdims=True) * fold_wide
-        products[2 * size :, part] = jnp.broadcast_to(pass_sum, (2 * EDGE, LANES)).astype(BF16)
-        grad_state[:, part] = fold_wide * grad_end
-    far[...] = dot(b_part, ending[...])
-    dbc_c = dbci_ref[:, ns:] + dot(carried[...], begun[...], ((1,), (1,)))
-    dbc_b = dbci_ref[:, :ns] + dot(held[...], ending[...], ((1,), (1,)))
-    grad_state[...] += dot(c_turned, carried[...])
-    own_b = flag[0] == 0
-    mine_ref[...] = jnp.where(own_b, dbc_b, dbc_c).astype(BF16)
-    theirs_ref[...] = jnp.where(own_b, dbc_c, dbc_b).astype(BF16)
-
-    first_chunk = chunk == 0
-    for i in range(width // LANES):
-        part = slice(i * LANES, (i + 1) * LANES)
-        dy = dy_ref[:, part].astype(F32)
-        x_conv = xc_ref[:, part].astype(F32)
-        dt_wide = wide[2 * size : 3 * size, part]
-        grad_far = wide[size : 2 * size, part] * far[:, part]
-        grad_weighted = dxi_ref[:, part].astype(F32) + grad_far
-        products[:size, part] = (x_conv * dt_wide * grad_far).astype(BF16)
-        products[size : 2 * size, part] = (x_conv * grad_weighted).astype(BF16)
-        skip_ref[0:1, part] += jnp.sum(dy * x_conv, axis=0, keepdims=True)
-        grad_conv = dt_wide * grad_weighted + rows_ref[1:2, part] * dy
-        ahead = jnp.where(first_chunk, edge_ref[:, part].astype(F32), before_ref[:, part].astype(F32))
-        ext = jnp.concatenate([ahead, x_ref[:, part].astype(F32)], axis=0)
-        raw, firsts, tap_sums = conv_back(
-            ext, same, taps_ref[:, part], grad_conv, [next_rows[k, :, part] for k in range(3)]
-        )
-        for k in range(3):
-            next_rows[k, :, part] = firsts[k]
-        for k in range(5):
-            conv_ref[k : k + 1, part] += tap_sums[k]
-        dx_ref[:, part] = raw[EDGE:].astype(BF16)
-        prior_ref[:, part] = raw[:EDGE]
-
-        @pl.when(step == 0)
-        def _(raw=raw, part=part):
-            last_ref[:, part] = raw[size:]
-
-    per_head = dot(products[...], gather_ref[...])
-    outward, direct, through = per_head[:size], per_head[size : 2 * size], per_head[2 * size : 2 * size + 1]
-    grad_rate = dot(sums_ref[...], jnp.concatenate([left_ref[...], outward], axis=0), precision=EXACT) + through
-    grad_dt = direct + head_ref[1:2] * grad_rate
-    grad_raw = grad_dt * cols[:, 3:4] * jax.nn.sigmoid(dt_ref[...] + head_ref[0:1])
-    ddt_ref[...] = grad_raw.astype(BF16)
-    heads_ref[0:1] += jnp.sum(grad_raw, axis=0, keepdims=True)
-    heads_ref[1:2] += jnp.sum(grad_rate * head_ref[1:2] * dt, axis=0, keepdims=True)
+
+    subs = len(chunks_of(xc_ref))
+    for sub, here in reversed(list(enumerate(chunks_of(xc_ref)))):
+        cols = cols_ref[here]
+        same = same_columns(cols, LANES)
+        cum = cum_ref[here]
+        dt = step_ref[here]
+        decay_in = cols[:, 4:5] * jnp.exp(cum)
+        decay_out = cols[:, 5:6] * jnp.exp(cum[size - 1 : size] - cum)
+        fold_rows = jnp.broadcast_to(decay_in[size - EDGE : size][EDGE - 1 : EDGE], (EDGE, LANES))
+        b_part = bc_ref[here, :ns]
+        c_part = bc_ref[here, ns:]
+        c_turned = c_part.astype(F32).T.astype(BF16)
+        stacked = jnp.concatenate([decay_in, decay_out, dt, fold_rows, phi_ref[sub]], axis=0)
+        wide[...] = expand(stacked, spread_ref[...])
+        fold_at = 3 * size
+        for i in range(width // LANES):
+            part = slice(i * LANES, (i + 1) * LANES)
+            dy = dy_ref[here, part].astype(F32)
+            weighted = xc_ref[here, part].astype(F32) * wide[2 * size : 3 * size, part]
+            fold_wide = wide[fold_at : fold_at + 1, part]
+            grad_end = grad_state[:, part]
+            start = enter_ref[sub, :, part].astype(F32) + wide[fold_at + EDGE : fold_at + EDGE + 1, part] * in_ref[:, part]
+            carried[:, part] = (dy * wide[:size, part]).astype(BF16)
+            held[:, part] = (weighted * wide[size : 2 * size, part]).astype(BF16)
+            begun[:, part] = start.astype(BF16)
+            ending[:, part] = grad_end.astype(BF16)
+            pass_sum = jnp.sum(start * grad_end, axis=0, keepdims=True) * fold_wide
+            products[2 * size :, part] = jnp.broadcast_to(pass_sum, (2 * EDGE, LANES)).astype(BF16)
+            grad_state[:, part] = fold_wide * grad_end
+        far[...] = dot(b_part, ending[...])
+        dbc_c = dbci_ref[here, ns:] + dot(carried[...], begun[...], ((1,), (1,)))
+        dbc_b = dbci_ref[here, :ns] + dot(held[...], ending[...], ((1,), (1,)))
+        grad_state[...] += dot(c_turned, carried[...])
+        own_b = flag[0] == 0
+        mine_ref[here] = jnp.where(own_b, dbc_b, dbc_c).astype(BF16)
+        theirs_ref[here] = jnp.where(own_b, dbc_c, dbc_b).astype(BF16)
+
+        for i in range(width // LANES):
+            part = slice(i * LANES, (i + 1) * LANES)
+            dy = dy_ref[here, part].astype(F32)
+            x_conv = xc_ref[here, part].astype(F32)
+            dt_wide = wide[2 * size : 3 * size, part]
+            grad_far = wide[size : 2 * size, part] * far[:, part]
+            grad_weighted = dxi_ref[here, part].astype(F32) + grad_far
+            products[:size, part] = (x_conv * dt_wide * grad_far).astype(BF16)
+            products[size : 2 * size, part] = (x_conv * grad_weighted).astype(BF16)
+            conv_ref[5:6, part] += jnp.sum(dy * x_conv, axis=0, keepdims=True)
+            grad_conv = dt_wide * grad_weighted + rows_ref[1:2, part] * dy
+            if sub:
+                ahead = x_ref[here.start - EDGE : here.start, part].astype(F32)
+            else:
+                ahead = jnp.where(first_block, edge_ref[:, part].astype(F32), before_ref[:, part].astype(F32))
+            ext = jnp.concatenate([ahead, x_ref[here, part].astype(F32)], axis=0)
+            raw, firsts, tap_sums = conv_back(
+                ext, same, taps_ref[:, part], grad_conv, [next_rows[k, :, part] for k in range(3)]
+            )
+            for k in range(3):
+                next_rows[k, :, part] = firsts[k]
+            for k in range(5):
+                conv_ref[k : k + 1, part] += tap_sums[k]
+            dx_ref[here, part] = raw[EDGE:].astype(BF16)
+            prior_ref[:, part] = raw[:EDGE]
+
+            if sub == subs - 1:
+
+                @pl.when(step == 0)
+                def _(raw=raw, part=part):
+                    last_ref[:, part] = raw[size:]
+
+        per_head = dot(products[...], gather_ref[...])
+        outward, direct, through = per_head[:size], per_head[size : 2 * size], per_head[2 * size : 2 * size + 1]
+        grad_rate = dot(sums_ref[...], jnp.concatenate([left_ref[here], outward], axis=0), precision=EXACT) + through
+        grad_dt = direct + head_ref[1:2] * grad_rate
+        grad_raw = grad_dt * cols[:, 3:4] * jax.nn.sigmoid(dt_ref[here] + head_ref[0:1])
+        ddt_ref[here] = grad_raw.astype(BF16)
+        heads_ref[0:1] += jnp.sum(grad_raw, axis=0, keepdims=True)
+        heads_ref[1:2] += jnp.sum(grad_rate * head_ref[1:2] * dt, axis=0, keepdims=True)
 
 
 def back_inter(
@@ -693,7 +710,9 @@
 ):
     rows, width = xc.shape
     ns = bc.shape[1] // 2
-    count = rows // CHUNK
+    block = min(256, rows)
+    subs = block // CHUNK
+    count = rows // block
 
     def back(i, *_):
         return (count - 1 - i, 0)
@@ -702,10 +721,10 @@
         return (count - 1 - i, 0, 0)
 
     def before(i, *_):
-        return (jnp.maximum((count - 1 - i) * (CHUNK // EDGE) - 1, 0), 0)
+        return (jnp.maximum((count - 1 - i) * (block // EDGE) - 1, 0), 0)
 
     def at(width_now):
-        return (CHUNK, width_now)
+        return (block, width_now)
 
     ins = [(p, p.shape, fixed) for p in payloads] + [
         (x_raw, at(width), back),
@@ -721,8 +740,8 @@
         (dx_in, at(width), back),
         (left, at(LANES), back),
         (dbc_in, at(2 * ns), back),
-        (entered, (1, ns, width), back3),
-        (phi, (1, EDGE, LANES), back3),
+        (entered, (subs, ns, width), back3),
+        (phi, (subs, EDGE, LANES), back3),
         (state_in, state_in.shape, fixed),
         (taps, taps.shape, fixed),
         (head, head.shape, fixed),
@@ -740,7 +759,6 @@
         ((rows, LANES), BF16, at(LANES), back),
         ((EDGE, width), F32, (EDGE, width), fixed),
         ((EDGE, LANES), F32, (EDGE, LANES), fixed),
-        ((EDGE, width), F32, (EDGE, width), fixed),
     ]
     scratch = [
         pltpu.VMEM((ns, width), F32),
@@ -789,20 +807,38 @@
     return call(back_bc_body, (1,), ins, outs, (), flag, name="back_bc")
 
 
-def back_low_body(flag, gate_ref, x_ref, bc_ref, dt_ref, wg_ref, wx_ref, wb_ref, wt_ref, out_ref):
-    over = ((1,), (1,))
-    total = dot(gate_ref[...], wg_ref[...], over) + dot(x_ref[...], wx_ref[...], over)
-    total = total + dot(bc_ref[...], wb_ref[...], over) + dot(dt_ref[...], wt_ref[...], over)
-    out_ref[...] = total.astype(BF16)
-
-
-def back_low(flag, dgate, dx, dbc, ddt, weights):
+def back_low_body(
+    flag, gate_ref, x_ref, bc_ref, dt_ref, last_x, last_bc, back_ref, wg_ref, wx_ref, wb_ref, wt_ref, out_ref
+):
+    def product(gate, x, bc, dt):
+        over = ((1,), (1,))
+        total = dot(gate, wg_ref[...], over) + dot(x, wx_ref[...], over)
+        return (total + dot(bc, wb_ref[...], over) + dot(dt, wt_ref[...], over)).astype(BF16)
+
+    out_ref[...] = product(gate_ref[...], x_ref[...], bc_ref[...], dt_ref[...])
+
+    @pl.when(pl.program_id(0) == pl.num_programs(0) - 1)
+    def _():
+        size, width = x_ref.shape
+        end = slice(size - 2 * EDGE, size)
+
+        def righted(ref, last, back):
+            kept = ref[end].astype(F32)[:EDGE]
+            return jnp.concatenate([kept, last[...] + back], axis=0).astype(BF16)
+
+        x = righted(x_ref, last_x, back_ref[:, :width])
+        bc = righted(bc_ref, last_bc, back_ref[:, width:])
+        out_ref[end] = product(gate_ref[end], x, bc, dt_ref[end])
+
+
+def back_low(flag, dgate, dx, dbc, ddt, last_x, last_bc, back_rows, weights):
     rows, width = dx.shape
     ns = dbc.shape[1]
     array, first = weights["lanes"]
     model = array.shape[0]
     block = min(256, rows)
     ins = [(v, (block, v.shape[1]), rows_at) for v in (dgate, dx, dbc, ddt)]
+    ins += [(v, v.shape, fixed) for v in (last_x, last_bc, back_rows)]
     ins += [
         block_of(weights["gate"]),
         block_of(weights["x"]),
@@ -825,7 +861,7 @@
     model = hidden.shape[1]
     norm = lax.rsqrt(jnp.mean(hidden * hidden, axis=1, keepdims=True) + EPSILON)
     normed = hidden * norm
-    sum_ref[0:1] += jnp.sum(grad * normed, axis=0, keepdims=True)
+    sum_ref[7:8] += jnp.sum(grad * normed, axis=0, keepdims=True)
     gained = grad * gain_ref[0:1]
     inner = jnp.sum(gained * normed, axis=1, keepdims=True) / model
     out_ref[...] = up_ref[...].astype(F32) + norm * (gained - normed * inner)
@@ -840,33 +876,51 @@
     return call(back_norm_body, (rows // block,), ins, outs, name="back_norm")
 
 
-def weight_grad_body(places, shards, cuts, owners, where, *refs):
-    lefts, refs = refs[: max(owners) + 1], refs[max(owners) + 1 :]
-    factors, outs, result = refs[: len(cuts)], refs[len(cuts) : len(cuts) + places], refs[len(cuts) + places]
+def weight_grad_body(places, shards, cuts, owners, ahead, where, *refs):
+    count = max(owners) + 1
+    lefts, refs = refs[:count], refs[count:]
+    factors, refs = refs[: len(cuts)], refs[len(cuts) :]
+    if ahead:
+        before, priors, refs = refs[0], refs[1 : 1 + len(cuts)], refs[1 + len(cuts) :]
+    outs, scratch = refs[:places], refs[places:]
     model = lefts[0].shape[0]
-    rows = model // (places * shards)
+    part = model // places
+    rows = part // shards
     step = pl.program_id(0)
-    for factor, owner, (start, end) in zip(factors, owners, cuts):
+    if shards > 1:
+
+        @pl.when(step == 0)
+        def _():
+            for source, ordered in zip(([lefts[0], before] if ahead else [lefts[0]]), scratch):
+                for k in range(places):
+                    for z in range(shards):
+                        at = pl.ds(pl.multiple_of((z * places + where[k]) * rows, rows), rows)
+                        ordered[k * part + z * rows : k * part + (z + 1) * rows] = source[at]
+
+    for i, (factor, owner, (start, end)) in enumerate(zip(factors, owners, cuts)):
 
         @pl.when((step >= start) & (step < end))
-        def _(factor=factor, owner=owner):
-            made = dot(lefts[owner][...], factor[...])
-            if places == 1:
-                outs[0][...] = made.astype(BF16)
-            else:
-                result[...] = made
-
-    if places == 1:
-        return
-    for k in range(places):
-        for z in range(shards):
-            start = pl.multiple_of((z * places + where[k]) * rows, rows)
-            outs[k][z * rows : (z + 1) * rows] = result[pl.ds(start, rows)].astype(BF16)
-
-
-def weight_grad(where, places, shards, products):
+        def _(i=i, factor=factor, owner=owner):
+            if ahead:
+                prior = priors[i][...]
+                empty = jnp.zeros((LANES - EDGE, prior.shape[1]), F32)
+                prior = jnp.concatenate([prior, empty], axis=0).astype(BF16)
+            for k in range(places):
+                if places == 1:
+                    at = slice(None)
+                elif shards == 1:
+                    at = pl.ds(pl.multiple_of(where[k] * part, part), part)
+                else:
+                    at = slice(k * part, (k + 1) * part)
+                made = dot((scratch[0] if shards > 1 else lefts[owner])[at], factor[...])
+                if ahead:
+                    made = made + dot((scratch[1] if shards > 1 else before)[at], prior)
+                outs[k][...] = made.astype(BF16)
+
+
+def weight_grad(where, places, shards, products, ahead=None):
     model, rows = products[0][0].shape
-    tile = 512 if places == 1 and all(b.shape[1] % 512 == 0 for _, factors in products for b in factors) else 256
+    tile = 512 if all(b.shape[1] % 512 == 0 for _, factors in products for b in factors) else 256
     cuts, owners, ins, at = [], [], [], 0
     for i, (a, factors) in enumerate(products):
         ins.append((a, a.shape, fixed))
@@ -874,14 +928,24 @@
             cuts.append((at, at + b.shape[1] // tile))
             owners.append(i)
             at = cuts[-1][1]
-    for b, (start, end) in zip([b for _, factors in products for b in factors], cuts):
-        ins.append((b, (rows, tile), lambda i, *_, s=start, e=end: (0, jnp.clip(i - s, 0, e - s - 1))))
+
+    def columns_of(arrays):
+        return [
+            (b, (b.shape[0], tile), lambda i, *_, s=start, e=end: (0, jnp.clip(i - s, 0, e - s - 1)))
+            for b, (start, end) in zip(arrays, cuts)
+        ]
+
+    ins += columns_of([b for _, factors in products for b in factors])
+    if ahead:
+        ins += [(ahead[0], ahead[0].shape, fixed)] + columns_of(ahead[1])
     width = at * tile
     part = model // places
     outs = [((part, width), BF16, (part, tile), columns_at)] * places
-    scratch = [pltpu.VMEM((model, tile), F32)]
+    scratch = []
+    if shards > 1:
+        scratch = [pltpu.VMEM((model, rows), BF16)] + ([pltpu.VMEM((model, LANES), BF16)] if ahead else [])
     return call(
-        functools.partial(weight_grad_body, places, shards, cuts, owners), (at,), ins, outs, scratch, where,
+        functools.partial(weight_grad_body, places, shards, cuts, owners, bool(ahead)), (at,), ins, outs, scratch, where,
         name="weight_grad",
     )
 
@@ -984,7 +1048,7 @@
         refs = refs[count:]
         zx_ref[layer, :, 0] = early[:, :width]
         zx_ref[layer, :, 1] = late[:, layer * span : layer * span + width]
-        out_ref[layer] = early[:, width:].T
+        out_ref[layer] = early[:, width:]
         small_ref[layer] = late[:, layer * span + width : (layer + 1) * span]
 
 
@@ -992,7 +1056,7 @@
     layers = len(early)
     rows, span = late[0].shape
     ins = [(v, v.shape, fixed) for parts in list(early) + [late] for v in parts]
-    shapes = [(layers, rows, 2, width), (layers, width, rows), (layers, rows, span // layers - width)]
+    shapes = [(layers, rows, 2, width), (layers, rows, width), (layers, rows, span // layers - width)]
     outs = [(v, F32, v, lambda *_, n=len(v): (0,) * n) for v in shapes]
     return call(functools.partial(finish_body, [len(parts) for parts in early]), (1,), ins, outs, name="finish")
 
@@ -1097,7 +1161,7 @@
         if more:
             main, dt_raw = tie((mains[layer + 1], dt_raw))
             coming = gather_shard(main)
-        edge, xc, bc, step, cum, entered, phi, ended = states(
+        edge, before_turned, xc, bc, step, cum, entered, phi, ended = states(
             x_raw, raw_bc, dt_raw, before, gain_in, weights[layer], cols, taps, taps_bc, head, spread, lower
         )
         y_in = within(xc, bc, step, cum, cols, segs, spread)
@@ -1113,7 +1177,7 @@
         parts = (p_own, swap(p_own))
         kept.append(
             dict(
-                hidden=hidden, turned=turned, x_raw=x_raw, raw_bc=raw_bc, dt_raw=dt_raw, edge=edge, gate=gate, xc=xc, bc=bc,
+                hidden=hidden, turned=turned, x_raw=x_raw, raw_bc=raw_bc, dt_raw=dt_raw, edge=edge, before_turned=before_turned, gate=gate, xc=xc, bc=bc,
                 step=step, cum=cum, entered=entered, phi=phi, ended=ended, state_in=state_in, ssm=ssm, parts=parts,
                 gain_in=gain_in, taps=taps, taps_bc=taps_bc, head=head, rowpack=rowpack,
             )
@@ -1146,7 +1210,7 @@
         quick = direct and layer == 0
         if quick:
             early = weight_grad(ring_order, shards, 1, early_pair)
-            dy, early = tie((dy, early))
+            dy, early, later = tie((dy, early, later))
             moving = around(early[0])
         else:
             early = weight_grad(ctx_order, 1, 1, early_pair)[0]
@@ -1162,7 +1226,7 @@
             later, rest_above = tie((later, rest_above))
             rest_above = near_rows(rest_above)
         edge = k["edge"]
-        dx, last, prior, dbc_mine, dbc_theirs, ddt, conv_rows, head_rows, skip_rows = back_inter(
+        dx, last, prior, dbc_mine, dbc_theirs, ddt, conv_rows, head_rows = back_inter(
             flag, later, k["x_raw"], edge, k["xc"], k["bc"], k["step"], k["cum"], cols, k["dt_raw"], dy,
             dx_in, left, dbc_in, k["entered"], k["phi"], k["state_in"], k["taps"], k["head"], k["rowpack"],
             spread, gather, sums,
@@ -1176,27 +1240,23 @@
             flag, k["raw_bc"], edge, cols, k["taps_bc"], dbc_mine, swap(dbc_theirs)
         )
         back_rows = shifted(jnp.concatenate([prior, prior_bc], axis=1), "ctx", -1)
-        dx = lax.dynamic_update_slice_in_dim(dx, (last + back_rows[:, :width]).astype(BF16), rows - EDGE, 0)
-        db = lax.dynamic_update_slice_in_dim(db, (last_bc + back_rows[:, width:]).astype(BF16), rows - EDGE, 0)
         late_pair = [(k["turned"], [dx, jnp.concatenate([db, ddt], axis=1)])]
+        ahead = (k["before_turned"], [prior, jnp.pad(prior_bc, ((0, 0), (0, LANES)))])
         if direct:
-            rest = weight_grad(ctx_order, places, shards, late_pair)
-            dgate, rest = tie((dgate, rest))
+            rest = weight_grad(ctx_order, places, shards, late_pair, ahead)
+            dgate, rest, back_rows = tie((dgate, rest, back_rows))
             if quick:
                 rest = near_rows(rest)
         else:
-            g_rest = owned(weight_grad(ctx_order, 1, 1, late_pair)[0])
-        dlow = back_low(flag, dgate, dx, db, ddt, weights[layer])
+            g_rest = owned(weight_grad(ctx_order, 1, 1, late_pair, ahead)[0])
+        dlow = back_low(flag, dgate, dx, db, ddt, last, last_bc, back_rows, weights[layer])
         if quick:
             dlow, moving = tie((dlow, moving))
             for one in early[2:-1]:
                 moving = around(add(moving, one))
             dlow, rest = tie((dlow, rest))
         up, norm_rows = back_norm(up, dlow, swap(dlow), k["hidden"], k["gain_in"])
-        packed = jnp.concatenate(
-            [norm_rows[0], conv_rows[:5].reshape(-1), gain_rows[0], skip_rows[0], conv_bc_rows[:5].reshape(-1),
-             head_rows[:2].reshape(-1)]
-        )
+        packed = jnp.concatenate([conv_rows + gain_rows + norm_rows, conv_bc_rows, head_rows], axis=1)
         smalls.insert(0, packed)
         if not direct:
             early_sums.insert(0, [g_early])
@@ -1208,38 +1268,36 @@
         else:
             late_sum = scattered(split_sum(shard_order, shards, [rest] + late_above), "shard")
             partial = axis_sum(jnp.concatenate(smalls), "ctx")
-            partial, moving, late_sum = tie((partial, moving, late_sum))
+            partial, moving = tie((partial, moving))
             early_sums.insert(0, scattered(split_sum(ctx_order, places, [[moving, early[-1]]]), "ctx"))
+            partial, late_sum, early_sums[0] = tie((partial, late_sum, early_sums[0]))
     if not direct:
         late_sum = [jnp.concatenate(late_above, axis=1)]
         partial = axis_sum(jnp.concatenate(smalls), "ctx")
-    packed = axis_sum(partial, "shard").reshape(layers, -1)
-    cuts = [model, 5 * width, width, width, 5 * ns, 2 * LANES]
-    ends = [sum(cuts[: i + 1]) for i in range(len(cuts))]
-    n_sum, cx_sum, gg_sum, sk_sum, cb_sum, hd_sum = jnp.split(packed, ends[:-1], axis=1)
-    cb_mine = cb_sum.reshape(layers, 5, ns)
+    packed = axis_sum(partial, "shard").reshape(layers, EDGE, -1)
     grad_zx, grad_out, grad_small = finish(early_sums, late_sum, width)
     small_mine = grad_small[:, :, :ns]
+    cb_mine = packed[:, :5, width : width + ns]
     cb_other, small_other = swap(cb_mine), swap(small_mine)
 
     def ordered(own, other):
         first = jnp.where(t == 0, own, other)
         return jnp.concatenate([first, jnp.where(t == 0, other, own)], axis=-1)
 
-    hd = hd_sum.reshape(layers, 2, LANES)[:, :, :heads]
-    skip_sum = jnp.sum(sk_sum.reshape(layers, heads, width // heads), axis=-1)
+    skip_sum = jnp.sum(packed[:, 5, :width].reshape(layers, heads, width // heads), axis=-1)
+    head_sums = packed[:, :2, width + ns : width + ns + heads]
     return (
         output[None],
         up[None],
         grad_zx,
         ordered(small_mine, small_other),
         grad_small[:, :, ns : ns + heads],
-        grad_out,
-        n_sum,
-        cx_sum.reshape(layers, 5, width),
+        jnp.swapaxes(grad_out, 1, 2),
+        packed[:, 7, :width],
+        packed[:, :5, :width],
         ordered(cb_mine, cb_other),
-        jnp.concatenate([hd, skip_sum[:, None]], axis=1),
-        gg_sum,
+        jnp.concatenate([head_sums, skip_sum[:, None]], axis=1),
+        packed[:, 6, :width],
     )
 
 

time: 586 us -> 550 us (0.939)
  Pallas kernels: 301 us -> 287 us
  starting transfers between devices: 117 us -> 107 us
    pallas_call x29, Pallas kernels: 301 us -> 287 us  [call(): return made(*([scalars] if count else []) + arrays)]
    ppermute x33, waiting for transfers between devices: 56.3 us -> 47.8 us  [relative(): return lax.ppermute(value, axis, [(i, i ^ by) for i in range(size)])]
    ppermute x8, starting transfers between devices: 31 us -> 24.4 us  [swap(): return lax.ppermute(value, 'tp', [(0, 1), (1, 0)])]
  transfers between devices with their start and end apart: 63 -> 63, of which waited for: 20 -> 21; matrix products, arithmetic and copies ran while one was open for 7% -> 6% of each run, Pallas kernels for 45% -> 46%
where the time goes in v3:
time: 550 us; the launch traced here: 542 us
  Pallas kernels  287 us (52%)
  starting transfers between devices  107 us (19%)
  waiting for transfers between devices  86.3 us (16%)
  local copies, waits for them, and re-layouts  27.8 us (5%)
  other arithmetic  19 us (3%)
  between operations  15.1 us (3%)
    pallas_call x29, Pallas kernels, call(): return made(*([scalars] if count else []) + arrays)  287 us
    ppermute x33, waiting for transfers between devices, relative(): return lax.ppermute(value, axis, [(i, i ^ by) for i in range(size)])  47.8 us
    ppermute x33, starting transfers between devices, relative(): return lax.ppermute(value, axis, [(i, i ^ by) for i in range(size)])  46.6 us
    ppermute x16, starting transfers between devices, shifted(): lax.ppermute(value, axis, [(i, i + by) for i in range(size) if 0 <= i + b...  32.4 us
    ppermute x8, starting transfers between devices, swap(): return lax.ppermute(value, 'tp', [(0, 1), (1, 0)])  24.4 us
    unnamed x152, local copies, waits for them, and re-layouts  16.8 us
    ppermute x8, waiting for transfers between devices, swap(): return lax.ppermute(value, 'tp', [(0, 1), (1, 0)])  15.7 us
    ppermute x16, waiting for transfers between devices, shifted(): lax.ppermute(value, axis, [(i, i + by) for i in range(size) if 0 <= i + b...  11.6 us
  transfers between devices with their start and end apart: 63, of which 21 were waited for; matrix products, arithmetic and copies ran while one was open for 6% of the time, Pallas kernels for 46%

profile of v3, /device:TPU:1, one launch (start us, length us, event | category | flops | bytes accessed | tf_op | source)
XLA Modules:
  0.0 542.4 jit_solution(12213755926697133442)
XLA Ops:
  29.3 5.0 collective-permute-start.8
  34.4 11.3 %collective-permute-done.7.refs_6_ = bf16[256,384]{1,0:T(8,128)(2,1)S(1)} collective-permute-done((bf16[256,384]{1,0:T(8,128)(2,1)}, bf16[256,384]{1,0:T(8,128)(2,1)S(1)}, u32[]{:S(2)}, u32[]{:S(2)}) %collective-permute-start.7) | collective-permute-done | bytes 196640 | tf_op jit(solution)/shard_map/ppermute | solution.py:955
  50.1 10.5 %enter.2 = (bf16[1024,1024]{1,0:T(8,128)(2,1)}, bf16[1024,1024]{1,0:T(8,128)(2,1)}, bf16[1024,1024]{1,0:T(8,128)(2,1)}, bf16[1024,256]{1,0:T(8,128)(2,1)}, f32[1...) custom-call(s32[8]{0:T(128)} %pad_add_fusion.where, bf16[256,1024]{1,0:T(8,128)(2,1)} %copy-done.9, ...), custom_call_target="tpu_custom_call" | custom-call | flops 1 | bytes 1 | tf_op jit(solution)/shard_map/enter/pallas_call | solution.py:112
  68.3 12.8 %states.2 = (bf16[8,1280]{1,0:T(8,128)(2,1)}, bf16[1024,128]{1,0:T(8,128)(2,1)}, bf16[1024,1024]{1,0:T(8,128)(2,1)}, bf16[1024,256]{1,0:T(8,128)(2,1)}, f32[1024...) custom-call(bf16[1024,1024]{1,0:T(8,128)(2,1)} %get-tuple-element.20, ...), custom_call_target="tpu_custom_call" | custom-call | flops 1 | bytes 1 | tf_op jit(solution)/shard_map/states/pallas_call | solution.py:112
  89.9 6.8 %within.2.refs_5_ = f32[1024,1024]{1,0:T(8,128)} custom-call(bf16[1024,1024]{1,0:T(8,128)(2,1)} %get-tuple-element.211.xc_ref.refs_7_.refs_4_.refs_6_, bf16[1024,256]{1,0:T(8,128)(2,1)} %get-tuple-element.212.bc_ref.refs_8_.refs_6_.refs_7_, f32[1024,128]{1,0:T(8,128)} %get-tuple-element.213.step_ref.refs_8_, ...), custom_call_target="tpu_custom_call" | custom-call | flops 1 | bytes 1 | tf_op jit(solution)/shard_map/within/pallas_call | solution.py:112
  103.9 8.6 %all-gather.3.cloned.1.call-done.refs_3_.refs_4_.refs_13_.wg_ref = bf16[1024,2048]{1,0:T(8,128)(2,1)} async-done(((bf16[64,2048]{1,0:T(8,128)(2,1)}), bf16[1024,2048]{1,0:T(8,128)(2,1)}) %all-gather.3.cloned.1.call-update) | async-done | bytes 4194320 | tf_op jit(solution)/shard_map/all_gather | solution.py:998
  112.6 13.5 %leave.2 = (f32[1024,1024]{1,0:T(8,128)}, f32[1024,1024]{1,0:T(8,128)}, bf16[1024,1152]{1,0:T(8,128)(2,1)}, f32[128,1024]{1,0:T(8,128)}) custom-call(bf16[136,1024]{1,0:T(8,128)(2,1)} %copy-done.31, bf16[136,1024]{1,0:T(8,128)(2,1)} %copy-done.32, bf16[136,1024]{1,0:T(8,128)(2,1)} %collective-permute-done.12.refs_2_, ...), custom_call_target="tpu_custom_call" | custom-call | flops 1 | bytes 1 | tf_op jit(solution)/shard_map/leave/pallas_call | solution.py:112
  127.7 16.9 %collective-permute-start.19 = (bf16[1024,1152]{1,0:T(8,128)(2,1)}, bf16[1024,1152]{1,0:T(8,128)(2,1)S(1)}, u32[]{:S(2)}, u32[]{:S(2)}) collective-permute-start(bf16[1024,1152]{1,0:T(8,128)(2,1)} %get-tuple-element.229.refs_5_.refs_1_), channel_id=1, source_target_pairs={{0,1},{1,0},{2,3},{3,2},{4,5},{5,4},{6,7},{7,6},{8,9},{9,8},{10,11... | collective-permute-start | bytes 7077896 | tf_op jit(solution)/shard_map/ppermute | solution.py:1078
  154.6 11.8 %enter.3 = (f32[1024,1024]{1,0:T(8,128)}, bf16[1024,1024]{1,0:T(8,128)(2,1)}, bf16[1024,1024]{1,0:T(8,128)(2,1)}, bf16[1024,1024]{1,0:T(8,128)(2,1)}, bf16[1024,...) custom-call(s32[8]{0:T(128)} %pad_add_fusion.where, ...), custom_call_target="tpu_custom_call" | custom-call | flops 1 | bytes 1 | tf_op jit(solution)/shard_map/enter/pallas_call | solution.py:112
  167.0 12.7 %states.3 = (bf16[8,1280]{1,0:T(8,128)(2,1)}, bf16[1024,128]{1,0:T(8,128)(2,1)}, bf16[1024,1024]{1,0:T(8,128)(2,1)}, bf16[1024,256]{1,0:T(8,128)(2,1)}, f32[1024...) custom-call(bf16[1024,1024]{1,0:T(8,128)(2,1)} %get-tuple-element.23, ...), custom_call_target="tpu_custom_call" | custom-call | flops 1 | bytes 1 | tf_op jit(solution)/shard_map/states/pallas_call | solution.py:112
  179.8 5.2 collective-permute-start.21
  188.6 6.8 %within.3.refs_5_ = f32[1024,1024]{1,0:T(8,128)} custom-call(bf16[1024,1024]{1,0:T(8,128)(2,1)} %get-tuple-element.238.xc_ref.refs_7_.refs_5_.refs_6_, bf16[1024,256]{1,0:T(8,128)(2,1)} %get-tuple-element.239.bc_ref.refs_8_.refs_7_, f32[1024,128]{1,0:T(8,128)} %get-tuple-element.240.step_ref.refs_8_, f32[1024,128]{1,0:T(8,128)} %get-tuple-element.241.cum_ref.refs_9_.refs_8_, ...), custom_call_target="tpu_custom_call" | custom-call | flops 1 | bytes 1 | tf_op jit(solution)/shard_map/within/pallas_call | solution.py:112
  198.2 13.6 %leave.3 = (f32[1024,1024]{1,0:T(8,128)}, f32[1024,1024]{1,0:T(8,128)}, bf16[1024,1152]{1,0:T(8,128)(2,1)}, f32[128,1024]{1,0:T(8,128)}) custom-call(bf16[136,1024]{1,0:T(8,128)(2,1)} %copy-done.33, bf16[136,1024]{1,0:T(8,128)(2,1)} %copy-done.34, bf16[136,1024]{1,0:T(8,128)(2,1)} %copy-done.35, ...), custom_call_target="tpu_custom_call" | custom-call | flops 1 | bytes 1 | tf_op jit(solution)/shard_map/leave/pallas_call | solution.py:112
  218.4 17.6 %back_gate.2 = (f32[1024,1024]{1,0:T(8,128)}, bf16[1024,1024]{1,0:T(8,128)(2,1)}, bf16[1024,1024]{1,0:T(8,128)(2,1)}, bf16[1024,1024]{1,0:T(8,128)(2,1)}, bf16[1...) custom-call(f32[1024,1024]{1,0:T(8,128)} %get-tuple-element.230.refs_0_.h_ref, ...), custom_call_target="tpu_custom_call" | custom-call | flops 1 | bytes 1 | tf_op jit(solution)/shard_map/back_gate/pallas_call | solution.py:112
  241.0 10.0 %weight_grad.4 = bf16[1024,2048]{1,0:T(8,128)(2,1)} custom-call(s32[4]{0:T(128)} %copy-done.66, bf16[1024,1024]{1,0:T(8,128)(2,1)} %get-tuple-element.250.refs_0_, bf16[1024,1024]{1,0:T(8,128)(2,1)} %get-tuple-element.252.refs_1_, bf16[1024,1024]{1,0:T(8,128)(2,1)} %get-tuple-element.278.refs_2_.gate_ref, bf16[1024,1024]{1,0:T(8,128)(2,1)} %get-tuple-element.253.refs_3_), custom_call_target="tpu_custom_call" | custom-call | flops 1 | bytes 1 | tf_op jit(solution)/shard_map/weight_grad/pallas_call | solution.py:112
  251.0 9.8 %back_within.2 = (bf16[1024,1024]{1,0:T(8,128)(2,1)}, f32[1024,128]{1,0:T(8,128)}, f32[1024,256]{1,0:T(8,128)}) custom-call(bf16[1024,1024]{1,0:T(8,128)(2,1)} %get-tuple-element.238.xc_ref.refs_7_.refs_5_.refs_6_, bf16[1024,256]{1,0:T(8,128)(2,1)} %get-tuple-element.239.bc_ref.refs_8_.refs_7_, f32[1024,128]{1,0:T(8,128)} %get-tuple-element.240.step_ref.refs_8_, ...), custom_call_target="tpu_custom_call" | custom-call | flops 1 | bytes 1 | tf_op jit(solution)/shard_map/back_within/pallas_call | solution.py:112
  262.5 23.9 %back_inter.2 = (bf16[1024,1024]{1,0:T(8,128)(2,1)}, f32[8,1024]{1,0:T(8,128)}, f32[8,1024]{1,0:T(8,128)}, bf16[1024,128]{1,0:T(8,128)(2,1)}, bf16[1024,128]{1,0...) custom-call(s32[1]{0:T(128)} %bitcast.27.flag, bf16[136,1024]{1,0:T(8,128)(2,1)} %copy-done.28, ...), custom_call_target="tpu_custom_call" | custom-call | flops 1 | bytes 1 | tf_op jit(solution)/shard_map/back_inter/pallas_call | solution.py:112
  297.6 8.4 %weight_grad.5 = (bf16[256,1280]{1,0:T(8,128)(2,1)}, bf16[256,1280]{1,0:T(8,128)(2,1)}, bf16[256,1280]{1,0:T(8,128)(2,1)}, bf16[256,1280]{1,0:T(8,128)(2,1)}) custom-call(s32[4]{0:T(128)} %copy-done.66, bf16[1024,1024]{1,0:T(8,128)(2,1)} %get-tuple-element.250.refs_0_, bf16[1024,1024]{1,0:T(8,128)(2,1)} %get-tuple-element.266.refs_1_.x_ref, ...), custom_call_target="tpu_custom_call" | custom-call | flops 1 | bytes 1 | tf_op jit(solution)/shard_map/weight_grad/pallas_call | solution.py:112
  306.5 11.4 %back_low.2.a_ref = bf16[1024,1024]{1,0:T(8,128)(2,1)} custom-call(s32[1]{0:T(128)} %bitcast.27.flag, bf16[1024,1024]{1,0:T(8,128)(2,1)} %get-tuple-element.278.refs_2_.gate_ref, bf16[1024,1024]{1,0:T(8,128)(2,1)} %get-tuple-element.266.refs_1_.x_ref, bf16[1024,128]{1,0:T(8,128)(2,1)} %get-tuple-element.269.bc_ref, ...), custom_call_target="tpu_custom_call" | custom-call | flops 1 | bytes 1 | tf_op jit(solution)/shard_map/back_low/pallas_call | solution.py:112
  323.7 7.5 %back_norm.2 = (f32[1024,1024]{1,0:T(8,128)}, f32[8,1024]{1,0:T(8,128)}) custom-call(bf16[1024,1024]{1,0:T(8,128)(2,1)} %bitcast.69, bf16[1024,1024]{1,0:T(8,128)(2,1)} %back_low.2.a_ref, bf16[1024,1024]{1,0:T(8,128)(2,1)} %copy-done.4, f32[1024,1024]{1,0:T(8,128)} %get-tuple-element.230.refs_0_.h_ref, f32[8,1024]{1,0:T(8,128)} %pad.48.refs_7_.gain_ref), custom_call_target="tpu_custom_call" | custom-call | flops 1 | bytes 1 | tf_op jit(solution)/shard_map/back_norm/pallas_call | solution.py:112
  331.2 15.8 %back_gate.3 = (bf16[1024,1024]{1,0:T(8,128)(2,1)}, bf16[1024,1024]{1,0:T(8,128)(2,1)}, bf16[1024,1024]{1,0:T(8,128)(2,1)}, bf16[1024,1024]{1,0:T(8,128)(2,1)}, ...) custom-call(f32[1024,1024]{1,0:T(8,128)} %get-tuple-element.282.refs_0_.up_ref, ...), custom_call_target="tpu_custom_call" | custom-call | flops 1 | bytes 1 | tf_op jit(solution)/shard_map/back_gate/pallas_call | solution.py:112
  351.5 10.1 %weight_grad.6 = (bf16[256,2048]{1,0:T(8,128)(2,1)}, bf16[256,2048]{1,0:T(8,128)(2,1)}, bf16[256,2048]{1,0:T(8,128)(2,1)}, bf16[256,2048]{1,0:T(8,128)(2,1)}) custom-call(s32[4]{0:T(128)} %and_select_fusion.where, bf16[1024,1024]{1,0:T(8,128)(2,1)} %get-tuple-element.286.refs_0_, bf16[1024,1024]{1,0:T(8,128)(2,1)} %get-tuple-element.288.refs_1_, ...), custom_call_target="tpu_custom_call" | custom-call | flops 1 | bytes 1 | tf_op jit(solution)/shard_map/weight_grad/pallas_call | solution.py:112
  362.6 5.7 %collective-permute-done.33.refs_2_ = bf16[136,1024]{1,0:T(8,128)(2,1)S(1)} collective-permute-done((bf16[136,1024]{1,0:T(8,128)(2,1)}, bf16[136,1024]{1,0:T(8,128)(2,1)S(1)}, u32[]{:S(2)}, u32[]{:S(2)}) %collective-permute-start.33) | collective-permute-done | bytes 278560 | tf_op jit(solution)/shard_map/ppermute | solution.py:960
  372.9 9.8 %back_within.3 = (bf16[1024,1024]{1,0:T(8,128)(2,1)}, f32[1024,128]{1,0:T(8,128)}, f32[1024,256]{1,0:T(8,128)}) custom-call(bf16[1024,1024]{1,0:T(8,128)(2,1)} %get-tuple-element.211.xc_ref.refs_7_.refs_4_.refs_6_, bf16[1024,256]{1,0:T(8,128)(2,1)} %get-tuple-element.212.bc_ref.refs_8_.refs_6_.refs_7_, f32[1024,128]{1,0:T(8,128)} %get-tuple-element.213.step_ref.refs_8_, ...), custom_call_target="tpu_custom_call" | custom-call | flops 1 | bytes 1 | tf_op jit(solution)/shard_map/back_within/pallas_call | solution.py:112
  382.8 24.0 %back_inter.3 = (bf16[1024,1024]{1,0:T(8,128)(2,1)}, f32[8,1024]{1,0:T(8,128)}, f32[8,1024]{1,0:T(8,128)}, bf16[1024,128]{1,0:T(8,128)(2,1)}, bf16[1024,128]{1,0...) custom-call(s32[1]{0:T(128)} %bitcast.27.flag, bf16[136,1024]{1,0:T(8,128)(2,1)} %copy-done.25, ...), custom_call_target="tpu_custom_call" | custom-call | flops 1 | bytes 1 | tf_op jit(solution)/shard_map/back_inter/pallas_call | solution.py:112
  419.4 8.3 %weight_grad.7 = (bf16[256,1280]{1,0:T(8,128)(2,1)}, bf16[256,1280]{1,0:T(8,128)(2,1)}, bf16[256,1280]{1,0:T(8,128)(2,1)}, bf16[256,1280]{1,0:T(8,128)(2,1)}) custom-call(s32[4]{0:T(128)} %copy-done.66, bf16[1024,1024]{1,0:T(8,128)(2,1)} %get-tuple-element.286.refs_0_, bf16[1024,1024]{1,0:T(8,128)(2,1)} %get-tuple-element.315.refs_1_.x_ref, ...), custom_call_target="tpu_custom_call" | custom-call | flops 1 | bytes 1 | tf_op jit(solution)/shard_map/weight_grad/pallas_call | solution.py:112
  431.4 11.5 %back_low.3.a_ref = bf16[1024,1024]{1,0:T(8,128)(2,1)} custom-call(s32[1]{0:T(128)} %bitcast.27.flag, bf16[1024,1024]{1,0:T(8,128)(2,1)} %get-tuple-element.332.refs_2_.gate_ref, bf16[1024,1024]{1,0:T(8,128)(2,1)} %get-tuple-element.315.refs_1_.x_ref, bf16[1024,128]{1,0:T(8,128)(2,1)} %get-tuple-element.323.bc_ref, ...), custom_call_target="tpu_custom_call" | custom-call | flops 1 | bytes 1 | tf_op jit(solution)/shard_map/back_low/pallas_call | solution.py:112
  445.5 14.4 %collective-permute-done.43.refs_3_ = bf16[256,1280]{1,0:T(8,128)(2,1)S(1)} collective-permute-done((bf16[256,1280]{1,0:T(8,128)(2,1)}, bf16[256,1280]{1,0:T(8,128)(2,1)S(1)}, u32[]{:S(2)}, u32[]{:S(2)}) %collective-permute-start.43) | collective-permute-done | bytes 655392 | tf_op jit(solution)/shard_map/ppermute | solution.py:955
  466.7 7.2 %back_norm.3 = (f32[1024,1024]{1,0:T(8,128)}, f32[8,1024]{1,0:T(8,128)}) custom-call(f32[1024,1024]{1,0:T(8,128)} %get-tuple-element.282.refs_0_.up_ref, bf16[1024,1024]{1,0:T(8,128)(2,1)} %back_low.3.a_ref, bf16[1024,1024]{1,0:T(8,128)(2,1)} %copy-done.3, bf16[1024,1024]{1,0:T(8,128)(2,1)} %bitcast.67, f32[8,1024]{1,0:T(8,128)} %pad.43.refs_9_.gain_ref), custom_call_target="tpu_custom_call" | custom-call | flops 1 | bytes 1 | tf_op jit(solution)/shard_map/back_norm/pallas_call | solution.py:112
  494.7 7.9 %collective-permute-done.49.refs_6_ = bf16[64,2560]{1,0:T(8,128)(2,1)S(1)} collective-permute-done((bf16[64,2560]{1,0:T(8,128)(2,1)}, bf16[64,2560]{1,0:T(8,128)(2,1)S(1)}, u32[]{:S(2)}, u32[]{:S(2)}) %collective-permute-start.49) | collective-permute-done | bytes 327712 | tf_op jit(solution)/shard_map/ppermute | solution.py:955
  504.3 5.2 collective-permute-done.51.refs_8_
  517.2 5.6 %collective-permute-start.56 = (f32[16,1280]{1,0:T(8,128)S(1)}, f32[16,1280]{1,0:T(8,128)S(1)}, u32[]{:S(2)}, u32[]{:S(2)}) collective-permute-start(f32[16,1280]{1,0:T(8,128)S(1)} %add_add_fusion), channel_id=1, source_target_pairs={{0,8},{8,0},{16,24},{24,16},{1,9},{9,1},{17,25},{25,17},{2,10},{10... | collective-permute-start | bytes 245768 | tf_op jit(solution)/shard_map/ppermute | solution.py:955
  (349 shorter events, 177.6 us)
Async XLA Ops:
  7.2 105.4 %all-gather.3.cloned.1.call-start = ((), (), s32[]{:S(2)}) async-start(), calls=%async_computation.1 | async-start | bytes 4456448 | tf_op jit(solution)/shard_map/all_gather | solution.py:998
  11.5 183.9 %all-gather.5.cloned.1.call-start = ((), (), s32[]{:S(2)}) async-start(), calls=%async_computation.2 | async-start | bytes 4456448 | tf_op jit(solution)/shard_map/all_gather | solution.py:998
  16.5 29.2 %collective-permute-start.7 = (bf16[256,384]{1,0:T(8,128)(2,1)}, bf16[256,384]{1,0:T(8,128)(2,1)S(1)}, u32[]{:S(2)}, u32[]{:S(2)}) collective-permute-start(bf16[256,384]{1,0:T(8,128)(2,1)} %get-tuple-element.201.refs_4_), channel_id=1, source_target_pairs={{0,16},{8,24},{16,0},{24,8},{1,17},{9,25},{17,1},{25,9},{2,18},{10... | collective-permute-start | bytes 589832 | tf_op jit(solution)/shard_map/ppermute | solution.py:955
  22.4 360.4 %reduce-scatter.2.cloned.1.call-start = ((), (), s32[]{:S(2)}) async-start(), calls=%async_computation.3 | async-start | bytes 4456448 | tf_op jit(solution)/shard_map/reduce_scatter | solution.py:1191
  26.0 22.9 %collective-permute-start.3 = (bf16[256,1024]{1,0:T(8,128)(2,1)S(1)}, bf16[256,1024]{1,0:T(8,128)(2,1)S(1)}, u32[]{:S(2)}, u32[]{:S(2)}) collective-permute-start(bf16[256,1024]{1,0:T(8,128)(2,1)S(1)} %constant_dynamic-update-slice_fusion.refs_0_), channel_id=1, source_target_pairs={{0,2},{2,0},{4,6},{6,4},{1,3},{3,1},{5,7},{7,5},{8,10},{10,8},{12,... | collective-permute-start | bytes 1572872 | tf_op jit(solution)/shard_map/ppermute | solution.py:955
  27.3 21.6 %collective-permute-start.4 = (bf16[256,1024]{1,0:T(8,128)(2,1)S(1)}, bf16[256,1024]{1,0:T(8,128)(2,1)S(1)}, u32[]{:S(2)}, u32[]{:S(2)}) collective-permute-start(bf16[256,1024]{1,0:T(8,128)(2,1)S(1)} %constant_dynamic-update-slice_fusion.refs_0_), channel_id=1, source_target_pairs={{0,4},{2,6},{4,0},{6,2},{1,5},{3,7},{5,1},{7,3},{8,12},{10,14},{12... | collective-permute-start | bytes 1572872 | tf_op jit(solution)/shard_map/ppermute | solution.py:955
  28.5 20.4 %collective-permute-start.5 = (bf16[256,1024]{1,0:T(8,128)(2,1)S(1)}, bf16[256,1024]{1,0:T(8,128)(2,1)S(1)}, u32[]{:S(2)}, u32[]{:S(2)}) collective-permute-start(bf16[256,1024]{1,0:T(8,128)(2,1)S(1)} %constant_dynamic-update-slice_fusion.refs_0_), channel_id=1, source_target_pairs={{0,6},{2,4},{4,2},{6,0},{1,7},{3,5},{5,3},{7,1},{8,14},{10,12},{12... | collective-permute-start | bytes 1572872 | tf_op jit(solution)/shard_map/ppermute | solution.py:955
  29.3 19.5 %collective-permute-start.8 = (bf16[256,384]{1,0:T(8,128)(2,1)S(1)}, bf16[256,384]{1,0:T(8,128)(2,1)S(1)}, u32[]{:S(2)}, u32[]{:S(2)}) collective-permute-start(bf16[256,384]{1,0:T(8,128)(2,1)S(1)} %copy-done.41), channel_id=1, source_target_pairs={{0,24},{8,16},{16,8},{24,0},{1,25},{9,17},{17,9},{25,1},{2,26},{10... | collective-permute-start | bytes 589832 | tf_op jit(solution)/shard_map/ppermute | solution.py:955
  45.7 22.0 %collective-permute-start.9 = (bf16[8,1024]{1,0:T(8,128)(2,1)S(1)}, bf16[8,1024]{1,0:T(8,128)(2,1)S(1)}, u32[]{:S(2)}, u32[]{:S(2)}) collective-permute-start(bf16[8,1024]{1,0:T(8,128)(2,1)S(1)} %slice_bitcast_fusion), channel_id=1, source_target_pairs={{0,2},{2,4},{4,6},{1,3},{3,5},{5,7},{8,10},{10,12},{12,14},{9,11},... | collective-permute-start | bytes 49160 | tf_op jit(solution)/shard_map/ppermute | solution.py:960
  60.5 26.2 %collective-permute-start.13 = (bf16[64,1408]{1,0:T(8,128)(2,1)S(1)}, bf16[64,1408]{1,0:T(8,128)(2,1)S(1)}, u32[]{:S(2)}, u32[]{:S(2)}) collective-permute-start(bf16[64,1408]{1,0:T(8,128)(2,1)S(1)} %copy-done.45), channel_id=1, source_target_pairs={{0,8},{8,0},{16,24},{24,16},{1,9},{9,1},{17,25},{25,17},{2,10},{10... | collective-permute-start | bytes 540680 | tf_op jit(solution)/shard_map/ppermute | solution.py:955
  61.3 35.5 %collective-permute-start.14 = (bf16[64,1408]{1,0:T(8,128)(2,1)S(1)}, bf16[64,1408]{1,0:T(8,128)(2,1)S(1)}, u32[]{:S(2)}, u32[]{:S(2)}) collective-permute-start(bf16[64,1408]{1,0:T(8,128)(2,1)S(1)} %copy-done.45), channel_id=1, source_target_pairs={{0,16},{8,24},{16,0},{24,8},{1,17},{9,25},{17,1},{25,9},{2,18},{10... | collective-permute-start | bytes 540680 | tf_op jit(solution)/shard_map/ppermute | solution.py:955
  63.3 33.5 %collective-permute-start.15 = (bf16[64,1408]{1,0:T(8,128)(2,1)S(1)}, bf16[64,1408]{1,0:T(8,128)(2,1)S(1)}, u32[]{:S(2)}, u32[]{:S(2)}) collective-permute-start(bf16[64,1408]{1,0:T(8,128)(2,1)S(1)} %copy-done.45), channel_id=1, source_target_pairs={{0,24},{8,16},{16,8},{24,0},{1,25},{9,17},{17,9},{25,1},{2,26},{10... | collective-permute-start | bytes 540680 | tf_op jit(solution)/shard_map/ppermute | solution.py:955
  99.7 26.4 %collective-permute-start.16 = (bf16[256,1408]{1,0:T(8,128)(2,1)S(1)}, bf16[256,1408]{1,0:T(8,128)(2,1)S(1)}, u32[]{:S(2)}, u32[]{:S(2)}) collective-permute-start(bf16[256,1408]{1,0:T(8,128)(2,1)S(1)} %pad_maximum_fusion.refs_0_), channel_id=1, source_target_pairs={{0,2},{2,0},{4,6},{6,4},{1,3},{3,1},{5,7},{7,5},{8,10},{10,8},{12,... | collective-permute-start | bytes 2162696 | tf_op jit(solution)/shard_map/ppermute | solution.py:955
  99.7 28.0 %collective-permute-start.17 = (bf16[256,1408]{1,0:T(8,128)(2,1)S(1)}, bf16[256,1408]{1,0:T(8,128)(2,1)S(1)}, u32[]{:S(2)}, u32[]{:S(2)}) collective-permute-start(bf16[256,1408]{1,0:T(8,128)(2,1)S(1)} %pad_maximum_fusion.refs_0_), channel_id=1, source_target_pairs={{0,4},{2,6},{4,0},{6,2},{1,5},{3,7},{5,1},{7,3},{8,12},{10,14},{12... | collective-permute-start | bytes 2162696 | tf_op jit(solution)/shard_map/ppermute | solution.py:955
  103.1 24.6 %collective-permute-start.18 = (bf16[256,1408]{1,0:T(8,128)(2,1)S(1)}, bf16[256,1408]{1,0:T(8,128)(2,1)S(1)}, u32[]{:S(2)}, u32[]{:S(2)}) collective-permute-start(bf16[256,1408]{1,0:T(8,128)(2,1)S(1)} %pad_maximum_fusion.refs_0_), channel_id=1, source_target_pairs={{0,6},{2,4},{4,2},{6,0},{1,7},{3,5},{5,3},{7,1},{8,14},{10,12},{12... | collective-permute-start | bytes 2162696 | tf_op jit(solution)/shard_map/ppermute | solution.py:955
  127.7 21.3 %collective-permute-start.19 = (bf16[1024,1152]{1,0:T(8,128)(2,1)}, bf16[1024,1152]{1,0:T(8,128)(2,1)S(1)}, u32[]{:S(2)}, u32[]{:S(2)}) collective-permute-start(bf16[1024,1152]{1,0:T(8,128)(2,1)} %get-tuple-element.229.refs_5_.refs_1_), channel_id=1, source_target_pairs={{0,1},{1,0},{2,3},{3,2},{4,5},{5,4},{6,7},{7,6},{8,9},{9,8},{10,11... | collective-permute-start | bytes 7077896 | tf_op jit(solution)/shard_map/ppermute | solution.py:1078
  236.0 24.9 %collective-permute-start.25 = (bf16[136,1024]{1,0:T(8,128)(2,1)}, bf16[136,1024]{1,0:T(8,128)(2,1)S(1)}, u32[]{:S(2)}, u32[]{:S(2)}) collective-permute-start(bf16[136,1024]{1,0:T(8,128)(2,1)} %get-tuple-element.256), channel_id=1, source_target_pairs={{2,0},{4,2},{6,4},{3,1},{5,3},{7,5},{10,8},{12,10},{14,12},{11,9},... | collective-permute-start | bytes 835592 | tf_op jit(solution)/shard_map/ppermute | solution.py:960
  237.3 23.6 %collective-permute-start.26 = (bf16[136,1024]{1,0:T(8,128)(2,1)}, bf16[136,1024]{1,0:T(8,128)(2,1)S(1)}, u32[]{:S(2)}, u32[]{:S(2)}) collective-permute-start(bf16[136,1024]{1,0:T(8,128)(2,1)} %get-tuple-element.256), channel_id=1, source_target_pairs={{4,0},{6,2},{5,1},{7,3},{12,8},{14,10},{13,9},{15,11},{20,16},{22,... | collective-permute-start | bytes 835592 | tf_op jit(solution)/shard_map/ppermute | solution.py:960
  238.6 22.3 %collective-permute-start.27 = (bf16[136,1024]{1,0:T(8,128)(2,1)}, bf16[136,1024]{1,0:T(8,128)(2,1)S(1)}, u32[]{:S(2)}, u32[]{:S(2)}) collective-permute-start(bf16[136,1024]{1,0:T(8,128)(2,1)} %get-tuple-element.256), channel_id=1, source_target_pairs={{6,0},{7,1},{14,8},{15,9},{22,16},{23,17},{30,24},{31,25}} | collective-permute-start | bytes 835592 | tf_op jit(solution)/shard_map/ppermute | solution.py:960
  349.6 18.6 %collective-permute-start.33 = (bf16[136,1024]{1,0:T(8,128)(2,1)}, bf16[136,1024]{1,0:T(8,128)(2,1)S(1)}, u32[]{:S(2)}, u32[]{:S(2)}) collective-permute-start(bf16[136,1024]{1,0:T(8,128)(2,1)} %get-tuple-element.294), channel_id=1, source_target_pairs={{6,0},{7,1},{14,8},{15,9},{22,16},{23,17},{30,24},{31,25}} | collective-permute-start | bytes 835592 | tf_op jit(solution)/shard_map/ppermute | solution.py:960
  368.9 37.8 %collective-permute-start.34 = (bf16[256,2048]{1,0:T(8,128)(2,1)}, bf16[256,2048]{1,0:T(8,128)(2,1)S(1)}, u32[]{:S(2)}, u32[]{:S(2)}) collective-permute-start(bf16[256,2048]{1,0:T(8,128)(2,1)} %get-tuple-element.314), channel_id=1, source_target_pairs={{0,8},{8,16},{16,24},{24,0},{1,9},{9,17},{17,25},{25,1},{2,10},{10... | collective-permute-start | bytes 3145736 | tf_op jit(solution)/shard_map/ppermute | solution.py:1070
  370.2 36.6 %collective-permute-start.35 = (bf16[256,1280]{1,0:T(8,128)(2,1)}, bf16[256,1280]{1,0:T(8,128)(2,1)S(1)}, u32[]{:S(2)}, u32[]{:S(2)}) collective-permute-start(bf16[256,1280]{1,0:T(8,128)(2,1)} %get-tuple-element.319), channel_id=1, source_target_pairs={{0,2},{2,0},{4,6},{6,4},{1,3},{3,1},{5,7},{7,5},{8,10},{10,8},{12,... | collective-permute-start | bytes 1966088 | tf_op jit(solution)/shard_map/ppermute | solution.py:955
  370.9 35.9 %collective-permute-start.36 = (bf16[256,1280]{1,0:T(8,128)(2,1)}, bf16[256,1280]{1,0:T(8,128)(2,1)S(1)}, u32[]{:S(2)}, u32[]{:S(2)}) collective-permute-start(bf16[256,1280]{1,0:T(8,128)(2,1)} %get-tuple-element.320), channel_id=1, source_target_pairs={{0,4},{2,6},{4,0},{6,2},{1,5},{3,7},{5,1},{7,3},{8,12},{10,14},{12... | collective-permute-start | bytes 1966088 | tf_op jit(solution)/shard_map/ppermute | solution.py:955
  370.9 36.0 %collective-permute-start.37 = (bf16[256,1280]{1,0:T(8,128)(2,1)}, bf16[256,1280]{1,0:T(8,128)(2,1)S(1)}, u32[]{:S(2)}, u32[]{:S(2)}) collective-permute-start(bf16[256,1280]{1,0:T(8,128)(2,1)} %get-tuple-element.321), channel_id=1, source_target_pairs={{0,6},{2,4},{4,2},{6,0},{1,7},{3,5},{5,3},{7,1},{8,14},{10,12},{12... | collective-permute-start | bytes 1966088 | tf_op jit(solution)/shard_map/ppermute | solution.py:955
  409.1 33.9 %collective-permute-start.40 = (bf16[256,2048]{1,0:T(8,128)(2,1)S(1)}, bf16[256,2048]{1,0:T(8,128)(2,1)S(1)}, u32[]{:S(2)}, u32[]{:S(2)}) collective-permute-start(bf16[256,2048]{1,0:T(8,128)(2,1)S(1)} %add_convert_fusion.1), channel_id=1, source_target_pairs={{0,8},{8,16},{16,24},{24,0},{1,9},{9,17},{17,25},{25,1},{2,10},{10... | collective-permute-start | bytes 3145736 | tf_op jit(solution)/shard_map/ppermute | solution.py:1070
  427.8 16.9 %collective-permute-start.41 = (bf16[256,1280]{1,0:T(8,128)(2,1)}, bf16[256,1280]{1,0:T(8,128)(2,1)S(1)}, u32[]{:S(2)}, u32[]{:S(2)}) collective-permute-start(bf16[256,1280]{1,0:T(8,128)(2,1)} %get-tuple-element.340), channel_id=1, source_target_pairs={{0,2},{2,0},{4,6},{6,4},{1,3},{3,1},{5,7},{7,5},{8,10},{10,8},{12,... | collective-permute-start | bytes 1966088 | tf_op jit(solution)/shard_map/ppermute | solution.py:955
  430.3 29.6 %collective-permute-start.43 = (bf16[256,1280]{1,0:T(8,128)(2,1)}, bf16[256,1280]{1,0:T(8,128)(2,1)S(1)}, u32[]{:S(2)}, u32[]{:S(2)}) collective-permute-start(bf16[256,1280]{1,0:T(8,128)(2,1)} %get-tuple-element.342), channel_id=1, source_target_pairs={{0,6},{2,4},{4,2},{6,0},{1,7},{3,5},{5,3},{7,1},{8,14},{10,12},{12... | collective-permute-start | bytes 1966088 | tf_op jit(solution)/shard_map/ppermute | solution.py:955
  461.8 26.6 %collective-permute-start.48 = (bf16[256,2048]{1,0:T(8,128)(2,1)S(1)}, bf16[256,2048]{1,0:T(8,128)(2,1)S(1)}, u32[]{:S(2)}, u32[]{:S(2)}) collective-permute-start(bf16[256,2048]{1,0:T(8,128)(2,1)S(1)} %add_convert_fusion), channel_id=1, source_target_pairs={{0,8},{8,16},{16,24},{24,0},{1,9},{9,17},{17,25},{25,1},{2,10},{10... | collective-permute-start | bytes 3145736 | tf_op jit(solution)/shard_map/ppermute | solution.py:1070
  482.3 20.3 %collective-permute-start.49 = (bf16[64,2560]{1,0:T(8,128)(2,1)}, bf16[64,2560]{1,0:T(8,128)(2,1)S(1)}, u32[]{:S(2)}, u32[]{:S(2)}) collective-permute-start(bf16[64,2560]{1,0:T(8,128)(2,1)} %get-tuple-element.367), channel_id=1, source_target_pairs={{0,8},{8,0},{16,24},{24,16},{1,9},{9,1},{17,25},{25,17},{2,10},{10... | collective-permute-start | bytes 983048 | tf_op jit(solution)/shard_map/ppermute | solution.py:955
  483.5 20.8 %collective-permute-start.50 = (bf16[64,2560]{1,0:T(8,128)(2,1)}, bf16[64,2560]{1,0:T(8,128)(2,1)S(1)}, u32[]{:S(2)}, u32[]{:S(2)}) collective-permute-start(bf16[64,2560]{1,0:T(8,128)(2,1)} %get-tuple-element.368), channel_id=1, source_target_pairs={{0,16},{8,24},{16,0},{24,8},{1,17},{9,25},{17,1},{25,9},{2,18},{10... | collective-permute-start | bytes 983048 | tf_op jit(solution)/shard_map/ppermute | solution.py:955
  484.8 24.7 %collective-permute-start.51 = (bf16[64,2560]{1,0:T(8,128)(2,1)}, bf16[64,2560]{1,0:T(8,128)(2,1)S(1)}, u32[]{:S(2)}, u32[]{:S(2)}) collective-permute-start(bf16[64,2560]{1,0:T(8,128)(2,1)} %get-tuple-element.369), channel_id=1, source_target_pairs={{0,24},{8,16},{16,8},{24,0},{1,25},{9,17},{17,9},{25,1},{2,26},{10... | collective-permute-start | bytes 983048 | tf_op jit(solution)/shard_map/ppermute | solution.py:955
  492.9 16.7 %collective-permute-start.52 = (bf16[64,2048]{1,0:T(8,128)(2,1)}, bf16[64,2048]{1,0:T(8,128)(2,1)S(1)}, u32[]{:S(2)}, u32[]{:S(2)}) collective-permute-start(bf16[64,2048]{1,0:T(8,128)(2,1)} %get-tuple-element.373), channel_id=1, source_target_pairs={{0,2},{2,0},{4,6},{6,4},{1,3},{3,1},{5,7},{7,5},{8,10},{10,8},{12,... | collective-permute-start | bytes 786440 | tf_op jit(solution)/shard_map/ppermute | solution.py:955
  (100 other events, 1067.0 us)
Sparse Core Ops, SparseCore 0:
  11.7 100.8 all-gather.2
  115.3 74.3 all-gather.4
  261.0 96.3 reduce-scatter.1

commit v4 on v3

--- a/solution.py
+++ b/solution.py
@@ -777,7 +777,7 @@
 
 
 def back_bc_body(
-    flag, raw_ref, edge_ref, cols_ref, taps_ref, mine_ref, theirs_ref, out_ref, last_ref, prior_ref, sums_ref
+    flag, raw_ref, edge_ref, cols_ref, taps_ref, mine_ref, theirs_ref, ddt_ref, out_ref, last_ref, prior_ref, sums_ref
 ):
     size, width = raw_ref.shape
     same = same_columns(cols_ref[...], width)
@@ -785,14 +785,17 @@
     grad = mine_ref[...].astype(F32) + theirs_ref[...].astype(F32)
     zero = jnp.zeros((EDGE, width), F32)
     raw, _, sums = conv_back(ext, same, taps_ref[...], grad, [zero] * 3)
-    out_ref[...] = raw[EDGE:].astype(BF16)
+    out_ref[:, :width] = raw[EDGE:].astype(BF16)
+    out_ref[:, width:] = ddt_ref[...]
     last_ref[...] = raw[size:]
-    prior_ref[...] = raw[:EDGE]
+    prior_ref[:, :width] = raw[:EDGE]
+    prior_ref[:, width:] = jnp.zeros((EDGE, ddt_ref.shape[1]), F32)
     sums_ref[...] = jnp.concatenate(sums + [zero[:3]], axis=0)
 
 
-def back_bc(flag, raw, edge, cols, taps, mine, theirs):
+def back_bc(flag, raw, edge, cols, taps, mine, theirs, ddt):
     rows, ns = mine.shape
+    joined = ns + ddt.shape[1]
     before = edge.shape[1] // ns - 2
     ins = [
         (raw, (rows, ns), lambda i, t: (0, t[0])),
@@ -801,43 +804,46 @@
         (taps, (EDGE, ns), lambda i, t: (0, t[0])),
         (mine, mine.shape, fixed),
         (theirs, theirs.shape, fixed),
-    ]
-    outs = [((rows, ns), BF16, (rows, ns), fixed)]
-    outs += [((EDGE, ns), F32, (EDGE, ns), fixed)] * 3
+        (ddt, ddt.shape, fixed),
+    ]
+    outs = [((rows, joined), BF16, (rows, joined), fixed)]
+    outs += [((EDGE, v), F32, (EDGE, v), fixed) for v in (ns, joined, ns)]
     return call(back_bc_body, (1,), ins, outs, (), flag, name="back_bc")
 
 
 def back_low_body(
-    flag, gate_ref, x_ref, bc_ref, dt_ref, last_x, last_bc, back_ref, wg_ref, wx_ref, wb_ref, wt_ref, out_ref
+    flag, gate_ref, x_ref, small_ref, last_x, last_bc, back_ref, wg_ref, wx_ref, wb_ref, wt_ref, out_ref
 ):
+    ns = last_bc.shape[1]
+
     def product(gate, x, bc, dt):
         over = ((1,), (1,))
         total = dot(gate, wg_ref[...], over) + dot(x, wx_ref[...], over)
         return (total + dot(bc, wb_ref[...], over) + dot(dt, wt_ref[...], over)).astype(BF16)
 
-    out_ref[...] = product(gate_ref[...], x_ref[...], bc_ref[...], dt_ref[...])
+    out_ref[...] = product(gate_ref[...], x_ref[...], small_ref[:, :ns], small_ref[:, ns:])
 
     @pl.when(pl.program_id(0) == pl.num_programs(0) - 1)
     def _():
         size, width = x_ref.shape
         end = slice(size - 2 * EDGE, size)
 
-        def righted(ref, last, back):
-            kept = ref[end].astype(F32)[:EDGE]
+        def righted(value, last, back):
+            kept = value.astype(F32)[:EDGE]
             return jnp.concatenate([kept, last[...] + back], axis=0).astype(BF16)
 
-        x = righted(x_ref, last_x, back_ref[:, :width])
-        bc = righted(bc_ref, last_bc, back_ref[:, width:])
-        out_ref[end] = product(gate_ref[end], x, bc, dt_ref[end])
-
-
-def back_low(flag, dgate, dx, dbc, ddt, last_x, last_bc, back_rows, weights):
+        x = righted(x_ref[end], last_x, back_ref[:, :width])
+        bc = righted(small_ref[end, :ns], last_bc, back_ref[:, width : width + ns])
+        out_ref[end] = product(gate_ref[end], x, bc, small_ref[end, ns:])
+
+
+def back_low(flag, dgate, dx, small, last_x, last_bc, back_rows, weights):
     rows, width = dx.shape
-    ns = dbc.shape[1]
+    ns = last_bc.shape[1]
     array, first = weights["lanes"]
     model = array.shape[0]
     block = min(256, rows)
-    ins = [(v, (block, v.shape[1]), rows_at) for v in (dgate, dx, dbc, ddt)]
+    ins = [(v, (block, v.shape[1]), rows_at) for v in (dgate, dx, small)]
     ins += [(v, v.shape, fixed) for v in (last_x, last_bc, back_rows)]
     ins += [
         block_of(weights["gate"]),
@@ -1133,9 +1139,7 @@
         weights.append(dict(gate=(rest, width, 0), out=(rest, width, 1)))
         mains.append(main_piece)
 
-    hidden = seq_in[0]
-    parts = None
-    kept = []
+    params = []
     for layer in range(layers):
         gain_in = pad_rows(norm_gain[layer][None])
         taps = pad_rows(conv_x[layer])
@@ -1146,6 +1150,19 @@
         )
         skip = jnp.repeat(head_params[layer, 2], width // heads)
         rowpack = pad_rows(jnp.stack([gate_gain[layer], skip]))
+        params.append((gain_in, taps, taps_bc, head, rowpack))
+    ctx_order = (c ^ jnp.arange(places)).astype(jnp.int32)
+    ring_order = ((z - 1 - jnp.arange(shards)) % shards).astype(jnp.int32)
+    shard_order = (z ^ jnp.arange(shards)).astype(jnp.int32)
+    constants = (cols, segs, spread, gather, lower, sums, flag, ctx_order, ring_order, shard_order)
+    near, far, params, constants = tie((near, far, params, constants))
+    cols, segs, spread, gather, lower, sums, flag, ctx_order, ring_order, shard_order = constants
+
+    hidden = seq_in[0]
+    parts = None
+    kept = []
+    for layer in range(layers):
+        gain_in, taps, taps_bc, head, rowpack = params[layer]
 
         if layer > 0:
             p_tail, q_tail = parts[0][rows - EDGE :].astype(F32), parts[1][rows - EDGE :].astype(F32)
@@ -1183,9 +1200,6 @@
             )
         )
     direct = own_count % 16 == 0
-    ctx_order = (c ^ jnp.arange(places)).astype(jnp.int32)
-    ring_order = ((z - 1 - jnp.arange(shards)) % shards).astype(jnp.int32)
-    shard_order = (z ^ jnp.arange(shards)).astype(jnp.int32)
 
     def owned(full):
         return lax.psum_scatter(full, ("shard", "ctx"), scatter_dimension=0, tiled=True)
@@ -1236,12 +1250,12 @@
             moving = around(add(moving, early[1]))
             if not last_layer:
                 dbc_theirs, late_above[0] = tie((dbc_theirs, rest_above))
-        db, last_bc, prior_bc, conv_bc_rows = back_bc(
-            flag, k["raw_bc"], edge, cols, k["taps_bc"], dbc_mine, swap(dbc_theirs)
+        small, last_bc, prior_bc, conv_bc_rows = back_bc(
+            flag, k["raw_bc"], edge, cols, k["taps_bc"], dbc_mine, swap(dbc_theirs), ddt
         )
         back_rows = shifted(jnp.concatenate([prior, prior_bc], axis=1), "ctx", -1)
-        late_pair = [(k["turned"], [dx, jnp.concatenate([db, ddt], axis=1)])]
-        ahead = (k["before_turned"], [prior, jnp.pad(prior_bc, ((0, 0), (0, LANES)))])
+        late_pair = [(k["turned"], [dx, small])]
+        ahead = (k["before_turned"], [prior, prior_bc])
         if direct:
             rest = weight_grad(ctx_order, places, shards, late_pair, ahead)
             dgate, rest, back_rows = tie((dgate, rest, back_rows))
@@ -1249,7 +1263,7 @@
                 rest = near_rows(rest)
         else:
             g_rest = owned(weight_grad(ctx_order, 1, 1, late_pair, ahead)[0])
-        dlow = back_low(flag, dgate, dx, db, ddt, last, last_bc, back_rows, weights[layer])
+        dlow = back_low(flag, dgate, dx, small, last, last_bc, back_rows, weights[layer])
         if quick:
             dlow, moving = tie((dlow, moving))
             for one in early[2:-1]:
@@ -1276,6 +1290,7 @@
         partial = axis_sum(jnp.concatenate(smalls), "ctx")
     packed = axis_sum(partial, "shard").reshape(layers, EDGE, -1)
     grad_zx, grad_out, grad_small = finish(early_sums, late_sum, width)
+    packed, grad_small = tie((packed, grad_small))
     small_mine = grad_small[:, :, :ns]
     cb_mine = packed[:, :5, width : width + ns]
     cb_other, small_other = swap(cb_mine), swap(small_mine)

time: 550 us -> 548 us (level)
  local copies, waits for them, and re-layouts: 27.8 us -> 22.3 us
    ppermute x8, starting transfers between devices: 24.4 us -> 37.5 us  [swap(): return lax.ppermute(value, 'tp', [(0, 1), (1, 0)])]
    ppermute x33, starting transfers between devices: 46.6 us -> 39.5 us  [relative(): return lax.ppermute(value, axis, [(i, i ^ by) for i in range(size)])]
    unnamed x152 -> x141, local copies, waits for them, and re-layouts: 16.8 us -> 12.6 us
  transfers between devices with their start and end apart: 63 -> 63, of which waited for: 21 -> 20; matrix products, arithmetic and copies ran while one was open for 6% -> 4% of each run, Pallas kernels for 46% -> 47%
where the time goes in v4:
time: 548 us; the launch traced here: 540 us
  Pallas kernels  288 us (53%)
  starting transfers between devices  111 us (20%)
  waiting for transfers between devices  88.8 us (16%)
  local copies, waits for them, and re-layouts  22.3 us (4%)
  between operations  15.1 us (3%)
  other arithmetic  14.1 us (3%)
    pallas_call x29, Pallas kernels, call(): return made(*([scalars] if count else []) + arrays)  288 us
    ppermute x33, waiting for transfers between devices, relative(): return lax.ppermute(value, axis, [(i, i ^ by) for i in range(size)])  49.4 us
    ppermute x33, starting transfers between devices, relative(): return lax.ppermute(value, axis, [(i, i ^ by) for i in range(size)])  39.5 us
    ppermute x8, starting transfers between devices, swap(): return lax.ppermute(value, 'tp', [(0, 1), (1, 0)])  37.5 us
    ppermute x16, starting transfers between devices, shifted(): lax.ppermute(value, axis, [(i, i + by) for i in range(size) if 0 <= i + b...  29.8 us
    ppermute x8, waiting for transfers between devices, swap(): return lax.ppermute(value, 'tp', [(0, 1), (1, 0)])  15.7 us
    ppermute x16, waiting for transfers between devices, shifted(): lax.ppermute(value, axis, [(i, i + by) for i in range(size) if 0 <= i + b...  14.7 us
    unnamed x141, local copies, waits for them, and re-layouts  12.6 us
  transfers between devices with their start and end apart: 63, of which 20 were waited for; matrix products, arithmetic and copies ran while one was open for 4% of the time, Pallas kernels for 47%

profile of v4, /device:TPU:1, one launch (start us, length us, event | category | flops | bytes accessed | tf_op | source)
XLA Modules:
  0.0 539.5 jit_solution(13608465596833026548)
XLA Ops:
  36.3 9.5 %collective-permute-done.7.refs_6_ = bf16[256,384]{1,0:T(8,128)(2,1)S(1)} collective-permute-done((bf16[256,384]{1,0:T(8,128)(2,1)}, bf16[256,384]{1,0:T(8,128)(2,1)S(1)}, u32[]{:S(2)}, u32[]{:S(2)}) %collective-permute-start.7) | collective-permute-done | bytes 196640 | tf_op jit(solution)/shard_map/ppermute | solution.py:961
  45.8 5.1 collective-permute-done.5.refs_3_
  51.7 10.5 %enter.2 = (bf16[1024,1024]{1,0:T(8,128)(2,1)}, bf16[1024,1024]{1,0:T(8,128)(2,1)}, bf16[1024,1024]{1,0:T(8,128)(2,1)}, bf16[1024,256]{1,0:T(8,128)(2,1)}, f32[1...) custom-call(s32[8]{0:T(128)} %pad_add_fusion.where, bf16[256,1024]{1,0:T(8,128)(2,1)} %copy-done.8, ...), custom_call_target="tpu_custom_call" | custom-call | flops 1 | bytes 1 | tf_op jit(solution)/shard_map/enter/pallas_call | solution.py:112
  72.0 12.7 %states.2 = (bf16[8,1280]{1,0:T(8,128)(2,1)}, bf16[1024,128]{1,0:T(8,128)(2,1)}, bf16[1024,1024]{1,0:T(8,128)(2,1)}, bf16[1024,256]{1,0:T(8,128)(2,1)}, f32[1024...) custom-call(bf16[1024,1024]{1,0:T(8,128)(2,1)} %get-tuple-element.24, ...), custom_call_target="tpu_custom_call" | custom-call | flops 1 | bytes 1 | tf_op jit(solution)/shard_map/states/pallas_call | solution.py:112
  93.1 6.9 %within.2.refs_5_ = f32[1024,1024]{1,0:T(8,128)} custom-call(bf16[1024,1024]{1,0:T(8,128)(2,1)} %get-tuple-element.256.xc_ref.refs_7_.refs_4_.refs_6_, bf16[1024,256]{1,0:T(8,128)(2,1)} %get-tuple-element.257.bc_ref.refs_8_.refs_6_.refs_7_, f32[1024,128]{1,0:T(8,128)} %get-tuple-element.258.step_ref.refs_8_, ...), custom_call_target="tpu_custom_call" | custom-call | flops 1 | bytes 1 | tf_op jit(solution)/shard_map/within/pallas_call | solution.py:112
  102.9 6.4 %all-gather.3.cloned.1.call-done.refs_3_.refs_4_.refs_13_.wg_ref = bf16[1024,2048]{1,0:T(8,128)(2,1)} async-done(((bf16[64,2048]{1,0:T(8,128)(2,1)}), bf16[1024,2048]{1,0:T(8,128)(2,1)}) %all-gather.3.cloned.1.call-update) | async-done | bytes 4194320 | tf_op jit(solution)/shard_map/all_gather | solution.py:1004
  109.3 13.6 %leave.2 = (f32[1024,1024]{1,0:T(8,128)}, f32[1024,1024]{1,0:T(8,128)}, bf16[1024,1152]{1,0:T(8,128)(2,1)}, f32[128,1024]{1,0:T(8,128)}) custom-call(bf16[136,1024]{1,0:T(8,128)(2,1)} %copy-done.29, bf16[136,1024]{1,0:T(8,128)(2,1)} %copy-done.31, bf16[136,1024]{1,0:T(8,128)(2,1)} %collective-permute-done.12.refs_2_, ...), custom_call_target="tpu_custom_call" | custom-call | flops 1 | bytes 1 | tf_op jit(solution)/shard_map/leave/pallas_call | solution.py:112
  124.1 28.8 %collective-permute-start.19 = (bf16[1024,1152]{1,0:T(8,128)(2,1)}, bf16[1024,1152]{1,0:T(8,128)(2,1)S(1)}, u32[]{:S(2)}, u32[]{:S(2)}) collective-permute-start(bf16[1024,1152]{1,0:T(8,128)(2,1)} %get-tuple-element.276.refs_5_.refs_1_), channel_id=1, source_target_pairs={{0,1},{1,0},{2,3},{3,2},{4,5},{5,4},{6,7},{7,6},{8,9},{9,8},{10,11... | collective-permute-start | bytes 7077896 | tf_op jit(solution)/shard_map/ppermute | solution.py:1084
  159.6 12.2 %enter.3 = (f32[1024,1024]{1,0:T(8,128)}, bf16[1024,1024]{1,0:T(8,128)(2,1)}, bf16[1024,1024]{1,0:T(8,128)(2,1)}, bf16[1024,1024]{1,0:T(8,128)(2,1)}, bf16[1024,...) custom-call(s32[8]{0:T(128)} %pad_add_fusion.where, ...), custom_call_target="tpu_custom_call" | custom-call | flops 1 | bytes 1 | tf_op jit(solution)/shard_map/enter/pallas_call | solution.py:112
  172.4 12.7 %states.3 = (bf16[8,1280]{1,0:T(8,128)(2,1)}, bf16[1024,128]{1,0:T(8,128)(2,1)}, bf16[1024,1024]{1,0:T(8,128)(2,1)}, bf16[1024,256]{1,0:T(8,128)(2,1)}, f32[1024...) custom-call(bf16[1024,1024]{1,0:T(8,128)(2,1)} %get-tuple-element.27, ...), custom_call_target="tpu_custom_call" | custom-call | flops 1 | bytes 1 | tf_op jit(solution)/shard_map/states/pallas_call | solution.py:112
  190.5 6.8 %within.3.refs_5_ = f32[1024,1024]{1,0:T(8,128)} custom-call(bf16[1024,1024]{1,0:T(8,128)(2,1)} %get-tuple-element.289.xc_ref.refs_7_.refs_5_.refs_6_, bf16[1024,256]{1,0:T(8,128)(2,1)} %get-tuple-element.290.bc_ref.refs_8_.refs_7_, f32[1024,128]{1,0:T(8,128)} %get-tuple-element.291.step_ref.refs_8_, f32[1024,128]{1,0:T(8,128)} %get-tuple-element.292.cum_ref.refs_9_.refs_8_, ...), custom_call_target="tpu_custom_call" | custom-call | flops 1 | bytes 1 | tf_op jit(solution)/shard_map/within/pallas_call | solution.py:112
  201.2 13.7 %leave.3 = (f32[1024,1024]{1,0:T(8,128)}, f32[1024,1024]{1,0:T(8,128)}, bf16[1024,1152]{1,0:T(8,128)(2,1)}, f32[128,1024]{1,0:T(8,128)}) custom-call(bf16[136,1024]{1,0:T(8,128)(2,1)} %copy-done.32, bf16[136,1024]{1,0:T(8,128)(2,1)} %copy-done.33, bf16[136,1024]{1,0:T(8,128)(2,1)} %copy-done.34, ...), custom_call_target="tpu_custom_call" | custom-call | flops 1 | bytes 1 | tf_op jit(solution)/shard_map/leave/pallas_call | solution.py:112
  221.2 17.6 %back_gate.2 = (f32[1024,1024]{1,0:T(8,128)}, bf16[1024,1024]{1,0:T(8,128)(2,1)}, bf16[1024,1024]{1,0:T(8,128)(2,1)}, bf16[1024,1024]{1,0:T(8,128)(2,1)}, bf16[1...) custom-call(f32[1024,1024]{1,0:T(8,128)} %get-tuple-element.278.refs_0_.h_ref, ...), custom_call_target="tpu_custom_call" | custom-call | flops 1 | bytes 1 | tf_op jit(solution)/shard_map/back_gate/pallas_call | solution.py:112
  242.9 10.0 %weight_grad.4 = bf16[1024,2048]{1,0:T(8,128)(2,1)} custom-call(s32[4]{0:T(128)} %copy-done.62, bf16[1024,1024]{1,0:T(8,128)(2,1)} %get-tuple-element.304.refs_0_, bf16[1024,1024]{1,0:T(8,128)(2,1)} %get-tuple-element.307.refs_1_, bf16[1024,1024]{1,0:T(8,128)(2,1)} %get-tuple-element.334.refs_2_.gate_ref, bf16[1024,1024]{1,0:T(8,128)(2,1)} %get-tuple-element.308.refs_3_), custom_call_target="tpu_custom_call" | custom-call | flops 1 | bytes 1 | tf_op jit(solution)/shard_map/weight_grad/pallas_call | solution.py:112
  252.9 9.8 %back_within.2 = (bf16[1024,1024]{1,0:T(8,128)(2,1)}, f32[1024,128]{1,0:T(8,128)}, f32[1024,256]{1,0:T(8,128)}) custom-call(bf16[1024,1024]{1,0:T(8,128)(2,1)} %get-tuple-element.289.xc_ref.refs_7_.refs_5_.refs_6_, bf16[1024,256]{1,0:T(8,128)(2,1)} %get-tuple-element.290.bc_ref.refs_8_.refs_7_, f32[1024,128]{1,0:T(8,128)} %get-tuple-element.291.step_ref.refs_8_, ...), custom_call_target="tpu_custom_call" | custom-call | flops 1 | bytes 1 | tf_op jit(solution)/shard_map/back_within/pallas_call | solution.py:112
  263.7 23.9 %back_inter.2 = (bf16[1024,1024]{1,0:T(8,128)(2,1)}, f32[8,1024]{1,0:T(8,128)}, f32[8,1024]{1,0:T(8,128)}, bf16[1024,128]{1,0:T(8,128)(2,1)}, bf16[1024,128]{1,0...) custom-call(s32[1]{0:T(128)} %bitcast.23.flag, bf16[136,1024]{1,0:T(8,128)(2,1)} %copy-done.27, ...), custom_call_target="tpu_custom_call" | custom-call | flops 1 | bytes 1 | tf_op jit(solution)/shard_map/back_inter/pallas_call | solution.py:112
  295.8 8.4 %weight_grad.5 = (bf16[256,1280]{1,0:T(8,128)(2,1)}, bf16[256,1280]{1,0:T(8,128)(2,1)}, bf16[256,1280]{1,0:T(8,128)(2,1)}, bf16[256,1280]{1,0:T(8,128)(2,1)}) custom-call(s32[4]{0:T(128)} %copy-done.62, bf16[1024,1024]{1,0:T(8,128)(2,1)} %get-tuple-element.304.refs_0_, bf16[1024,1024]{1,0:T(8,128)(2,1)} %get-tuple-element.322.refs_1_.x_ref, ...), custom_call_target="tpu_custom_call" | custom-call | flops 1 | bytes 1 | tf_op jit(solution)/shard_map/weight_grad/pallas_call | solution.py:112
  304.8 11.4 %back_low.2.a_ref = bf16[1024,1024]{1,0:T(8,128)(2,1)} custom-call(s32[1]{0:T(128)} %bitcast.23.flag, bf16[1024,1024]{1,0:T(8,128)(2,1)} %get-tuple-element.334.refs_2_.gate_ref, bf16[1024,1024]{1,0:T(8,128)(2,1)} %get-tuple-element.322.refs_1_.x_ref, bf16[1024,256]{1,0:T(8,128)(2,1)} %get-tuple-element.326.refs_2_.small_ref, ...), custom_call_target="tpu_custom_call" | custom-call | flops 1 | bytes 1 | tf_op jit(solution)/shard_map/back_low/pallas_call | solution.py:112
  322.0 7.5 %back_norm.2 = (f32[1024,1024]{1,0:T(8,128)}, f32[8,1024]{1,0:T(8,128)}) custom-call(bf16[1024,1024]{1,0:T(8,128)(2,1)} %bitcast.63, bf16[1024,1024]{1,0:T(8,128)(2,1)} %back_low.2.a_ref, bf16[1024,1024]{1,0:T(8,128)(2,1)} %copy-done.4, f32[1024,1024]{1,0:T(8,128)} %get-tuple-element.278.refs_0_.h_ref, f32[8,1024]{1,0:T(8,128)} %pad.41.refs_7_.gain_ref), custom_call_target="tpu_custom_call" | custom-call | flops 1 | bytes 1 | tf_op jit(solution)/shard_map/back_norm/pallas_call | solution.py:112
  329.5 15.8 %back_gate.3 = (bf16[1024,1024]{1,0:T(8,128)(2,1)}, bf16[1024,1024]{1,0:T(8,128)(2,1)}, bf16[1024,1024]{1,0:T(8,128)(2,1)}, bf16[1024,1024]{1,0:T(8,128)(2,1)}, ...) custom-call(f32[1024,1024]{1,0:T(8,128)} %get-tuple-element.338.refs_0_.up_ref, ...), custom_call_target="tpu_custom_call" | custom-call | flops 1 | bytes 1 | tf_op jit(solution)/shard_map/back_gate/pallas_call | solution.py:112
  349.2 10.1 %weight_grad.6 = (bf16[256,2048]{1,0:T(8,128)(2,1)}, bf16[256,2048]{1,0:T(8,128)(2,1)}, bf16[256,2048]{1,0:T(8,128)(2,1)}, bf16[256,2048]{1,0:T(8,128)(2,1)}) custom-call(s32[4]{0:T(128)} %and_select_fusion.where, bf16[1024,1024]{1,0:T(8,128)(2,1)} %get-tuple-element.342.refs_0_, bf16[1024,1024]{1,0:T(8,128)(2,1)} %get-tuple-element.345.refs_1_, ...), custom_call_target="tpu_custom_call" | custom-call | flops 1 | bytes 1 | tf_op jit(solution)/shard_map/weight_grad/pallas_call | solution.py:112
  363.1 7.7 %collective-permute-done.33.refs_2_ = bf16[136,1024]{1,0:T(8,128)(2,1)S(1)} collective-permute-done((bf16[136,1024]{1,0:T(8,128)(2,1)}, bf16[136,1024]{1,0:T(8,128)(2,1)S(1)}, u32[]{:S(2)}, u32[]{:S(2)}) %collective-permute-start.33) | collective-permute-done | bytes 278560 | tf_op jit(solution)/shard_map/ppermute | solution.py:966
  375.2 9.8 %back_within.3 = (bf16[1024,1024]{1,0:T(8,128)(2,1)}, f32[1024,128]{1,0:T(8,128)}, f32[1024,256]{1,0:T(8,128)}) custom-call(bf16[1024,1024]{1,0:T(8,128)(2,1)} %get-tuple-element.256.xc_ref.refs_7_.refs_4_.refs_6_, bf16[1024,256]{1,0:T(8,128)(2,1)} %get-tuple-element.257.bc_ref.refs_8_.refs_6_.refs_7_, f32[1024,128]{1,0:T(8,128)} %get-tuple-element.258.step_ref.refs_8_, ...), custom_call_target="tpu_custom_call" | custom-call | flops 1 | bytes 1 | tf_op jit(solution)/shard_map/back_within/pallas_call | solution.py:112
  385.1 24.0 %back_inter.3 = (bf16[1024,1024]{1,0:T(8,128)(2,1)}, f32[8,1024]{1,0:T(8,128)}, f32[8,1024]{1,0:T(8,128)}, bf16[1024,128]{1,0:T(8,128)(2,1)}, bf16[1024,128]{1,0...) custom-call(s32[1]{0:T(128)} %bitcast.23.flag, bf16[136,1024]{1,0:T(8,128)(2,1)} %copy-done.24, ...), custom_call_target="tpu_custom_call" | custom-call | flops 1 | bytes 1 | tf_op jit(solution)/shard_map/back_inter/pallas_call | solution.py:112
  418.7 8.3 %weight_grad.7 = (bf16[256,1280]{1,0:T(8,128)(2,1)}, bf16[256,1280]{1,0:T(8,128)(2,1)}, bf16[256,1280]{1,0:T(8,128)(2,1)}, bf16[256,1280]{1,0:T(8,128)(2,1)}) custom-call(s32[4]{0:T(128)} %copy-done.62, bf16[1024,1024]{1,0:T(8,128)(2,1)} %get-tuple-element.342.refs_0_, bf16[1024,1024]{1,0:T(8,128)(2,1)} %get-tuple-element.372.refs_1_.x_ref, ...), custom_call_target="tpu_custom_call" | custom-call | flops 1 | bytes 1 | tf_op jit(solution)/shard_map/weight_grad/pallas_call | solution.py:112
  430.5 11.5 %back_low.3.a_ref = bf16[1024,1024]{1,0:T(8,128)(2,1)} custom-call(s32[1]{0:T(128)} %bitcast.23.flag, bf16[1024,1024]{1,0:T(8,128)(2,1)} %get-tuple-element.389.refs_2_.gate_ref, bf16[1024,1024]{1,0:T(8,128)(2,1)} %get-tuple-element.372.refs_1_.x_ref, bf16[1024,256]{1,0:T(8,128)(2,1)} %get-tuple-element.381.refs_2_.small_ref, ...), custom_call_target="tpu_custom_call" | custom-call | flops 1 | bytes 1 | tf_op jit(solution)/shard_map/back_low/pallas_call | solution.py:112
  445.3 13.0 %collective-permute-done.43.refs_3_ = bf16[256,1280]{1,0:T(8,128)(2,1)S(1)} collective-permute-done((bf16[256,1280]{1,0:T(8,128)(2,1)}, bf16[256,1280]{1,0:T(8,128)(2,1)S(1)}, u32[]{:S(2)}, u32[]{:S(2)}) %collective-permute-start.43) | collective-permute-done | bytes 655392 | tf_op jit(solution)/shard_map/ppermute | solution.py:961
  466.0 7.2 %back_norm.3 = (f32[1024,1024]{1,0:T(8,128)}, f32[8,1024]{1,0:T(8,128)}) custom-call(f32[1024,1024]{1,0:T(8,128)} %get-tuple-element.338.refs_0_.up_ref, bf16[1024,1024]{1,0:T(8,128)(2,1)} %back_low.3.a_ref, bf16[1024,1024]{1,0:T(8,128)(2,1)} %copy-done.3, bf16[1024,1024]{1,0:T(8,128)(2,1)} %bitcast.61, f32[8,1024]{1,0:T(8,128)} %pad.36.refs_9_.gain_ref), custom_call_target="tpu_custom_call" | custom-call | flops 1 | bytes 1 | tf_op jit(solution)/shard_map/back_norm/pallas_call | solution.py:112
  476.8 4.7 split_sum.2
  493.3 8.6 %collective-permute-done.49.refs_6_ = bf16[64,2560]{1,0:T(8,128)(2,1)S(1)} collective-permute-done((bf16[64,2560]{1,0:T(8,128)(2,1)}, bf16[64,2560]{1,0:T(8,128)(2,1)S(1)}, u32[]{:S(2)}, u32[]{:S(2)}) %collective-permute-start.49) | collective-permute-done | bytes 327712 | tf_op jit(solution)/shard_map/ppermute | solution.py:961
  502.7 6.1 %collective-permute-done.51.refs_8_ = bf16[64,2560]{1,0:T(8,128)(2,1)S(1)} collective-permute-done((bf16[64,2560]{1,0:T(8,128)(2,1)}, bf16[64,2560]{1,0:T(8,128)(2,1)S(1)}, u32[]{:S(2)}, u32[]{:S(2)}) %collective-permute-start.51) | collective-permute-done | bytes 327712 | tf_op jit(solution)/shard_map/ppermute | solution.py:961
  510.3 5.9 %collective-permute-start.55 = (f32[16,1280]{1,0:T(8,128)S(1)}, f32[16,1280]{1,0:T(8,128)S(1)}, u32[]{:S(2)}, u32[]{:S(2)}) collective-permute-start(f32[16,1280]{1,0:T(8,128)S(1)} %add_add_fusion), channel_id=1, source_target_pairs={{0,8},{8,0},{16,24},{24,16},{1,9},{9,1},{17,25},{25,17},{2,10},{10... | collective-permute-start | bytes 245768 | tf_op jit(solution)/shard_map/ppermute | solution.py:961
  (335 shorter events, 164.0 us)
Async XLA Ops:
  7.2 102.1 %all-gather.3.cloned.1.call-start = ((), (), s32[]{:S(2)}) async-start(), calls=%async_computation.1 | async-start | bytes 4456448 | tf_op jit(solution)/shard_map/all_gather | solution.py:1004
  11.6 185.7 %all-gather.5.cloned.1.call-start = ((), (), s32[]{:S(2)}) async-start(), calls=%async_computation.2 | async-start | bytes 4456448 | tf_op jit(solution)/shard_map/all_gather | solution.py:1004
  16.1 19.1 %collective-permute-start.6 = (bf16[256,384]{1,0:T(8,128)(2,1)}, bf16[256,384]{1,0:T(8,128)(2,1)S(1)}, u32[]{:S(2)}, u32[]{:S(2)}) collective-permute-start(bf16[256,384]{1,0:T(8,128)(2,1)} %get-tuple-element.236.refs_4_), channel_id=1, source_target_pairs={{0,8},{8,0},{16,24},{24,16},{1,9},{9,1},{17,25},{25,17},{2,10},{10... | collective-permute-start | bytes 589832 | tf_op jit(solution)/shard_map/ppermute | solution.py:961
  16.5 29.3 %collective-permute-start.7 = (bf16[256,384]{1,0:T(8,128)(2,1)}, bf16[256,384]{1,0:T(8,128)(2,1)S(1)}, u32[]{:S(2)}, u32[]{:S(2)}) collective-permute-start(bf16[256,384]{1,0:T(8,128)(2,1)} %get-tuple-element.236.refs_4_), channel_id=1, source_target_pairs={{0,16},{8,24},{16,0},{24,8},{1,17},{9,25},{17,1},{25,9},{2,18},{10... | collective-permute-start | bytes 589832 | tf_op jit(solution)/shard_map/ppermute | solution.py:961
  22.3 362.7 %reduce-scatter.2.cloned.1.call-start = ((), (), s32[]{:S(2)}) async-start(), calls=%async_computation.3 | async-start | bytes 4456448 | tf_op jit(solution)/shard_map/reduce_scatter | solution.py:1205
  27.2 18.5 %collective-permute-start.3 = (bf16[256,1024]{1,0:T(8,128)(2,1)S(1)}, bf16[256,1024]{1,0:T(8,128)(2,1)S(1)}, u32[]{:S(2)}, u32[]{:S(2)}) collective-permute-start(bf16[256,1024]{1,0:T(8,128)(2,1)S(1)} %constant_dynamic-update-slice_fusion.refs_0_), channel_id=1, source_target_pairs={{0,2},{2,0},{4,6},{6,4},{1,3},{3,1},{5,7},{7,5},{8,10},{10,8},{12,... | collective-permute-start | bytes 1572872 | tf_op jit(solution)/shard_map/ppermute | solution.py:961
  28.5 17.3 %collective-permute-start.4 = (bf16[256,1024]{1,0:T(8,128)(2,1)S(1)}, bf16[256,1024]{1,0:T(8,128)(2,1)S(1)}, u32[]{:S(2)}, u32[]{:S(2)}) collective-permute-start(bf16[256,1024]{1,0:T(8,128)(2,1)S(1)} %constant_dynamic-update-slice_fusion.refs_0_), channel_id=1, source_target_pairs={{0,4},{2,6},{4,0},{6,2},{1,5},{3,7},{5,1},{7,3},{8,12},{10,14},{12... | collective-permute-start | bytes 1572872 | tf_op jit(solution)/shard_map/ppermute | solution.py:961
  29.8 21.1 %collective-permute-start.5 = (bf16[256,1024]{1,0:T(8,128)(2,1)S(1)}, bf16[256,1024]{1,0:T(8,128)(2,1)S(1)}, u32[]{:S(2)}, u32[]{:S(2)}) collective-permute-start(bf16[256,1024]{1,0:T(8,128)(2,1)S(1)} %constant_dynamic-update-slice_fusion.refs_0_), channel_id=1, source_target_pairs={{0,6},{2,4},{4,2},{6,0},{1,7},{3,5},{5,3},{7,1},{8,14},{10,12},{12... | collective-permute-start | bytes 1572872 | tf_op jit(solution)/shard_map/ppermute | solution.py:961
  62.2 28.5 %collective-permute-start.13 = (bf16[64,1408]{1,0:T(8,128)(2,1)S(1)}, bf16[64,1408]{1,0:T(8,128)(2,1)S(1)}, u32[]{:S(2)}, u32[]{:S(2)}) collective-permute-start(bf16[64,1408]{1,0:T(8,128)(2,1)S(1)} %copy-done.44), channel_id=1, source_target_pairs={{0,8},{8,0},{16,24},{24,16},{1,9},{9,1},{17,25},{25,17},{2,10},{10... | collective-permute-start | bytes 540680 | tf_op jit(solution)/shard_map/ppermute | solution.py:961
  62.3 37.8 %collective-permute-start.14 = (bf16[64,1408]{1,0:T(8,128)(2,1)S(1)}, bf16[64,1408]{1,0:T(8,128)(2,1)S(1)}, u32[]{:S(2)}, u32[]{:S(2)}) collective-permute-start(bf16[64,1408]{1,0:T(8,128)(2,1)S(1)} %copy-done.44), channel_id=1, source_target_pairs={{0,16},{8,24},{16,0},{24,8},{1,17},{9,25},{17,1},{25,9},{2,18},{10... | collective-permute-start | bytes 540680 | tf_op jit(solution)/shard_map/ppermute | solution.py:961
  62.5 37.6 %collective-permute-start.15 = (bf16[64,1408]{1,0:T(8,128)(2,1)S(1)}, bf16[64,1408]{1,0:T(8,128)(2,1)S(1)}, u32[]{:S(2)}, u32[]{:S(2)}) collective-permute-start(bf16[64,1408]{1,0:T(8,128)(2,1)S(1)} %copy-done.44), channel_id=1, source_target_pairs={{0,24},{8,16},{16,8},{24,0},{1,25},{9,17},{17,9},{25,1},{2,26},{10... | collective-permute-start | bytes 540680 | tf_op jit(solution)/shard_map/ppermute | solution.py:961
  100.2 22.7 %collective-permute-start.16 = (bf16[256,1408]{1,0:T(8,128)(2,1)S(1)}, bf16[256,1408]{1,0:T(8,128)(2,1)S(1)}, u32[]{:S(2)}, u32[]{:S(2)}) collective-permute-start(bf16[256,1408]{1,0:T(8,128)(2,1)S(1)} %pad_maximum_fusion.refs_0_), channel_id=1, source_target_pairs={{0,2},{2,0},{4,6},{6,4},{1,3},{3,1},{5,7},{7,5},{8,10},{10,8},{12,... | collective-permute-start | bytes 2162696 | tf_op jit(solution)/shard_map/ppermute | solution.py:961
  100.2 22.7 %collective-permute-start.17 = (bf16[256,1408]{1,0:T(8,128)(2,1)S(1)}, bf16[256,1408]{1,0:T(8,128)(2,1)S(1)}, u32[]{:S(2)}, u32[]{:S(2)}) collective-permute-start(bf16[256,1408]{1,0:T(8,128)(2,1)S(1)} %pad_maximum_fusion.refs_0_), channel_id=1, source_target_pairs={{0,4},{2,6},{4,0},{6,2},{1,5},{3,7},{5,1},{7,3},{8,12},{10,14},{12... | collective-permute-start | bytes 2162696 | tf_op jit(solution)/shard_map/ppermute | solution.py:961
  100.3 23.8 %collective-permute-start.18 = (bf16[256,1408]{1,0:T(8,128)(2,1)S(1)}, bf16[256,1408]{1,0:T(8,128)(2,1)S(1)}, u32[]{:S(2)}, u32[]{:S(2)}) collective-permute-start(bf16[256,1408]{1,0:T(8,128)(2,1)S(1)} %pad_maximum_fusion.refs_0_), channel_id=1, source_target_pairs={{0,6},{2,4},{4,2},{6,0},{1,7},{3,5},{5,3},{7,1},{8,14},{10,12},{12... | collective-permute-start | bytes 2162696 | tf_op jit(solution)/shard_map/ppermute | solution.py:961
  124.1 33.2 %collective-permute-start.19 = (bf16[1024,1152]{1,0:T(8,128)(2,1)}, bf16[1024,1152]{1,0:T(8,128)(2,1)S(1)}, u32[]{:S(2)}, u32[]{:S(2)}) collective-permute-start(bf16[1024,1152]{1,0:T(8,128)(2,1)} %get-tuple-element.276.refs_5_.refs_1_), channel_id=1, source_target_pairs={{0,1},{1,0},{2,3},{3,2},{4,5},{5,4},{6,7},{7,6},{8,9},{9,8},{10,11... | collective-permute-start | bytes 7077896 | tf_op jit(solution)/shard_map/ppermute | solution.py:1084
  238.8 24.0 %collective-permute-start.25 = (bf16[136,1024]{1,0:T(8,128)(2,1)}, bf16[136,1024]{1,0:T(8,128)(2,1)S(1)}, u32[]{:S(2)}, u32[]{:S(2)}) collective-permute-start(bf16[136,1024]{1,0:T(8,128)(2,1)} %get-tuple-element.311), channel_id=1, source_target_pairs={{2,0},{4,2},{6,4},{3,1},{5,3},{7,5},{10,8},{12,10},{14,12},{11,9},... | collective-permute-start | bytes 835592 | tf_op jit(solution)/shard_map/ppermute | solution.py:966
  240.1 22.7 %collective-permute-start.26 = (bf16[136,1024]{1,0:T(8,128)(2,1)}, bf16[136,1024]{1,0:T(8,128)(2,1)S(1)}, u32[]{:S(2)}, u32[]{:S(2)}) collective-permute-start(bf16[136,1024]{1,0:T(8,128)(2,1)} %get-tuple-element.311), channel_id=1, source_target_pairs={{4,0},{6,2},{5,1},{7,3},{12,8},{14,10},{13,9},{15,11},{20,16},{22,... | collective-permute-start | bytes 835592 | tf_op jit(solution)/shard_map/ppermute | solution.py:966
  241.4 21.4 %collective-permute-start.27 = (bf16[136,1024]{1,0:T(8,128)(2,1)}, bf16[136,1024]{1,0:T(8,128)(2,1)S(1)}, u32[]{:S(2)}, u32[]{:S(2)}) collective-permute-start(bf16[136,1024]{1,0:T(8,128)(2,1)} %get-tuple-element.311), channel_id=1, source_target_pairs={{6,0},{7,1},{14,8},{15,9},{22,16},{23,17},{30,24},{31,25}} | collective-permute-start | bytes 835592 | tf_op jit(solution)/shard_map/ppermute | solution.py:966
  345.3 17.8 %collective-permute-start.31 = (bf16[136,1024]{1,0:T(8,128)(2,1)}, bf16[136,1024]{1,0:T(8,128)(2,1)S(1)}, u32[]{:S(2)}, u32[]{:S(2)}) collective-permute-start(bf16[136,1024]{1,0:T(8,128)(2,1)} %get-tuple-element.351), channel_id=1, source_target_pairs={{2,0},{4,2},{6,4},{3,1},{5,3},{7,5},{10,8},{12,10},{14,12},{11,9},... | collective-permute-start | bytes 835592 | tf_op jit(solution)/shard_map/ppermute | solution.py:966
  347.9 23.0 %collective-permute-start.33 = (bf16[136,1024]{1,0:T(8,128)(2,1)}, bf16[136,1024]{1,0:T(8,128)(2,1)S(1)}, u32[]{:S(2)}, u32[]{:S(2)}) collective-permute-start(bf16[136,1024]{1,0:T(8,128)(2,1)} %get-tuple-element.351), channel_id=1, source_target_pairs={{6,0},{7,1},{14,8},{15,9},{22,16},{23,17},{30,24},{31,25}} | collective-permute-start | bytes 835592 | tf_op jit(solution)/shard_map/ppermute | solution.py:966
  370.9 38.2 %collective-permute-start.34 = (bf16[256,2048]{1,0:T(8,128)(2,1)}, bf16[256,2048]{1,0:T(8,128)(2,1)S(1)}, u32[]{:S(2)}, u32[]{:S(2)}) collective-permute-start(bf16[256,2048]{1,0:T(8,128)(2,1)} %get-tuple-element.371), channel_id=1, source_target_pairs={{0,8},{8,16},{16,24},{24,0},{1,9},{9,17},{17,25},{25,1},{2,10},{10... | collective-permute-start | bytes 3145736 | tf_op jit(solution)/shard_map/ppermute | solution.py:1076
  372.5 36.6 %collective-permute-start.35 = (bf16[256,1280]{1,0:T(8,128)(2,1)}, bf16[256,1280]{1,0:T(8,128)(2,1)S(1)}, u32[]{:S(2)}, u32[]{:S(2)}) collective-permute-start(bf16[256,1280]{1,0:T(8,128)(2,1)} %get-tuple-element.376), channel_id=1, source_target_pairs={{0,2},{2,0},{4,6},{6,4},{1,3},{3,1},{5,7},{7,5},{8,10},{10,8},{12,... | collective-permute-start | bytes 1966088 | tf_op jit(solution)/shard_map/ppermute | solution.py:961
  372.5 36.6 %collective-permute-start.36 = (bf16[256,1280]{1,0:T(8,128)(2,1)}, bf16[256,1280]{1,0:T(8,128)(2,1)S(1)}, u32[]{:S(2)}, u32[]{:S(2)}) collective-permute-start(bf16[256,1280]{1,0:T(8,128)(2,1)} %get-tuple-element.377), channel_id=1, source_target_pairs={{0,4},{2,6},{4,0},{6,2},{1,5},{3,7},{5,1},{7,3},{8,12},{10,14},{12... | collective-permute-start | bytes 1966088 | tf_op jit(solution)/shard_map/ppermute | solution.py:961
  372.5 36.6 %collective-permute-start.37 = (bf16[256,1280]{1,0:T(8,128)(2,1)}, bf16[256,1280]{1,0:T(8,128)(2,1)S(1)}, u32[]{:S(2)}, u32[]{:S(2)}) collective-permute-start(bf16[256,1280]{1,0:T(8,128)(2,1)} %get-tuple-element.378), channel_id=1, source_target_pairs={{0,6},{2,4},{4,2},{6,0},{1,7},{3,5},{5,3},{7,1},{8,14},{10,12},{12... | collective-permute-start | bytes 1966088 | tf_op jit(solution)/shard_map/ppermute | solution.py:961
  411.2 30.7 %collective-permute-start.40 = (bf16[256,2048]{1,0:T(8,128)(2,1)S(1)}, bf16[256,2048]{1,0:T(8,128)(2,1)S(1)}, u32[]{:S(2)}, u32[]{:S(2)}) collective-permute-start(bf16[256,2048]{1,0:T(8,128)(2,1)S(1)} %add_convert_fusion.1), channel_id=1, source_target_pairs={{0,8},{8,16},{16,24},{24,0},{1,9},{9,17},{17,25},{25,1},{2,10},{10... | collective-permute-start | bytes 3145736 | tf_op jit(solution)/shard_map/ppermute | solution.py:1076
  427.1 16.9 %collective-permute-start.41 = (bf16[256,1280]{1,0:T(8,128)(2,1)}, bf16[256,1280]{1,0:T(8,128)(2,1)S(1)}, u32[]{:S(2)}, u32[]{:S(2)}) collective-permute-start(bf16[256,1280]{1,0:T(8,128)(2,1)} %get-tuple-element.397), channel_id=1, source_target_pairs={{0,2},{2,0},{4,6},{6,4},{1,3},{3,1},{5,7},{7,5},{8,10},{10,8},{12,... | collective-permute-start | bytes 1966088 | tf_op jit(solution)/shard_map/ppermute | solution.py:961
  429.2 29.2 %collective-permute-start.43 = (bf16[256,1280]{1,0:T(8,128)(2,1)}, bf16[256,1280]{1,0:T(8,128)(2,1)S(1)}, u32[]{:S(2)}, u32[]{:S(2)}) collective-permute-start(bf16[256,1280]{1,0:T(8,128)(2,1)} %get-tuple-element.399), channel_id=1, source_target_pairs={{0,6},{2,4},{4,2},{6,0},{1,7},{3,5},{5,3},{7,1},{8,14},{10,12},{12... | collective-permute-start | bytes 1966088 | tf_op jit(solution)/shard_map/ppermute | solution.py:961
  461.1 26.6 %collective-permute-start.48 = (bf16[256,2048]{1,0:T(8,128)(2,1)S(1)}, bf16[256,2048]{1,0:T(8,128)(2,1)S(1)}, u32[]{:S(2)}, u32[]{:S(2)}) collective-permute-start(bf16[256,2048]{1,0:T(8,128)(2,1)S(1)} %add_convert_fusion), channel_id=1, source_target_pairs={{0,8},{8,16},{16,24},{24,0},{1,9},{9,17},{17,25},{25,1},{2,10},{10... | collective-permute-start | bytes 3145736 | tf_op jit(solution)/shard_map/ppermute | solution.py:1076
  481.6 20.3 %collective-permute-start.49 = (bf16[64,2560]{1,0:T(8,128)(2,1)}, bf16[64,2560]{1,0:T(8,128)(2,1)S(1)}, u32[]{:S(2)}, u32[]{:S(2)}) collective-permute-start(bf16[64,2560]{1,0:T(8,128)(2,1)} %get-tuple-element.425), channel_id=1, source_target_pairs={{0,8},{8,0},{16,24},{24,16},{1,9},{9,1},{17,25},{25,17},{2,10},{10... | collective-permute-start | bytes 983048 | tf_op jit(solution)/shard_map/ppermute | solution.py:961
  482.8 19.9 %collective-permute-start.50 = (bf16[64,2560]{1,0:T(8,128)(2,1)}, bf16[64,2560]{1,0:T(8,128)(2,1)S(1)}, u32[]{:S(2)}, u32[]{:S(2)}) collective-permute-start(bf16[64,2560]{1,0:T(8,128)(2,1)} %get-tuple-element.426), channel_id=1, source_target_pairs={{0,16},{8,24},{16,0},{24,8},{1,17},{9,25},{17,1},{25,9},{2,18},{10... | collective-permute-start | bytes 983048 | tf_op jit(solution)/shard_map/ppermute | solution.py:961
  483.9 24.9 %collective-permute-start.51 = (bf16[64,2560]{1,0:T(8,128)(2,1)}, bf16[64,2560]{1,0:T(8,128)(2,1)S(1)}, u32[]{:S(2)}, u32[]{:S(2)}) collective-permute-start(bf16[64,2560]{1,0:T(8,128)(2,1)} %get-tuple-element.427), channel_id=1, source_target_pairs={{0,24},{8,16},{16,8},{24,0},{1,25},{9,17},{17,9},{25,1},{2,26},{10... | collective-permute-start | bytes 983048 | tf_op jit(solution)/shard_map/ppermute | solution.py:961
  492.1 16.7 %collective-permute-start.52 = (bf16[64,2048]{1,0:T(8,128)(2,1)}, bf16[64,2048]{1,0:T(8,128)(2,1)S(1)}, u32[]{:S(2)}, u32[]{:S(2)}) collective-permute-start(bf16[64,2048]{1,0:T(8,128)(2,1)} %get-tuple-element.431), channel_id=1, source_target_pairs={{0,2},{2,0},{4,6},{6,4},{1,3},{3,1},{5,7},{7,5},{8,10},{10,8},{12,... | collective-permute-start | bytes 786440 | tf_op jit(solution)/shard_map/ppermute | solution.py:961
  (99 other events, 1102.3 us)
Sparse Core Ops, SparseCore 0:
  11.7 97.5 all-gather.2
  112.1 77.0 all-gather.4
  262.9 101.3 reduce-scatter.1

commit v5 on v4

--- a/solution.py
+++ b/solution.py
@@ -1155,7 +1155,7 @@
     ring_order = ((z - 1 - jnp.arange(shards)) % shards).astype(jnp.int32)
     shard_order = (z ^ jnp.arange(shards)).astype(jnp.int32)
     constants = (cols, segs, spread, gather, lower, sums, flag, ctx_order, ring_order, shard_order)
-    near, far, params, constants = tie((near, far, params, constants))
+    near, far, before, params, constants = tie((near, far, before, params, constants))
     cols, segs, spread, gather, lower, sums, flag, ctx_order, ring_order, shard_order = constants
 
     hidden = seq_in[0]

time: 548 us -> 549 us (level)
  waiting for transfers between devices: 88.8 us -> 105 us
  starting transfers between devices: 111 us -> 95.7 us
    ppermute x8, starting transfers between devices: 37.5 us -> 11.4 us  [swap(): return lax.ppermute(value, 'tp', [(0, 1), (1, 0)])]
    ppermute x33, waiting for transfers between devices: 49.4 us -> 71.3 us  [relative(): return lax.ppermute(value, axis, [(i, i ^ by) for i in range(size)])]
    ppermute x33, starting transfers between devices: 39.5 us -> 48 us  [relative(): return lax.ppermute(value, axis, [(i, i ^ by) for i in range(size)])]
    all_gather x2, waiting for transfers between devices: 6.44 us -> 0.01 us  [gather_rows(): return lax.all_gather(piece, ('shard', 'ctx'), axis=0, tiled=True)]
  transfers between devices with their start and end apart: 63 -> 63, of which waited for: 20 -> 21; matrix products, arithmetic and copies ran while one was open for 4% -> 4% of each run, Pallas kernels for 47% -> 47%
where the time goes in v5:
time: 549 us; the launch traced here: 540 us
  Pallas kernels  288 us (52%)
  waiting for transfers between devices  105 us (19%)
  starting transfers between devices  95.7 us (17%)
  local copies, waits for them, and re-layouts  21.7 us (4%)
  between operations  15 us (3%)
  other arithmetic  14.1 us (3%)
    pallas_call x29, Pallas kernels, call(): return made(*([scalars] if count else []) + arrays)  288 us
    ppermute x33, waiting for transfers between devices, relative(): return lax.ppermute(value, axis, [(i, i ^ by) for i in range(size)])  71.3 us
    ppermute x33, starting transfers between devices, relative(): return lax.ppermute(value, axis, [(i, i ^ by) for i in range(size)])  48 us
    ppermute x16, starting transfers between devices, shifted(): lax.ppermute(value, axis, [(i, i + by) for i in range(size) if 0 <= i + b...  31.9 us
    ppermute x8, waiting for transfers between devices, swap(): return lax.ppermute(value, 'tp', [(0, 1), (1, 0)])  15.7 us
    ppermute x16, waiting for transfers between devices, shifted(): lax.ppermute(value, axis, [(i, i + by) for i in range(size) if 0 <= i + b...  15.6 us
    unnamed x141, local copies, waits for them, and re-layouts  12 us
    ppermute x8, starting transfers between devices, swap(): return lax.ppermute(value, 'tp', [(0, 1), (1, 0)])  11.4 us
  transfers between devices with their start and end apart: 63, of which 21 were waited for; matrix products, arithmetic and copies ran while one was open for 4% of the time, Pallas kernels for 47%

profile of v5, /device:TPU:1, one launch (start us, length us, event | category | flops | bytes accessed | tf_op | source)
XLA Modules:
  0.0 540.3 jit_solution(13085397428140716395)
XLA Ops:
  40.2 16.5 %collective-permute-done.7.refs_6_ = bf16[256,384]{1,0:T(8,128)(2,1)S(1)} collective-permute-done((bf16[256,384]{1,0:T(8,128)(2,1)S(1)}, bf16[256,384]{1,0:T(8,128)(2,1)S(1)}, u32[]{:S(2)}, u32[]{:S(2)}) %collective-permute-start.7) | collective-permute-done | bytes 196640 | tf_op jit(solution)/shard_map/ppermute | solution.py:961
  59.2 10.5 %enter.2 = (bf16[1024,1024]{1,0:T(8,128)(2,1)}, bf16[1024,1024]{1,0:T(8,128)(2,1)}, bf16[1024,1024]{1,0:T(8,128)(2,1)}, bf16[1024,256]{1,0:T(8,128)(2,1)}, f32[1...) custom-call(s32[8]{0:T(128)} %pad_add_fusion.where, bf16[256,1024]{1,0:T(8,128)(2,1)} %copy-done.8, ...), custom_call_target="tpu_custom_call" | custom-call | flops 1 | bytes 1 | tf_op jit(solution)/shard_map/enter/pallas_call | solution.py:112
  69.7 8.3 %collective-permute-start.13 = (bf16[64,1408]{1,0:T(8,128)(2,1)S(1)}, bf16[64,1408]{1,0:T(8,128)(2,1)S(1)}, u32[]{:S(2)}, u32[]{:S(2)}) collective-permute-start(bf16[64,1408]{1,0:T(8,128)(2,1)S(1)} %copy-done.44), channel_id=1, source_target_pairs={{0,8},{8,0},{16,24},{24,16},{1,9},{9,1},{17,25},{25,17},{2,10},{10... | collective-permute-start | bytes 540680 | tf_op jit(solution)/shard_map/ppermute | solution.py:961
  82.1 12.8 %states.2 = (bf16[8,1280]{1,0:T(8,128)(2,1)}, bf16[1024,128]{1,0:T(8,128)(2,1)}, bf16[1024,1024]{1,0:T(8,128)(2,1)}, bf16[1024,256]{1,0:T(8,128)(2,1)}, f32[1024...) custom-call(bf16[1024,1024]{1,0:T(8,128)(2,1)} %get-tuple-element.24, ...), custom_call_target="tpu_custom_call" | custom-call | flops 1 | bytes 1 | tf_op jit(solution)/shard_map/states/pallas_call | solution.py:112
  102.5 6.8 %within.2.refs_5_ = f32[1024,1024]{1,0:T(8,128)} custom-call(bf16[1024,1024]{1,0:T(8,128)(2,1)} %get-tuple-element.258.xc_ref.refs_7_.refs_4_.refs_6_, bf16[1024,256]{1,0:T(8,128)(2,1)} %get-tuple-element.259.bc_ref.refs_8_.refs_6_.refs_7_, f32[1024,128]{1,0:T(8,128)} %get-tuple-element.260.step_ref.refs_8_, ...), custom_call_target="tpu_custom_call" | custom-call | flops 1 | bytes 1 | tf_op jit(solution)/shard_map/within/pallas_call | solution.py:112
  114.9 13.6 %leave.2 = (f32[1024,1024]{1,0:T(8,128)}, f32[1024,1024]{1,0:T(8,128)}, bf16[1024,1152]{1,0:T(8,128)(2,1)}, f32[128,1024]{1,0:T(8,128)}) custom-call(bf16[136,1024]{1,0:T(8,128)(2,1)} %copy-done.29, bf16[136,1024]{1,0:T(8,128)(2,1)} %copy-done.31, bf16[136,1024]{1,0:T(8,128)(2,1)} %collective-permute-done.12.refs_2_, ...), custom_call_target="tpu_custom_call" | custom-call | flops 1 | bytes 1 | tf_op jit(solution)/shard_map/leave/pallas_call | solution.py:112
  129.5 18.6 %collective-permute-done.18.refs_3_ = bf16[256,1408]{1,0:T(8,128)(2,1)S(1)} collective-permute-done((bf16[256,1408]{1,0:T(8,128)(2,1)S(1)}, bf16[256,1408]{1,0:T(8,128)(2,1)S(1)}, u32[]{:S(2)}, u32[]{:S(2)}) %collective-permute-start.18) | collective-permute-done | bytes 720928 | tf_op jit(solution)/shard_map/ppermute | solution.py:961
  159.2 12.6 %enter.3 = (f32[1024,1024]{1,0:T(8,128)}, bf16[1024,1024]{1,0:T(8,128)(2,1)}, bf16[1024,1024]{1,0:T(8,128)(2,1)}, bf16[1024,1024]{1,0:T(8,128)(2,1)}, bf16[1024,...) custom-call(s32[8]{0:T(128)} %pad_add_fusion.where, ...), custom_call_target="tpu_custom_call" | custom-call | flops 1 | bytes 1 | tf_op jit(solution)/shard_map/enter/pallas_call | solution.py:112
  172.4 12.8 %states.3 = (bf16[8,1280]{1,0:T(8,128)(2,1)}, bf16[1024,128]{1,0:T(8,128)(2,1)}, bf16[1024,1024]{1,0:T(8,128)(2,1)}, bf16[1024,256]{1,0:T(8,128)(2,1)}, f32[1024...) custom-call(bf16[1024,1024]{1,0:T(8,128)(2,1)} %get-tuple-element.28, ...), custom_call_target="tpu_custom_call" | custom-call | flops 1 | bytes 1 | tf_op jit(solution)/shard_map/states/pallas_call | solution.py:112
  192.3 6.8 %within.3.refs_5_ = f32[1024,1024]{1,0:T(8,128)} custom-call(bf16[1024,1024]{1,0:T(8,128)(2,1)} %get-tuple-element.291.xc_ref.refs_7_.refs_5_.refs_6_, bf16[1024,256]{1,0:T(8,128)(2,1)} %get-tuple-element.292.bc_ref.refs_8_.refs_7_, f32[1024,128]{1,0:T(8,128)} %get-tuple-element.293.step_ref.refs_8_, f32[1024,128]{1,0:T(8,128)} %get-tuple-element.294.cum_ref.refs_9_.refs_8_, ...), custom_call_target="tpu_custom_call" | custom-call | flops 1 | bytes 1 | tf_op jit(solution)/shard_map/within/pallas_call | solution.py:112
  203.2 13.7 %leave.3 = (f32[1024,1024]{1,0:T(8,128)}, f32[1024,1024]{1,0:T(8,128)}, bf16[1024,1152]{1,0:T(8,128)(2,1)}, f32[128,1024]{1,0:T(8,128)}) custom-call(bf16[136,1024]{1,0:T(8,128)(2,1)} %copy-done.32, bf16[136,1024]{1,0:T(8,128)(2,1)} %copy-done.33, bf16[136,1024]{1,0:T(8,128)(2,1)} %copy-done.34, ...), custom_call_target="tpu_custom_call" | custom-call | flops 1 | bytes 1 | tf_op jit(solution)/shard_map/leave/pallas_call | solution.py:112
  217.4 4.4 collective-permute-done.24.refs_3_
  223.2 17.6 %back_gate.2 = (f32[1024,1024]{1,0:T(8,128)}, bf16[1024,1024]{1,0:T(8,128)(2,1)}, bf16[1024,1024]{1,0:T(8,128)(2,1)}, bf16[1024,1024]{1,0:T(8,128)(2,1)}, bf16[1...) custom-call(f32[1024,1024]{1,0:T(8,128)} %get-tuple-element.280.refs_0_.h_ref, ...), custom_call_target="tpu_custom_call" | custom-call | flops 1 | bytes 1 | tf_op jit(solution)/shard_map/back_gate/pallas_call | solution.py:112
  244.9 10.0 %weight_grad.4 = bf16[1024,2048]{1,0:T(8,128)(2,1)} custom-call(s32[4]{0:T(128)} %copy-done.62, bf16[1024,1024]{1,0:T(8,128)(2,1)} %get-tuple-element.306.refs_0_, bf16[1024,1024]{1,0:T(8,128)(2,1)} %get-tuple-element.309.refs_1_, bf16[1024,1024]{1,0:T(8,128)(2,1)} %get-tuple-element.336.refs_2_.gate_ref, bf16[1024,1024]{1,0:T(8,128)(2,1)} %get-tuple-element.310.refs_3_), custom_call_target="tpu_custom_call" | custom-call | flops 1 | bytes 1 | tf_op jit(solution)/shard_map/weight_grad/pallas_call | solution.py:112
  254.9 9.8 %back_within.2 = (bf16[1024,1024]{1,0:T(8,128)(2,1)}, f32[1024,128]{1,0:T(8,128)}, f32[1024,256]{1,0:T(8,128)}) custom-call(bf16[1024,1024]{1,0:T(8,128)(2,1)} %get-tuple-element.291.xc_ref.refs_7_.refs_5_.refs_6_, bf16[1024,256]{1,0:T(8,128)(2,1)} %get-tuple-element.292.bc_ref.refs_8_.refs_7_, f32[1024,128]{1,0:T(8,128)} %get-tuple-element.293.step_ref.refs_8_, ...), custom_call_target="tpu_custom_call" | custom-call | flops 1 | bytes 1 | tf_op jit(solution)/shard_map/back_within/pallas_call | solution.py:112
  265.8 23.9 %back_inter.2 = (bf16[1024,1024]{1,0:T(8,128)(2,1)}, f32[8,1024]{1,0:T(8,128)}, f32[8,1024]{1,0:T(8,128)}, bf16[1024,128]{1,0:T(8,128)(2,1)}, bf16[1024,128]{1,0...) custom-call(s32[1]{0:T(128)} %bitcast.24.flag, bf16[136,1024]{1,0:T(8,128)(2,1)} %copy-done.27, ...), custom_call_target="tpu_custom_call" | custom-call | flops 1 | bytes 1 | tf_op jit(solution)/shard_map/back_inter/pallas_call | solution.py:112
  297.8 8.4 %weight_grad.5 = (bf16[256,1280]{1,0:T(8,128)(2,1)}, bf16[256,1280]{1,0:T(8,128)(2,1)}, bf16[256,1280]{1,0:T(8,128)(2,1)}, bf16[256,1280]{1,0:T(8,128)(2,1)}) custom-call(s32[4]{0:T(128)} %copy-done.62, bf16[1024,1024]{1,0:T(8,128)(2,1)} %get-tuple-element.306.refs_0_, bf16[1024,1024]{1,0:T(8,128)(2,1)} %get-tuple-element.324.refs_1_.x_ref, ...), custom_call_target="tpu_custom_call" | custom-call | flops 1 | bytes 1 | tf_op jit(solution)/shard_map/weight_grad/pallas_call | solution.py:112
  306.8 11.4 %back_low.2.a_ref = bf16[1024,1024]{1,0:T(8,128)(2,1)} custom-call(s32[1]{0:T(128)} %bitcast.24.flag, bf16[1024,1024]{1,0:T(8,128)(2,1)} %get-tuple-element.336.refs_2_.gate_ref, bf16[1024,1024]{1,0:T(8,128)(2,1)} %get-tuple-element.324.refs_1_.x_ref, bf16[1024,256]{1,0:T(8,128)(2,1)} %get-tuple-element.328.refs_2_.small_ref, ...), custom_call_target="tpu_custom_call" | custom-call | flops 1 | bytes 1 | tf_op jit(solution)/shard_map/back_low/pallas_call | solution.py:112
  324.0 7.5 %back_norm.2 = (f32[1024,1024]{1,0:T(8,128)}, f32[8,1024]{1,0:T(8,128)}) custom-call(bf16[1024,1024]{1,0:T(8,128)(2,1)} %bitcast.63, bf16[1024,1024]{1,0:T(8,128)(2,1)} %back_low.2.a_ref, bf16[1024,1024]{1,0:T(8,128)(2,1)} %copy-done.4, f32[1024,1024]{1,0:T(8,128)} %get-tuple-element.280.refs_0_.h_ref, f32[8,1024]{1,0:T(8,128)} %pad.41.refs_7_.gain_ref), custom_call_target="tpu_custom_call" | custom-call | flops 1 | bytes 1 | tf_op jit(solution)/shard_map/back_norm/pallas_call | solution.py:112
  331.5 15.9 %back_gate.3 = (bf16[1024,1024]{1,0:T(8,128)(2,1)}, bf16[1024,1024]{1,0:T(8,128)(2,1)}, bf16[1024,1024]{1,0:T(8,128)(2,1)}, bf16[1024,1024]{1,0:T(8,128)(2,1)}, ...) custom-call(f32[1024,1024]{1,0:T(8,128)} %get-tuple-element.340.refs_0_.up_ref, ...), custom_call_target="tpu_custom_call" | custom-call | flops 1 | bytes 1 | tf_op jit(solution)/shard_map/back_gate/pallas_call | solution.py:112
  351.3 10.1 %weight_grad.6 = (bf16[256,2048]{1,0:T(8,128)(2,1)}, bf16[256,2048]{1,0:T(8,128)(2,1)}, bf16[256,2048]{1,0:T(8,128)(2,1)}, bf16[256,2048]{1,0:T(8,128)(2,1)}) custom-call(s32[4]{0:T(128)} %and_select_fusion.where, bf16[1024,1024]{1,0:T(8,128)(2,1)} %get-tuple-element.344.refs_0_, bf16[1024,1024]{1,0:T(8,128)(2,1)} %get-tuple-element.347.refs_1_, ...), custom_call_target="tpu_custom_call" | custom-call | flops 1 | bytes 1 | tf_op jit(solution)/shard_map/weight_grad/pallas_call | solution.py:112
  364.8 6.9 %collective-permute-done.33.refs_2_ = bf16[136,1024]{1,0:T(8,128)(2,1)S(1)} collective-permute-done((bf16[136,1024]{1,0:T(8,128)(2,1)}, bf16[136,1024]{1,0:T(8,128)(2,1)S(1)}, u32[]{:S(2)}, u32[]{:S(2)}) %collective-permute-start.33) | collective-permute-done | bytes 278560 | tf_op jit(solution)/shard_map/ppermute | solution.py:966
  376.1 9.8 %back_within.3 = (bf16[1024,1024]{1,0:T(8,128)(2,1)}, f32[1024,128]{1,0:T(8,128)}, f32[1024,256]{1,0:T(8,128)}) custom-call(bf16[1024,1024]{1,0:T(8,128)(2,1)} %get-tuple-element.258.xc_ref.refs_7_.refs_4_.refs_6_, bf16[1024,256]{1,0:T(8,128)(2,1)} %get-tuple-element.259.bc_ref.refs_8_.refs_6_.refs_7_, f32[1024,128]{1,0:T(8,128)} %get-tuple-element.260.step_ref.refs_8_, ...), custom_call_target="tpu_custom_call" | custom-call | flops 1 | bytes 1 | tf_op jit(solution)/shard_map/back_within/pallas_call | solution.py:112
  386.0 24.0 %back_inter.3 = (bf16[1024,1024]{1,0:T(8,128)(2,1)}, f32[8,1024]{1,0:T(8,128)}, f32[8,1024]{1,0:T(8,128)}, bf16[1024,128]{1,0:T(8,128)(2,1)}, bf16[1024,128]{1,0...) custom-call(s32[1]{0:T(128)} %bitcast.24.flag, bf16[136,1024]{1,0:T(8,128)(2,1)} %copy-done.24, ...), custom_call_target="tpu_custom_call" | custom-call | flops 1 | bytes 1 | tf_op jit(solution)/shard_map/back_inter/pallas_call | solution.py:112
  419.5 8.3 %weight_grad.7 = (bf16[256,1280]{1,0:T(8,128)(2,1)}, bf16[256,1280]{1,0:T(8,128)(2,1)}, bf16[256,1280]{1,0:T(8,128)(2,1)}, bf16[256,1280]{1,0:T(8,128)(2,1)}) custom-call(s32[4]{0:T(128)} %copy-done.62, bf16[1024,1024]{1,0:T(8,128)(2,1)} %get-tuple-element.344.refs_0_, bf16[1024,1024]{1,0:T(8,128)(2,1)} %get-tuple-element.374.refs_1_.x_ref, ...), custom_call_target="tpu_custom_call" | custom-call | flops 1 | bytes 1 | tf_op jit(solution)/shard_map/weight_grad/pallas_call | solution.py:112
  431.3 11.5 %back_low.3.a_ref = bf16[1024,1024]{1,0:T(8,128)(2,1)} custom-call(s32[1]{0:T(128)} %bitcast.24.flag, bf16[1024,1024]{1,0:T(8,128)(2,1)} %get-tuple-element.391.refs_2_.gate_ref, bf16[1024,1024]{1,0:T(8,128)(2,1)} %get-tuple-element.374.refs_1_.x_ref, bf16[1024,256]{1,0:T(8,128)(2,1)} %get-tuple-element.383.refs_2_.small_ref, ...), custom_call_target="tpu_custom_call" | custom-call | flops 1 | bytes 1 | tf_op jit(solution)/shard_map/back_low/pallas_call | solution.py:112
  446.1 13.0 %collective-permute-done.43.refs_3_ = bf16[256,1280]{1,0:T(8,128)(2,1)S(1)} collective-permute-done((bf16[256,1280]{1,0:T(8,128)(2,1)}, bf16[256,1280]{1,0:T(8,128)(2,1)S(1)}, u32[]{:S(2)}, u32[]{:S(2)}) %collective-permute-start.43) | collective-permute-done | bytes 655392 | tf_op jit(solution)/shard_map/ppermute | solution.py:961
  466.8 7.2 %back_norm.3 = (f32[1024,1024]{1,0:T(8,128)}, f32[8,1024]{1,0:T(8,128)}) custom-call(f32[1024,1024]{1,0:T(8,128)} %get-tuple-element.340.refs_0_.up_ref, bf16[1024,1024]{1,0:T(8,128)(2,1)} %back_low.3.a_ref, bf16[1024,1024]{1,0:T(8,128)(2,1)} %copy-done.3, bf16[1024,1024]{1,0:T(8,128)(2,1)} %bitcast.61, f32[8,1024]{1,0:T(8,128)} %pad.36.refs_9_.gain_ref), custom_call_target="tpu_custom_call" | custom-call | flops 1 | bytes 1 | tf_op jit(solution)/shard_map/back_norm/pallas_call | solution.py:112
  477.6 4.7 split_sum.2
  494.1 8.6 %collective-permute-done.49.refs_6_ = bf16[64,2560]{1,0:T(8,128)(2,1)S(1)} collective-permute-done((bf16[64,2560]{1,0:T(8,128)(2,1)}, bf16[64,2560]{1,0:T(8,128)(2,1)S(1)}, u32[]{:S(2)}, u32[]{:S(2)}) %collective-permute-start.49) | collective-permute-done | bytes 327712 | tf_op jit(solution)/shard_map/ppermute | solution.py:961
  503.5 6.1 %collective-permute-done.51.refs_8_ = bf16[64,2560]{1,0:T(8,128)(2,1)S(1)} collective-permute-done((bf16[64,2560]{1,0:T(8,128)(2,1)}, bf16[64,2560]{1,0:T(8,128)(2,1)S(1)}, u32[]{:S(2)}, u32[]{:S(2)}) %collective-permute-start.51) | collective-permute-done | bytes 327712 | tf_op jit(solution)/shard_map/ppermute | solution.py:961
  511.1 5.9 %collective-permute-start.55 = (f32[16,1280]{1,0:T(8,128)S(1)}, f32[16,1280]{1,0:T(8,128)S(1)}, u32[]{:S(2)}, u32[]{:S(2)}) collective-permute-start(f32[16,1280]{1,0:T(8,128)S(1)} %add_add_fusion), channel_id=1, source_target_pairs={{0,8},{8,0},{16,24},{24,16},{1,9},{9,1},{17,25},{25,17},{2,10},{10... | collective-permute-start | bytes 245768 | tf_op jit(solution)/shard_map/ppermute | solution.py:961
  (335 shorter events, 167.3 us)
Async XLA Ops:
  7.2 107.8 %all-gather.3.cloned.1.call-start = ((), (), s32[]{:S(2)}) async-start(), calls=%async_computation.1 | async-start | bytes 4456448 | tf_op jit(solution)/shard_map/all_gather | solution.py:1004
  11.6 187.6 %all-gather.5.cloned.1.call-start = ((), (), s32[]{:S(2)}) async-start(), calls=%async_computation.2 | async-start | bytes 4456448 | tf_op jit(solution)/shard_map/all_gather | solution.py:1004
  16.1 23.2 %collective-permute-start.6 = (bf16[256,384]{1,0:T(8,128)(2,1)}, bf16[256,384]{1,0:T(8,128)(2,1)S(1)}, u32[]{:S(2)}, u32[]{:S(2)}) collective-permute-start(bf16[256,384]{1,0:T(8,128)(2,1)} %get-tuple-element.237.refs_4_), channel_id=1, source_target_pairs={{0,8},{8,0},{16,24},{24,16},{1,9},{9,1},{17,25},{25,17},{2,10},{10... | collective-permute-start | bytes 589832 | tf_op jit(solution)/shard_map/ppermute | solution.py:961
  17.2 18.8 %collective-permute-start.9 = (bf16[8,1024]{1,0:T(8,128)(2,1)S(1)}, bf16[8,1024]{1,0:T(8,128)(2,1)S(1)}, u32[]{:S(2)}, u32[]{:S(2)}) collective-permute-start(bf16[8,1024]{1,0:T(8,128)(2,1)S(1)} %slice_bitcast_fusion), channel_id=1, source_target_pairs={{0,2},{2,4},{4,6},{1,3},{3,5},{5,7},{8,10},{10,12},{12,14},{9,11},... | collective-permute-start | bytes 49160 | tf_op jit(solution)/shard_map/ppermute | solution.py:966
  23.1 362.9 %reduce-scatter.2.cloned.1.call-start = ((), (), s32[]{:S(2)}) async-start(), calls=%async_computation.3 | async-start | bytes 4456448 | tf_op jit(solution)/shard_map/reduce_scatter | solution.py:1205
  28.3 28.4 %collective-permute-start.3 = (bf16[256,1024]{1,0:T(8,128)(2,1)S(1)}, bf16[256,1024]{1,0:T(8,128)(2,1)S(1)}, u32[]{:S(2)}, u32[]{:S(2)}) collective-permute-start(bf16[256,1024]{1,0:T(8,128)(2,1)S(1)} %constant_dynamic-update-slice_fusion.refs_0_), channel_id=1, source_target_pairs={{0,2},{2,0},{4,6},{6,4},{1,3},{3,1},{5,7},{7,5},{8,10},{10,8},{12,... | collective-permute-start | bytes 1572872 | tf_op jit(solution)/shard_map/ppermute | solution.py:961
  29.6 27.1 %collective-permute-start.4 = (bf16[256,1024]{1,0:T(8,128)(2,1)S(1)}, bf16[256,1024]{1,0:T(8,128)(2,1)S(1)}, u32[]{:S(2)}, u32[]{:S(2)}) collective-permute-start(bf16[256,1024]{1,0:T(8,128)(2,1)S(1)} %constant_dynamic-update-slice_fusion.refs_0_), channel_id=1, source_target_pairs={{0,4},{2,6},{4,0},{6,2},{1,5},{3,7},{5,1},{7,3},{8,12},{10,14},{12... | collective-permute-start | bytes 1572872 | tf_op jit(solution)/shard_map/ppermute | solution.py:961
  29.7 28.6 %collective-permute-start.5 = (bf16[256,1024]{1,0:T(8,128)(2,1)S(1)}, bf16[256,1024]{1,0:T(8,128)(2,1)S(1)}, u32[]{:S(2)}, u32[]{:S(2)}) collective-permute-start(bf16[256,1024]{1,0:T(8,128)(2,1)S(1)} %constant_dynamic-update-slice_fusion.refs_0_), channel_id=1, source_target_pairs={{0,6},{2,4},{4,2},{6,0},{1,7},{3,5},{5,3},{7,1},{8,14},{10,12},{12... | collective-permute-start | bytes 1572872 | tf_op jit(solution)/shard_map/ppermute | solution.py:961
  36.0 20.7 %collective-permute-start.7 = (bf16[256,384]{1,0:T(8,128)(2,1)S(1)}, bf16[256,384]{1,0:T(8,128)(2,1)S(1)}, u32[]{:S(2)}, u32[]{:S(2)}) collective-permute-start(bf16[256,384]{1,0:T(8,128)(2,1)S(1)} %copy-done.40), channel_id=1, source_target_pairs={{0,16},{8,24},{16,0},{24,8},{1,17},{9,25},{17,1},{25,9},{2,18},{10... | collective-permute-start | bytes 589832 | tf_op jit(solution)/shard_map/ppermute | solution.py:961
  39.3 17.4 %collective-permute-start.8 = (bf16[256,384]{1,0:T(8,128)(2,1)S(1)}, bf16[256,384]{1,0:T(8,128)(2,1)S(1)}, u32[]{:S(2)}, u32[]{:S(2)}) collective-permute-start(bf16[256,384]{1,0:T(8,128)(2,1)S(1)} %copy-done.40), channel_id=1, source_target_pairs={{0,24},{8,16},{16,8},{24,0},{1,25},{9,17},{17,9},{25,1},{2,26},{10... | collective-permute-start | bytes 589832 | tf_op jit(solution)/shard_map/ppermute | solution.py:961
  69.7 30.3 %collective-permute-start.13 = (bf16[64,1408]{1,0:T(8,128)(2,1)S(1)}, bf16[64,1408]{1,0:T(8,128)(2,1)S(1)}, u32[]{:S(2)}, u32[]{:S(2)}) collective-permute-start(bf16[64,1408]{1,0:T(8,128)(2,1)S(1)} %copy-done.44), channel_id=1, source_target_pairs={{0,8},{8,0},{16,24},{24,16},{1,9},{9,1},{17,25},{25,17},{2,10},{10... | collective-permute-start | bytes 540680 | tf_op jit(solution)/shard_map/ppermute | solution.py:961
  78.0 31.3 %collective-permute-start.14 = (bf16[64,1408]{1,0:T(8,128)(2,1)S(1)}, bf16[64,1408]{1,0:T(8,128)(2,1)S(1)}, u32[]{:S(2)}, u32[]{:S(2)}) collective-permute-start(bf16[64,1408]{1,0:T(8,128)(2,1)S(1)} %copy-done.44), channel_id=1, source_target_pairs={{0,16},{8,24},{16,0},{24,8},{1,17},{9,25},{17,1},{25,9},{2,18},{10... | collective-permute-start | bytes 540680 | tf_op jit(solution)/shard_map/ppermute | solution.py:961
  80.0 29.4 %collective-permute-start.15 = (bf16[64,1408]{1,0:T(8,128)(2,1)S(1)}, bf16[64,1408]{1,0:T(8,128)(2,1)S(1)}, u32[]{:S(2)}, u32[]{:S(2)}) collective-permute-start(bf16[64,1408]{1,0:T(8,128)(2,1)S(1)} %copy-done.44), channel_id=1, source_target_pairs={{0,24},{8,16},{16,8},{24,0},{1,25},{9,17},{17,9},{25,1},{2,26},{10... | collective-permute-start | bytes 540680 | tf_op jit(solution)/shard_map/ppermute | solution.py:961
  111.5 17.0 %collective-permute-start.16 = (bf16[256,1408]{1,0:T(8,128)(2,1)S(1)}, bf16[256,1408]{1,0:T(8,128)(2,1)S(1)}, u32[]{:S(2)}, u32[]{:S(2)}) collective-permute-start(bf16[256,1408]{1,0:T(8,128)(2,1)S(1)} %pad_maximum_fusion.refs_0_), channel_id=1, source_target_pairs={{0,2},{2,0},{4,6},{6,4},{1,3},{3,1},{5,7},{7,5},{8,10},{10,8},{12,... | collective-permute-start | bytes 2162696 | tf_op jit(solution)/shard_map/ppermute | solution.py:961
  111.5 17.9 %collective-permute-start.17 = (bf16[256,1408]{1,0:T(8,128)(2,1)S(1)}, bf16[256,1408]{1,0:T(8,128)(2,1)S(1)}, u32[]{:S(2)}, u32[]{:S(2)}) collective-permute-start(bf16[256,1408]{1,0:T(8,128)(2,1)S(1)} %pad_maximum_fusion.refs_0_), channel_id=1, source_target_pairs={{0,4},{2,6},{4,0},{6,2},{1,5},{3,7},{5,1},{7,3},{8,12},{10,14},{12... | collective-permute-start | bytes 2162696 | tf_op jit(solution)/shard_map/ppermute | solution.py:961
  113.8 34.3 %collective-permute-start.18 = (bf16[256,1408]{1,0:T(8,128)(2,1)S(1)}, bf16[256,1408]{1,0:T(8,128)(2,1)S(1)}, u32[]{:S(2)}, u32[]{:S(2)}) collective-permute-start(bf16[256,1408]{1,0:T(8,128)(2,1)S(1)} %pad_maximum_fusion.refs_0_), channel_id=1, source_target_pairs={{0,6},{2,4},{4,2},{6,0},{1,7},{3,5},{5,3},{7,1},{8,14},{10,12},{12... | collective-permute-start | bytes 2162696 | tf_op jit(solution)/shard_map/ppermute | solution.py:961
  240.8 24.0 %collective-permute-start.25 = (bf16[136,1024]{1,0:T(8,128)(2,1)}, bf16[136,1024]{1,0:T(8,128)(2,1)S(1)}, u32[]{:S(2)}, u32[]{:S(2)}) collective-permute-start(bf16[136,1024]{1,0:T(8,128)(2,1)} %get-tuple-element.313), channel_id=1, source_target_pairs={{2,0},{4,2},{6,4},{3,1},{5,3},{7,5},{10,8},{12,10},{14,12},{11,9},... | collective-permute-start | bytes 835592 | tf_op jit(solution)/shard_map/ppermute | solution.py:966
  242.1 22.7 %collective-permute-start.26 = (bf16[136,1024]{1,0:T(8,128)(2,1)}, bf16[136,1024]{1,0:T(8,128)(2,1)S(1)}, u32[]{:S(2)}, u32[]{:S(2)}) collective-permute-start(bf16[136,1024]{1,0:T(8,128)(2,1)} %get-tuple-element.313), channel_id=1, source_target_pairs={{4,0},{6,2},{5,1},{7,3},{12,8},{14,10},{13,9},{15,11},{20,16},{22,... | collective-permute-start | bytes 835592 | tf_op jit(solution)/shard_map/ppermute | solution.py:966
  243.4 21.4 %collective-permute-start.27 = (bf16[136,1024]{1,0:T(8,128)(2,1)}, bf16[136,1024]{1,0:T(8,128)(2,1)S(1)}, u32[]{:S(2)}, u32[]{:S(2)}) collective-permute-start(bf16[136,1024]{1,0:T(8,128)(2,1)} %get-tuple-element.313), channel_id=1, source_target_pairs={{6,0},{7,1},{14,8},{15,9},{22,16},{23,17},{30,24},{31,25}} | collective-permute-start | bytes 835592 | tf_op jit(solution)/shard_map/ppermute | solution.py:966
  347.4 17.4 %collective-permute-start.31 = (bf16[136,1024]{1,0:T(8,128)(2,1)}, bf16[136,1024]{1,0:T(8,128)(2,1)S(1)}, u32[]{:S(2)}, u32[]{:S(2)}) collective-permute-start(bf16[136,1024]{1,0:T(8,128)(2,1)} %get-tuple-element.353), channel_id=1, source_target_pairs={{2,0},{4,2},{6,4},{3,1},{5,3},{7,5},{10,8},{12,10},{14,12},{11,9},... | collective-permute-start | bytes 835592 | tf_op jit(solution)/shard_map/ppermute | solution.py:966
  350.0 21.6 %collective-permute-start.33 = (bf16[136,1024]{1,0:T(8,128)(2,1)}, bf16[136,1024]{1,0:T(8,128)(2,1)S(1)}, u32[]{:S(2)}, u32[]{:S(2)}) collective-permute-start(bf16[136,1024]{1,0:T(8,128)(2,1)} %get-tuple-element.353), channel_id=1, source_target_pairs={{6,0},{7,1},{14,8},{15,9},{22,16},{23,17},{30,24},{31,25}} | collective-permute-start | bytes 835592 | tf_op jit(solution)/shard_map/ppermute | solution.py:966
  371.6 38.3 %collective-permute-start.34 = (bf16[256,2048]{1,0:T(8,128)(2,1)}, bf16[256,2048]{1,0:T(8,128)(2,1)S(1)}, u32[]{:S(2)}, u32[]{:S(2)}) collective-permute-start(bf16[256,2048]{1,0:T(8,128)(2,1)} %get-tuple-element.373), channel_id=1, source_target_pairs={{0,8},{8,16},{16,24},{24,0},{1,9},{9,17},{17,25},{25,1},{2,10},{10... | collective-permute-start | bytes 3145736 | tf_op jit(solution)/shard_map/ppermute | solution.py:1076
  373.4 36.6 %collective-permute-start.35 = (bf16[256,1280]{1,0:T(8,128)(2,1)}, bf16[256,1280]{1,0:T(8,128)(2,1)S(1)}, u32[]{:S(2)}, u32[]{:S(2)}) collective-permute-start(bf16[256,1280]{1,0:T(8,128)(2,1)} %get-tuple-element.378), channel_id=1, source_target_pairs={{0,2},{2,0},{4,6},{6,4},{1,3},{3,1},{5,7},{7,5},{8,10},{10,8},{12,... | collective-permute-start | bytes 1966088 | tf_op jit(solution)/shard_map/ppermute | solution.py:961
  373.4 36.6 %collective-permute-start.36 = (bf16[256,1280]{1,0:T(8,128)(2,1)}, bf16[256,1280]{1,0:T(8,128)(2,1)S(1)}, u32[]{:S(2)}, u32[]{:S(2)}) collective-permute-start(bf16[256,1280]{1,0:T(8,128)(2,1)} %get-tuple-element.379), channel_id=1, source_target_pairs={{0,4},{2,6},{4,0},{6,2},{1,5},{3,7},{5,1},{7,3},{8,12},{10,14},{12... | collective-permute-start | bytes 1966088 | tf_op jit(solution)/shard_map/ppermute | solution.py:961
  373.4 36.6 %collective-permute-start.37 = (bf16[256,1280]{1,0:T(8,128)(2,1)}, bf16[256,1280]{1,0:T(8,128)(2,1)S(1)}, u32[]{:S(2)}, u32[]{:S(2)}) collective-permute-start(bf16[256,1280]{1,0:T(8,128)(2,1)} %get-tuple-element.380), channel_id=1, source_target_pairs={{0,6},{2,4},{4,2},{6,0},{1,7},{3,5},{5,3},{7,1},{8,14},{10,12},{12... | collective-permute-start | bytes 1966088 | tf_op jit(solution)/shard_map/ppermute | solution.py:961
  412.1 30.7 %collective-permute-start.40 = (bf16[256,2048]{1,0:T(8,128)(2,1)S(1)}, bf16[256,2048]{1,0:T(8,128)(2,1)S(1)}, u32[]{:S(2)}, u32[]{:S(2)}) collective-permute-start(bf16[256,2048]{1,0:T(8,128)(2,1)S(1)} %add_convert_fusion.1), channel_id=1, source_target_pairs={{0,8},{8,16},{16,24},{24,0},{1,9},{9,17},{17,25},{25,1},{2,10},{10... | collective-permute-start | bytes 3145736 | tf_op jit(solution)/shard_map/ppermute | solution.py:1076
  427.9 16.9 %collective-permute-start.41 = (bf16[256,1280]{1,0:T(8,128)(2,1)}, bf16[256,1280]{1,0:T(8,128)(2,1)S(1)}, u32[]{:S(2)}, u32[]{:S(2)}) collective-permute-start(bf16[256,1280]{1,0:T(8,128)(2,1)} %get-tuple-element.399), channel_id=1, source_target_pairs={{0,2},{2,0},{4,6},{6,4},{1,3},{3,1},{5,7},{7,5},{8,10},{10,8},{12,... | collective-permute-start | bytes 1966088 | tf_op jit(solution)/shard_map/ppermute | solution.py:961
  430.0 29.2 %collective-permute-start.43 = (bf16[256,1280]{1,0:T(8,128)(2,1)}, bf16[256,1280]{1,0:T(8,128)(2,1)S(1)}, u32[]{:S(2)}, u32[]{:S(2)}) collective-permute-start(bf16[256,1280]{1,0:T(8,128)(2,1)} %get-tuple-element.401), channel_id=1, source_target_pairs={{0,6},{2,4},{4,2},{6,0},{1,7},{3,5},{5,3},{7,1},{8,14},{10,12},{12... | collective-permute-start | bytes 1966088 | tf_op jit(solution)/shard_map/ppermute | solution.py:961
  461.9 26.6 %collective-permute-start.48 = (bf16[256,2048]{1,0:T(8,128)(2,1)S(1)}, bf16[256,2048]{1,0:T(8,128)(2,1)S(1)}, u32[]{:S(2)}, u32[]{:S(2)}) collective-permute-start(bf16[256,2048]{1,0:T(8,128)(2,1)S(1)} %add_convert_fusion), channel_id=1, source_target_pairs={{0,8},{8,16},{16,24},{24,0},{1,9},{9,17},{17,25},{25,1},{2,10},{10... | collective-permute-start | bytes 3145736 | tf_op jit(solution)/shard_map/ppermute | solution.py:1076
  482.4 20.3 %collective-permute-start.49 = (bf16[64,2560]{1,0:T(8,128)(2,1)}, bf16[64,2560]{1,0:T(8,128)(2,1)S(1)}, u32[]{:S(2)}, u32[]{:S(2)}) collective-permute-start(bf16[64,2560]{1,0:T(8,128)(2,1)} %get-tuple-element.427), channel_id=1, source_target_pairs={{0,8},{8,0},{16,24},{24,16},{1,9},{9,1},{17,25},{25,17},{2,10},{10... | collective-permute-start | bytes 983048 | tf_op jit(solution)/shard_map/ppermute | solution.py:961
  483.6 19.9 %collective-permute-start.50 = (bf16[64,2560]{1,0:T(8,128)(2,1)}, bf16[64,2560]{1,0:T(8,128)(2,1)S(1)}, u32[]{:S(2)}, u32[]{:S(2)}) collective-permute-start(bf16[64,2560]{1,0:T(8,128)(2,1)} %get-tuple-element.428), channel_id=1, source_target_pairs={{0,16},{8,24},{16,0},{24,8},{1,17},{9,25},{17,1},{25,9},{2,18},{10... | collective-permute-start | bytes 983048 | tf_op jit(solution)/shard_map/ppermute | solution.py:961
  484.7 24.9 %collective-permute-start.51 = (bf16[64,2560]{1,0:T(8,128)(2,1)}, bf16[64,2560]{1,0:T(8,128)(2,1)S(1)}, u32[]{:S(2)}, u32[]{:S(2)}) collective-permute-start(bf16[64,2560]{1,0:T(8,128)(2,1)} %get-tuple-element.429), channel_id=1, source_target_pairs={{0,24},{8,16},{16,8},{24,0},{1,25},{9,17},{17,9},{25,1},{2,26},{10... | collective-permute-start | bytes 983048 | tf_op jit(solution)/shard_map/ppermute | solution.py:961
  (99 other events, 1103.3 us)
Sparse Core Ops, SparseCore 0:
  11.7 101.3 all-gather.2
  115.8 77.3 all-gather.4
  265.0 99.3 reduce-scatter.1
